TPU v7x, 32 devices: a whole 2x2x4 slice. The times are simulated.
32 devices in a mesh: row: 2 (over y), col: 4 (over x, core), band: 4 (over z).
Axes of the slice: x: 2, y: 2, z: 4, core: 2. Of those that a mesh axis runs over, the one named last changes fastest.
Arguments:
- vis: bfloat16 [64, 4, 2, 512, 512], P('band', None, None, 'row', 'col'), may hold values from -200 to 200
- flags: int32 [64, 4, 512], P('band'), may hold values 0 or 1
- positions: float32 [4, 3, 512], replicated, may hold values from -4 to 4
- lmn: float32 [3, 8], replicated, may hold values from -3 to 3
- flux: float32 [64, 8], P('band'), may hold values from 0.5 to 2
- gains: float32 [64, 4, 2, 8, 512], P('band', None, None, None, ('row', 'col')), may hold values from -6 to 6
- duals: float32 [64, 4, 2, 8, 512], P('band', None, None, None, ('row', 'col')), may hold values from -2 to 2
Outputs:
- gains_out: float32 [64, 4, 2, 8, 512], P('band', None, None, None, ('row', 'col'))
- duals_out: float32 [64, 4, 2, 8, 512], P('band', None, None, None, ('row', 'col'))
All inputs are finite; a program needn't handle non-finite values. No bound on the sum of `flags` on one device may be relied on, other than what follows from the above.
Results may differ from a plain program's by a relative error of at most 0.0003.
Values sent between devices are 32-bit elements; how exact they have to be, the bound alone decides.
No kernel may reach another device: no remote copies, remote signals or barrier semaphores. Data moves between devices by JAX's collectives and lax.ppermute only.
A program may use at most 128 MiB of HBM per device.

v0:
```python
import math

import jax
import jax.numpy as jnp
from jax import lax
from jax.sharding import PartitionSpec as P

S = 512
F = 64
ITERS = 2


PENALTY = 0.05
HIGH = lax.Precision.HIGHEST


def basis(count):
    grid = 2.0 * jnp.arange(count, dtype=jnp.float32) / (count - 1) - 1.0
    return jnp.stack([grid**power for power in range(4)], axis=1)


def rotate(positions, lmn, freq):
    geometry = jnp.einsum("tks,kd->tds", positions, lmn, precision=HIGH)
    angle = 2.0 * math.pi * freq[:, None, None, None] * geometry[None]
    return (jnp.cos(angle), -jnp.sin(angle))


def complex_mul(a_re, a_im, b_re, b_im):
    return (a_re * b_re - a_im * b_im, a_re * b_im + a_im * b_re)


def solve_fit(rhs):
    full = basis(F)
    gram = jnp.dot(full.T, full, precision=HIGH)
    factor = jnp.linalg.cholesky(gram)
    flat = rhs.reshape(rhs.shape[0], -1)
    return jax.scipy.linalg.cho_solve((factor, True), flat).reshape(rhs.shape)


def shards(vis, flags, positions, lmn, flux, gains, duals):
    width = gains.shape[0]
    first = lax.axis_index("band") * width
    local_basis = lax.dynamic_slice_in_dim(basis(F), first, width, 0)
    freq = 1.0 + (first + jnp.arange(width, dtype=jnp.int32)).astype(jnp.float32) / F
    row_index = lax.axis_index("row")
    col_index = lax.axis_index("col")
    row_count = vis.shape[3]
    col_count = vis.shape[4]
    owned = gains.shape[4]
    own_start = (row_index * lax.axis_size("col") + col_index) * owned
    row_start = row_index * row_count
    col_start = col_index * col_count
    own_cos, own_sin = rotate(lax.dynamic_slice_in_dim(positions, own_start, owned, 2), lmn, freq)
    row_cos, row_sin = rotate(
        lax.dynamic_slice_in_dim(positions, row_start, row_count, 2), lmn, freq
    )
    col_cos, col_sin = rotate(
        lax.dynamic_slice_in_dim(positions, col_start, col_count, 2), lmn, freq
    )
    all_live = flags.astype(jnp.float32)
    row_live = lax.dynamic_slice_in_dim(all_live, row_start, row_count, 2)
    col_live = lax.dynamic_slice_in_dim(all_live, col_start, col_count, 2)
    own_live = lax.dynamic_slice_in_dim(all_live, own_start, owned, 2)
    row_ids = row_start + jnp.arange(row_count, dtype=jnp.int32)
    col_ids = col_start + jnp.arange(col_count, dtype=jnp.int32)
    distinct = (row_ids[:, None] != col_ids[None, :]).astype(jnp.float32)
    weight = row_live[:, :, :, None] * col_live[:, :, None, :] * distinct
    vis_re = vis[:, :, 0].astype(jnp.float32)
    vis_im = vis[:, :, 1].astype(jnp.float32)
    scale = flux[:, None, :, None]

    def fit(gain, dual):
        rhs = jnp.einsum("fk,ftcds->ktcds", local_basis, gain + dual, precision=HIGH)
        return solve_fit(lax.psum(rhs, "band"))

    gain, dual = (gains, duals)
    coeffs = fit(gain, dual)
    for step in range(ITERS):
        target = jnp.einsum("fk,ktcds->ftcds", local_basis, coeffs, precision=HIGH) - dual
        every = lax.all_gather(gain, ("row", "col"), axis=4, tiled=True)
        row_gain = lax.dynamic_slice_in_dim(every, row_start, row_count, 4)
        col_gain = lax.dynamic_slice_in_dim(every, col_start, col_count, 4)
        row_re, row_im = complex_mul(row_gain[:, :, 0], row_gain[:, :, 1], row_cos, row_sin)
        col_re, col_im = complex_mul(col_gain[:, :, 0], col_gain[:, :, 1], col_cos, col_sin)
        col_re = scale * col_re
        col_im = scale * col_im
        model_re = jnp.einsum("ftdp,ftdq->ftpq", row_re, col_re, precision=HIGH) + jnp.einsum(
            "ftdp,ftdq->ftpq", row_im, col_im, precision=HIGH
        )
        model_im = jnp.einsum("ftdp,ftdq->ftpq", row_im, col_re, precision=HIGH) - jnp.einsum(
            "ftdp,ftdq->ftpq", row_re, col_im, precision=HIGH
        )
        resid_re = weight * (vis_re - model_re)
        resid_im = weight * (vis_im - model_im)
        squares, samples = lax.psum(
            (jnp.sum(resid_re * resid_re + resid_im * resid_im), jnp.sum(weight)),
            ("row", "col", "band"),
        )
        sum_re = jnp.einsum("ftpq,ftdq->ftdp", resid_re, col_re, precision=HIGH) - jnp.einsum(
            "ftpq,ftdq->ftdp", resid_im, col_im, precision=HIGH
        )
        sum_im = jnp.einsum("ftpq,ftdq->ftdp", resid_re, col_im, precision=HIGH) + jnp.einsum(
            "ftpq,ftdq->ftdp", resid_im, col_re, precision=HIGH
        )
        pairs = lax.psum_scatter(
            jnp.stack([sum_re, sum_im], axis=2), "col", scatter_dimension=4, tiled=True
        )
        every_mag = every[:, :, 0] * every[:, :, 0] + every[:, :, 1] * every[:, :, 1]
        total_mag = jnp.einsum("ftds,fts->ftd", every_mag, all_live, precision=HIGH)
        own_mag = gain[:, :, 0] * gain[:, :, 0] + gain[:, :, 1] * gain[:, :, 1]
        own_flag = own_live[:, :, None, :]
        own_denom = (scale * scale * own_flag * (total_mag[:, :, :, None] - own_flag * own_mag))[
            :, :, None
        ]
        num_re, num_im = complex_mul(own_cos, -own_sin, pairs[:, :, 0], pairs[:, :, 1])
        numer = jnp.stack([num_re, num_im], axis=2)
        rho = PENALTY * S * (squares / samples + 1e-06)
        fresh = (numer + own_denom * gain + rho * target) / (own_denom + rho)
        gain = 0.5 * (gain + fresh)
        coeffs = fit(gain, dual)
        dual = dual + gain - jnp.einsum("fk,ktcds->ftcds", local_basis, coeffs, precision=HIGH)
    return (gain, dual)


def solution(mesh):
    return jax.shard_map(
        shards,
        mesh=mesh,
        in_specs=(
            P("band", None, None, "row", "col"),
            P("band", None, None),
            P(),
            P(),
            P("band", None),
            P("band", None, None, None, ("row", "col")),
            P("band", None, None, None, ("row", "col")),
        ),
        out_specs=(
            P("band", None, None, None, ("row", "col")),
            P("band", None, None, None, ("row", "col")),
        ),
        check_vma=False,
    )
```

profile of v0, /device:TPU:0, one launch (start us, length us, event | category | flops | bytes accessed | tf_op | source)
XLA Modules:
  0.0 711.8 jit_solution(12807473664040143431)
XLA Ops:
  8.1 3.9 copy.135
  20.6 84.0 %all-gather.3.cloned.1.call-done = f32[16,4,2,8,512]{0,3,2,1,4:T(8,128)} async-done(((f32[16,4,2,8,64]{0,3,2,1,4:T(8,128)}), f32[16,4,2,8,512]{0,3,2,1,4:T(8,128)}) %all-gather.3.cloned.1.call-update) | async-done | bytes 2097168 | tf_op jit(solution)/shard_map/all_gather | solution.py:80
  104.6 4.0 constant_dynamic-slice_fusion.3
  108.6 2.7 copy.192
  112.7 7.7 %constant_dynamic-slice_fusion.2 = (f32[16,4,1,8,256]{0,3,2,1,4:T(8,128)}, f32[16,4,1,8,256]{0,3,2,1,4:T(8,128)}) fusion(f32[16,4,2,8,512]{0,3,2,1,4:T(8,128)} %all-gather.3.cloned.1.call-done, s32[]{:T(128)S(6)} %select_n.24, s32[]{:T(128)S(6)} %add.262), kind=kLoop, calls=%fused_computation.128 | loop fusion | bytes 2097160 | tf_op jit(solution)/shard_map/slice | solution.py:83
  120.4 3.8 copy.197
  124.1 3.8 copy.195
  129.4 16.0 %fusion.122 = f32[16,4,256,128]{3,2,1,0:T(8,128)S(1)} fusion(f32[16,4,8,128]{3,2,1,0:T(8,128)S(1)} %get-tuple-element.34, f32[16,4,1,8,256]{4,3,1,0,2:T(8,128)S(1)} %copy.197, f32[16,4,1,8,256]{4,3,1,0,2:T(8,128)S(1)} %copy.195, f32[4,8,256]{2,1,0:T(8,128)S(1)} %convolution_bitcast_fusion, f32[16]{0:T(128)S(1)} %add_multiply_fusion), kind=kOutput, calls=%fused_computation.178 | convolution fusion | flops 201981952 | bytes 9732160 | tf_op jit(solution)/shard_map/ftdp,ftdq->ftpq/dot_general | solution.py:87
  145.4 15.8 %fusion.118 = f32[16,4,256,128]{3,2,1,0:T(8,128)S(1)} fusion(f32[16,4,8,128]{3,2,1,0:T(8,128)S(1)} %get-tuple-element.34, f32[16,4,1,8,256]{4,3,1,0,2:T(8,128)S(1)} %copy.197, f32[16,4,1,8,256]{4,3,1,0,2:T(8,128)S(1)} %copy.195, f32[4,8,256]{2,1,0:T(8,128)S(1)} %convolution_bitcast_fusion, f32[16]{0:T(128)S(1)} %add_multiply_fusion), kind=kOutput, calls=%fused_computation.177 | convolution fusion | flops 201981952 | bytes 9732160 | tf_op jit(solution)/shard_map/ftdp,ftdq->ftpq/dot_general | solution.py:90
  161.3 19.3 %fusion = f32[16,4,256,128]{3,2,1,0:T(8,128)S(1)} fusion(f32[16,4,256,128]{3,2,1,0:T(8,128)S(1)} %fusion.122, f32[256,128]{1,0:T(8,128)S(1)} %compare_convert_fusion, f32[16,4,128]{2,1,0:T(4,128)S(1)} %constant_dynamic-slice_fusion.10, f32[16,4,256]{2,1,0:T(4,128)S(1)} %constant_dynamic-slice_fusion.11, bf16[16,4,2,256,128]{4,3,2,1,0:T(8,128)(2,1)S(1)} %bitcast.197, ...), kind=kOutput, calls=%fused_computation.4 | convolution fusion | flops 214564864 | bytes 22544448 | tf_op jit(solution)/shard_map/ftdp,ftdq->ftpq/dot_general | solution.py:87
  180.6 7.4 %fusion.128 = f32[16,4,8,256]{3,2,1,0:T(8,128)S(1)} fusion(f32[16,4,8,128]{3,2,1,0:T(8,128)S(1)} %get-tuple-element.35, f32[16,4,256,128]{3,2,1,0:T(8,128)S(1)} %fusion), kind=kOutput, calls=%fused_computation.182 | convolution fusion | flops 201326592 | bytes 9175040 | tf_op jit(solution)/shard_map/ftpq,ftdq->ftdp/dot_general | solution.py:102
  188.0 7.0 fusion.127
  195.0 20.0 %add_reduce_fusion.1 = (f32[]{:T(128)}, f32[16,4,256,128]{3,2,1,0:T(8,128)S(1)}) fusion(f32[16,4,256,128]{3,2,1,0:T(8,128)S(1)} %fusion, f32[16,4,256,128]{3,2,1,0:T(8,128)S(1)} %fusion.118, f32[16,4,8,128]{3,2,1,0:T(8,128)S(1)} %get-tuple-element.35, f32[16,4,1,8,256]{4,3,1,0,2:T(8,128)S(1)} %copy.197, f32[16,4,1,8,256]{4,3,1,0,2:T(8,128)S(1)} %copy.195, ...), kind=kOutput, calls=%fused_computation.21 | convolution fusion | flops 222953472 | bytes 30933060 | tf_op jit(solution)/shard_map/ftdp,ftdq->ftpq/dot_general | solution.py:90
  215.0 7.0 fusion.14
  222.1 7.4 %fusion.13 = f32[16,4,1,8,256]{4,3,1,0,2:T(8,128)S(1)} fusion(f32[16,4,8,256]{3,2,1,0:T(8,128)S(1)} %fusion.127, f32[16,4,8,128]{3,2,1,0:T(8,128)S(1)} %get-tuple-element.35, f32[16,4,256,128]{3,2,1,0:T(8,128)S(1)} %get-tuple-element.41), kind=kOutput, calls=%fused_computation.30 | convolution fusion | flops 201457664 | bytes 9699328 | tf_op jit(solution)/shard_map/ftpq,ftdq->ftdp/dot_general | solution.py:99
  229.6 12.1 %copy.182 = f32[16,4,2,8,256]{3,1,0,2,4:T(4,128)} copy(f32[16,4,2,8,256]{4,3,1,0,2:T(8,128)S(1)} %pad_maximum_fusion) | data formatting | bytes 2097152
  241.8 22.3 %reshape.149 = f32[256,1024]{1,0:T(8,128)} reshape(f32[256,2,16,4,8]{4,3,2,1,0:T(4,128)} %bitcast.194) | data formatting | bytes 2097152
  265.7 3.1 fusion.12
  271.0 40.0 %all-reduce = (f32[]{:T(128)}, f32[]{:T(128)}) all-reduce(f32[]{:T(128)} %get-tuple-element.40, f32[]{:T(128)} %fusion.12), channel_id=1, replica_groups=mesh['row'=2,'col'=4,'band'=4] {'row','col','band'}, use_global_device_ids=true, to_apply=%region_2.3 | all-reduce | flops 2 | bytes 16 | tf_op jit(solution)/shard_map/psum | solution.py:95
  312.4 7.0 fusion.11
  319.6 7.2 %reshape.150 = f32[64,2,16,4,8]{4,3,2,1,0:T(4,128)} reshape(f32[64,1024]{1,0:T(8,128)} %reduce-scatter.7.cloned.1.call-done) | data formatting | bytes 524288
  326.8 4.8 fusion.126
  334.0 2.4 copy.199
  337.5 3.0 broadcast_multiply_fusion
  340.5 2.8 copy.155
  346.2 88.0 %all-gather.5.cloned.1.call-done = f32[16,4,2,8,512]{0,3,2,1,4:T(8,128)} async-done(((f32[16,4,2,8,64]{0,3,2,1,4:T(8,128)}), f32[16,4,2,8,512]{0,3,2,1,4:T(8,128)}) %all-gather.5.cloned.1.call-update) | async-done | bytes 2097168 | tf_op jit(solution)/shard_map/all_gather | solution.py:80
  434.2 4.6 constant_dynamic-slice_fusion
  438.8 2.7 copy.203
  441.5 2.7 copy.202
  444.3 7.7 %constant_dynamic-slice_fusion.1 = (f32[16,4,1,8,256]{0,3,2,1,4:T(8,128)}, f32[16,4,1,8,256]{0,3,2,1,4:T(8,128)}) fusion(f32[16,4,2,8,512]{0,3,2,1,4:T(8,128)} %all-gather.5.cloned.1.call-done, s32[]{:T(128)S(6)} %select_n.24, s32[]{:T(128)S(6)} %add.262), kind=kLoop, calls=%fused_computation.127 | loop fusion | bytes 2097160 | tf_op jit(solution)/shard_map/slice | solution.py:83
  451.9 3.8 copy.206
  455.7 3.8 copy.205
  461.1 15.8 %fusion.116 = f32[16,4,256,128]{3,2,1,0:T(8,128)S(1)} fusion(f32[16,4,8,128]{3,2,1,0:T(8,128)S(1)} %get-tuple-element.33, f32[16,4,1,8,256]{4,3,1,0,2:T(8,128)S(1)} %copy.206, f32[16,4,1,8,256]{4,3,1,0,2:T(8,128)S(1)} %copy.205, f32[4,8,256]{2,1,0:T(8,128)S(1)} %convolution_bitcast_fusion, f32[16]{0:T(128)S(1)} %add_multiply_fusion), kind=kOutput, calls=%fused_computation.176 | convolution fusion | flops 201981952 | bytes 9732160 | tf_op jit(solution)/shard_map/ftdp,ftdq->ftpq/dot_general | solution.py:87
  477.0 15.9 %fusion.112 = f32[16,4,256,128]{3,2,1,0:T(8,128)S(1)} fusion(f32[16,4,8,128]{3,2,1,0:T(8,128)S(1)} %get-tuple-element.33, f32[16,4,1,8,256]{4,3,1,0,2:T(8,128)S(1)} %copy.206, f32[16,4,1,8,256]{4,3,1,0,2:T(8,128)S(1)} %copy.205, f32[4,8,256]{2,1,0:T(8,128)S(1)} %convolution_bitcast_fusion, f32[16]{0:T(128)S(1)} %add_multiply_fusion), kind=kOutput, calls=%fused_computation.175 | convolution fusion | flops 201981952 | bytes 9732160 | tf_op jit(solution)/shard_map/ftdp,ftdq->ftpq/dot_general | solution.py:90
  492.9 19.5 %fusion.1 = f32[16,4,256,128]{3,2,1,0:T(8,128)S(1)} fusion(f32[16,4,256,128]{3,2,1,0:T(8,128)S(1)} %fusion.116, f32[256,128]{1,0:T(8,128)S(1)} %compare_convert_fusion, f32[16,4,128]{2,1,0:T(4,128)S(1)} %constant_dynamic-slice_fusion.10, f32[16,4,256]{2,1,0:T(4,128)S(1)} %constant_dynamic-slice_fusion.11, bf16[16,4,2,256,128]{4,3,2,1,0:T(8,128)(2,1)S(1)} %bitcast.199, ...), kind=kOutput, calls=%fused_computation.5 | convolution fusion | flops 214564864 | bytes 22544448 | tf_op jit(solution)/shard_map/ftdp,ftdq->ftpq/dot_general | solution.py:87
  512.3 7.2 %fusion.131 = f32[16,4,8,256]{3,2,1,0:T(8,128)S(1)} fusion(f32[16,4,8,128]{3,2,1,0:T(8,128)S(1)} %get-tuple-element.32, f32[16,4,256,128]{3,2,1,0:T(8,128)S(1)} %fusion.1), kind=kOutput, calls=%fused_computation.185 | convolution fusion | flops 201326592 | bytes 9175040 | tf_op jit(solution)/shard_map/ftpq,ftdq->ftdp/dot_general | solution.py:102
  519.5 7.0 fusion.130
  526.6 20.2 %add_reduce_fusion = (f32[]{:T(128)}, f32[16,4,256,128]{3,2,1,0:T(8,128)S(1)}) fusion(f32[16,4,256,128]{3,2,1,0:T(8,128)S(1)} %fusion.1, f32[16,4,256,128]{3,2,1,0:T(8,128)S(1)} %fusion.112, f32[16,4,8,128]{3,2,1,0:T(8,128)S(1)} %get-tuple-element.32, f32[16,4,1,8,256]{4,3,1,0,2:T(8,128)S(1)} %copy.206, f32[16,4,1,8,256]{4,3,1,0,2:T(8,128)S(1)} %copy.205, ...), kind=kOutput, calls=%fused_computation.20 | convolution fusion | flops 222953472 | bytes 30933060 | tf_op jit(solution)/shard_map/ftdp,ftdq->ftpq/dot_general | solution.py:90
  546.8 7.0 fusion.18
  553.8 7.2 %fusion.17 = f32[16,4,1,8,256]{4,3,1,0,2:T(8,128)S(1)} fusion(f32[16,4,8,256]{3,2,1,0:T(8,128)S(1)} %fusion.130, f32[16,4,8,128]{3,2,1,0:T(8,128)S(1)} %get-tuple-element.32, f32[16,4,256,128]{3,2,1,0:T(8,128)S(1)} %get-tuple-element.45), kind=kOutput, calls=%fused_computation.34 | convolution fusion | flops 201457664 | bytes 9699328 | tf_op jit(solution)/shard_map/ftpq,ftdq->ftdp/dot_general | solution.py:99
  561.1 12.1 %copy.184 = f32[16,4,2,8,256]{3,1,0,2,4:T(4,128)} copy(f32[16,4,2,8,256]{4,3,1,0,2:T(8,128)S(1)} %pad_maximum_fusion.1) | data formatting | bytes 2097152
  573.3 22.3 %reshape.151 = f32[256,1024]{1,0:T(8,128)} reshape(f32[256,2,16,4,8]{4,3,2,1,0:T(4,128)} %bitcast.195) | data formatting | bytes 2097152
  597.2 39.7 %psum.48 = f32[]{:T(128)} all-reduce(f32[]{:T(128)} %get-tuple-element.44), channel_id=1, replica_groups=mesh['row'=2,'col'=4,'band'=4] {'row','col','band'}, use_global_device_ids=true, to_apply=%region_10.0 | all-reduce | flops 1 | bytes 8 | tf_op jit(solution)/shard_map/psum | solution.py:95
  638.3 7.0 fusion.7
  646.3 7.2 %reshape.152 = f32[64,2,16,4,8]{4,3,2,1,0:T(4,128)} reshape(f32[64,1024]{1,0:T(8,128)} %reduce-scatter.9.cloned.1.call-done) | data formatting | bytes 524288
  653.5 4.0 fusion.125
  657.5 2.4 copy.208
  666.8 34.2 %all-reduce.9.cloned.1.call-done = f32[4,4096]{1,0:T(4,128)} async-done(((f32[4,4096]{1,0:T(4,128)}), f32[4,4096]{1,0:T(4,128)}) %all-reduce.9.cloned.1.call-update) | async-done | bytes 65552 | tf_op jit(solution)/shard_map/psum | solution.py:74
  (109 shorter events, 35.9 us)
Async XLA Ops:
  8.0 7.9 %copy-start = (f32[4,3,512]{2,0,1:T(4,128)S(1)}, f32[4,3,512]{2,0,1:T(4,128)}, u32[]{:S(2)}) copy-start(f32[4,3,512]{2,0,1:T(4,128)} %param.12) | copy-start | bytes 73732
  8.0 96.6 %all-gather.3.cloned.1.call-start = ((), (), s32[]{:S(2)}) async-start(), calls=%async_computation.2 | async-start | bytes 18874368 | tf_op jit(solution)/shard_map/all_gather | solution.py:80
  11.9 256.9 %all-reduce.5.cloned.1.call-start = ((), (), s32[]{:S(2)}) async-start(), calls=%async_computation.3 | async-start | bytes 131072 | tf_op jit(solution)/shard_map/psum | solution.py:74
  14.9 304.7 %reduce-scatter.7.cloned.1.call-start = ((), (), s32[]{:S(2)}) async-start(), calls=%async_computation.7 | async-start | bytes 1310720
  129.3 31.9 %slice-start = ((s8[8388608]{0:T(1024)(128)(4,1)}), s8[4194304]{0:T(1024)(128)(4,1)S(1)}, s32[]{:S(2)}) async-start(s8[8388608]{0:T(1024)(128)(4,1)} %bitcast.196), calls=%async_computation.9 | async-start | bytes 8388608
  145.4 15.8 %slice-start.1 = ((s8[8388608]{0:T(1024)(128)(4,1)}), s8[4194304]{0:T(1024)(128)(4,1)S(1)}, s32[]{:S(2)}) async-start(s8[8388608]{0:T(1024)(128)(4,1)} %bitcast.196), calls=%async_computation.10 | async-start | bytes 8388608
  241.8 22.5 %copy-start.2 = (f32[16,4,2,8,64]{4,3,2,1,0:T(8,128)S(1)}, f32[16,4,2,8,64]{4,3,2,1,0:T(8,128)}, u32[]{:S(2)}) copy-start(f32[16,4,2,8,64]{4,3,2,1,0:T(8,128)} %param.15) | copy-start | bytes 786436
  241.8 23.2 %copy-start.6 = (f32[16,8]{0,1:T(8,128)S(1)}, f32[16,8]{0,1:T(8,128)}, u32[]{:S(2)}) copy-start(f32[16,8]{0,1:T(8,128)} %param.14) | copy-start | bytes 1540
  241.8 23.7 %copy-start.7 = (f32[3,8]{1,0:T(4,128)S(1)}, f32[3,8]{1,0:T(4,128)}, u32[]{:S(2)}) copy-start(f32[3,8]{1,0:T(4,128)} %param.13) | copy-start | bytes 292
  264.1 170.0 %all-gather.5.cloned.1.call-start = ((), (), s32[]{:S(2)}) async-start(), calls=%async_computation.4 | async-start | bytes 18874368 | tf_op jit(solution)/shard_map/all_gather | solution.py:80
  319.5 18.0 %copy-start.3 = (f32[16,4,2,8,64]{4,3,2,1,0:T(8,128)S(1)}, f32[16,4,2,8,64]{4,3,2,1,0:T(8,128)}, u32[]{:S(2)}) copy-start(f32[16,4,2,8,64]{4,3,2,1,0:T(8,128)} %param.16) | copy-start | bytes 786436
  340.5 101.0 %copy-start.4 = (f32[16,4,2,8,64]{4,0,3,2,1:T(8,128)}, f32[16,4,2,8,64]{4,0,3,2,1:T(8,128)S(1)}, u32[]{:S(2)}) copy-start(f32[16,4,2,8,64]{4,0,3,2,1:T(8,128)S(1)} %get-tuple-element.42) | copy-start | bytes 786436
  343.4 252.3 %all-reduce.7.cloned.1.call-start = ((), (), s32[]{:S(2)}) async-start(), calls=%async_computation.5 | async-start | bytes 131072 | tf_op jit(solution)/shard_map/psum | solution.py:74
  345.9 300.3 %reduce-scatter.9.cloned.1.call-start = ((), (), s32[]{:S(2)}) async-start(), calls=%async_computation.8 | async-start | bytes 1310720
  461.1 31.7 %slice-start.2 = ((s8[8388608]{0:T(1024)(128)(4,1)}), s8[4194304]{0:T(1024)(128)(4,1)S(1)}, s32[]{:S(2)}) async-start(s8[8388608]{0:T(1024)(128)(4,1)} %bitcast.198), calls=%async_computation.11 | async-start | bytes 8388608
  477.0 15.9 %slice-start.3 = ((s8[8388608]{0:T(1024)(128)(4,1)}), s8[4194304]{0:T(1024)(128)(4,1)S(1)}, s32[]{:S(2)}) async-start(s8[8388608]{0:T(1024)(128)(4,1)} %bitcast.198), calls=%async_computation.12 | async-start | bytes 8388608
  595.6 105.4 %all-reduce.9.cloned.1.call-start = ((), (), s32[]{:S(2)}) async-start(), calls=%async_computation.6 | async-start | bytes 131072 | tf_op jit(solution)/shard_map/psum | solution.py:74
  638.3 7.0 copy-start.5
  653.5 50.8 %copy-start.1 = (f32[4,3,512]{2,0,1:T(4,128)S(1)}, f32[4,3,512]{2,0,1:T(4,128)}, u32[]{:S(2)}) copy-start(f32[4,3,512]{2,0,1:T(4,128)} %param.12) | copy-start | bytes 73732
Sparse Core Ops, SparseCore 0:
  12.1 92.4 all-gather.2
  264.3 24.9 reduce-scatter.6
  343.5 90.6 all-gather.4
  595.7 24.7 reduce-scatter.8
Sparse Core Ops, SparseCore 1:
  15.3 36.8 all-reduce.4
  346.2 35.0 all-reduce.6
  665.9 35.0 all-reduce.8
where the time goes:
time: 719 us; the launch traced here: 712 us
  matrix products  215 us (30%)
  waiting for transfers between devices  206 us (29%)
  local copies, waits for them, and re-layouts  163 us (23%)
  blocking collectives  79.7 us (11%)
  other arithmetic  28.2 us (4%)
  between operations  19 us (3%)
    all_gather x2, waiting for transfers between devices, shards(): every = lax.all_gather(gain, ('row', 'col'), axis=4, tiled=True)  172 us
    unnamed x48, local copies, waits for them, and re-layouts  124 us
    psum x2, blocking collectives, shards(): lax.psum((jnp.sum(resid_re * resid_re + resid_im * resid_im), jnp.sum(wei...  79.7 us
    dot_general x2, matrix products, shards(): jnp.einsum('ftdp,ftdq->ftpq', row_re, col_im, precision=HIGH)  40.2 us
    dot_general x2, matrix products, shards(): jnp.einsum('ftdp,ftdq->ftpq', row_im, col_im, precision=HIGH)  38.7 us
    psum x3, waiting for transfers between devices, fit(): return solve_fit(lax.psum(rhs, 'band'))  34.2 us
    dot_general x2, matrix products, shards(): jnp.einsum('ftdp,ftdq->ftpq', row_re, col_re, precision=HIGH)  31.9 us
    dot_general x2, matrix products, shards(): jnp.einsum('ftdp,ftdq->ftpq', row_im, col_re, precision=HIGH)  31.7 us
  transfers between devices with their start and end apart: 7, of which 3 were waited for; matrix products, arithmetic and copies ran while one was open for 50% of the time, Pallas kernels for 0%

commit v1 on v0

--- a/solution.py
+++ b/solution.py
@@ -1,17 +1,467 @@
+import functools
 import math
 
 import jax
 import jax.numpy as jnp
+import numpy as np
 from jax import lax
+from jax.experimental import pallas as pl
+from jax.experimental.pallas import tpu as pltpu
 from jax.sharding import PartitionSpec as P
 
-S = 512
-F = 64
 ITERS = 2
-
-
 PENALTY = 0.05
 HIGH = lax.Precision.HIGHEST
+CHUNKS = 2
+AXES = ("row", "col", "band")
+
+
+def swap(x):
+    half = x.shape[-1] // 2
+    return pltpu.roll(x, half, x.ndim - 1)
+
+
+def low_lanes(shape):
+    return lax.broadcasted_iota(jnp.int32, shape, len(shape) - 1) < shape[-1] // 2
+
+
+def join_low(a, b):
+    return jnp.where(low_lanes(a.shape), a, swap(b))
+
+
+def join_high(a, b):
+    return jnp.where(low_lanes(a.shape), swap(a), b)
+
+
+def column(ref, index, dirs, lanes):
+    rows = lax.broadcasted_iota(jnp.int32, (dirs, lanes), 0)
+    out = jnp.full((dirs, lanes), ref[0, index], jnp.float32)
+    for d in range(1, dirs):
+        out = jnp.where(rows == d, ref[d, index], out)
+    return out
+
+
+def cos_turns(r):
+    t = 0.25 - jnp.abs(r)
+    x = t * t
+    coef = [(-1) ** n * (2.0 * math.pi) ** (2 * n + 1) / math.factorial(2 * n + 1) for n in range(7)]
+    out = jnp.full_like(x, coef[-1])
+    for c in coef[-2::-1]:
+        out = out * x + c
+    return out * t
+
+
+def rotated(g, e):
+    low = low_lanes(e.shape)
+    turned = swap(e)
+    cos2 = jnp.where(low, e, turned)
+    sin2 = jnp.where(low, -turned, e)
+    return g * cos2 + swap(g) * sin2
+
+
+def counter_rotated(g, e):
+    low = low_lanes(e.shape)
+    turned = swap(e)
+    cos2 = jnp.where(low, e, turned)
+    sin2 = jnp.where(low, -turned, e)
+    return g * cos2 - swap(g) * sin2
+
+
+def start_kernel(dims, pos_ref, lmn_ref, freq_ref, gains_ref, e_ref, g_ref, *p_refs):
+    F, T, D, O, R, C = dims
+    W = 2 * O
+    own = lax.axis_index("row") * C + lax.axis_index("col")
+    first = lax.axis_index("band") * F
+    low = low_lanes((D, W))
+    shape = pos_ref[:, :, :O].shape
+    pos = jnp.zeros(shape, jnp.float32)
+    for k in range(R * C):
+        pos = jnp.where(own == k, pos_ref[:, :, k * O : (k + 1) * O], pos)
+    pos = jnp.concatenate([pos, pos], axis=-1)
+    geometry = []
+    for t in range(T):
+        total = jnp.zeros((D, W), jnp.float32)
+        for k in range(3):
+            rows = lax.broadcasted_iota(jnp.int32, (D, W), 0)
+            lm = jnp.full((D, W), lmn_ref[k, 0], jnp.float32)
+            for d in range(1, D):
+                lm = jnp.where(rows == d, lmn_ref[k, d], lm)
+            total = total + lm * pos[k, t : t + 1, :]
+        geometry.append(total)
+    shift = jnp.where(low, 0.0, 0.25)
+    per = F * T // len(p_refs)
+    for f in range(F):
+        nu = freq_ref[first + f]
+        for t in range(T):
+            ft = f * T + t
+            turns = nu * geometry[t]
+            r = turns - jnp.round(turns) + shift
+            e = cos_turns(r - jnp.round(r))
+            g = jnp.concatenate([gains_ref[f, t, 0], gains_ref[f, t, 1]], axis=-1)
+            e_ref[ft] = e
+            g_ref[ft] = g
+            p_refs[ft // per][ft % per] = rotated(g, e)
+
+
+def fit_kernel(dims, basis_ref, duals_ref, g_ref, u_ref, rhs_ref):
+    F, T, D, O, R, C = dims
+    first = lax.axis_index("band") * F
+    for t in range(T):
+        acc = [jnp.zeros((D, 2 * O), jnp.float32) for _ in range(4)]
+        for f in range(F):
+            ft = f * T + t
+            u = jnp.concatenate([duals_ref[f, t, 0], duals_ref[f, t, 1]], axis=-1)
+            u_ref[ft] = u
+            total = u + g_ref[ft]
+            for k in range(4):
+                acc[k] = acc[k] + basis_ref[first + f, k] * total
+        for k in range(4):
+            rhs_ref[k * T + t] = acc[k]
+
+
+def sum_kernel(dims, offset, flux_ref, live_ref, vis_ref, *refs):
+    F, T, D, O, R, C = dims
+    blocks, (keep_ref, send_ref, distinct) = refs[:R], refs[R:]
+    rows, cols = vis_ref.shape[3], vis_ref.shape[4]
+    step = pl.program_id(0)
+    row = lax.axis_index("row")
+    col = lax.axis_index("col")
+    parity = col % 2
+
+    @pl.when(step == 0)
+    def _():
+        p = lax.broadcasted_iota(jnp.int32, (rows, cols), 0) + row * rows
+        q = lax.broadcasted_iota(jnp.int32, (rows, cols), 1) + col * cols
+        distinct[...] = jnp.where(p == q, 0.0, 1.0).astype(jnp.bfloat16)
+
+    group = vis_ref.shape[0]
+    highs, lows = [], []
+    mask = distinct[...]
+    for i in range(group):
+        scale = column(flux_ref, (offset + step) * group + i, D, cols)
+        for t in range(T):
+            ft = i * T + t
+            a, b = blocks[0][ft], blocks[1][ft]
+            first = jnp.where(row == 0, a, b)
+            second = jnp.where(row == 0, b, a)
+            weight = scale * live_ref[ft : ft + 1, :]
+            re = join_low(first, second) * weight
+            im = join_high(first, second) * weight
+            x = jnp.concatenate(
+                [jnp.concatenate([re, -im], axis=1), jnp.concatenate([im, re], axis=1)], axis=0
+            )
+            high = x.astype(jnp.bfloat16)
+            low = (x - high.astype(jnp.float32)).astype(jnp.bfloat16)
+            highs.append(high)
+            lows.append(low)
+            both = jnp.concatenate([high, low], axis=0)
+            seen = jnp.concatenate([vis_ref[i, t, 0] * mask, vis_ref[i, t, 1] * mask], axis=1)
+            v = lax.dot_general(
+                both, seen, (((1,), (1,)), ((), ())), preferred_element_type=jnp.float32
+            )
+            v = v[: 2 * D] + v[2 * D :]
+            v0, v1 = v[:, : 2 * O], v[:, 2 * O :]
+            even, odd = join_low(v0, v1), join_high(v0, v1)
+            keep_ref[ft] = jnp.where(parity == 0, even, odd)
+            send_ref[ft] = jnp.where(parity == 0, odd, even)
+    high = jnp.concatenate(highs, axis=0)
+    low = jnp.concatenate(lows, axis=0)
+    nt = (((1,), (1,)), ((), ()))
+    gram = lax.dot_general(high, high, nt, preferred_element_type=jnp.float32)
+    gram = gram + lax.dot_general(high, low, nt, preferred_element_type=jnp.float32)
+    gram = gram + lax.dot_general(low, high, nt, preferred_element_type=jnp.float32)
+    gram = jnp.where(block_mask(2 * D), gram, 0.0)
+    folded = gram[: 2 * D]
+    for i in range(1, 8):
+        folded = folded + gram[i * 2 * D : (i + 1) * 2 * D]
+    keep_ref[8] = folded
+    send_ref[8] = folded
+
+
+def block_mask(size):
+    shape = (8 * size, 8 * size)
+    a = lax.broadcasted_iota(jnp.int32, shape, 0) // size
+    b = lax.broadcasted_iota(jnp.int32, shape, 1) // size
+    return a == b
+
+
+def residual_kernel(dims, live_ref, extra_ref, *refs):
+    F, T, D, O, R, C = dims
+    n = CHUNKS
+    keeps, others, mine, theirs = refs[:n], refs[n : 2 * n], refs[2 * n : 3 * n], refs[3 * n : 4 * n]
+    keep_ref, send_ref, scalar_ref = refs[4 * n :]
+    W = 2 * O
+    near = (lax.axis_index("col") // 2) == 0
+    mask = block_mask(2 * D)
+    eye = lax.broadcasted_iota(jnp.int32, (2 * D, W), 0) == (
+        lax.broadcasted_iota(jnp.int32, (2 * D, W), 1) % (2 * D)
+    )
+    groups = F * T // 8
+    per = groups // n
+    total = jnp.zeros((2 * D, W), jnp.float32)
+    for group in range(groups):
+        ch, base = group // per, group % per
+        gram = keeps[ch][base * 9 + 8] + others[ch][base * 9 + 8]
+        diagonal = jnp.sum(jnp.where(eye, gram, 0.0), axis=0, keepdims=True)
+        keep_ref[F * T, group : group + 1, :] = diagonal
+        send_ref[F * T, group : group + 1, :] = diagonal
+        spread = jnp.where(mask, jnp.concatenate([gram] * 8, axis=0), 0.0)
+        station = []
+        for i in range(8):
+            a, b = mine[ch][base * 8 + i], theirs[ch][base * 8 + i]
+            first = jnp.where(near, a, b)
+            second = jnp.where(near, b, a)
+            station += [join_low(first, second), join_high(first, second)]
+        model = jnp.dot(
+            spread, jnp.concatenate(station, axis=0), precision=HIGH,
+            preferred_element_type=jnp.float32,
+        )
+        for i in range(8):
+            ft = group * 8 + i
+            live = live_ref[ft : ft + 1, :]
+            v = keeps[ch][base * 9 + i] + others[ch][base * 9 + i]
+            num = (v - model[i * 2 * D : (i + 1) * 2 * D]) * live
+            z = jnp.concatenate(station[2 * i : 2 * i + 2], axis=0)
+            total = total + z * (v * live + num)
+            low, high = join_low(num[:D], num[D:]), join_high(num[:D], num[D:])
+            keep_ref[ft] = jnp.where(near, low, high)
+            send_ref[ft] = jnp.where(near, high, low)
+    squares = -jnp.sum(total, axis=0, keepdims=True)
+    squares = squares + swap(squares)
+    scalar = jnp.where(low_lanes(squares.shape), squares, 0.0) + extra_ref[...]
+    scalar_ref[...] = jnp.broadcast_to(scalar, scalar_ref.shape)
+
+
+def update_kernel(dims, last, full, *refs):
+    F, T, D, O, R, C = dims
+    n = CHUNKS
+    (flux_ref, basis_ref, coef_ref, keep_ref, come_ref, scalar_ref, live_ref, e_ref, g_ref,
+     u_ref) = refs[:10]
+    refs = refs[10:]
+    p_refs, refs = refs[:n], refs[n:]
+    rhs_refs, refs = refs[:4], refs[4:]
+    first = lax.axis_index("band") * F
+    W = 2 * O
+    sums = jnp.sum(scalar_ref[...], axis=0, keepdims=True)
+    low = low_lanes(sums.shape)
+    squares = jnp.sum(jnp.where(low, sums, 0.0), axis=1, keepdims=True)
+    samples = jnp.sum(jnp.where(low, 0.0, sums), axis=1, keepdims=True)
+    squares = jnp.maximum(squares, 0.0)
+    rho = PENALTY * full * (squares / samples + 1e-06)
+    rho = jnp.broadcast_to(rho, (D, W))
+    eye = lax.broadcasted_iota(jnp.int32, (8 * 2 * D, W), 0) == lax.broadcasted_iota(
+        jnp.int32, (8 * 2 * D, W), 1
+    )
+    rhs_sum = []
+    for k in range(4):
+        rhs_sum.append([rhs_refs[0][k * T + t] + rhs_refs[1][k * T + t]
+                        + rhs_refs[2][k * T + t] + rhs_refs[3][k * T + t] for t in range(T)])
+    acc = [[jnp.zeros((D, W), jnp.float32) for _ in range(T)] for _ in range(4)]
+    per = F * T // n
+    for group in range(F * T // 8):
+        diagonal = keep_ref[F * T, group : group + 1, :] + come_ref[F * T, group : group + 1, :]
+        spread = jnp.sum(jnp.where(eye, jnp.broadcast_to(diagonal, eye.shape), 0.0), axis=1, keepdims=True)
+        for i in range(8):
+            ft = group * 8 + i
+            f, t = ft // T, ft % T
+            live = live_ref[ft : ft + 1, :]
+            flux = column(flux_ref, f, D, W)
+            p = p_refs[ft // per][ft % per]
+            e = e_ref[ft]
+            g = g_ref[ft]
+            u = u_ref[ft]
+            power = p * p
+            power = power + swap(power)
+            own = jnp.sum(flux * power, axis=0, keepdims=True)
+            num = keep_ref[ft] + come_ref[ft] + live * own * flux * p
+            num = counter_rotated(num, e)
+            den = live * (spread[i * 2 * D : i * 2 * D + D] - flux * flux * power)
+            smooth = coef_ref[first + f, 0] * rhs_sum[0][t]
+            for k in range(1, 4):
+                smooth = smooth + coef_ref[first + f, k] * rhs_sum[k][t]
+            if last:
+                u = u + g - smooth
+            target = smooth - u
+            fresh = (num + den * g + rho * target) / (den + rho)
+            g = 0.5 * (g + fresh)
+            total = u + g
+            for k in range(4):
+                acc[k][t] = acc[k][t] + basis_ref[first + f, k] * total
+            if last:
+                out_ref, total_ref, rhs_ref = refs
+                out_ref[f, t, 0] = g[:, :O]
+                out_ref[f, t, 1] = g[:, O:]
+                total_ref[ft] = total
+            else:
+                g_out, rhs_ref = refs[:2]
+                g_out[ft] = g
+                refs[2 + ft // per][ft % per] = rotated(g, e)
+    for k in range(4):
+        for t in range(T):
+            rhs_ref[k * T + t] = acc[k][t]
+
+
+def final_kernel(dims, coef_ref, total_ref, *refs):
+    F, T, D, O, R, C = dims
+    rhs_refs, out_ref = refs[:4], refs[4]
+    first = lax.axis_index("band") * F
+    for t in range(T):
+        rhs = [rhs_refs[0][k * T + t] + rhs_refs[1][k * T + t]
+               + rhs_refs[2][k * T + t] + rhs_refs[3][k * T + t] for k in range(4)]
+        for f in range(F):
+            dual = total_ref[f * T + t]
+            for k in range(4):
+                dual = dual - coef_ref[first + f, k] * rhs[k]
+            out_ref[f, t, 0] = dual[:, :O]
+            out_ref[f, t, 1] = dual[:, O:]
+
+
+def shards(sizes, vis, flags, positions, lmn, flux, gains, duals):
+    R, C, Z = sizes
+    F, T, _, D, O = gains.shape
+    rows, cols = vis.shape[3], vis.shape[4]
+    full = flags.shape[2]
+    total_f = F * Z
+    FT, W = F * T, 2 * O
+    dims = (F, T, D, O, R, C)
+    row = lax.axis_index("row")
+    col = lax.axis_index("col")
+    f32 = jnp.float32
+    sds = jax.ShapeDtypeStruct
+    smem = pl.BlockSpec(memory_space=pltpu.SMEM)
+    vmem = pl.BlockSpec(memory_space=pltpu.VMEM)
+
+    grid = 2.0 * np.arange(total_f, dtype=np.float64) / (total_f - 1) - 1.0
+    basis = np.stack([grid**k for k in range(4)], axis=1)
+    solved = basis @ np.linalg.inv(basis.T @ basis)
+    basis_t = jnp.asarray(basis, f32)
+    coef_t = jnp.asarray(solved, f32)
+    freq_t = jnp.asarray(1.0 + np.arange(total_f) / total_f, f32)
+
+    def where(r, c, z):
+        return (r * C + c) * Z + z
+
+    def permute(x, move):
+        pairs = [
+            (where(r, c, z), where(*move(r, c, z)))
+            for r in range(R) for c in range(C) for z in range(Z)
+        ]
+        return lax.ppermute(x, AXES, pairs)
+
+    def gather(x, m):
+        return permute(x, lambda r, c, z: (((r * C + c) % R + m) % R, (r * C + c) // R, z))
+
+    def bands(x):
+        return [x] + [permute(x, lambda r, c, z, k=k: (r, c, (z + k) % Z)) for k in range(1, Z)]
+
+    live_all = flags.astype(f32).reshape(FT, full)
+    own_start = (row * C + col) * O
+    live_own = lax.dynamic_slice_in_dim(live_all, own_start, O, 1)
+    live_own = jnp.concatenate([live_own, live_own], axis=1)
+    halves = [lax.dynamic_slice_in_dim(live_all, row * rows + (col % 2 + 2 * k) * O, O, 1) for k in range(2)]
+    live_half = jnp.concatenate(halves, axis=1)
+    live_row = lax.dynamic_slice_in_dim(live_all, row * rows, rows, 1)
+    live_col = lax.dynamic_slice_in_dim(live_all, col * cols, cols, 1)
+
+    part = sds((FT // CHUNKS, D, W), f32)
+    whole = sds((FT, D, W), f32)
+    rhs_shape = sds((4 * T, D, W), f32)
+    flux_t = flux.T
+    rot, g, *p = pl.pallas_call(
+        functools.partial(start_kernel, dims),
+        out_shape=[whole, whole] + [part] * CHUNKS,
+        in_specs=[vmem, smem, smem, vmem],
+        out_specs=[vmem] * (2 + CHUNKS),
+        name="start",
+    )(positions.transpose(1, 0, 2), lmn, freq_t, gains)
+    u, rhs = pl.pallas_call(
+        functools.partial(fit_kernel, dims),
+        out_shape=[whole, rhs_shape],
+        in_specs=[smem, vmem, vmem],
+        out_specs=[vmem] * 2,
+        name="fit",
+    )(basis_t, duals, g)
+
+    ids_p = row * rows + jnp.arange(rows, dtype=jnp.int32)
+    ids_q = col * cols + jnp.arange(cols, dtype=jnp.int32)
+    weight = (
+        live_row.reshape(F, T, rows, 1) * live_col.reshape(F, T, 1, cols)
+        * (ids_p[:, None] != ids_q[None, :]).astype(f32)
+    )
+    vis_re, vis_im = vis[:, :, 0].astype(f32), vis[:, :, 1].astype(f32)
+    power = jnp.sum(weight * (vis_re * vis_re + vis_im * vis_im))
+    counts = jnp.sum(live_all, axis=1)
+    samples = jnp.sum(counts * counts - counts) / (R * C)
+
+    group = 8 // T
+    steps = F // CHUNKS // group
+    lanes = lax.broadcasted_iota(jnp.int32, (1, W), 1)
+    for step in range(ITERS):
+        last = step == ITERS - 1
+        got = [[gather(x, m) for m in range(R)] for x in p]
+        theirs = [permute(x, lambda r, c, z: (r, c ^ 2, z)) for x in p]
+        rhs_all = bands(rhs)
+        keeps, comes = [], []
+        for ch in range(CHUNKS):
+            off = ch * steps
+            pair = sds((steps * 9, 2 * D, W), f32)
+            keep, send = pl.pallas_call(
+                functools.partial(sum_kernel, dims, off),
+                grid=(steps,),
+                out_shape=[pair, pair],
+                in_specs=[
+                    smem,
+                    pl.BlockSpec((8, cols), lambda i, off=off: (off + i, 0)),
+                    pl.BlockSpec((group, T, 2, rows, cols), lambda i, off=off: (off + i, 0, 0, 0, 0)),
+                ] + [pl.BlockSpec((8, D, W), lambda i: (i, 0, 0))] * R,
+                out_specs=[pl.BlockSpec((9, 2 * D, W), lambda i: (i, 0, 0))] * 2,
+                scratch_shapes=[pltpu.VMEM((rows, cols), jnp.bfloat16)],
+                name="sums",
+            )(flux_t, live_col, vis, *got[ch])
+            keeps.append(keep)
+            comes.append(permute(send, lambda r, c, z: (r, c ^ 1, z)))
+        own_model = []
+        for ch in range(CHUNKS):
+            x = p[ch].reshape(F // CHUNKS, T, D, 2, O)
+            fl = lax.dynamic_slice_in_dim(flux, ch * (F // CHUNKS), F // CHUNKS, 0)
+            m = jnp.einsum("ftdco,fd->fto", x * x, fl, precision=HIGH)
+            lv = live_own.reshape(F, T, 2 * O)[ch * (F // CHUNKS) : (ch + 1) * (F // CHUNKS), :, :O]
+            own_model.append(jnp.sum(m * m * lv))
+        extra = power - sum(own_model)
+        extra = jnp.where(lanes == 0, extra, 0.0) + jnp.where(lanes == O, samples, 0.0)
+        line = sds((FT + 1, D, W), f32)
+        keep, send, scalar = pl.pallas_call(
+            functools.partial(residual_kernel, dims),
+            out_shape=[line, line, sds((R * C * Z, W), f32)],
+            in_specs=[vmem] * (2 + 4 * CHUNKS),
+            out_specs=[vmem] * 3,
+            name="residual",
+        )(live_half, extra, *keeps, *comes, *p, *theirs)
+        come = permute(send, lambda r, c, z: (r, c ^ 2, z))
+        scalar = lax.all_to_all(scalar, AXES, 0, 0, tiled=True)
+        outs = (
+            [sds(gains.shape, f32), whole, rhs_shape] if last
+            else [whole, rhs_shape] + [part] * CHUNKS
+        )
+        result = pl.pallas_call(
+            functools.partial(update_kernel, dims, last, float(full)),
+            out_shape=outs,
+            in_specs=[smem] * 3 + [vmem] * (7 + CHUNKS + 4),
+            out_specs=[vmem] * len(outs),
+            name="update",
+        )(flux_t, basis_t, coef_t, keep, come, scalar, live_own, rot, g, u, *p, *rhs_all)
+        if last:
+            gain, total, rhs = result
+        else:
+            g, rhs, *p = result
+    dual = pl.pallas_call(
+        functools.partial(final_kernel, dims),
+        out_shape=sds(gains.shape, f32),
+        in_specs=[smem] + [vmem] * 5,
+        out_specs=vmem,
+        name="final",
+    )(coef_t, total, *bands(rhs))
+    return (gain, dual)
 
 
 def basis(count):
@@ -29,19 +479,20 @@
     return (a_re * b_re - a_im * b_im, a_re * b_im + a_im * b_re)
 
 
-def solve_fit(rhs):
-    full = basis(F)
+def solve_fit(rhs, total_f):
+    full = basis(total_f)
     gram = jnp.dot(full.T, full, precision=HIGH)
     factor = jnp.linalg.cholesky(gram)
     flat = rhs.reshape(rhs.shape[0], -1)
     return jax.scipy.linalg.cho_solve((factor, True), flat).reshape(rhs.shape)
 
 
-def shards(vis, flags, positions, lmn, flux, gains, duals):
+def plain_shards(vis, flags, positions, lmn, flux, gains, duals):
     width = gains.shape[0]
+    total_f = width * lax.axis_size("band")
     first = lax.axis_index("band") * width
-    local_basis = lax.dynamic_slice_in_dim(basis(F), first, width, 0)
-    freq = 1.0 + (first + jnp.arange(width, dtype=jnp.int32)).astype(jnp.float32) / F
+    local_basis = lax.dynamic_slice_in_dim(basis(total_f), first, width, 0)
+    freq = 1.0 + (first + jnp.arange(width, dtype=jnp.int32)).astype(jnp.float32) / total_f
     row_index = lax.axis_index("row")
     col_index = lax.axis_index("col")
     row_count = vis.shape[3]
@@ -71,7 +522,7 @@
 
     def fit(gain, dual):
         rhs = jnp.einsum("fk,ftcds->ktcds", local_basis, gain + dual, precision=HIGH)
-        return solve_fit(lax.psum(rhs, "band"))
+        return solve_fit(lax.psum(rhs, "band"), total_f)
 
     gain, dual = (gains, duals)
     coeffs = fit(gain, dual)
@@ -114,7 +565,7 @@
         ]
         num_re, num_im = complex_mul(own_cos, -own_sin, pairs[:, :, 0], pairs[:, :, 1])
         numer = jnp.stack([num_re, num_im], axis=2)
-        rho = PENALTY * S * (squares / samples + 1e-06)
+        rho = PENALTY * flags.shape[2] * (squares / samples + 1e-06)
         fresh = (numer + own_denom * gain + rho * target) / (own_denom + rho)
         gain = 0.5 * (gain + fresh)
         coeffs = fit(gain, dual)
@@ -123,8 +574,16 @@
 
 
 def solution(mesh):
+    sizes = tuple(mesh.shape[a] for a in AXES)
+
+    def body(*args):
+        vis, gains = args[0], args[5]
+        if sizes[0] == 2 and sizes[1:] == (4, 4) and gains.shape[4] == 64 and gains.shape[3] == 8 and 8 % gains.shape[1] == 0:
+            return shards(sizes, *args)
+        return plain_shards(*args)
+
     return jax.shard_map(
-        shards,
+        body,
         mesh=mesh,
         in_specs=(
             P("band", None, None, "row", "col"),

time: 719 us -> 147 us (0.20)
  matrix products: 215 us -> 0.99 us
  waiting for transfers between devices: 206 us -> 19.2 us
  local copies, waits for them, and re-layouts: 163 us -> 9.63 us
  blocking collectives: 79.7 us -> 0 us
  Pallas kernels: 0 us -> 47.7 us
  starting transfers between devices: 0.51 us -> 45.5 us
  between operations: 19 us -> 5.49 us
  other arithmetic: 28.2 us -> 17.1 us
    dot_general x26 -> x4, matrix products: 211 us -> 0.99 us  [shards(): m = jnp.einsum('ftdco,fd->fto', x * x, fl, precision=HIGH)]
    all_gather x2 -> x0, waiting for transfers between devices: 172 us -> none  [shards(): every = lax.all_gather(gain, ('row', 'col'), axis=4, tiled=True)]
    unnamed x48 -> x68, local copies, waits for them, and re-layouts: 124 us -> 7.64 us
    psum x2 -> x0, blocking collectives: 79.7 us -> none  [shards(): lax.psum((jnp.sum(resid_re * resid_re + resid_im * resid_im), jnp.sum(wei...]
    pallas_call x0 -> x11, Pallas kernels: none -> 47.7 us  [the longest x4 20.3 us: shards(): pl.pallas_call(functools.partial(sum_kernel, dims, off), grid=(steps,), o...]
    ppermute x0 -> x27, starting transfers between devices: none -> 37.2 us  [permute(): return lax.ppermute(x, AXES, pairs)]
    psum x3 -> x0, waiting for transfers between devices: 34.2 us -> none  [fit(): return solve_fit(lax.psum(rhs, 'band'))]
    slice x6 -> x0, local copies, waits for them, and re-layouts: 32.8 us -> none  [the longest x2 15.4 us: shards(): row_gain[:, :, 0]]
  transfers between devices with their start and end apart: 7 -> 29, of which waited for: 3 -> 6; matrix products, arithmetic and copies ran while one was open for 50% -> 14% of each run, Pallas kernels for 0% -> 15%
where the time goes in v1:
time: 147 us; the launch traced here: 146 us
  Pallas kernels  47.7 us (32%)
  starting transfers between devices  45.5 us (31%)
  waiting for transfers between devices  19.2 us (13%)
  other arithmetic  17.1 us (12%)
  local copies, waits for them, and re-layouts  9.63 us (7%)
  between operations  5.49 us (4%)
    ppermute x27, starting transfers between devices, permute(): return lax.ppermute(x, AXES, pairs)  37.2 us
    pallas_call x4, Pallas kernels, shards(): pl.pallas_call(functools.partial(sum_kernel, dims, off), grid=(steps,), o...  20.3 us
    pallas_call x2, Pallas kernels, shards(): pl.pallas_call(functools.partial(update_kernel, dims, last, float(full)),...  12.7 us
    all_to_all x2, waiting for transfers between devices, shards(): scalar = lax.all_to_all(scalar, AXES, 0, 0, tiled=True)  12.5 us
    all_to_all x2, starting transfers between devices, shards(): scalar = lax.all_to_all(scalar, AXES, 0, 0, tiled=True)  8.23 us
    unnamed x68, local copies, waits for them, and re-layouts  7.64 us
    ppermute x27, waiting for transfers between devices, permute(): return lax.ppermute(x, AXES, pairs)  6.73 us
    pallas_call x2, Pallas kernels, shards(): pl.pallas_call(functools.partial(residual_kernel, dims), out_shape=[line,...  6.05 us
  transfers between devices with their start and end apart: 29, of which 6 were waited for; matrix products, arithmetic and copies ran while one was open for 14% of the time, Pallas kernels for 15%

profile of v1, /device:TPU:0, one launch (start us, length us, event | category | flops | bytes accessed | tf_op | source)
XLA Modules:
  0.0 145.6 jit_solution(1328106534517910200)
XLA Ops:
  0.6 4.0 %start.1 = (f32[64,8,128]{2,1,0:T(8,128)}, f32[64,8,128]{2,1,0:T(8,128)}, f32[32,8,128]{2,1,0:T(8,128)}, f32[32,8,128]{2,1,0:T(8,128)}) custom-call(f32[3,4,512]{2,1,0:T(4,128)} %bitcast.51, f32[3,8]{1,0:T(4,128)} %lmn_ref.1, f32[64]{0:T(128)} %constant.52.clone.freq_ref, f32[16,4,2,8,64]{4,3,2,1,0:T(8,128)} %gains_ref.1), custom_call_target="tpu_custom_call" | custom-call | tf_op jit(solution)/shard_map/start/pallas_call | solution.py:370
  4.6 1.7 %collective-permute-start = (f32[32,8,128]{2,1,0:T(8,128)}, f32[32,8,128]{2,1,0:T(8,128)S(1)}, u32[]{:S(2)}, u32[]{:S(2)}) collective-permute-start(f32[32,8,128]{2,1,0:T(8,128)} %get-tuple-element.29.refs_4_.refs_10_), channel_id=1, source_target_pairs={{0,0},{1,1},{2,2},{3,3},{4,16},{5,17},{6,18},{7,19},{8,4},{9,5},{1... | collective-permute-start | bytes 393224 | tf_op jit(solution)/shard_map/ppermute | solution.py:349
  6.3 4.8 %collective-permute-start.1 = (f32[32,8,128]{2,1,0:T(8,128)}, f32[32,8,128]{2,1,0:T(8,128)S(1)}, u32[]{:S(2)}, u32[]{:S(2)}) collective-permute-start(f32[32,8,128]{2,1,0:T(8,128)} %get-tuple-element.29.refs_4_.refs_10_), channel_id=1, source_target_pairs={{0,16},{1,17},{2,18},{3,19},{4,0},{5,1},{6,2},{7,3},{8,20},{9,21},... | collective-permute-start | bytes 393224 | tf_op jit(solution)/shard_map/ppermute | solution.py:349
  11.1 1.6 %collective-permute-start.2 = (f32[32,8,128]{2,1,0:T(8,128)}, f32[32,8,128]{2,1,0:T(8,128)S(1)}, u32[]{:S(2)}, u32[]{:S(2)}) collective-permute-start(f32[32,8,128]{2,1,0:T(8,128)} %get-tuple-element.30.refs_5_.refs_11_), channel_id=1, source_target_pairs={{0,0},{1,1},{2,2},{3,3},{4,16},{5,17},{6,18},{7,19},{8,4},{9,5},{1... | collective-permute-start | bytes 393224 | tf_op jit(solution)/shard_map/ppermute | solution.py:349
  12.7 3.1 %collective-permute-start.3 = (f32[32,8,128]{2,1,0:T(8,128)}, f32[32,8,128]{2,1,0:T(8,128)S(1)}, u32[]{:S(2)}, u32[]{:S(2)}) collective-permute-start(f32[32,8,128]{2,1,0:T(8,128)} %get-tuple-element.30.refs_5_.refs_11_), channel_id=1, source_target_pairs={{0,16},{1,17},{2,18},{3,19},{4,0},{5,1},{6,2},{7,3},{8,20},{9,21},... | collective-permute-start | bytes 393224 | tf_op jit(solution)/shard_map/ppermute | solution.py:349
  15.8 1.0 mul.130
  16.8 1.0 mul.124
  17.8 0.9 convert_element_type.18
  18.7 1.0 convert_reduce_fusion
  20.0 0.8 slice_bitcast_fusion.1
  22.6 6.0 %fusion = f32[]{:T(128)} fusion(bf16[16,4,2,256,128]{4,3,2,1,0:T(8,128)(2,1)} %vis_ref.7, f32[256,128]{1,0:T(8,128)S(1)} %compare_convert_fusion, f32[16,4,128]{2,1,0:T(4,128)S(1)} %bitcast.36, f32[16,4,256]{2,1,0:T(4,128)S(1)} %mul.113), kind=kLoop, calls=%fused_computation.1 | loop fusion | flops 18874368 | bytes 8617988 | tf_op jit(solution)/shard_map/reduce_sum | solution.py:392
  31.2 2.1 %collective-permute-start.7 = (f32[32,8,128]{2,1,0:T(8,128)S(1)}, f32[32,8,128]{2,1,0:T(8,128)S(1)}, u32[]{:S(2)}, u32[]{:S(2)}) collective-permute-start(f32[32,8,128]{2,1,0:T(8,128)S(1)} %copy-done), channel_id=1, source_target_pairs={{0,8},{1,9},{2,10},{3,11},{4,12},{5,13},{6,14},{7,15},{8,0},{9,1},... | collective-permute-start | bytes 393224 | tf_op jit(solution)/shard_map/ppermute | solution.py:349
  33.4 0.6 copy-done.13
  34.0 5.1 %sums.4 = (f32[36,16,128]{2,1,0:T(8,128)}, f32[36,16,128]{2,1,0:T(8,128)}) custom-call(f32[8,16]{1,0:T(8,128)} %bitcast.39, f32[64,128]{1,0:T(8,128)} %copy-done.1, bf16[16,4,2,256,128]{4,3,2,1,0:T(8,128)(2,1)} %vis_ref.7, f32[32,8,128]{2,1,0:T(8,128)} %copy-done.12, f32[32,8,128]{2,1,0:T(8,128)} %copy-done.13), custom_call_target="tpu_custom_call" | custom-call | tf_op jit(solution)/shard_map/sums/pallas_call | solution.py:408
  39.7 0.7 copy-done.11
  40.4 5.1 %sums.5 = (f32[36,16,128]{2,1,0:T(8,128)}, f32[36,16,128]{2,1,0:T(8,128)}) custom-call(f32[8,16]{1,0:T(8,128)} %bitcast.40, f32[64,128]{1,0:T(8,128)} %copy-done.1, bf16[16,4,2,256,128]{4,3,2,1,0:T(8,128)(2,1)} %vis_ref.7, f32[32,8,128]{2,1,0:T(8,128)} %copy-done.10, f32[32,8,128]{2,1,0:T(8,128)} %copy-done.11), custom_call_target="tpu_custom_call" | custom-call | tf_op jit(solution)/shard_map/sums/pallas_call | solution.py:408
  47.9 0.7 pad_maximum_fusion.live_ref
  49.5 3.0 %residual.2 = (f32[65,8,128]{2,1,0:T(8,128)}, f32[65,8,128]{2,1,0:T(8,128)}, f32[32,128]{1,0:T(8,128)}) custom-call(f32[64,128]{1,0:T(8,128)} %pad_maximum_fusion.live_ref, f32[1,128]{1,0:T(1,128)} %fusion.2.extra_ref, f32[36,16,128]{2,1,0:T(8,128)} %get-tuple-element.31.refs_0_, f32[36,16,128]{2,1,0:T(8,128)} %get-tuple-element.32.refs_1_, ...), custom_call_target="tpu_custom_call" | custom-call | tf_op jit(solution)/shard_map/residual/pallas_call | solution.py:433
  52.5 2.2 %fit.1 = (f32[64,8,128]{2,1,0:T(8,128)}, f32[16,8,128]{2,1,0:T(8,128)}) custom-call(f32[64,4]{1,0:T(8,128)} %constant.50.clone.basis_ref.refs_1_, f32[16,4,2,8,64]{4,3,2,1,0:T(8,128)} %duals_ref.1, f32[64,8,128]{2,1,0:T(8,128)} %get-tuple-element.39.g_ref.refs_8_), custom_call_target="tpu_custom_call" | custom-call | tf_op jit(solution)/shard_map/fit/pallas_call | solution.py:377
  54.7 2.6 %collective-permute-start.10 = (f32[16,8,128]{2,1,0:T(8,128)}, f32[16,8,128]{2,1,0:T(8,128)S(1)}, u32[]{:S(2)}, u32[]{:S(2)}) collective-permute-start(f32[16,8,128]{2,1,0:T(8,128)} %get-tuple-element.41.refs_12_), channel_id=1, source_target_pairs={{0,2},{1,3},{2,0},{3,1},{4,6},{5,7},{6,4},{7,5},{8,10},{9,11},{10,... | collective-permute-start | bytes 196616 | tf_op jit(solution)/shard_map/ppermute | solution.py:349
  57.3 1.3 collective-permute-start.11
  58.7 0.7 collective-permute-start.9
  59.4 5.0 %all-to-all-start = ((f32[32,1,128]{2,1,0:T(1,128)}), f32[32,1,128]{2,1,0:T(1,128)S(1)}, u32[]{:S(2)}, u32[]{:S(2)}) async-start(f32[32,1,128]{2,1,0:T(1,128)} %bitcast.52), calls=%async_computation | async-start | bytes 32768 | tf_op jit(solution)/shard_map/all_to_all | solution.py:441
  65.0 6.6 %all-to-all-done = f32[32,1,128]{2,1,0:T(1,128)S(1)} async-done(((f32[32,1,128]{2,1,0:T(1,128)}), f32[32,1,128]{2,1,0:T(1,128)S(1)}, u32[]{:S(2)}, u32[]{:S(2)}) %all-to-all-start) | async-done | bytes 16416 | tf_op jit(solution)/shard_map/all_to_all | solution.py:441
  72.2 6.3 %update.2 = (f32[64,8,128]{2,1,0:T(8,128)}, f32[16,8,128]{2,1,0:T(8,128)}, f32[32,8,128]{2,1,0:T(8,128)}, f32[32,8,128]{2,1,0:T(8,128)}) custom-call(f32[8,16]{1,0:T(8,128)} %bitcast.41, f32[64,4]{1,0:T(8,128)} %constant.50.clone.basis_ref.refs_1_, f32[64,4]{1,0:T(8,128)} %constant.51.clone.refs_2_.coef_ref, f32[65,8,128]{2,1,0:T(8,128)} %get-tuple-element.35.refs_3_, ...), custom_call_target="tpu_custom_call" | custom-call | tf_op jit(solution)/shard_map/update/pallas_call | solution.py:446
  78.6 1.6 %collective-permute-start.14 = (f32[32,8,128]{2,1,0:T(8,128)}, f32[32,8,128]{2,1,0:T(8,128)S(1)}, u32[]{:S(2)}, u32[]{:S(2)}) collective-permute-start(f32[32,8,128]{2,1,0:T(8,128)} %get-tuple-element.43.refs_5_.refs_11_), channel_id=1, source_target_pairs={{0,0},{1,1},{2,2},{3,3},{4,16},{5,17},{6,18},{7,19},{8,4},{9,5},{1... | collective-permute-start | bytes 393224 | tf_op jit(solution)/shard_map/ppermute | solution.py:349
  80.1 2.5 %collective-permute-start.15 = (f32[32,8,128]{2,1,0:T(8,128)}, f32[32,8,128]{2,1,0:T(8,128)S(1)}, u32[]{:S(2)}, u32[]{:S(2)}) collective-permute-start(f32[32,8,128]{2,1,0:T(8,128)} %get-tuple-element.43.refs_5_.refs_11_), channel_id=1, source_target_pairs={{0,16},{1,17},{2,18},{3,19},{4,0},{5,1},{6,2},{7,3},{8,20},{9,21},... | collective-permute-start | bytes 393224 | tf_op jit(solution)/shard_map/ppermute | solution.py:349
  82.6 1.6 %collective-permute-start.12 = (f32[32,8,128]{2,1,0:T(8,128)}, f32[32,8,128]{2,1,0:T(8,128)S(1)}, u32[]{:S(2)}, u32[]{:S(2)}) collective-permute-start(f32[32,8,128]{2,1,0:T(8,128)} %get-tuple-element.42.refs_4_.refs_10_), channel_id=1, source_target_pairs={{0,0},{1,1},{2,2},{3,3},{4,16},{5,17},{6,18},{7,19},{8,4},{9,5},{1... | collective-permute-start | bytes 393224 | tf_op jit(solution)/shard_map/ppermute | solution.py:349
  84.1 2.3 %collective-permute-start.13 = (f32[32,8,128]{2,1,0:T(8,128)}, f32[32,8,128]{2,1,0:T(8,128)S(1)}, u32[]{:S(2)}, u32[]{:S(2)}) collective-permute-start(f32[32,8,128]{2,1,0:T(8,128)} %get-tuple-element.42.refs_4_.refs_10_), channel_id=1, source_target_pairs={{0,16},{1,17},{2,18},{3,19},{4,0},{5,1},{6,2},{7,3},{8,20},{9,21},... | collective-permute-start | bytes 393224 | tf_op jit(solution)/shard_map/ppermute | solution.py:349
  86.4 1.0 mul.135
  87.4 1.0 mul.139
  90.1 1.8 %collective-permute-start.19 = (f32[32,8,128]{2,1,0:T(8,128)}, f32[32,8,128]{2,1,0:T(8,128)S(1)}, u32[]{:S(2)}, u32[]{:S(2)}) collective-permute-start(f32[32,8,128]{2,1,0:T(8,128)} %get-tuple-element.43.refs_5_.refs_11_), channel_id=1, source_target_pairs={{0,8},{1,9},{2,10},{3,11},{4,12},{5,13},{6,14},{7,15},{8,0},{9,1},... | collective-permute-start | bytes 393224 | tf_op jit(solution)/shard_map/ppermute | solution.py:349
  91.9 0.7 copy-done.17
  92.6 5.1 %sums.7 = (f32[36,16,128]{2,1,0:T(8,128)}, f32[36,16,128]{2,1,0:T(8,128)}) custom-call(f32[8,16]{1,0:T(8,128)} %bitcast.42, f32[64,128]{1,0:T(8,128)} %copy-done.1, bf16[16,4,2,256,128]{4,3,2,1,0:T(8,128)(2,1)} %vis_ref.7, f32[32,8,128]{2,1,0:T(8,128)} %copy-done.16, f32[32,8,128]{2,1,0:T(8,128)} %copy-done.17), custom_call_target="tpu_custom_call" | custom-call | tf_op jit(solution)/shard_map/sums/pallas_call | solution.py:408
  98.3 0.7 copy-done.15
  99.0 5.1 %sums.6 = (f32[36,16,128]{2,1,0:T(8,128)}, f32[36,16,128]{2,1,0:T(8,128)}) custom-call(f32[8,16]{1,0:T(8,128)} %bitcast.43, f32[64,128]{1,0:T(8,128)} %copy-done.1, bf16[16,4,2,256,128]{4,3,2,1,0:T(8,128)(2,1)} %vis_ref.7, f32[32,8,128]{2,1,0:T(8,128)} %copy-done.14, f32[32,8,128]{2,1,0:T(8,128)} %copy-done.15), custom_call_target="tpu_custom_call" | custom-call | tf_op jit(solution)/shard_map/sums/pallas_call | solution.py:408
  104.8 0.7 multiply_reduce_fusion
  108.8 3.0 %residual.3 = (f32[65,8,128]{2,1,0:T(8,128)}, f32[65,8,128]{2,1,0:T(8,128)}, f32[32,128]{1,0:T(8,128)}) custom-call(f32[64,128]{1,0:T(8,128)} %pad_maximum_fusion.live_ref, f32[1,128]{1,0:T(1,128)} %fusion.3.extra_ref, f32[36,16,128]{2,1,0:T(8,128)} %get-tuple-element.44.refs_0_, f32[36,16,128]{2,1,0:T(8,128)} %get-tuple-element.45.refs_1_, ...), custom_call_target="tpu_custom_call" | custom-call | tf_op jit(solution)/shard_map/residual/pallas_call | solution.py:433
  113.5 2.7 %collective-permute-start.23 = (f32[16,8,128]{2,1,0:T(8,128)S(1)}, f32[16,8,128]{2,1,0:T(8,128)S(1)}, u32[]{:S(2)}, u32[]{:S(2)}) collective-permute-start(f32[16,8,128]{2,1,0:T(8,128)S(1)} %copy-done.24), channel_id=1, source_target_pairs={{0,3},{1,0},{2,1},{3,2},{4,7},{5,4},{6,5},{7,6},{8,11},{9,8},{10,9... | collective-permute-start | bytes 196616 | tf_op jit(solution)/shard_map/ppermute | solution.py:349
  116.2 3.3 %all-to-all-start.1 = ((f32[32,1,128]{2,1,0:T(1,128)}), f32[32,1,128]{2,1,0:T(1,128)S(1)}, u32[]{:S(2)}, u32[]{:S(2)}) async-start(f32[32,1,128]{2,1,0:T(1,128)} %bitcast.53), calls=%async_computation.1 | async-start | bytes 32768 | tf_op jit(solution)/shard_map/all_to_all | solution.py:441
  119.5 1.2 collective-permute-done.22.refs_14_
  120.8 5.9 %all-to-all-done.1 = f32[32,1,128]{2,1,0:T(1,128)S(1)} async-done(((f32[32,1,128]{2,1,0:T(1,128)}), f32[32,1,128]{2,1,0:T(1,128)S(1)}, u32[]{:S(2)}, u32[]{:S(2)}) %all-to-all-start.1) | async-done | bytes 16416 | tf_op jit(solution)/shard_map/all_to_all | solution.py:441
  127.4 6.4 %update.3 = (f32[16,4,2,8,64]{4,3,2,1,0:T(8,128)}, f32[64,8,128]{2,1,0:T(8,128)}, f32[16,8,128]{2,1,0:T(8,128)}) custom-call(f32[8,16]{1,0:T(8,128)} %bitcast.44, f32[64,4]{1,0:T(8,128)} %constant.50.clone.basis_ref.refs_1_, f32[64,4]{1,0:T(8,128)} %constant.51.clone.refs_2_.coef_ref, f32[65,8,128]{2,1,0:T(8,128)} %get-tuple-element.48.refs_3_, ...), custom_call_target="tpu_custom_call" | custom-call | tf_op jit(solution)/shard_map/update/pallas_call | solution.py:446
  134.3 0.6 collective-permute-start.25
  134.9 2.7 %collective-permute-start.26 = (f32[16,8,128]{2,1,0:T(8,128)}, f32[16,8,128]{2,1,0:T(8,128)S(1)}, u32[]{:S(2)}, u32[]{:S(2)}) collective-permute-start(f32[16,8,128]{2,1,0:T(8,128)} %get-tuple-element.55.refs_0_), channel_id=1, source_target_pairs={{0,3},{1,0},{2,1},{3,2},{4,7},{5,4},{6,5},{7,6},{8,11},{9,8},{10,9... | collective-permute-start | bytes 196616 | tf_op jit(solution)/shard_map/ppermute | solution.py:349
  137.7 3.1 %collective-permute-done.24.refs_1_ = f32[16,8,128]{2,1,0:T(8,128)S(1)} collective-permute-done((f32[16,8,128]{2,1,0:T(8,128)}, f32[16,8,128]{2,1,0:T(8,128)S(1)}, u32[]{:S(2)}, u32[]{:S(2)}) %collective-permute-start.24) | collective-permute-done | bytes 65568 | tf_op jit(solution)/shard_map/ppermute | solution.py:349
  140.8 1.7 %collective-permute-done.25.refs_2_ = f32[16,8,128]{2,1,0:T(8,128)S(1)} collective-permute-done((f32[16,8,128]{2,1,0:T(8,128)}, f32[16,8,128]{2,1,0:T(8,128)S(1)}, u32[]{:S(2)}, u32[]{:S(2)}) %collective-permute-start.25) | collective-permute-done | bytes 65568 | tf_op jit(solution)/shard_map/ppermute | solution.py:349
  143.1 2.4 %final.1 = f32[16,4,2,8,64]{4,3,2,1,0:T(8,128)} custom-call(f32[64,4]{1,0:T(8,128)} %constant.51.clone.refs_2_.coef_ref, f32[64,8,128]{2,1,0:T(8,128)} %get-tuple-element.54.total_ref, f32[16,8,128]{2,1,0:T(8,128)} %get-tuple-element.55.refs_0_, f32[16,8,128]{2,1,0:T(8,128)} %copy-done.31, f32[16,8,128]{2,1,0:T(8,128)} %copy-done.32, f32[16,8,128]{2,1,0:T(8,128)} %copy-done.33), custom_call_target="tpu_custom_call" | custom-call | tf_op jit(solution)/shard_map/final/pallas_call | solution.py:457
  (127 shorter events, 15.2 us)
Async XLA Ops:
  4.6 26.6 %copy-start = (f32[32,8,128]{2,1,0:T(8,128)S(1)}, f32[32,8,128]{2,1,0:T(8,128)}, u32[]{:S(2)}) copy-start(f32[32,8,128]{2,1,0:T(8,128)} %get-tuple-element.30.refs_5_.refs_11_) | copy-start | bytes 393220
  4.6 26.6 %collective-permute-start = (f32[32,8,128]{2,1,0:T(8,128)}, f32[32,8,128]{2,1,0:T(8,128)S(1)}, u32[]{:S(2)}, u32[]{:S(2)}) collective-permute-start(f32[32,8,128]{2,1,0:T(8,128)} %get-tuple-element.29.refs_4_.refs_10_), channel_id=1, source_target_pairs={{0,0},{1,1},{2,2},{3,3},{4,16},{5,17},{6,18},{7,19},{8,4},{9,5},{1... | collective-permute-start | bytes 393224 | tf_op jit(solution)/shard_map/ppermute | solution.py:349
  6.3 27.1 %collective-permute-start.1 = (f32[32,8,128]{2,1,0:T(8,128)}, f32[32,8,128]{2,1,0:T(8,128)S(1)}, u32[]{:S(2)}, u32[]{:S(2)}) collective-permute-start(f32[32,8,128]{2,1,0:T(8,128)} %get-tuple-element.29.refs_4_.refs_10_), channel_id=1, source_target_pairs={{0,16},{1,17},{2,18},{3,19},{4,0},{5,1},{6,2},{7,3},{8,20},{9,21},... | collective-permute-start | bytes 393224 | tf_op jit(solution)/shard_map/ppermute | solution.py:349
  11.1 28.0 %collective-permute-start.2 = (f32[32,8,128]{2,1,0:T(8,128)}, f32[32,8,128]{2,1,0:T(8,128)S(1)}, u32[]{:S(2)}, u32[]{:S(2)}) collective-permute-start(f32[32,8,128]{2,1,0:T(8,128)} %get-tuple-element.30.refs_5_.refs_11_), channel_id=1, source_target_pairs={{0,0},{1,1},{2,2},{3,3},{4,16},{5,17},{6,18},{7,19},{8,4},{9,5},{1... | collective-permute-start | bytes 393224 | tf_op jit(solution)/shard_map/ppermute | solution.py:349
  12.7 26.4 %collective-permute-start.3 = (f32[32,8,128]{2,1,0:T(8,128)}, f32[32,8,128]{2,1,0:T(8,128)S(1)}, u32[]{:S(2)}, u32[]{:S(2)}) collective-permute-start(f32[32,8,128]{2,1,0:T(8,128)} %get-tuple-element.30.refs_5_.refs_11_), channel_id=1, source_target_pairs={{0,16},{1,17},{2,18},{3,19},{4,0},{5,1},{6,2},{7,3},{8,20},{9,21},... | collective-permute-start | bytes 393224 | tf_op jit(solution)/shard_map/ppermute | solution.py:349
  15.8 32.8 %collective-permute-start.6 = (f32[32,8,128]{2,1,0:T(8,128)}, f32[32,8,128]{2,1,0:T(8,128)S(1)}, u32[]{:S(2)}, u32[]{:S(2)}) collective-permute-start(f32[32,8,128]{2,1,0:T(8,128)} %get-tuple-element.29.refs_4_.refs_10_), channel_id=1, source_target_pairs={{0,8},{1,9},{2,10},{3,11},{4,12},{5,13},{6,14},{7,15},{8,0},{9,1},... | collective-permute-start | bytes 393224 | tf_op jit(solution)/shard_map/ppermute | solution.py:349
  21.8 11.5 %copy-start.1 = (f32[64,128]{1,0:T(8,128)}, f32[64,128]{1,0:T(8,128)S(1)}, u32[]{:S(2)}) copy-start(f32[64,128]{1,0:T(8,128)S(1)} %constant_dynamic-slice_fusion.1.live_ref) | copy-start | bytes 98308
  28.7 16.8 %copy-start.2 = (f32[64,128]{1,0:T(8,128)}, f32[64,128]{1,0:T(8,128)S(1)}, u32[]{:S(2)}) copy-start(f32[64,128]{1,0:T(8,128)S(1)} %pad_maximum_fusion.1.refs_6_) | copy-start | bytes 98308
  31.2 2.1 %copy-start.12 = (f32[32,8,128]{2,1,0:T(8,128)}, f32[32,8,128]{2,1,0:T(8,128)S(1)}, u32[]{:S(2)}) copy-start(f32[32,8,128]{2,1,0:T(8,128)S(1)} %collective-permute-done.refs_0_) | copy-start | bytes 393220
  31.2 17.3 %collective-permute-start.7 = (f32[32,8,128]{2,1,0:T(8,128)S(1)}, f32[32,8,128]{2,1,0:T(8,128)S(1)}, u32[]{:S(2)}, u32[]{:S(2)}) collective-permute-start(f32[32,8,128]{2,1,0:T(8,128)S(1)} %copy-done), channel_id=1, source_target_pairs={{0,8},{1,9},{2,10},{3,11},{4,12},{5,13},{6,14},{7,15},{8,0},{9,1},... | collective-permute-start | bytes 393224 | tf_op jit(solution)/shard_map/ppermute | solution.py:349
  39.1 9.5 %collective-permute-start.4 = (f32[36,16,128]{2,1,0:T(8,128)}, f32[36,16,128]{2,1,0:T(8,128)S(1)}, u32[]{:S(2)}, u32[]{:S(2)}) collective-permute-start(f32[36,16,128]{2,1,0:T(8,128)} %get-tuple-element.33), channel_id=1, source_target_pairs={{0,4},{1,5},{2,6},{3,7},{4,0},{5,1},{6,2},{7,3},{8,12},{9,13},{10,... | collective-permute-start | bytes 884744 | tf_op jit(solution)/shard_map/ppermute | solution.py:349
  45.5 3.1 %collective-permute-start.5 = (f32[36,16,128]{2,1,0:T(8,128)}, f32[36,16,128]{2,1,0:T(8,128)S(1)}, u32[]{:S(2)}, u32[]{:S(2)}) collective-permute-start(f32[36,16,128]{2,1,0:T(8,128)} %get-tuple-element.34), channel_id=1, source_target_pairs={{0,4},{1,5},{2,6},{3,7},{4,0},{5,1},{6,2},{7,3},{8,12},{9,13},{10,... | collective-permute-start | bytes 884744 | tf_op jit(solution)/shard_map/ppermute | solution.py:349
  48.6 0.8 copy-start.5
  48.6 0.9 copy-start.7
  52.5 19.0 %collective-permute-start.8 = (f32[65,8,128]{2,1,0:T(8,128)}, f32[65,8,128]{2,1,0:T(8,128)S(1)}, u32[]{:S(2)}, u32[]{:S(2)}) collective-permute-start(f32[65,8,128]{2,1,0:T(8,128)} %get-tuple-element.36), channel_id=1, source_target_pairs={{0,8},{1,9},{2,10},{3,11},{4,12},{5,13},{6,14},{7,15},{8,0},{9,1},... | collective-permute-start | bytes 798728 | tf_op jit(solution)/shard_map/ppermute | solution.py:349
  54.7 9.6 %collective-permute-start.10 = (f32[16,8,128]{2,1,0:T(8,128)}, f32[16,8,128]{2,1,0:T(8,128)S(1)}, u32[]{:S(2)}, u32[]{:S(2)}) collective-permute-start(f32[16,8,128]{2,1,0:T(8,128)} %get-tuple-element.41.refs_12_), channel_id=1, source_target_pairs={{0,2},{1,3},{2,0},{3,1},{4,6},{5,7},{6,4},{7,5},{8,10},{9,11},{10,... | collective-permute-start | bytes 196616 | tf_op jit(solution)/shard_map/ppermute | solution.py:349
  57.3 7.0 %collective-permute-start.11 = (f32[16,8,128]{2,1,0:T(8,128)}, f32[16,8,128]{2,1,0:T(8,128)S(1)}, u32[]{:S(2)}, u32[]{:S(2)}) collective-permute-start(f32[16,8,128]{2,1,0:T(8,128)} %get-tuple-element.41.refs_12_), channel_id=1, source_target_pairs={{0,3},{1,0},{2,1},{3,2},{4,7},{5,4},{6,5},{7,6},{8,11},{9,8},{10,9... | collective-permute-start | bytes 196616 | tf_op jit(solution)/shard_map/ppermute | solution.py:349
  58.7 6.3 %collective-permute-start.9 = (f32[16,8,128]{2,1,0:T(8,128)}, f32[16,8,128]{2,1,0:T(8,128)S(1)}, u32[]{:S(2)}, u32[]{:S(2)}) collective-permute-start(f32[16,8,128]{2,1,0:T(8,128)} %get-tuple-element.41.refs_12_), channel_id=1, source_target_pairs={{0,1},{1,2},{2,3},{3,0},{4,5},{5,6},{6,7},{7,4},{8,9},{9,10},{10,1... | collective-permute-start | bytes 196616 | tf_op jit(solution)/shard_map/ppermute | solution.py:349
  59.4 12.2 %all-to-all-start = ((f32[32,1,128]{2,1,0:T(1,128)}), f32[32,1,128]{2,1,0:T(1,128)S(1)}, u32[]{:S(2)}, u32[]{:S(2)}) async-start(f32[32,1,128]{2,1,0:T(1,128)} %bitcast.52), calls=%async_computation | async-start | bytes 32768 | tf_op jit(solution)/shard_map/all_to_all | solution.py:441
  64.3 7.2 %copy-start.26 = (f32[16,8,128]{2,1,0:T(8,128)}, f32[16,8,128]{2,1,0:T(8,128)S(1)}, u32[]{:S(2)}) copy-start(f32[16,8,128]{2,1,0:T(8,128)S(1)} %collective-permute-done.10.refs_14_) | copy-start | bytes 196612
  64.4 7.2 %copy-start.28 = (f32[16,8,128]{2,1,0:T(8,128)}, f32[16,8,128]{2,1,0:T(8,128)S(1)}, u32[]{:S(2)}) copy-start(f32[16,8,128]{2,1,0:T(8,128)S(1)} %collective-permute-done.11.refs_15_) | copy-start | bytes 196612
  65.0 6.6 %copy-start.30 = (f32[16,8,128]{2,1,0:T(8,128)}, f32[16,8,128]{2,1,0:T(8,128)S(1)}, u32[]{:S(2)}) copy-start(f32[16,8,128]{2,1,0:T(8,128)S(1)} %collective-permute-done.9.refs_13_) | copy-start | bytes 196612
  78.6 11.5 %collective-permute-start.14 = (f32[32,8,128]{2,1,0:T(8,128)}, f32[32,8,128]{2,1,0:T(8,128)S(1)}, u32[]{:S(2)}, u32[]{:S(2)}) collective-permute-start(f32[32,8,128]{2,1,0:T(8,128)} %get-tuple-element.43.refs_5_.refs_11_), channel_id=1, source_target_pairs={{0,0},{1,1},{2,2},{3,3},{4,16},{5,17},{6,18},{7,19},{8,4},{9,5},{1... | collective-permute-start | bytes 393224 | tf_op jit(solution)/shard_map/ppermute | solution.py:349
  80.1 11.8 %collective-permute-start.15 = (f32[32,8,128]{2,1,0:T(8,128)}, f32[32,8,128]{2,1,0:T(8,128)S(1)}, u32[]{:S(2)}, u32[]{:S(2)}) collective-permute-start(f32[32,8,128]{2,1,0:T(8,128)} %get-tuple-element.43.refs_5_.refs_11_), channel_id=1, source_target_pairs={{0,16},{1,17},{2,18},{3,19},{4,0},{5,1},{6,2},{7,3},{8,20},{9,21},... | collective-permute-start | bytes 393224 | tf_op jit(solution)/shard_map/ppermute | solution.py:349
  82.6 15.1 %collective-permute-start.12 = (f32[32,8,128]{2,1,0:T(8,128)}, f32[32,8,128]{2,1,0:T(8,128)S(1)}, u32[]{:S(2)}, u32[]{:S(2)}) collective-permute-start(f32[32,8,128]{2,1,0:T(8,128)} %get-tuple-element.42.refs_4_.refs_10_), channel_id=1, source_target_pairs={{0,0},{1,1},{2,2},{3,3},{4,16},{5,17},{6,18},{7,19},{8,4},{9,5},{1... | collective-permute-start | bytes 393224 | tf_op jit(solution)/shard_map/ppermute | solution.py:349
  84.1 13.6 %collective-permute-start.13 = (f32[32,8,128]{2,1,0:T(8,128)}, f32[32,8,128]{2,1,0:T(8,128)S(1)}, u32[]{:S(2)}, u32[]{:S(2)}) collective-permute-start(f32[32,8,128]{2,1,0:T(8,128)} %get-tuple-element.42.refs_4_.refs_10_), channel_id=1, source_target_pairs={{0,16},{1,17},{2,18},{3,19},{4,0},{5,1},{6,2},{7,3},{8,20},{9,21},... | collective-permute-start | bytes 393224 | tf_op jit(solution)/shard_map/ppermute | solution.py:349
  88.4 19.5 %collective-permute-start.18 = (f32[32,8,128]{2,1,0:T(8,128)}, f32[32,8,128]{2,1,0:T(8,128)S(1)}, u32[]{:S(2)}, u32[]{:S(2)}) collective-permute-start(f32[32,8,128]{2,1,0:T(8,128)} %get-tuple-element.42.refs_4_.refs_10_), channel_id=1, source_target_pairs={{0,8},{1,9},{2,10},{3,11},{4,12},{5,13},{6,14},{7,15},{8,0},{9,1},... | collective-permute-start | bytes 393224 | tf_op jit(solution)/shard_map/ppermute | solution.py:349
  90.1 14.7 %copy-start.3 = (f32[64,128]{1,0:T(8,128)S(1)}, f32[64,128]{1,0:T(8,128)}, u32[]{:S(2)}) copy-start(f32[64,128]{1,0:T(8,128)} %copy-done.2) | copy-start | bytes 98308
  90.1 22.3 %copy-start.24 = (f32[16,8,128]{2,1,0:T(8,128)S(1)}, f32[16,8,128]{2,1,0:T(8,128)}, u32[]{:S(2)}) copy-start(f32[16,8,128]{2,1,0:T(8,128)} %get-tuple-element.52.refs_12_) | copy-start | bytes 196612
  90.1 1.8 %copy-start.16 = (f32[32,8,128]{2,1,0:T(8,128)}, f32[32,8,128]{2,1,0:T(8,128)S(1)}, u32[]{:S(2)}) copy-start(f32[32,8,128]{2,1,0:T(8,128)S(1)} %collective-permute-done.14.refs_0_) | copy-start | bytes 393220
  90.1 17.8 %collective-permute-start.19 = (f32[32,8,128]{2,1,0:T(8,128)}, f32[32,8,128]{2,1,0:T(8,128)S(1)}, u32[]{:S(2)}, u32[]{:S(2)}) collective-permute-start(f32[32,8,128]{2,1,0:T(8,128)} %get-tuple-element.43.refs_5_.refs_11_), channel_id=1, source_target_pairs={{0,8},{1,9},{2,10},{3,11},{4,12},{5,13},{6,14},{7,15},{8,0},{9,1},... | collective-permute-start | bytes 393224 | tf_op jit(solution)/shard_map/ppermute | solution.py:349
  97.7 10.2 %collective-permute-start.17 = (f32[36,16,128]{2,1,0:T(8,128)}, f32[36,16,128]{2,1,0:T(8,128)S(1)}, u32[]{:S(2)}, u32[]{:S(2)}) collective-permute-start(f32[36,16,128]{2,1,0:T(8,128)} %get-tuple-element.47), channel_id=1, source_target_pairs={{0,4},{1,5},{2,6},{3,7},{4,0},{5,1},{6,2},{7,3},{8,12},{9,13},{10,... | collective-permute-start | bytes 884744 | tf_op jit(solution)/shard_map/ppermute | solution.py:349
  104.1 3.9 %collective-permute-start.16 = (f32[36,16,128]{2,1,0:T(8,128)}, f32[36,16,128]{2,1,0:T(8,128)S(1)}, u32[]{:S(2)}, u32[]{:S(2)}) collective-permute-start(f32[36,16,128]{2,1,0:T(8,128)} %get-tuple-element.46), channel_id=1, source_target_pairs={{0,4},{1,5},{2,6},{3,7},{4,0},{5,1},{6,2},{7,3},{8,12},{9,13},{10,... | collective-permute-start | bytes 884744 | tf_op jit(solution)/shard_map/ppermute | solution.py:349
  107.9 0.7 copy-start.20
  107.9 0.8 copy-start.4
  107.9 0.8 copy-start.6
  111.8 14.9 %collective-permute-start.20 = (f32[65,8,128]{2,1,0:T(8,128)}, f32[65,8,128]{2,1,0:T(8,128)S(1)}, u32[]{:S(2)}, u32[]{:S(2)}) collective-permute-start(f32[65,8,128]{2,1,0:T(8,128)} %get-tuple-element.49), channel_id=1, source_target_pairs={{0,8},{1,9},{2,10},{3,11},{4,12},{5,13},{6,14},{7,15},{8,0},{9,1},... | collective-permute-start | bytes 798728 | tf_op jit(solution)/shard_map/ppermute | solution.py:349
  112.4 7.1 %collective-permute-start.21 = (f32[16,8,128]{2,1,0:T(8,128)S(1)}, f32[16,8,128]{2,1,0:T(8,128)S(1)}, u32[]{:S(2)}, u32[]{:S(2)}) collective-permute-start(f32[16,8,128]{2,1,0:T(8,128)S(1)} %copy-done.24), channel_id=1, source_target_pairs={{0,1},{1,2},{2,3},{3,0},{4,5},{5,6},{6,7},{7,4},{8,9},{9,10},{10,1... | collective-permute-start | bytes 196616 | tf_op jit(solution)/shard_map/ppermute | solution.py:349
  112.9 7.8 %collective-permute-start.22 = (f32[16,8,128]{2,1,0:T(8,128)S(1)}, f32[16,8,128]{2,1,0:T(8,128)S(1)}, u32[]{:S(2)}, u32[]{:S(2)}) collective-permute-start(f32[16,8,128]{2,1,0:T(8,128)S(1)} %copy-done.24), channel_id=1, source_target_pairs={{0,2},{1,3},{2,0},{3,1},{4,6},{5,7},{6,4},{7,5},{8,10},{9,11},{10,... | collective-permute-start | bytes 196616 | tf_op jit(solution)/shard_map/ppermute | solution.py:349
  113.5 7.3 %collective-permute-start.23 = (f32[16,8,128]{2,1,0:T(8,128)S(1)}, f32[16,8,128]{2,1,0:T(8,128)S(1)}, u32[]{:S(2)}, u32[]{:S(2)}) collective-permute-start(f32[16,8,128]{2,1,0:T(8,128)S(1)} %copy-done.24), channel_id=1, source_target_pairs={{0,3},{1,0},{2,1},{3,2},{4,7},{5,4},{6,5},{7,6},{8,11},{9,8},{10,9... | collective-permute-start | bytes 196616 | tf_op jit(solution)/shard_map/ppermute | solution.py:349
  116.2 10.5 %all-to-all-start.1 = ((f32[32,1,128]{2,1,0:T(1,128)}), f32[32,1,128]{2,1,0:T(1,128)S(1)}, u32[]{:S(2)}, u32[]{:S(2)}) async-start(f32[32,1,128]{2,1,0:T(1,128)} %bitcast.53), calls=%async_computation.1 | async-start | bytes 32768 | tf_op jit(solution)/shard_map/all_to_all | solution.py:441
  119.5 7.2 %copy-start.25 = (f32[16,8,128]{2,1,0:T(8,128)}, f32[16,8,128]{2,1,0:T(8,128)S(1)}, u32[]{:S(2)}) copy-start(f32[16,8,128]{2,1,0:T(8,128)S(1)} %collective-permute-done.21.refs_13_) | copy-start | bytes 196612
  120.8 6.0 %copy-start.27 = (f32[16,8,128]{2,1,0:T(8,128)}, f32[16,8,128]{2,1,0:T(8,128)S(1)}, u32[]{:S(2)}) copy-start(f32[16,8,128]{2,1,0:T(8,128)S(1)} %collective-permute-done.22.refs_14_) | copy-start | bytes 196612
  120.8 6.0 %copy-start.29 = (f32[16,8,128]{2,1,0:T(8,128)}, f32[16,8,128]{2,1,0:T(8,128)S(1)}, u32[]{:S(2)}) copy-start(f32[16,8,128]{2,1,0:T(8,128)S(1)} %collective-permute-done.23.refs_15_) | copy-start | bytes 196612
  133.8 7.0 %collective-permute-start.24 = (f32[16,8,128]{2,1,0:T(8,128)}, f32[16,8,128]{2,1,0:T(8,128)S(1)}, u32[]{:S(2)}, u32[]{:S(2)}) collective-permute-start(f32[16,8,128]{2,1,0:T(8,128)} %get-tuple-element.55.refs_0_), channel_id=1, source_target_pairs={{0,1},{1,2},{2,3},{3,0},{4,5},{5,6},{6,7},{7,4},{8,9},{9,10},{10,1... | collective-permute-start | bytes 196616 | tf_op jit(solution)/shard_map/ppermute | solution.py:349
  134.3 8.2 %collective-permute-start.25 = (f32[16,8,128]{2,1,0:T(8,128)}, f32[16,8,128]{2,1,0:T(8,128)S(1)}, u32[]{:S(2)}, u32[]{:S(2)}) collective-permute-start(f32[16,8,128]{2,1,0:T(8,128)} %get-tuple-element.55.refs_0_), channel_id=1, source_target_pairs={{0,2},{1,3},{2,0},{3,1},{4,6},{5,7},{6,4},{7,5},{8,10},{9,11},{10,... | collective-permute-start | bytes 196616 | tf_op jit(solution)/shard_map/ppermute | solution.py:349
  134.9 7.6 %collective-permute-start.26 = (f32[16,8,128]{2,1,0:T(8,128)}, f32[16,8,128]{2,1,0:T(8,128)S(1)}, u32[]{:S(2)}, u32[]{:S(2)}) collective-permute-start(f32[16,8,128]{2,1,0:T(8,128)} %get-tuple-element.55.refs_0_), channel_id=1, source_target_pairs={{0,3},{1,0},{2,1},{3,2},{4,7},{5,4},{6,5},{7,6},{8,11},{9,8},{10,9... | collective-permute-start | bytes 196616 | tf_op jit(solution)/shard_map/ppermute | solution.py:349
  140.8 1.7 %copy-start.31 = (f32[16,8,128]{2,1,0:T(8,128)}, f32[16,8,128]{2,1,0:T(8,128)S(1)}, u32[]{:S(2)}) copy-start(f32[16,8,128]{2,1,0:T(8,128)S(1)} %collective-permute-done.24.refs_1_) | copy-start | bytes 196612
  (15 other events, 9.8 us)

commit v2 on v1

v2 whole, which is shorter than its diff:
```python
import functools
import math

import jax
import jax.numpy as jnp
import numpy as np
from jax import lax
from jax.experimental import pallas as pl
from jax.experimental.pallas import tpu as pltpu
from jax.sharding import PartitionSpec as P

ITERS = 2
PENALTY = 0.05
HIGH = lax.Precision.HIGHEST
AXES = ("row", "col", "band")
LIMIT = pltpu.CompilerParams(vmem_limit_bytes=16 * 2**20)


def swap(x):
    half = x.shape[-1] // 2
    return pltpu.roll(x, half, x.ndim - 1)


def low_lanes(shape):
    return lax.broadcasted_iota(jnp.int32, shape, len(shape) - 1) < shape[-1] // 2


def join_low(a, b):
    return jnp.where(low_lanes(a.shape), a, swap(b))


def join_high(a, b):
    return jnp.where(low_lanes(a.shape), swap(a), b)


def column(ref, index, dirs, lanes):
    rows = lax.broadcasted_iota(jnp.int32, (dirs, lanes), 0)
    out = jnp.full((dirs, lanes), ref[0, index], jnp.float32)
    for d in range(1, dirs):
        out = jnp.where(rows == d, ref[d, index], out)
    return out


def cos_turns(r):
    t = 0.25 - jnp.abs(r)
    x = t * t
    coef = [(-1) ** n * (2.0 * math.pi) ** (2 * n + 1) / math.factorial(2 * n + 1) for n in range(7)]
    out = jnp.full_like(x, coef[-1])
    for c in coef[-2::-1]:
        out = out * x + c
    return out * t


def rotated(g, e):
    low = low_lanes(e.shape)
    turned = swap(e)
    cos2 = jnp.where(low, e, turned)
    sin2 = jnp.where(low, -turned, e)
    return g * cos2 + swap(g) * sin2


def counter_rotated(g, e):
    low = low_lanes(e.shape)
    turned = swap(e)
    cos2 = jnp.where(low, e, turned)
    sin2 = jnp.where(low, -turned, e)
    return g * cos2 - swap(g) * sin2


def start_kernel(dims, pos_ref, lmn_ref, freq_ref, gains_ref, e_ref, g_ref, p_ref):
    F, T, D, O, R, C = dims
    W = 2 * O
    own = lax.axis_index("row") * C + lax.axis_index("col")
    first = lax.axis_index("band") * F
    low = low_lanes((D, W))
    shape = pos_ref[:, :, :O].shape
    pos = jnp.zeros(shape, jnp.float32)
    for k in range(R * C):
        pos = jnp.where(own == k, pos_ref[:, :, k * O : (k + 1) * O], pos)
    pos = jnp.concatenate([pos, pos], axis=-1)
    geometry = []
    for t in range(T):
        total = jnp.zeros((D, W), jnp.float32)
        for k in range(3):
            rows = lax.broadcasted_iota(jnp.int32, (D, W), 0)
            lm = jnp.full((D, W), lmn_ref[k, 0], jnp.float32)
            for d in range(1, D):
                lm = jnp.where(rows == d, lmn_ref[k, d], lm)
            total = total + lm * pos[k, t : t + 1, :]
        geometry.append(total)
    shift = jnp.where(low, 0.0, 0.25)
    for f in range(F):
        nu = freq_ref[first + f]
        for t in range(T):
            ft = f * T + t
            turns = nu * geometry[t]
            r = turns - jnp.round(turns) + shift
            e = cos_turns(r - jnp.round(r))
            g = jnp.concatenate([gains_ref[f, t, 0], gains_ref[f, t, 1]], axis=-1)
            e_ref[ft] = e
            g_ref[ft] = g
            p_ref[ft] = rotated(g, e)


def own_terms(dims, flux_ref, live_ref, g_ref, held_ref, slope_ref):
    F, T, D, O, _, _ = dims
    total = jnp.zeros((1, 2 * O), jnp.float32)
    for f in range(F):
        flux = column(flux_ref, f, D, 2 * O)
        for t in range(T):
            ft = f * T + t
            live = live_ref[ft : ft + 1, :]
            g = g_ref[ft]
            power = g * g
            power = (power + swap(power)) * flux
            own = jnp.sum(power, axis=0, keepdims=True)
            total = total + live * own * own
            power = power * flux
            slope_ref[ft] = -live * power
            held_ref[ft] = live * (own * flux - power) * g
    return total


def fit_sums(dims, basis_ref, value, rhs_ref):
    F, T, D, O, _, _ = dims
    first = lax.axis_index("band") * F
    for t in range(T):
        acc = [jnp.zeros((D, 2 * O), jnp.float32) for _ in range(4)]
        for f in range(F):
            total = value(f, t)
            for k in range(4):
                acc[k] = acc[k] + basis_ref[first + f, k] * total
        for k in range(4):
            rhs_ref[k * T + t] = acc[k]


def pick(index, parts):
    out = parts[0]
    for k in range(1, len(parts)):
        out = jnp.where(index == k, parts[k], out)
    return out


def setup_kernel(dims, flux_ref, basis_ref, flags_ref, vis_ref, duals_ref, g_ref,
                 live_col_ref, live_half_ref, live_own_ref, u_ref, rhs_ref, held_ref, slope_ref,
                 power_ref, extra_ref, distinct):
    F, T, _, O, R, C = dims
    rows, cols = vis_ref.shape[3], vis_ref.shape[4]
    row = lax.axis_index("row")
    col = lax.axis_index("col")
    p = lax.broadcasted_iota(jnp.int32, (rows, cols), 0) + row * rows
    q = lax.broadcasted_iota(jnp.int32, (rows, cols), 1) + col * cols
    distinct[...] = jnp.where(p == q, 0.0, 1.0).astype(jnp.bfloat16)
    counts = jnp.zeros((T, 1), jnp.float32)
    for f in range(F):
        live = flags_ref[f].astype(jnp.float32)
        count = jnp.sum(live, axis=1, keepdims=True)
        counts = counts + count * (count - 1.0)
        at = slice(f * T, (f + 1) * T)
        mine = pick(row, [live[:, r * rows : (r + 1) * rows] for r in range(R)])
        blocks = [mine[:, c * O : (c + 1) * O] for c in range(C)]
        live_col_ref[at, :] = pick(col, [live[:, c * cols : (c + 1) * cols] for c in range(C)])
        even = jnp.concatenate([blocks[0], blocks[2]], axis=1)
        odd = jnp.concatenate([blocks[1], blocks[3]], axis=1)
        live_half_ref[at, :] = pick(col % 2, [even, odd])
        own = pick(col, blocks)
        live_own_ref[at, :] = jnp.concatenate([own, own], axis=1)
    samples = jnp.sum(counts) / (R * C)

    def channel(f, acc):
        live = flags_ref[f].astype(jnp.float32)
        mine = pick(row, [live[:, r * rows : (r + 1) * rows] for r in range(R)])
        pair = pick(col, [live[:, c * cols : (c + 1) * cols] for c in range(C)])
        upright = jnp.transpose(jnp.concatenate([mine] * (8 // T), axis=0))
        for t in range(T):
            weight = jnp.broadcast_to(upright[:, t : t + 1], (rows, cols)) * pair[t : t + 1, :]
            weight = weight.astype(jnp.bfloat16) * distinct[...]
            for part in range(2):
                seen = (vis_ref[f, t, part] * weight).astype(jnp.float32)
                acc = acc + jnp.sum((seen * seen).reshape(rows // 32, 32, cols), axis=0)
        return acc

    power = lax.fori_loop(0, F, channel, jnp.zeros((32, cols), jnp.float32))
    power = jnp.sum(power, axis=0, keepdims=True)
    low = low_lanes(power.shape)
    lanes = lax.broadcasted_iota(jnp.int32, power.shape, 1)
    row_power = jnp.where(low, power + swap(power), jnp.where(lanes == O, samples, 0.0))
    power_ref[...] = row_power
    for f in range(F):
        for t in range(T):
            u_ref[f * T + t] = jnp.concatenate([duals_ref[f, t, 0], duals_ref[f, t, 1]], axis=-1)
    fit_sums(dims, basis_ref, lambda f, t: u_ref[f * T + t] + g_ref[f * T + t], rhs_ref)
    own = own_terms(dims, flux_ref, live_own_ref, g_ref, held_ref, slope_ref)
    extra_ref[...] = row_power - jnp.where(low, own, 0.0)


def again_kernel(dims, flux_ref, basis_ref, power_ref, live_ref, u_ref, g_ref,
                 rhs_ref, held_ref, slope_ref, extra_ref):
    _, T, _, _, _, _ = dims
    fit_sums(dims, basis_ref, lambda f, t: u_ref[f * T + t] + g_ref[f * T + t], rhs_ref)
    own = own_terms(dims, flux_ref, live_ref, g_ref, held_ref, slope_ref)
    extra_ref[...] = power_ref[...] - jnp.where(low_lanes(own.shape), own, 0.0)


def target_kernel(dims, first_pass, coef_ref, u_ref, g_ref, *refs):
    F, T, _, _, _, _ = dims
    rhs_refs, outs = refs[:4], refs[4:]
    first = lax.axis_index("band") * F
    for t in range(T):
        rhs = [rhs_refs[0][k * T + t] + rhs_refs[1][k * T + t]
               + rhs_refs[2][k * T + t] + rhs_refs[3][k * T + t] for k in range(4)]
        for f in range(F):
            ft = f * T + t
            smooth = coef_ref[first + f, 0] * rhs[0]
            for k in range(1, 4):
                smooth = smooth + coef_ref[first + f, k] * rhs[k]
            u = u_ref[ft]
            if not first_pass:
                u = u + g_ref[ft] - smooth
                outs[1][ft] = u
            outs[0][ft] = smooth - u


def block_mask(size):
    shape = (8 * size, 8 * size)
    a = lax.broadcasted_iota(jnp.int32, shape, 0) // size
    b = lax.broadcasted_iota(jnp.int32, shape, 1) // size
    return a == b


def sum_kernel(dims, flux_ref, live_ref, vis_ref, a_ref, b_ref, keep_ref, send_ref, distinct):
    F, T, D, O, _, _ = dims
    rows, cols = vis_ref.shape[3], vis_ref.shape[4]
    row = lax.axis_index("row")
    col = lax.axis_index("col")
    parity = col % 2
    p = lax.broadcasted_iota(jnp.int32, (rows, cols), 0) + row * rows
    q = lax.broadcasted_iota(jnp.int32, (rows, cols), 1) + col * cols
    distinct[...] = jnp.where(p == q, 0.0, 1.0).astype(jnp.bfloat16)
    group = 8 // T
    blocks = block_mask(2 * D)
    nt = (((1,), (1,)), ((), ()))

    def body(step, carry):
        highs, lows = [], []
        lives = live_ref[pl.ds(step * 8, 8), :]
        for i in range(group):
            f = step * group + i
            scale = column(flux_ref, f, D, cols)
            for t in range(T):
                j = i * T + t
                ft = step * 8 + j
                a, b = a_ref[ft], b_ref[ft]
                first = jnp.where(row == 0, a, b)
                second = jnp.where(row == 0, b, a)
                weight = scale * lives[j : j + 1, :]
                re = join_low(first, second) * weight
                im = join_high(first, second) * weight
                x = jnp.concatenate(
                    [jnp.concatenate([re, -im], axis=1), jnp.concatenate([im, re], axis=1)], axis=0
                )
                high = x.astype(jnp.bfloat16)
                low = (x - high.astype(jnp.float32)).astype(jnp.bfloat16)
                highs.append(high)
                lows.append(low)
                both = jnp.concatenate([high, low], axis=0)
                mask = distinct[...]
                seen = jnp.concatenate([vis_ref[f, t, 0] * mask, vis_ref[f, t, 1] * mask], axis=1)
                v = lax.dot_general(both, seen, nt, preferred_element_type=jnp.float32)
                v = v[: 2 * D] + v[2 * D :]
                v0, v1 = v[:, : 2 * O], v[:, 2 * O :]
                even, odd = join_low(v0, v1), join_high(v0, v1)
                keep_ref[step * 9 + j] = jnp.where(parity == 0, even, odd)
                send_ref[step * 9 + j] = jnp.where(parity == 0, odd, even)
        high = jnp.concatenate(highs, axis=0)
        low = jnp.concatenate(lows, axis=0)
        gram = lax.dot_general(high, high, nt, preferred_element_type=jnp.float32)
        gram = gram + lax.dot_general(high, low, nt, preferred_element_type=jnp.float32)
        gram = gram + lax.dot_general(low, high, nt, preferred_element_type=jnp.float32)
        gram = jnp.where(blocks, gram, 0.0)
        folded = gram[: 2 * D]
        for i in range(1, 8):
            folded = folded + gram[i * 2 * D : (i + 1) * 2 * D]
        keep_ref[step * 9 + 8] = folded
        send_ref[step * 9 + 8] = folded
        return carry

    lax.fori_loop(0, F * T // 8, body, 0)


def residual_kernel(dims, live_ref, extra_ref, kept_ref, other_ref, mine_ref, theirs_ref,
                    keep_ref, send_ref, scalar_ref):
    F, T, D, O, _, _ = dims
    W = 2 * O
    near = (lax.axis_index("col") // 2) == 0
    mask = block_mask(2 * D)
    eye = lax.broadcasted_iota(jnp.int32, (2 * D, W), 0) == (
        lax.broadcasted_iota(jnp.int32, (2 * D, W), 1) % (2 * D)
    )
    total = jnp.zeros((2 * D, W), jnp.float32)
    for group in range(F * T // 8):
        gram = kept_ref[group * 9 + 8] + other_ref[group * 9 + 8]
        diagonal = jnp.sum(jnp.where(eye, gram, 0.0), axis=0, keepdims=True)
        keep_ref[F * T, group : group + 1, :] = diagonal
        send_ref[F * T, group : group + 1, :] = diagonal
        spread = jnp.where(mask, jnp.concatenate([gram] * 8, axis=0), 0.0)
        station = []
        for i in range(8):
            a, b = mine_ref[group * 8 + i], theirs_ref[group * 8 + i]
            first = jnp.where(near, a, b)
            second = jnp.where(near, b, a)
            station += [join_low(first, second), join_high(first, second)]
        model = jnp.dot(
            spread, jnp.concatenate(station, axis=0), precision=HIGH,
            preferred_element_type=jnp.float32,
        )
        for i in range(8):
            ft = group * 8 + i
            live = live_ref[ft : ft + 1, :]
            v = kept_ref[group * 9 + i] + other_ref[group * 9 + i]
            num = (v - model[i * 2 * D : (i + 1) * 2 * D]) * live
            z = jnp.concatenate(station[2 * i : 2 * i + 2], axis=0)
            total = total + z * (v * live + num)
            low, high = join_low(num[:D], num[D:]), join_high(num[:D], num[D:])
            keep_ref[ft] = jnp.where(near, low, high)
            send_ref[ft] = jnp.where(near, high, low)
    squares = -jnp.sum(total, axis=0, keepdims=True)
    squares = squares + swap(squares)
    scalar = jnp.where(low_lanes(squares.shape), squares, 0.0) + extra_ref[...]
    scalar_ref[...] = jnp.broadcast_to(scalar, scalar_ref.shape)


def update_kernel(dims, last, full, basis_ref, keep_ref, come_ref, scalar_ref, live_ref, e_ref,
                  g_ref, held_ref, slope_ref, target_ref, *refs):
    F, T, D, O, _, _ = dims
    first = lax.axis_index("band") * F
    W = 2 * O
    sums = jnp.sum(scalar_ref[...], axis=0, keepdims=True)
    low = low_lanes(sums.shape)
    squares = jnp.sum(jnp.where(low, sums, 0.0), axis=1, keepdims=True)
    samples = jnp.sum(jnp.where(low, 0.0, sums), axis=1, keepdims=True)
    squares = jnp.maximum(squares, 0.0)
    rho = PENALTY * full * (squares / samples + 1e-06)
    rho = jnp.broadcast_to(rho, (D, W))
    shape = (8 * D, W)
    a = lax.broadcasted_iota(jnp.int32, shape, 0)
    b = lax.broadcasted_iota(jnp.int32, shape, 1)
    eye = a // D * (2 * D) + a % D == b
    acc = [[jnp.zeros((D, W), jnp.float32) for _ in range(T)] for _ in range(4)]
    for group in range(F * T // 8):
        diagonal = keep_ref[F * T, group : group + 1, :] + come_ref[F * T, group : group + 1, :]
        spread = jnp.sum(jnp.where(eye, diagonal, 0.0), axis=1, keepdims=True)
        for i in range(8):
            ft = group * 8 + i
            f, t = ft // T, ft % T
            e = e_ref[ft]
            g = g_ref[ft]
            around = live_ref[ft : ft + 1, :] * spread[i * D : (i + 1) * D]
            num = counter_rotated(keep_ref[ft] + come_ref[ft], e) + held_ref[ft]
            fresh = (num + around * g + rho * target_ref[ft]) / (around + slope_ref[ft] + rho)
            g = 0.5 * (g + fresh)
            if last:
                u_ref, out_ref, total_ref, rhs_ref = refs
                out_ref[f, t, 0] = g[:, :O]
                out_ref[f, t, 1] = g[:, O:]
                total = u_ref[ft] + g
                total_ref[ft] = total
                for k in range(4):
                    acc[k][t] = acc[k][t] + basis_ref[first + f, k] * total
            else:
                g_out, p_out = refs
                g_out[ft] = g
                p_out[ft] = rotated(g, e)
    if last:
        for k in range(4):
            for t in range(T):
                rhs_ref[k * T + t] = acc[k][t]


def final_kernel(dims, coef_ref, total_ref, *refs):
    F, T, _, O, _, _ = dims
    rhs_refs, out_ref = refs[:4], refs[4]
    first = lax.axis_index("band") * F
    for t in range(T):
        rhs = [rhs_refs[0][k * T + t] + rhs_refs[1][k * T + t]
               + rhs_refs[2][k * T + t] + rhs_refs[3][k * T + t] for k in range(4)]
        for f in range(F):
            dual = total_ref[f * T + t]
            for k in range(4):
                dual = dual - coef_ref[first + f, k] * rhs[k]
            out_ref[f, t, 0] = dual[:, :O]
            out_ref[f, t, 1] = dual[:, O:]


def shards(sizes, vis, flags, positions, lmn, flux, gains, duals):
    R, C, Z = sizes
    F, T, _, D, O = gains.shape
    rows, cols = vis.shape[3], vis.shape[4]
    full = flags.shape[2]
    total_f = F * Z
    FT, W = F * T, 2 * O
    dims = (F, T, D, O, R, C)
    f32 = jnp.float32
    smem = pl.BlockSpec(memory_space=pltpu.SMEM)
    vmem = pl.BlockSpec(memory_space=pltpu.VMEM)

    def array(*shape):
        return jax.ShapeDtypeStruct(shape, f32)

    def call(kernel, outs, scalars, arrays, scratch=()):
        return pl.pallas_call(
            kernel,
            out_shape=outs,
            in_specs=[smem] * len(scalars) + [vmem] * len(arrays),
            out_specs=[vmem] * len(outs),
            scratch_shapes=list(scratch),
            compiler_params=LIMIT,
        )(*scalars, *arrays)

    grid = 2.0 * np.arange(total_f, dtype=np.float64) / (total_f - 1) - 1.0
    basis = np.stack([grid**k for k in range(4)], axis=1)
    solved = basis @ np.linalg.inv(basis.T @ basis)
    basis_t = jnp.asarray(basis, f32)
    coef_t = jnp.asarray(solved, f32)
    freq_t = jnp.asarray(1.0 + np.arange(total_f) / total_f, f32)

    def where(r, c, z):
        return (r * C + c) * Z + z

    def permute(x, move):
        pairs = [
            (where(r, c, z), where(*move(r, c, z)))
            for r in range(R) for c in range(C) for z in range(Z)
        ]
        return lax.ppermute(x, AXES, pairs)

    def gather(x, m):
        return permute(x, lambda r, c, z: (((r * C + c) % R + m) % R, (r * C + c) // R, z))

    def bands(x):
        return [x] + [permute(x, lambda r, c, z, k=k: (r, c, (z + k) % Z)) for k in range(1, Z)]

    whole, line, fit = array(FT, D, W), array(FT + 1, D, W), array(4 * T, D, W)
    pair, text, mask = array(FT // 8 * 9, 2 * D, W), array(1, W), pltpu.VMEM((rows, cols), jnp.bfloat16)
    flux_t = flux.T
    rot, g, p = pl.pallas_call(
        functools.partial(start_kernel, dims),
        out_shape=[whole] * 3,
        in_specs=[vmem, smem, smem, vmem],
        out_specs=[vmem] * 3,
        compiler_params=LIMIT,
        name="start",
    )(positions.transpose(1, 0, 2), lmn, freq_t, gains)
    for step in range(ITERS):
        last = step == ITERS - 1
        got = [gather(p, m) for m in range(R)]
        if step == 0:
            (live_col, live_half, live_own, u, rhs, held, slope, power, extra) = call(
                functools.partial(setup_kernel, dims),
                [array(FT, cols), array(FT, W), array(FT, W), whole, fit, whole, whole, text, text],
                [flux_t, basis_t], [flags, vis, duals, g], [mask],
            )
        else:
            rhs, held, slope, extra = call(
                functools.partial(again_kernel, dims),
                [fit, whole, whole, text], [flux_t, basis_t], [power, live_own, u, g],
            )
        rhs_all = bands(rhs)
        theirs = permute(p, lambda r, c, z: (r, c ^ 2, z))
        keep, send = call(
            functools.partial(sum_kernel, dims), [pair, pair], [flux_t],
            [live_col, vis, *got], [mask],
        )
        other = permute(send, lambda r, c, z: (r, c ^ 1, z))
        keep, send, scalar = call(
            functools.partial(residual_kernel, dims), [line, line, array(R * C * Z, W)],
            [], [live_half, extra, keep, other, p, theirs],
        )
        come = permute(send, lambda r, c, z: (r, c ^ 2, z))
        scalar = lax.all_to_all(scalar, AXES, 0, 0, tiled=True)
        target = call(
            functools.partial(target_kernel, dims, step == 0),
            [whole] * (1 if step == 0 else 2), [coef_t], [u, g, *rhs_all],
        )
        update = functools.partial(update_kernel, dims, last, float(full))
        arrays = [keep, come, scalar, live_own, rot, g, held, slope, target[0]]
        if last:
            gain, total, rhs = call(
                update, [array(*gains.shape), whole, fit], [basis_t], arrays + [target[1]]
            )
        else:
            g, p = call(update, [whole, whole], [basis_t], arrays)
    (dual,) = call(
        functools.partial(final_kernel, dims), [array(*gains.shape)], [coef_t],
        [total, *bands(rhs)],
    )
    return (gain, dual)


def basis(count):
    grid = 2.0 * jnp.arange(count, dtype=jnp.float32) / (count - 1) - 1.0
    return jnp.stack([grid**power for power in range(4)], axis=1)


def rotate(positions, lmn, freq):
    geometry = jnp.einsum("tks,kd->tds", positions, lmn, precision=HIGH)
    angle = 2.0 * math.pi * freq[:, None, None, None] * geometry[None]
    return (jnp.cos(angle), -jnp.sin(angle))


def complex_mul(a_re, a_im, b_re, b_im):
    return (a_re * b_re - a_im * b_im, a_re * b_im + a_im * b_re)


def solve_fit(rhs, total_f):
    full = basis(total_f)
    gram = jnp.dot(full.T, full, precision=HIGH)
    factor = jnp.linalg.cholesky(gram)
    flat = rhs.reshape(rhs.shape[0], -1)
    return jax.scipy.linalg.cho_solve((factor, True), flat).reshape(rhs.shape)


def plain_shards(vis, flags, positions, lmn, flux, gains, duals):
    width = gains.shape[0]
    total_f = width * lax.axis_size("band")
    first = lax.axis_index("band") * width
    local_basis = lax.dynamic_slice_in_dim(basis(total_f), first, width, 0)
    freq = 1.0 + (first + jnp.arange(width, dtype=jnp.int32)).astype(jnp.float32) / total_f
    row_index = lax.axis_index("row")
    col_index = lax.axis_index("col")
    row_count = vis.shape[3]
    col_count = vis.shape[4]
    owned = gains.shape[4]
    own_start = (row_index * lax.axis_size("col") + col_index) * owned
    row_start = row_index * row_count
    col_start = col_index * col_count
    own_cos, own_sin = rotate(lax.dynamic_slice_in_dim(positions, own_start, owned, 2), lmn, freq)
    row_cos, row_sin = rotate(
        lax.dynamic_slice_in_dim(positions, row_start, row_count, 2), lmn, freq
    )
    col_cos, col_sin = rotate(
        lax.dynamic_slice_in_dim(positions, col_start, col_count, 2), lmn, freq
    )
    all_live = flags.astype(jnp.float32)
    row_live = lax.dynamic_slice_in_dim(all_live, row_start, row_count, 2)
    col_live = lax.dynamic_slice_in_dim(all_live, col_start, col_count, 2)
    own_live = lax.dynamic_slice_in_dim(all_live, own_start, owned, 2)
    row_ids = row_start + jnp.arange(row_count, dtype=jnp.int32)
    col_ids = col_start + jnp.arange(col_count, dtype=jnp.int32)
    distinct = (row_ids[:, None] != col_ids[None, :]).astype(jnp.float32)
    weight = row_live[:, :, :, None] * col_live[:, :, None, :] * distinct
    vis_re = vis[:, :, 0].astype(jnp.float32)
    vis_im = vis[:, :, 1].astype(jnp.float32)
    scale = flux[:, None, :, None]

    def fit(gain, dual):
        rhs = jnp.einsum("fk,ftcds->ktcds", local_basis, gain + dual, precision=HIGH)
        return solve_fit(lax.psum(rhs, "band"), total_f)

    gain, dual = (gains, duals)
    coeffs = fit(gain, dual)
    for _ in range(ITERS):
        target = jnp.einsum("fk,ktcds->ftcds", local_basis, coeffs, precision=HIGH) - dual
        every = lax.all_gather(gain, ("row", "col"), axis=4, tiled=True)
        row_gain = lax.dynamic_slice_in_dim(every, row_start, row_count, 4)
        col_gain = lax.dynamic_slice_in_dim(every, col_start, col_count, 4)
        row_re, row_im = complex_mul(row_gain[:, :, 0], row_gain[:, :, 1], row_cos, row_sin)
        col_re, col_im = complex_mul(col_gain[:, :, 0], col_gain[:, :, 1], col_cos, col_sin)
        col_re = scale * col_re
        col_im = scale * col_im
        model_re = jnp.einsum("ftdp,ftdq->ftpq", row_re, col_re, precision=HIGH) + jnp.einsum(
            "ftdp,ftdq->ftpq", row_im, col_im, precision=HIGH
        )
        model_im = jnp.einsum("ftdp,ftdq->ftpq", row_im, col_re, precision=HIGH) - jnp.einsum(
            "ftdp,ftdq->ftpq", row_re, col_im, precision=HIGH
        )
        resid_re = weight * (vis_re - model_re)
        resid_im = weight * (vis_im - model_im)
        squares, samples = lax.psum(
            (jnp.sum(resid_re * resid_re + resid_im * resid_im), jnp.sum(weight)),
            ("row", "col", "band"),
        )
        sum_re = jnp.einsum("ftpq,ftdq->ftdp", resid_re, col_re, precision=HIGH) - jnp.einsum(
            "ftpq,ftdq->ftdp", resid_im, col_im, precision=HIGH
        )
        sum_im = jnp.einsum("ftpq,ftdq->ftdp", resid_re, col_im, precision=HIGH) + jnp.einsum(
            "ftpq,ftdq->ftdp", resid_im, col_re, precision=HIGH
        )
        pairs = lax.psum_scatter(
            jnp.stack([sum_re, sum_im], axis=2), "col", scatter_dimension=4, tiled=True
        )
        every_mag = every[:, :, 0] * every[:, :, 0] + every[:, :, 1] * every[:, :, 1]
        total_mag = jnp.einsum("ftds,fts->ftd", every_mag, all_live, precision=HIGH)
        own_mag = gain[:, :, 0] * gain[:, :, 0] + gain[:, :, 1] * gain[:, :, 1]
        own_flag = own_live[:, :, None, :]
        own_denom = (scale * scale * own_flag * (total_mag[:, :, :, None] - own_flag * own_mag))[
            :, :, None
        ]
        num_re, num_im = complex_mul(own_cos, -own_sin, pairs[:, :, 0], pairs[:, :, 1])
        numer = jnp.stack([num_re, num_im], axis=2)
        rho = PENALTY * flags.shape[2] * (squares / samples + 1e-06)
        fresh = (numer + own_denom * gain + rho * target) / (own_denom + rho)
        gain = 0.5 * (gain + fresh)
        coeffs = fit(gain, dual)
        dual = dual + gain - jnp.einsum("fk,ktcds->ftcds", local_basis, coeffs, precision=HIGH)
    return (gain, dual)


def solution(mesh):
    sizes = tuple(mesh.shape[a] for a in AXES)

    fits = sizes == (2, 4, 4)

    def body(*args):
        gains = args[5]
        if fits and gains.shape[3:] == (8, 64) and 8 % gains.shape[1] == 0:
            return shards(sizes, *args)
        return plain_shards(*args)

    return jax.shard_map(
        body,
        mesh=mesh,
        in_specs=(
            P("band", None, None, "row", "col"),
            P("band", None, None),
            P(),
            P(),
            P("band", None),
            P("band", None, None, None, ("row", "col")),
            P("band", None, None, None, ("row", "col")),
        ),
        out_specs=(
            P("band", None, None, None, ("row", "col")),
            P("band", None, None, None, ("row", "col")),
        ),
        check_vma=False,
    )
```

time: 147 us -> 130 us (0.88)
  waiting for transfers between devices: 19.2 us -> 37.9 us
  other arithmetic: 17.1 us -> 0 us
  starting transfers between devices: 45.5 us -> 37.2 us
  Pallas kernels: 47.7 us -> 40.7 us
  between operations: 5.49 us -> 0.78 us
  local copies, waits for them, and re-layouts: 9.63 us -> 13.3 us
    ppermute x27 -> x19, waiting for transfers between devices: 6.73 us -> 27.3 us  [permute(): return lax.ppermute(x, AXES, pairs)]
    reduce_sum x9 -> x0, other arithmetic: 10.2 us -> none  [the longest x1 5.97 us: shards(): power = jnp.sum(weight * (vis_re * vis_re + vis_im * vis_im))]
    pallas_call x11 -> x12, Pallas kernels: 47.7 us -> 40.7 us  [the longest x11 38 us: call(): pl.pallas_call(kernel, out_shape=outs, in_specs=[smem] * len(scalars) + [...]
    ppermute x27 -> x19, starting transfers between devices: 37.2 us -> 31 us  [permute(): return lax.ppermute(x, AXES, pairs)]
    unnamed x68 -> x28, local copies, waits for them, and re-layouts: 7.64 us -> 13.3 us
    mul x4 -> x0, other arithmetic: 3.96 us -> none  [shards(): m = jnp.einsum('ftdco,fd->fto', x * x, fl, precision=HIGH)]
    all_to_all x2, starting transfers between devices: 8.23 us -> 6.16 us  [shards(): scalar = lax.all_to_all(scalar, AXES, 0, 0, tiled=True)]
    all_to_all x2, waiting for transfers between devices: 12.5 us -> 10.6 us  [shards(): scalar = lax.all_to_all(scalar, AXES, 0, 0, tiled=True)]
  transfers between devices with their start and end apart: 29 -> 21, of which waited for: 6 -> 10; matrix products, arithmetic and copies ran while one was open for 14% -> 0% of each run, Pallas kernels for 15% -> 10%
where the time goes in v2:
time: 130 us
  Pallas kernels  40.7 us (31%)
  waiting for transfers between devices  37.9 us (29%)
  starting transfers between devices  37.2 us (29%)
  local copies, waits for them, and re-layouts  13.3 us (10%)
    pallas_call x11, Pallas kernels, call(): pl.pallas_call(kernel, out_shape=outs, in_specs=[smem] * len(scalars) + [...  38 us
    ppermute x19, starting transfers between devices, permute(): return lax.ppermute(x, AXES, pairs)  31 us
    ppermute x19, waiting for transfers between devices, permute(): return lax.ppermute(x, AXES, pairs)  27.3 us
    unnamed x28, local copies, waits for them, and re-layouts  13.3 us
    all_to_all x2, waiting for transfers between devices, shards(): scalar = lax.all_to_all(scalar, AXES, 0, 0, tiled=True)  10.6 us
    all_to_all x2, starting transfers between devices, shards(): scalar = lax.all_to_all(scalar, AXES, 0, 0, tiled=True)  6.16 us
    pallas_call x1, Pallas kernels, shards(): pl.pallas_call(functools.partial(start_kernel, dims), out_shape=[whole] *...  2.64 us
  transfers between devices with their start and end apart: 21, of which 10 were waited for; matrix products, arithmetic and copies ran while one was open for 0% of the time, Pallas kernels for 10%

profile of v2, /device:TPU:0, one launch (start us, length us, event | category | flops | bytes accessed | tf_op | source)
XLA Modules:
  0.0 129.9 jit_solution(6559213273116443916)
XLA Ops:
  0.6 1.0 copy-done.6
  1.7 0.7 copy-done.11
  2.4 0.7 copy-done.12
  3.1 0.7 copy-done.13
  3.7 2.6 %start.1 = (f32[64,8,128]{2,1,0:T(8,128)S(1)}, f32[64,8,128]{2,1,0:T(8,128)S(1)}, f32[64,8,128]{2,1,0:T(8,128)S(1)}) custom-call(f32[3,4,512]{2,1,0:T(4,128)S(1)} %bitcast.16, f32[3,8]{1,0:T(4,128)S(1)} %copy-done.12, f32[64]{0:T(128)S(1)} %copy-done.13, f32[16,4,2,8,64]{4,3,2,1,0:T(8,128)S(1)} %copy-done.6), custom_call_target="tpu_custom_call" | custom-call | tf_op jit(solution)/shard_map/start/pallas_call | solution.py:446
  6.4 0.7 collective-permute-start
  7.1 5.7 %collective-permute-start.1 = (f32[64,8,128]{2,1,0:T(8,128)S(1)}, f32[64,8,128]{2,1,0:T(8,128)S(1)}, u32[]{:S(2)}, u32[]{:S(2)}) collective-permute-start(f32[64,8,128]{2,1,0:T(8,128)S(1)} %get-tuple-element.42.mine_ref), channel_id=1, source_target_pairs={{0,16},{1,17},{2,18},{3,19},{4,0},{5,1},{6,2},{7,3},{8,20},{9,21},... | collective-permute-start | bytes 786440 | tf_op jit(solution)/shard_map/ppermute | solution.py:435
  12.8 3.4 %copy-done = bf16[16,4,2,256,128]{4,3,2,1,0:T(8,128)(2,1)S(1)} copy-done((bf16[16,4,2,256,128]{4,3,2,1,0:T(8,128)(2,1)S(1)}, bf16[16,4,2,256,128]{4,3,2,1,0:T(8,128)(2,1)}, u32[]{:S(2)}) %copy-start) | copy-done | bytes 8388632
  16.2 0.8 copy-done.3
  16.9 1.0 copy-done.5
  18.0 0.9 copy-done.8
  18.9 0.7 copy-done.9
  19.6 9.4 %shard_map.113 = (f32[64,128]{1,0:T(8,128)S(1)}, f32[64,128]{1,0:T(8,128)S(1)}, f32[64,128]{1,0:T(8,128)S(1)}, f32[64,8,128]{2,1,0:T(8,128)S(1)}, f32[16,8,128]{...) custom-call(f32[8,16]{1,0:T(8,128)S(1)} %bitcast.10, ...), custom_call_target="tpu_custom_call" | custom-call | tf_op jit(solution)/shard_map/pallas_call | solution.py:411
  29.0 5.2 %shard_map.114 = (f32[72,16,128]{2,1,0:T(8,128)S(1)}, f32[72,16,128]{2,1,0:T(8,128)S(1)}) custom-call(f32[8,16]{1,0:T(8,128)S(1)} %bitcast.11, f32[64,128]{1,0:T(8,128)S(1)} %get-tuple-element.41.live_ref, bf16[16,4,2,256,128]{4,3,2,1,0:T(8,128)(2,1)S(1)} %copy-done.1, f32[64,8,128]{2,1,0:T(8,128)S(1)} %collective-permute-done.a_ref, ...), custom_call_target="tpu_custom_call" | custom-call | tf_op jit(solution)/shard_map/pallas_call | solution.py:411
  34.2 1.3 %collective-permute-start.3 = (f32[64,8,128]{2,1,0:T(8,128)S(1)}, f32[64,8,128]{2,1,0:T(8,128)S(1)}, u32[]{:S(2)}, u32[]{:S(2)}) collective-permute-start(f32[64,8,128]{2,1,0:T(8,128)S(1)} %get-tuple-element.42.mine_ref), channel_id=1, source_target_pairs={{0,8},{1,9},{2,10},{3,11},{4,12},{5,13},{6,14},{7,15},{8,0},{9,1},... | collective-permute-start | bytes 786440 | tf_op jit(solution)/shard_map/ppermute | solution.py:435
  35.5 7.4 %collective-permute-done.3.theirs_ref = f32[64,8,128]{2,1,0:T(8,128)S(1)} collective-permute-done((f32[64,8,128]{2,1,0:T(8,128)S(1)}, f32[64,8,128]{2,1,0:T(8,128)S(1)}, u32[]{:S(2)}, u32[]{:S(2)}) %collective-permute-start.3) | collective-permute-done | bytes 262176 | tf_op jit(solution)/shard_map/ppermute | solution.py:435
  42.9 1.5 %shard_map.115 = (f32[65,8,128]{2,1,0:T(8,128)S(1)}, f32[65,8,128]{2,1,0:T(8,128)S(1)}, f32[32,128]{1,0:T(8,128)}) custom-call(f32[64,128]{1,0:T(8,128)S(1)} %get-tuple-element.36.live_ref, f32[1,128]{1,0:T(1,128)S(1)} %get-tuple-element.40.extra_ref, f32[72,16,128]{2,1,0:T(8,128)S(1)} %get-tuple-element.43.kept_ref, ...), custom_call_target="tpu_custom_call" | custom-call | tf_op jit(solution)/shard_map/pallas_call | solution.py:411
  44.4 1.2 collective-permute-start.4
  45.6 1.6 %collective-permute-start.5 = (f32[16,8,128]{2,1,0:T(8,128)S(1)}, f32[16,8,128]{2,1,0:T(8,128)S(1)}, u32[]{:S(2)}, u32[]{:S(2)}) collective-permute-start(f32[16,8,128]{2,1,0:T(8,128)S(1)} %get-tuple-element.51.refs_0_), channel_id=1, source_target_pairs={{0,1},{1,2},{2,3},{3,0},{4,5},{5,6},{6,7},{7,4},{8,9},{9,10},{10,1... | collective-permute-start | bytes 196616 | tf_op jit(solution)/shard_map/ppermute | solution.py:435
  47.2 2.6 %collective-permute-start.6 = (f32[16,8,128]{2,1,0:T(8,128)S(1)}, f32[16,8,128]{2,1,0:T(8,128)S(1)}, u32[]{:S(2)}, u32[]{:S(2)}) collective-permute-start(f32[16,8,128]{2,1,0:T(8,128)S(1)} %get-tuple-element.51.refs_0_), channel_id=1, source_target_pairs={{0,2},{1,3},{2,0},{3,1},{4,6},{5,7},{6,4},{7,5},{8,10},{9,11},{10,... | collective-permute-start | bytes 196616 | tf_op jit(solution)/shard_map/ppermute | solution.py:435
  49.8 1.3 %collective-permute-start.7 = (f32[16,8,128]{2,1,0:T(8,128)S(1)}, f32[16,8,128]{2,1,0:T(8,128)S(1)}, u32[]{:S(2)}, u32[]{:S(2)}) collective-permute-start(f32[16,8,128]{2,1,0:T(8,128)S(1)} %get-tuple-element.51.refs_0_), channel_id=1, source_target_pairs={{0,3},{1,0},{2,1},{3,2},{4,7},{5,4},{6,5},{7,6},{8,11},{9,8},{10,9... | collective-permute-start | bytes 196616 | tf_op jit(solution)/shard_map/ppermute | solution.py:435
  51.1 2.5 %all-to-all-start = ((f32[32,1,128]{2,1,0:T(1,128)}), f32[32,1,128]{2,1,0:T(1,128)S(1)}, u32[]{:S(2)}, u32[]{:S(2)}) async-start(f32[32,1,128]{2,1,0:T(1,128)} %bitcast.3), calls=%async_computation | async-start | bytes 32768 | tf_op jit(solution)/shard_map/all_to_all | solution.py:480
  53.7 0.7 collective-permute-done.6.refs_2_
  54.4 1.3 shard_map.116.target_ref
  55.7 5.1 %all-to-all-done = f32[32,1,128]{2,1,0:T(1,128)S(1)} async-done(((f32[32,1,128]{2,1,0:T(1,128)}), f32[32,1,128]{2,1,0:T(1,128)S(1)}, u32[]{:S(2)}, u32[]{:S(2)}) %all-to-all-start) | async-done | bytes 16416 | tf_op jit(solution)/shard_map/all_to_all | solution.py:480
  60.8 4.1 %shard_map.117 = (f32[64,8,128]{2,1,0:T(8,128)S(1)}, f32[64,8,128]{2,1,0:T(8,128)S(1)}) custom-call(f32[64,4]{1,0:T(8,128)S(1)} %copy-done.4, f32[65,8,128]{2,1,0:T(8,128)S(1)} %get-tuple-element.45.keep_ref, f32[65,8,128]{2,1,0:T(8,128)S(1)} %collective-permute-done.4.come_ref, f32[32,128]{1,0:T(8,128)S(1)} %bitcast.15, ...), custom_call_target="tpu_custom_call" | custom-call | tf_op jit(solution)/shard_map/pallas_call | solution.py:411
  64.9 0.7 collective-permute-start.8
  65.6 3.3 %collective-permute-start.9 = (f32[64,8,128]{2,1,0:T(8,128)S(1)}, f32[64,8,128]{2,1,0:T(8,128)S(1)}, u32[]{:S(2)}, u32[]{:S(2)}) collective-permute-start(f32[64,8,128]{2,1,0:T(8,128)S(1)} %get-tuple-element.54.mine_ref), channel_id=1, source_target_pairs={{0,16},{1,17},{2,18},{3,19},{4,0},{5,1},{6,2},{7,3},{8,20},{9,21},... | collective-permute-start | bytes 786440 | tf_op jit(solution)/shard_map/ppermute | solution.py:435
  68.9 9.2 %collective-permute-done.9.b_ref = f32[64,8,128]{2,1,0:T(8,128)S(1)} collective-permute-done((f32[64,8,128]{2,1,0:T(8,128)S(1)}, f32[64,8,128]{2,1,0:T(8,128)S(1)}, u32[]{:S(2)}, u32[]{:S(2)}) %collective-permute-start.9) | collective-permute-done | bytes 262176 | tf_op jit(solution)/shard_map/ppermute | solution.py:435
  78.2 3.4 %copy-done.2 = bf16[16,4,2,256,128]{4,3,2,1,0:T(8,128)(2,1)S(1)} copy-done((bf16[16,4,2,256,128]{4,3,2,1,0:T(8,128)(2,1)S(1)}, bf16[16,4,2,256,128]{4,3,2,1,0:T(8,128)(2,1)}, u32[]{:S(2)}) %copy-start.2) | copy-done | bytes 8388632
  81.6 5.2 %shard_map.119 = (f32[72,16,128]{2,1,0:T(8,128)S(1)}, f32[72,16,128]{2,1,0:T(8,128)S(1)}) custom-call(f32[8,16]{1,0:T(8,128)S(1)} %bitcast.12, f32[64,128]{1,0:T(8,128)S(1)} %get-tuple-element.41.live_ref, bf16[16,4,2,256,128]{4,3,2,1,0:T(8,128)(2,1)S(1)} %copy-done.2, f32[64,8,128]{2,1,0:T(8,128)S(1)} %collective-permute-done.8.a_ref, ...), custom_call_target="tpu_custom_call" | custom-call | tf_op jit(solution)/shard_map/pallas_call | solution.py:411
  86.8 1.5 %collective-permute-start.10 = (f32[72,16,128]{2,1,0:T(8,128)S(1)}, f32[72,16,128]{2,1,0:T(8,128)S(1)}, u32[]{:S(2)}, u32[]{:S(2)}) collective-permute-start(f32[72,16,128]{2,1,0:T(8,128)S(1)} %get-tuple-element.56), channel_id=1, source_target_pairs={{0,4},{1,5},{2,6},{3,7},{4,0},{5,1},{6,2},{7,3},{8,12},{9,13},{10,... | collective-permute-start | bytes 1769480 | tf_op jit(solution)/shard_map/ppermute | solution.py:435
  88.3 1.7 %collective-permute-start.11 = (f32[64,8,128]{2,1,0:T(8,128)S(1)}, f32[64,8,128]{2,1,0:T(8,128)S(1)}, u32[]{:S(2)}, u32[]{:S(2)}) collective-permute-start(f32[64,8,128]{2,1,0:T(8,128)S(1)} %get-tuple-element.54.mine_ref), channel_id=1, source_target_pairs={{0,8},{1,9},{2,10},{3,11},{4,12},{5,13},{6,14},{7,15},{8,0},{9,1},... | collective-permute-start | bytes 786440 | tf_op jit(solution)/shard_map/ppermute | solution.py:435
  90.0 1.6 %shard_map.118 = (f32[16,8,128]{2,1,0:T(8,128)S(1)}, f32[64,8,128]{2,1,0:T(8,128)S(1)}, f32[64,8,128]{2,1,0:T(8,128)S(1)}, f32[1,128]{1,0:T(1,128)S(1)}) custom-call(f32[8,16]{1,0:T(8,128)S(1)} %bitcast.13, f32[64,4]{1,0:T(8,128)S(1)} %copy-done.4, f32[1,128]{1,0:T(1,128)S(1)} %get-tuple-element.37.power_ref, f32[64,128]{1,0:T(8,128)S(1)} %get-tuple-element.38.live_ref, ...), custom_call_target="tpu_custom_call" | custom-call | tf_op jit(solution)/shard_map/pallas_call | solution.py:411
  91.6 5.0 %collective-permute-done.11.theirs_ref = f32[64,8,128]{2,1,0:T(8,128)S(1)} collective-permute-done((f32[64,8,128]{2,1,0:T(8,128)S(1)}, f32[64,8,128]{2,1,0:T(8,128)S(1)}, u32[]{:S(2)}, u32[]{:S(2)}) %collective-permute-start.11) | collective-permute-done | bytes 262176 | tf_op jit(solution)/shard_map/ppermute | solution.py:435
  96.6 1.5 %shard_map.120 = (f32[65,8,128]{2,1,0:T(8,128)S(1)}, f32[65,8,128]{2,1,0:T(8,128)S(1)}, f32[32,128]{1,0:T(8,128)}) custom-call(f32[64,128]{1,0:T(8,128)S(1)} %get-tuple-element.36.live_ref, f32[1,128]{1,0:T(1,128)S(1)} %get-tuple-element.53.extra_ref, f32[72,16,128]{2,1,0:T(8,128)S(1)} %get-tuple-element.55.kept_ref, ...), custom_call_target="tpu_custom_call" | custom-call | tf_op jit(solution)/shard_map/pallas_call | solution.py:411
  98.1 1.7 %collective-permute-start.12 = (f32[65,8,128]{2,1,0:T(8,128)S(1)}, f32[65,8,128]{2,1,0:T(8,128)S(1)}, u32[]{:S(2)}, u32[]{:S(2)}) collective-permute-start(f32[65,8,128]{2,1,0:T(8,128)S(1)} %get-tuple-element.58), channel_id=1, source_target_pairs={{0,8},{1,9},{2,10},{3,11},{4,12},{5,13},{6,14},{7,15},{8,0},{9,1},... | collective-permute-start | bytes 798728 | tf_op jit(solution)/shard_map/ppermute | solution.py:435
  99.8 0.6 collective-permute-start.13
  100.9 2.7 %collective-permute-start.15 = (f32[16,8,128]{2,1,0:T(8,128)S(1)}, f32[16,8,128]{2,1,0:T(8,128)S(1)}, u32[]{:S(2)}, u32[]{:S(2)}) collective-permute-start(f32[16,8,128]{2,1,0:T(8,128)S(1)} %get-tuple-element.62.refs_0_), channel_id=1, source_target_pairs={{0,3},{1,0},{2,1},{3,2},{4,7},{5,4},{6,5},{7,6},{8,11},{9,8},{10,9... | collective-permute-start | bytes 196616 | tf_op jit(solution)/shard_map/ppermute | solution.py:435
  103.6 3.6 %all-to-all-start.1 = ((f32[32,1,128]{2,1,0:T(1,128)}), f32[32,1,128]{2,1,0:T(1,128)S(1)}, u32[]{:S(2)}, u32[]{:S(2)}) async-start(f32[32,1,128]{2,1,0:T(1,128)} %bitcast.6), calls=%async_computation.1 | async-start | bytes 32768 | tf_op jit(solution)/shard_map/all_to_all | solution.py:480
  107.5 1.3 %shard_map.121 = (f32[64,8,128]{2,1,0:T(8,128)S(1)}, f32[64,8,128]{2,1,0:T(8,128)S(1)}) custom-call(f32[64,4]{1,0:T(8,128)S(1)} %copy-done.7, f32[64,8,128]{2,1,0:T(8,128)S(1)} %get-tuple-element.39.u_ref, f32[64,8,128]{2,1,0:T(8,128)S(1)} %get-tuple-element.52.g_ref, f32[16,8,128]{2,1,0:T(8,128)S(1)} %get-tuple-element.62.refs_0_, ...), custom_call_target="tpu_custom_call" | custom-call | tf_op jit(solution)/shard_map/pallas_call | solution.py:411
  108.8 5.6 %all-to-all-done.1 = f32[32,1,128]{2,1,0:T(1,128)S(1)} async-done(((f32[32,1,128]{2,1,0:T(1,128)}), f32[32,1,128]{2,1,0:T(1,128)S(1)}, u32[]{:S(2)}, u32[]{:S(2)}) %all-to-all-start.1) | async-done | bytes 16416 | tf_op jit(solution)/shard_map/all_to_all | solution.py:480
  114.3 4.9 %shard_map.122 = (f32[16,4,2,8,64]{4,3,2,1,0:T(8,128)}, f32[64,8,128]{2,1,0:T(8,128)S(1)}, f32[16,8,128]{2,1,0:T(8,128)S(1)}) custom-call(f32[64,4]{1,0:T(8,128)S(1)} %copy-done.4, f32[65,8,128]{2,1,0:T(8,128)S(1)} %get-tuple-element.57.keep_ref, f32[65,8,128]{2,1,0:T(8,128)S(1)} %collective-permute-done.12.come_ref, f32[32,128]{1,0:T(8,128)S(1)} %bitcast.14, ...), custom_call_target="tpu_custom_call" | custom-call | tf_op jit(solution)/shard_map/pallas_call | solution.py:411
  119.7 0.6 collective-permute-start.17
  120.4 2.7 %collective-permute-start.18 = (f32[16,8,128]{2,1,0:T(8,128)S(1)}, f32[16,8,128]{2,1,0:T(8,128)S(1)}, u32[]{:S(2)}, u32[]{:S(2)}) collective-permute-start(f32[16,8,128]{2,1,0:T(8,128)S(1)} %get-tuple-element.67.refs_0_), channel_id=1, source_target_pairs={{0,3},{1,0},{2,1},{3,2},{4,7},{5,4},{6,5},{7,6},{8,11},{9,8},{10,9... | collective-permute-start | bytes 196616 | tf_op jit(solution)/shard_map/ppermute | solution.py:435
  123.1 2.9 %collective-permute-done.16.refs_1_ = f32[16,8,128]{2,1,0:T(8,128)S(1)} collective-permute-done((f32[16,8,128]{2,1,0:T(8,128)S(1)}, f32[16,8,128]{2,1,0:T(8,128)S(1)}, u32[]{:S(2)}, u32[]{:S(2)}) %collective-permute-start.16) | collective-permute-done | bytes 65568 | tf_op jit(solution)/shard_map/ppermute | solution.py:435
  126.0 1.7 %collective-permute-done.17.refs_2_ = f32[16,8,128]{2,1,0:T(8,128)S(1)} collective-permute-done((f32[16,8,128]{2,1,0:T(8,128)S(1)}, f32[16,8,128]{2,1,0:T(8,128)S(1)}, u32[]{:S(2)}, u32[]{:S(2)}) %collective-permute-start.17) | collective-permute-done | bytes 65568 | tf_op jit(solution)/shard_map/ppermute | solution.py:435
  127.7 2.2 %shard_map.123 = f32[16,4,2,8,64]{4,3,2,1,0:T(8,128)} custom-call(f32[64,4]{1,0:T(8,128)S(1)} %copy-done.7, f32[64,8,128]{2,1,0:T(8,128)S(1)} %get-tuple-element.66.total_ref, f32[16,8,128]{2,1,0:T(8,128)S(1)} %get-tuple-element.67.refs_0_, f32[16,8,128]{2,1,0:T(8,128)S(1)} %collective-permute-done.16.refs_1_, ...), custom_call_target="tpu_custom_call" | custom-call | tf_op jit(solution)/shard_map/pallas_call | solution.py:411
  (34 shorter events, 1.3 us)
Async XLA Ops:
  0.6 1.0 copy-start.6
  1.7 0.7 copy-start.11
  2.4 0.7 copy-start.12
  3.1 0.7 copy-start.13
  6.4 22.6 %collective-permute-start = (f32[64,8,128]{2,1,0:T(8,128)S(1)}, f32[64,8,128]{2,1,0:T(8,128)S(1)}, u32[]{:S(2)}, u32[]{:S(2)}) collective-permute-start(f32[64,8,128]{2,1,0:T(8,128)S(1)} %get-tuple-element.42.mine_ref), channel_id=1, source_target_pairs={{0,0},{1,1},{2,2},{3,3},{4,16},{5,17},{6,18},{7,19},{8,4},{9,5},{1... | collective-permute-start | bytes 786440 | tf_op jit(solution)/shard_map/ppermute | solution.py:435
  7.1 21.9 %collective-permute-start.1 = (f32[64,8,128]{2,1,0:T(8,128)S(1)}, f32[64,8,128]{2,1,0:T(8,128)S(1)}, u32[]{:S(2)}, u32[]{:S(2)}) collective-permute-start(f32[64,8,128]{2,1,0:T(8,128)S(1)} %get-tuple-element.42.mine_ref), channel_id=1, source_target_pairs={{0,16},{1,17},{2,18},{3,19},{4,0},{5,1},{6,2},{7,3},{8,20},{9,21},... | collective-permute-start | bytes 786440 | tf_op jit(solution)/shard_map/ppermute | solution.py:435
  12.8 3.4 %copy-start = (bf16[16,4,2,256,128]{4,3,2,1,0:T(8,128)(2,1)S(1)}, bf16[16,4,2,256,128]{4,3,2,1,0:T(8,128)(2,1)}, u32[]{:S(2)}) copy-start(bf16[16,4,2,256,128]{4,3,2,1,0:T(8,128)(2,1)} %vis_ref.5) | copy-start | bytes 25165828
  16.2 0.8 copy-start.3
  16.9 1.0 copy-start.5
  18.0 0.9 copy-start.8
  18.9 0.7 copy-start.9
  19.6 9.4 %copy-start.1 = (bf16[16,4,2,256,128]{4,3,2,1,0:T(8,128)(2,1)S(1)}, bf16[16,4,2,256,128]{4,3,2,1,0:T(8,128)(2,1)}, u32[]{:S(2)}) copy-start(bf16[16,4,2,256,128]{4,3,2,1,0:T(8,128)(2,1)} %vis_ref.5) | copy-start | bytes 25165828
  19.6 34.9 %copy-start.7 = (f32[64,4]{1,0:T(8,128)S(1)}, f32[64,4]{1,0:T(8,128)}, u32[]{:S(2)}) copy-start(f32[64,4]{1,0:T(8,128)} %constant.7.clone.coef_ref) | copy-start | bytes 3076
  19.6 41.2 %copy-start.4 = (f32[64,4]{1,0:T(8,128)S(1)}, f32[64,4]{1,0:T(8,128)}, u32[]{:S(2)}) copy-start(f32[64,4]{1,0:T(8,128)} %constant.6.clone.basis_ref) | copy-start | bytes 3076
  28.9 49.2 %copy-start.10 = (f32[16,8]{0,1:T(8,128)S(1)}, f32[16,8]{0,1:T(8,128)}, u32[]{:S(2)}) copy-start(f32[16,8]{0,1:T(8,128)} %param.14) | copy-start | bytes 1540
  34.2 8.7 %collective-permute-start.2 = (f32[72,16,128]{2,1,0:T(8,128)S(1)}, f32[72,16,128]{2,1,0:T(8,128)S(1)}, u32[]{:S(2)}, u32[]{:S(2)}) collective-permute-start(f32[72,16,128]{2,1,0:T(8,128)S(1)} %get-tuple-element.44), channel_id=1, source_target_pairs={{0,4},{1,5},{2,6},{3,7},{4,0},{5,1},{6,2},{7,3},{8,12},{9,13},{10,... | collective-permute-start | bytes 1769480 | tf_op jit(solution)/shard_map/ppermute | solution.py:435
  34.2 8.7 %collective-permute-start.3 = (f32[64,8,128]{2,1,0:T(8,128)S(1)}, f32[64,8,128]{2,1,0:T(8,128)S(1)}, u32[]{:S(2)}, u32[]{:S(2)}) collective-permute-start(f32[64,8,128]{2,1,0:T(8,128)S(1)} %get-tuple-element.42.mine_ref), channel_id=1, source_target_pairs={{0,8},{1,9},{2,10},{3,11},{4,12},{5,13},{6,14},{7,15},{8,0},{9,1},... | collective-permute-start | bytes 786440 | tf_op jit(solution)/shard_map/ppermute | solution.py:435
  44.4 16.4 %collective-permute-start.4 = (f32[65,8,128]{2,1,0:T(8,128)S(1)}, f32[65,8,128]{2,1,0:T(8,128)S(1)}, u32[]{:S(2)}, u32[]{:S(2)}) collective-permute-start(f32[65,8,128]{2,1,0:T(8,128)S(1)} %get-tuple-element.46), channel_id=1, source_target_pairs={{0,8},{1,9},{2,10},{3,11},{4,12},{5,13},{6,14},{7,15},{8,0},{9,1},... | collective-permute-start | bytes 798728 | tf_op jit(solution)/shard_map/ppermute | solution.py:435
  45.6 8.1 %collective-permute-start.5 = (f32[16,8,128]{2,1,0:T(8,128)S(1)}, f32[16,8,128]{2,1,0:T(8,128)S(1)}, u32[]{:S(2)}, u32[]{:S(2)}) collective-permute-start(f32[16,8,128]{2,1,0:T(8,128)S(1)} %get-tuple-element.51.refs_0_), channel_id=1, source_target_pairs={{0,1},{1,2},{2,3},{3,0},{4,5},{5,6},{6,7},{7,4},{8,9},{9,10},{10,1... | collective-permute-start | bytes 196616 | tf_op jit(solution)/shard_map/ppermute | solution.py:435
  47.2 7.2 %collective-permute-start.6 = (f32[16,8,128]{2,1,0:T(8,128)S(1)}, f32[16,8,128]{2,1,0:T(8,128)S(1)}, u32[]{:S(2)}, u32[]{:S(2)}) collective-permute-start(f32[16,8,128]{2,1,0:T(8,128)S(1)} %get-tuple-element.51.refs_0_), channel_id=1, source_target_pairs={{0,2},{1,3},{2,0},{3,1},{4,6},{5,7},{6,4},{7,5},{8,10},{9,11},{10,... | collective-permute-start | bytes 196616 | tf_op jit(solution)/shard_map/ppermute | solution.py:435
  49.8 4.7 %collective-permute-start.7 = (f32[16,8,128]{2,1,0:T(8,128)S(1)}, f32[16,8,128]{2,1,0:T(8,128)S(1)}, u32[]{:S(2)}, u32[]{:S(2)}) collective-permute-start(f32[16,8,128]{2,1,0:T(8,128)S(1)} %get-tuple-element.51.refs_0_), channel_id=1, source_target_pairs={{0,3},{1,0},{2,1},{3,2},{4,7},{5,4},{6,5},{7,6},{8,11},{9,8},{10,9... | collective-permute-start | bytes 196616 | tf_op jit(solution)/shard_map/ppermute | solution.py:435
  51.1 9.7 %all-to-all-start = ((f32[32,1,128]{2,1,0:T(1,128)}), f32[32,1,128]{2,1,0:T(1,128)S(1)}, u32[]{:S(2)}, u32[]{:S(2)}) async-start(f32[32,1,128]{2,1,0:T(1,128)} %bitcast.3), calls=%async_computation | async-start | bytes 32768 | tf_op jit(solution)/shard_map/all_to_all | solution.py:480
  64.9 4.0 %collective-permute-start.8 = (f32[64,8,128]{2,1,0:T(8,128)S(1)}, f32[64,8,128]{2,1,0:T(8,128)S(1)}, u32[]{:S(2)}, u32[]{:S(2)}) collective-permute-start(f32[64,8,128]{2,1,0:T(8,128)S(1)} %get-tuple-element.54.mine_ref), channel_id=1, source_target_pairs={{0,0},{1,1},{2,2},{3,3},{4,16},{5,17},{6,18},{7,19},{8,4},{9,5},{1... | collective-permute-start | bytes 786440 | tf_op jit(solution)/shard_map/ppermute | solution.py:435
  65.6 12.6 %collective-permute-start.9 = (f32[64,8,128]{2,1,0:T(8,128)S(1)}, f32[64,8,128]{2,1,0:T(8,128)S(1)}, u32[]{:S(2)}, u32[]{:S(2)}) collective-permute-start(f32[64,8,128]{2,1,0:T(8,128)S(1)} %get-tuple-element.54.mine_ref), channel_id=1, source_target_pairs={{0,16},{1,17},{2,18},{3,19},{4,0},{5,1},{6,2},{7,3},{8,20},{9,21},... | collective-permute-start | bytes 786440 | tf_op jit(solution)/shard_map/ppermute | solution.py:435
  78.2 3.4 %copy-start.2 = (bf16[16,4,2,256,128]{4,3,2,1,0:T(8,128)(2,1)S(1)}, bf16[16,4,2,256,128]{4,3,2,1,0:T(8,128)(2,1)}, u32[]{:S(2)}) copy-start(bf16[16,4,2,256,128]{4,3,2,1,0:T(8,128)(2,1)} %vis_ref.5) | copy-start | bytes 25165828
  86.8 9.8 %collective-permute-start.10 = (f32[72,16,128]{2,1,0:T(8,128)S(1)}, f32[72,16,128]{2,1,0:T(8,128)S(1)}, u32[]{:S(2)}, u32[]{:S(2)}) collective-permute-start(f32[72,16,128]{2,1,0:T(8,128)S(1)} %get-tuple-element.56), channel_id=1, source_target_pairs={{0,4},{1,5},{2,6},{3,7},{4,0},{5,1},{6,2},{7,3},{8,12},{9,13},{10,... | collective-permute-start | bytes 1769480 | tf_op jit(solution)/shard_map/ppermute | solution.py:435
  88.3 8.3 %collective-permute-start.11 = (f32[64,8,128]{2,1,0:T(8,128)S(1)}, f32[64,8,128]{2,1,0:T(8,128)S(1)}, u32[]{:S(2)}, u32[]{:S(2)}) collective-permute-start(f32[64,8,128]{2,1,0:T(8,128)S(1)} %get-tuple-element.54.mine_ref), channel_id=1, source_target_pairs={{0,8},{1,9},{2,10},{3,11},{4,12},{5,13},{6,14},{7,15},{8,0},{9,1},... | collective-permute-start | bytes 786440 | tf_op jit(solution)/shard_map/ppermute | solution.py:435
  98.1 16.3 %collective-permute-start.12 = (f32[65,8,128]{2,1,0:T(8,128)S(1)}, f32[65,8,128]{2,1,0:T(8,128)S(1)}, u32[]{:S(2)}, u32[]{:S(2)}) collective-permute-start(f32[65,8,128]{2,1,0:T(8,128)S(1)} %get-tuple-element.58), channel_id=1, source_target_pairs={{0,8},{1,9},{2,10},{3,11},{4,12},{5,13},{6,14},{7,15},{8,0},{9,1},... | collective-permute-start | bytes 798728 | tf_op jit(solution)/shard_map/ppermute | solution.py:435
  99.8 7.5 %collective-permute-start.13 = (f32[16,8,128]{2,1,0:T(8,128)S(1)}, f32[16,8,128]{2,1,0:T(8,128)S(1)}, u32[]{:S(2)}, u32[]{:S(2)}) collective-permute-start(f32[16,8,128]{2,1,0:T(8,128)S(1)} %get-tuple-element.62.refs_0_), channel_id=1, source_target_pairs={{0,1},{1,2},{2,3},{3,0},{4,5},{5,6},{6,7},{7,4},{8,9},{9,10},{10,1... | collective-permute-start | bytes 196616 | tf_op jit(solution)/shard_map/ppermute | solution.py:435
  100.4 7.1 %collective-permute-start.14 = (f32[16,8,128]{2,1,0:T(8,128)S(1)}, f32[16,8,128]{2,1,0:T(8,128)S(1)}, u32[]{:S(2)}, u32[]{:S(2)}) collective-permute-start(f32[16,8,128]{2,1,0:T(8,128)S(1)} %get-tuple-element.62.refs_0_), channel_id=1, source_target_pairs={{0,2},{1,3},{2,0},{3,1},{4,6},{5,7},{6,4},{7,5},{8,10},{9,11},{10,... | collective-permute-start | bytes 196616 | tf_op jit(solution)/shard_map/ppermute | solution.py:435
  100.9 6.6 %collective-permute-start.15 = (f32[16,8,128]{2,1,0:T(8,128)S(1)}, f32[16,8,128]{2,1,0:T(8,128)S(1)}, u32[]{:S(2)}, u32[]{:S(2)}) collective-permute-start(f32[16,8,128]{2,1,0:T(8,128)S(1)} %get-tuple-element.62.refs_0_), channel_id=1, source_target_pairs={{0,3},{1,0},{2,1},{3,2},{4,7},{5,4},{6,5},{7,6},{8,11},{9,8},{10,9... | collective-permute-start | bytes 196616 | tf_op jit(solution)/shard_map/ppermute | solution.py:435
  103.6 10.8 %all-to-all-start.1 = ((f32[32,1,128]{2,1,0:T(1,128)}), f32[32,1,128]{2,1,0:T(1,128)S(1)}, u32[]{:S(2)}, u32[]{:S(2)}) async-start(f32[32,1,128]{2,1,0:T(1,128)} %bitcast.6), calls=%async_computation.1 | async-start | bytes 32768 | tf_op jit(solution)/shard_map/all_to_all | solution.py:480
  119.2 6.8 %collective-permute-start.16 = (f32[16,8,128]{2,1,0:T(8,128)S(1)}, f32[16,8,128]{2,1,0:T(8,128)S(1)}, u32[]{:S(2)}, u32[]{:S(2)}) collective-permute-start(f32[16,8,128]{2,1,0:T(8,128)S(1)} %get-tuple-element.67.refs_0_), channel_id=1, source_target_pairs={{0,1},{1,2},{2,3},{3,0},{4,5},{5,6},{6,7},{7,4},{8,9},{9,10},{10,1... | collective-permute-start | bytes 196616 | tf_op jit(solution)/shard_map/ppermute | solution.py:435
  119.7 8.0 %collective-permute-start.17 = (f32[16,8,128]{2,1,0:T(8,128)S(1)}, f32[16,8,128]{2,1,0:T(8,128)S(1)}, u32[]{:S(2)}, u32[]{:S(2)}) collective-permute-start(f32[16,8,128]{2,1,0:T(8,128)S(1)} %get-tuple-element.67.refs_0_), channel_id=1, source_target_pairs={{0,2},{1,3},{2,0},{3,1},{4,6},{5,7},{6,4},{7,5},{8,10},{9,11},{10,... | collective-permute-start | bytes 196616 | tf_op jit(solution)/shard_map/ppermute | solution.py:435
  120.4 7.4 %collective-permute-start.18 = (f32[16,8,128]{2,1,0:T(8,128)S(1)}, f32[16,8,128]{2,1,0:T(8,128)S(1)}, u32[]{:S(2)}, u32[]{:S(2)}) collective-permute-start(f32[16,8,128]{2,1,0:T(8,128)S(1)} %get-tuple-element.67.refs_0_), channel_id=1, source_target_pairs={{0,3},{1,0},{2,1},{3,2},{4,7},{5,4},{6,5},{7,6},{8,11},{9,8},{10,9... | collective-permute-start | bytes 196616 | tf_op jit(solution)/shard_map/ppermute | solution.py:435

commit v3 on v2

--- a/solution.py
+++ b/solution.py
@@ -67,30 +67,40 @@
     return g * cos2 - swap(g) * sin2
 
 
-def start_kernel(dims, pos_ref, lmn_ref, freq_ref, gains_ref, e_ref, g_ref, p_ref):
+def start_kernel(dims, pos_hbm, lmn_hbm, gains_hbm, e_ref, g_ref, p_ref, pos_ref, lmn_ref, gains_ref, sems):
     F, T, D, O, R, C = dims
     W = 2 * O
+    copies = [
+        pltpu.make_async_copy(pos_hbm, pos_ref, sems.at[0]),
+        pltpu.make_async_copy(lmn_hbm, lmn_ref, sems.at[1]),
+        pltpu.make_async_copy(gains_hbm, gains_ref, sems.at[2]),
+    ]
+    for copy in copies:
+        copy.start()
     own = lax.axis_index("row") * C + lax.axis_index("col")
     first = lax.axis_index("band") * F
     low = low_lanes((D, W))
-    shape = pos_ref[:, :, :O].shape
-    pos = jnp.zeros(shape, jnp.float32)
-    for k in range(R * C):
+    rows = lax.broadcasted_iota(jnp.int32, (D, W), 0)
+    shift = jnp.where(low, 0.0, 0.25)
+    copies[0].wait()
+    copies[1].wait()
+    pos = pos_ref[:, :, :O]
+    for k in range(1, R * C):
         pos = jnp.where(own == k, pos_ref[:, :, k * O : (k + 1) * O], pos)
     pos = jnp.concatenate([pos, pos], axis=-1)
     geometry = []
     for t in range(T):
         total = jnp.zeros((D, W), jnp.float32)
         for k in range(3):
-            rows = lax.broadcasted_iota(jnp.int32, (D, W), 0)
             lm = jnp.full((D, W), lmn_ref[k, 0], jnp.float32)
             for d in range(1, D):
                 lm = jnp.where(rows == d, lmn_ref[k, d], lm)
             total = total + lm * pos[k, t : t + 1, :]
         geometry.append(total)
-    shift = jnp.where(low, 0.0, 0.25)
+    copies[2].wait()
+    total_f = F * lax.axis_size("band")
     for f in range(F):
-        nu = freq_ref[first + f]
+        nu = 1.0 + (first + f).astype(jnp.float32) * (1.0 / total_f)
         for t in range(T):
             ft = f * T + t
             turns = nu * geometry[t]
@@ -121,17 +131,45 @@
     return total
 
 
-def fit_sums(dims, basis_ref, value, rhs_ref):
+def place(dims, f):
+    F = dims[0]
+    full = F * lax.axis_size("band")
+    at = (lax.axis_index("band") * F + f).astype(jnp.float32)
+    return at * (2.0 / (full - 1)) - 1.0
+
+
+def fit_sums(dims, value, rhs_ref):
     F, T, D, O, _, _ = dims
-    first = lax.axis_index("band") * F
     for t in range(T):
         acc = [jnp.zeros((D, 2 * O), jnp.float32) for _ in range(4)]
         for f in range(F):
             total = value(f, t)
+            x = place(dims, f)
             for k in range(4):
-                acc[k] = acc[k] + basis_ref[first + f, k] * total
+                acc[k] = acc[k] + total
+                total = total * x if k < 3 else total
         for k in range(4):
             rhs_ref[k * T + t] = acc[k]
+
+
+def solve(dims, rhs_refs, t):
+    T = dims[1]
+    full = dims[0] * lax.axis_size("band")
+    grid = 2.0 * np.arange(full, dtype=np.float64) / (full - 1) - 1.0
+    basis = np.stack([grid**k for k in range(4)], axis=1)
+    inverse = np.linalg.inv(basis.T @ basis)
+    rhs = [sum(ref[k * T + t] for ref in rhs_refs) for k in range(4)]
+    out = []
+    for k in range(4):
+        total = float(inverse[k, 0]) * rhs[0]
+        for j in range(1, 4):
+            total = total + float(inverse[k, j]) * rhs[j]
+        out.append(total)
+    return out
+
+
+def curve(coeffs, x):
+    return coeffs[0] + x * (coeffs[1] + x * (coeffs[2] + x * coeffs[3]))
 
 
 def pick(index, parts):
@@ -141,21 +179,27 @@
     return out
 
 
-def setup_kernel(dims, flux_ref, basis_ref, flags_ref, vis_ref, duals_ref, g_ref,
-                 live_col_ref, live_half_ref, live_own_ref, u_ref, rhs_ref, held_ref, slope_ref,
-                 power_ref, extra_ref, distinct):
+def setup_kernel(dims, flux_ref, flags_hbm, vis_hbm, duals_hbm, g_ref,
+                 live_col_ref, live_half_ref, live_own_ref, u_ref, rhs_ref, held_ref,
+                 slope_ref, power_ref, extra_ref, vis_ref, flags_ref, duals_ref, sems):
     F, T, _, O, R, C = dims
     rows, cols = vis_ref.shape[3], vis_ref.shape[4]
     row = lax.axis_index("row")
     col = lax.axis_index("col")
-    p = lax.broadcasted_iota(jnp.int32, (rows, cols), 0) + row * rows
-    q = lax.broadcasted_iota(jnp.int32, (rows, cols), 1) + col * cols
-    distinct[...] = jnp.where(p == q, 0.0, 1.0).astype(jnp.bfloat16)
-    counts = jnp.zeros((T, 1), jnp.float32)
+    flags_copy = pltpu.make_async_copy(flags_hbm, flags_ref, sems.at[F])
+    duals_copy = pltpu.make_async_copy(duals_hbm, duals_ref, sems.at[F + 1])
+    flags_copy.start()
+    duals_copy.start()
+
+    def vis_copy(f):
+        return pltpu.make_async_copy(vis_hbm.at[f], vis_ref.at[f], sems.at[f])
+
+    for f in range(F):
+        vis_copy(f).start()
+    flags_copy.wait()
+    counts = jnp.zeros((T, full_lanes(flags_ref)), jnp.float32)
     for f in range(F):
         live = flags_ref[f].astype(jnp.float32)
-        count = jnp.sum(live, axis=1, keepdims=True)
-        counts = counts + count * (count - 1.0)
         at = slice(f * T, (f + 1) * T)
         mine = pick(row, [live[:, r * rows : (r + 1) * rows] for r in range(R)])
         blocks = [mine[:, c * O : (c + 1) * O] for c in range(C)]
@@ -165,55 +209,73 @@
         live_half_ref[at, :] = pick(col % 2, [even, odd])
         own = pick(col, blocks)
         live_own_ref[at, :] = jnp.concatenate([own, own], axis=1)
+        count = jnp.sum(live, axis=1, keepdims=True)
+        counts = counts + live * (count - 1.0)
     samples = jnp.sum(counts) / (R * C)
+    duals_copy.wait()
+    for f in range(F):
+        for t in range(T):
+            u_ref[f * T + t] = jnp.concatenate([duals_ref[f, t, 0], duals_ref[f, t, 1]], axis=-1)
+    fit_sums(dims, lambda f, t: u_ref[f * T + t] + g_ref[f * T + t], rhs_ref)
+    own = own_terms(dims, flux_ref, live_own_ref, g_ref, held_ref, slope_ref)
+    per = rows // cols
+    p = lax.broadcasted_iota(jnp.int32, (cols, cols), 0)
+    q = lax.broadcasted_iota(jnp.int32, (cols, cols), 1)
+    distinct = jnp.where(p == q, 0.0, 1.0).astype(jnp.bfloat16)
+    corner = pl.multiple_of((col % per) * cols, cols)
 
     def channel(f, acc):
+        vis_copy(f).wait()
+
+        @pl.when(col // per == row)
+        def _():
+            for t in range(T):
+                for part in range(2):
+                    at = vis_ref.at[f, t, part, pl.ds(corner, cols), :]
+                    at[...] = at[...] * distinct
+
         live = flags_ref[f].astype(jnp.float32)
         mine = pick(row, [live[:, r * rows : (r + 1) * rows] for r in range(R)])
         pair = pick(col, [live[:, c * cols : (c + 1) * cols] for c in range(C)])
         upright = jnp.transpose(jnp.concatenate([mine] * (8 // T), axis=0))
         for t in range(T):
-            weight = jnp.broadcast_to(upright[:, t : t + 1], (rows, cols)) * pair[t : t + 1, :]
-            weight = weight.astype(jnp.bfloat16) * distinct[...]
+            weight = jnp.broadcast_to(upright[:, t : t + 1], (rows, cols)).astype(jnp.bfloat16)
+            total = jnp.zeros((16, cols), jnp.float32)
             for part in range(2):
                 seen = (vis_ref[f, t, part] * weight).astype(jnp.float32)
-                acc = acc + jnp.sum((seen * seen).reshape(rows // 32, 32, cols), axis=0)
+                total = total + jnp.sum((seen * seen).reshape(rows // 16, 16, cols), axis=0)
+            acc = acc + total * pair[t : t + 1, :]
         return acc
 
-    power = lax.fori_loop(0, F, channel, jnp.zeros((32, cols), jnp.float32))
+    power = lax.fori_loop(0, F, channel, jnp.zeros((16, cols), jnp.float32))
     power = jnp.sum(power, axis=0, keepdims=True)
     low = low_lanes(power.shape)
     lanes = lax.broadcasted_iota(jnp.int32, power.shape, 1)
     row_power = jnp.where(low, power + swap(power), jnp.where(lanes == O, samples, 0.0))
     power_ref[...] = row_power
-    for f in range(F):
-        for t in range(T):
-            u_ref[f * T + t] = jnp.concatenate([duals_ref[f, t, 0], duals_ref[f, t, 1]], axis=-1)
-    fit_sums(dims, basis_ref, lambda f, t: u_ref[f * T + t] + g_ref[f * T + t], rhs_ref)
-    own = own_terms(dims, flux_ref, live_own_ref, g_ref, held_ref, slope_ref)
     extra_ref[...] = row_power - jnp.where(low, own, 0.0)
 
 
-def again_kernel(dims, flux_ref, basis_ref, power_ref, live_ref, u_ref, g_ref,
+def full_lanes(ref):
+    return ref.shape[-1]
+
+
+def again_kernel(dims, flux_ref, power_ref, live_ref, u_ref, g_ref,
                  rhs_ref, held_ref, slope_ref, extra_ref):
     _, T, _, _, _, _ = dims
-    fit_sums(dims, basis_ref, lambda f, t: u_ref[f * T + t] + g_ref[f * T + t], rhs_ref)
+    fit_sums(dims, lambda f, t: u_ref[f * T + t] + g_ref[f * T + t], rhs_ref)
     own = own_terms(dims, flux_ref, live_ref, g_ref, held_ref, slope_ref)
     extra_ref[...] = power_ref[...] - jnp.where(low_lanes(own.shape), own, 0.0)
 
 
-def target_kernel(dims, first_pass, coef_ref, u_ref, g_ref, *refs):
+def target_kernel(dims, first_pass, u_ref, g_ref, *refs):
     F, T, _, _, _, _ = dims
     rhs_refs, outs = refs[:4], refs[4:]
-    first = lax.axis_index("band") * F
     for t in range(T):
-        rhs = [rhs_refs[0][k * T + t] + rhs_refs[1][k * T + t]
-               + rhs_refs[2][k * T + t] + rhs_refs[3][k * T + t] for k in range(4)]
+        coeffs = solve(dims, rhs_refs, t)
         for f in range(F):
             ft = f * T + t
-            smooth = coef_ref[first + f, 0] * rhs[0]
-            for k in range(1, 4):
-                smooth = smooth + coef_ref[first + f, k] * rhs[k]
+            smooth = curve(coeffs, place(dims, f))
             u = u_ref[ft]
             if not first_pass:
                 u = u + g_ref[ft] - smooth
@@ -228,12 +290,18 @@
     return a == b
 
 
-def sum_kernel(dims, flux_ref, live_ref, vis_ref, a_ref, b_ref, keep_ref, send_ref, distinct):
+def sum_kernel(dims, flux_ref, vis_hbm, live_ref, a_ref, b_ref, keep_ref, send_ref, vis_ref, distinct, sems):
     F, T, D, O, _, _ = dims
     rows, cols = vis_ref.shape[3], vis_ref.shape[4]
     row = lax.axis_index("row")
     col = lax.axis_index("col")
     parity = col % 2
+
+    def vis_copy(f):
+        return pltpu.make_async_copy(vis_hbm.at[f], vis_ref.at[f], sems.at[f])
+
+    for f in range(F):
+        vis_copy(f).start()
     p = lax.broadcasted_iota(jnp.int32, (rows, cols), 0) + row * rows
     q = lax.broadcasted_iota(jnp.int32, (rows, cols), 1) + col * cols
     distinct[...] = jnp.where(p == q, 0.0, 1.0).astype(jnp.bfloat16)
@@ -246,6 +314,7 @@
         lives = live_ref[pl.ds(step * 8, 8), :]
         for i in range(group):
             f = step * group + i
+            vis_copy(f).wait()
             scale = column(flux_ref, f, D, cols)
             for t in range(T):
                 j = i * T + t
@@ -285,7 +354,7 @@
         send_ref[step * 9 + 8] = folded
         return carry
 
-    lax.fori_loop(0, F * T // 8, body, 0)
+    lax.fori_loop(0, F * T // 8, body, 0, unroll=2)
 
 
 def residual_kernel(dims, live_ref, extra_ref, kept_ref, other_ref, mine_ref, theirs_ref,
@@ -330,10 +399,31 @@
     scalar_ref[...] = jnp.broadcast_to(scalar, scalar_ref.shape)
 
 
-def update_kernel(dims, last, full, basis_ref, keep_ref, come_ref, scalar_ref, live_ref, e_ref,
-                  g_ref, held_ref, slope_ref, target_ref, *refs):
+def merge_kernel(dims, keep_ref, come_ref, live_ref, e_ref, g_ref, held_ref, slope_ref,
+                 num_ref, den_ref):
     F, T, D, O, _, _ = dims
-    first = lax.axis_index("band") * F
+    W = 2 * O
+    shape = (8 * D, W)
+    a = lax.broadcasted_iota(jnp.int32, shape, 0)
+    b = lax.broadcasted_iota(jnp.int32, shape, 1)
+    eye = a // D * (2 * D) + a % D == b
+    ones = jnp.ones((W, W), jnp.float32)
+    for group in range(F * T // 8):
+        diagonal = keep_ref[F * T, group : group + 1, :] + come_ref[F * T, group : group + 1, :]
+        spread = jnp.dot(
+            jnp.where(eye, diagonal, 0.0), ones, precision=HIGH, preferred_element_type=jnp.float32
+        )
+        for i in range(8):
+            ft = group * 8 + i
+            around = live_ref[ft : ft + 1, :] * spread[i * D : (i + 1) * D]
+            num = counter_rotated(keep_ref[ft] + come_ref[ft], e_ref[ft])
+            num_ref[ft] = num + held_ref[ft] + around * g_ref[ft]
+            den_ref[ft] = around + slope_ref[ft]
+
+
+def update_kernel(dims, last, full, *refs):
+    F, T, D, O, _, _ = dims
+    scalar_ref, num_ref, den_ref, target_ref, g_ref, other_ref = refs[:6]
     W = 2 * O
     sums = jnp.sum(scalar_ref[...], axis=0, keepdims=True)
     low = low_lanes(sums.shape)
@@ -342,52 +432,38 @@
     squares = jnp.maximum(squares, 0.0)
     rho = PENALTY * full * (squares / samples + 1e-06)
     rho = jnp.broadcast_to(rho, (D, W))
-    shape = (8 * D, W)
-    a = lax.broadcasted_iota(jnp.int32, shape, 0)
-    b = lax.broadcasted_iota(jnp.int32, shape, 1)
-    eye = a // D * (2 * D) + a % D == b
-    acc = [[jnp.zeros((D, W), jnp.float32) for _ in range(T)] for _ in range(4)]
-    for group in range(F * T // 8):
-        diagonal = keep_ref[F * T, group : group + 1, :] + come_ref[F * T, group : group + 1, :]
-        spread = jnp.sum(jnp.where(eye, diagonal, 0.0), axis=1, keepdims=True)
-        for i in range(8):
-            ft = group * 8 + i
-            f, t = ft // T, ft % T
-            e = e_ref[ft]
-            g = g_ref[ft]
-            around = live_ref[ft : ft + 1, :] * spread[i * D : (i + 1) * D]
-            num = counter_rotated(keep_ref[ft] + come_ref[ft], e) + held_ref[ft]
-            fresh = (num + around * g + rho * target_ref[ft]) / (around + slope_ref[ft] + rho)
-            g = 0.5 * (g + fresh)
+    for t in range(T):
+        acc = [jnp.zeros((D, W), jnp.float32) for _ in range(4)]
+        for f in range(F):
+            ft = f * T + t
+            fresh = (num_ref[ft] + rho * target_ref[ft]) / (den_ref[ft] + rho)
+            g = 0.5 * (g_ref[ft] + fresh)
             if last:
-                u_ref, out_ref, total_ref, rhs_ref = refs
+                out_ref, total_ref, rhs_ref = refs[6:]
                 out_ref[f, t, 0] = g[:, :O]
                 out_ref[f, t, 1] = g[:, O:]
-                total = u_ref[ft] + g
+                total = other_ref[ft] + g
                 total_ref[ft] = total
+                x = place(dims, f)
                 for k in range(4):
-                    acc[k][t] = acc[k][t] + basis_ref[first + f, k] * total
+                    acc[k] = acc[k] + total
+                    total = total * x if k < 3 else total
             else:
-                g_out, p_out = refs
+                g_out, p_out = refs[6:]
                 g_out[ft] = g
-                p_out[ft] = rotated(g, e)
-    if last:
-        for k in range(4):
-            for t in range(T):
-                rhs_ref[k * T + t] = acc[k][t]
-
-
-def final_kernel(dims, coef_ref, total_ref, *refs):
+                p_out[ft] = rotated(g, other_ref[ft])
+        if last:
+            for k in range(4):
+                rhs_ref[k * T + t] = acc[k]
+
+
+def final_kernel(dims, total_ref, *refs):
     F, T, _, O, _, _ = dims
-    rhs_refs, out_ref = refs[:4], refs[4]
-    first = lax.axis_index("band") * F
+    rhs_refs, out_ref = refs[:-1], refs[-1]
     for t in range(T):
-        rhs = [rhs_refs[0][k * T + t] + rhs_refs[1][k * T + t]
-               + rhs_refs[2][k * T + t] + rhs_refs[3][k * T + t] for k in range(4)]
+        coeffs = solve(dims, rhs_refs, t)
         for f in range(F):
-            dual = total_ref[f * T + t]
-            for k in range(4):
-                dual = dual - coef_ref[first + f, k] * rhs[k]
+            dual = total_ref[f * T + t] - curve(coeffs, place(dims, f))
             out_ref[f, t, 0] = dual[:, :O]
             out_ref[f, t, 1] = dual[:, O:]
 
@@ -397,15 +473,18 @@
     F, T, _, D, O = gains.shape
     rows, cols = vis.shape[3], vis.shape[4]
     full = flags.shape[2]
-    total_f = F * Z
     FT, W = F * T, 2 * O
     dims = (F, T, D, O, R, C)
     f32 = jnp.float32
     smem = pl.BlockSpec(memory_space=pltpu.SMEM)
     vmem = pl.BlockSpec(memory_space=pltpu.VMEM)
+    hbm = pl.BlockSpec(memory_space=pltpu.HBM)
 
     def array(*shape):
         return jax.ShapeDtypeStruct(shape, f32)
+
+    def far(x):
+        return pltpu.with_memory_space_constraint(x, pltpu.HBM)
 
     def call(kernel, outs, scalars, arrays, scratch=()):
         return pl.pallas_call(
@@ -417,13 +496,6 @@
             compiler_params=LIMIT,
         )(*scalars, *arrays)
 
-    grid = 2.0 * np.arange(total_f, dtype=np.float64) / (total_f - 1) - 1.0
-    basis = np.stack([grid**k for k in range(4)], axis=1)
-    solved = basis @ np.linalg.inv(basis.T @ basis)
-    basis_t = jnp.asarray(basis, f32)
-    coef_t = jnp.asarray(solved, f32)
-    freq_t = jnp.asarray(1.0 + np.arange(total_f) / total_f, f32)
-
     def where(r, c, z):
         return (r * C + c) * Z + z
 
@@ -441,36 +513,65 @@
         return [x] + [permute(x, lambda r, c, z, k=k: (r, c, (z + k) % Z)) for k in range(1, Z)]
 
     whole, line, fit = array(FT, D, W), array(FT + 1, D, W), array(4 * T, D, W)
-    pair, text, mask = array(FT // 8 * 9, 2 * D, W), array(1, W), pltpu.VMEM((rows, cols), jnp.bfloat16)
+    pair, text = array(FT // 8 * 9, 2 * D, W), array(1, W)
     flux_t = flux.T
     rot, g, p = pl.pallas_call(
         functools.partial(start_kernel, dims),
         out_shape=[whole] * 3,
-        in_specs=[vmem, smem, smem, vmem],
+        in_specs=[hbm] * 3,
         out_specs=[vmem] * 3,
+        scratch_shapes=[
+            pltpu.VMEM((3, T, full), f32),
+            pltpu.SMEM(lmn.shape, f32),
+            pltpu.VMEM(gains.shape, f32),
+            pltpu.SemaphoreType.DMA((3,)),
+        ],
         compiler_params=LIMIT,
         name="start",
-    )(positions.transpose(1, 0, 2), lmn, freq_t, gains)
+    )(far(positions.transpose(1, 0, 2)), far(lmn), far(gains))
     for step in range(ITERS):
         last = step == ITERS - 1
         got = [gather(p, m) for m in range(R)]
         if step == 0:
-            (live_col, live_half, live_own, u, rhs, held, slope, power, extra) = call(
-                functools.partial(setup_kernel, dims),
-                [array(FT, cols), array(FT, W), array(FT, W), whole, fit, whole, whole, text, text],
-                [flux_t, basis_t], [flags, vis, duals, g], [mask],
+            (live_col, live_half, live_own, u, rhs, held, slope, power, extra) = (
+                pl.pallas_call(
+                    functools.partial(setup_kernel, dims),
+                    out_shape=[
+                        array(FT, cols), array(FT, W), array(FT, W), whole, fit, whole, whole,
+                        text, text,
+                    ],
+                    in_specs=[smem] + [hbm] * 3 + [vmem],
+                    out_specs=[vmem] * 9,
+                    scratch_shapes=[
+                        pltpu.VMEM(vis.shape, vis.dtype),
+                        pltpu.VMEM(flags.shape, flags.dtype),
+                        pltpu.VMEM(duals.shape, f32),
+                        pltpu.SemaphoreType.DMA((F + 2,)),
+                    ],
+                    compiler_params=LIMIT,
+                    name="setup",
+                )(flux_t, far(flags), far(vis), far(duals), g)
             )
         else:
             rhs, held, slope, extra = call(
                 functools.partial(again_kernel, dims),
-                [fit, whole, whole, text], [flux_t, basis_t], [power, live_own, u, g],
+                [fit, whole, whole, text], [flux_t], [power, live_own, u, g],
             )
         rhs_all = bands(rhs)
         theirs = permute(p, lambda r, c, z: (r, c ^ 2, z))
-        keep, send = call(
-            functools.partial(sum_kernel, dims), [pair, pair], [flux_t],
-            [live_col, vis, *got], [mask],
-        )
+        keep, send = pl.pallas_call(
+            functools.partial(sum_kernel, dims),
+            out_shape=[pair, pair],
+            in_specs=[smem, hbm] + [vmem] * 3,
+            out_specs=[vmem] * 2,
+            scratch_shapes=[
+                pltpu.VMEM(vis.shape, vis.dtype),
+                pltpu.VMEM((rows, cols), vis.dtype),
+                pltpu.SemaphoreType.DMA((F,)),
+            ],
+            compiler_params=LIMIT,
+            name="sums",
+        )(flux_t, far(vis), live_col, *got)
         other = permute(send, lambda r, c, z: (r, c ^ 1, z))
         keep, send, scalar = call(
             functools.partial(residual_kernel, dims), [line, line, array(R * C * Z, W)],
@@ -480,18 +581,23 @@
         scalar = lax.all_to_all(scalar, AXES, 0, 0, tiled=True)
         target = call(
             functools.partial(target_kernel, dims, step == 0),
-            [whole] * (1 if step == 0 else 2), [coef_t], [u, g, *rhs_all],
+            [whole] * (1 if step == 0 else 2), [], [u, g, *rhs_all],
+        )
+        num, den = call(
+            functools.partial(merge_kernel, dims), [whole, whole], [],
+            [keep, come, live_own, rot, g, held, slope],
         )
         update = functools.partial(update_kernel, dims, last, float(full))
-        arrays = [keep, come, scalar, live_own, rot, g, held, slope, target[0]]
+        arrays = [scalar, num, den, target[0], g]
         if last:
             gain, total, rhs = call(
-                update, [array(*gains.shape), whole, fit], [basis_t], arrays + [target[1]]
+                update, [array(*gains.shape), whole, fit], [],
+                arrays + [target[1]],
             )
         else:
-            g, p = call(update, [whole, whole], [basis_t], arrays)
+            g, p = call(update, [whole, whole], [], arrays + [rot])
     (dual,) = call(
-        functools.partial(final_kernel, dims), [array(*gains.shape)], [coef_t],
+        functools.partial(final_kernel, dims), [array(*gains.shape)], [],
         [total, *bands(rhs)],
     )
     return (gain, dual)

time: 130 us -> 116 us (0.89)
  local copies, waits for them, and re-layouts: 13.3 us -> 0.69 us
  Pallas kernels: 40.7 us -> 34.8 us
  starting transfers between devices: 37.2 us -> 39.5 us
  waiting for transfers between devices: 37.9 us -> 39.9 us
    pallas_call x11 -> x10, Pallas kernels: 38 us -> 7.4 us  [call(): pl.pallas_call(kernel, out_shape=outs, in_specs=[smem] * len(scalars) + [...]
    pallas_call x0 -> x3, Pallas kernels: none -> 25.1 us  [the longest x2 16 us: shards(): pl.pallas_call(functools.partial(sum_kernel, dims), out_shape=[pair, pair...]
    unnamed x28 -> x4, local copies, waits for them, and re-layouts: 13.3 us -> 0.69 us
    ppermute x19, starting transfers between devices: 31 us -> 33.3 us  [permute(): return lax.ppermute(x, AXES, pairs)]
    all_to_all x2, waiting for transfers between devices: 10.6 us -> 12 us  [shards(): scalar = lax.all_to_all(scalar, AXES, 0, 0, tiled=True)]
  transfers between devices with their start and end apart: 21 -> 21, of which waited for: 10 -> 11; matrix products, arithmetic and copies ran while one was open for 0% -> 0% of each run, Pallas kernels for 10% -> 10%
where the time goes in v3:
time: 116 us
  waiting for transfers between devices  39.9 us (34%)
  starting transfers between devices  39.5 us (34%)
  Pallas kernels  34.8 us (30%)
    ppermute x19, starting transfers between devices, permute(): return lax.ppermute(x, AXES, pairs)  33.3 us
    ppermute x19, waiting for transfers between devices, permute(): return lax.ppermute(x, AXES, pairs)  27.9 us
    pallas_call x2, Pallas kernels, shards(): pl.pallas_call(functools.partial(sum_kernel, dims), out_shape=[pair, pair...  16 us
    all_to_all x2, waiting for transfers between devices, shards(): scalar = lax.all_to_all(scalar, AXES, 0, 0, tiled=True)  12 us
    pallas_call x1, Pallas kernels, shards(): pl.pallas_call(functools.partial(setup_kernel, dims), out_shape=[array(FT...  9.09 us
    pallas_call x10, Pallas kernels, call(): pl.pallas_call(kernel, out_shape=outs, in_specs=[smem] * len(scalars) + [...  7.4 us
    all_to_all x2, starting transfers between devices, shards(): scalar = lax.all_to_all(scalar, AXES, 0, 0, tiled=True)  6.16 us
    pallas_call x1, Pallas kernels, shards(): pl.pallas_call(functools.partial(start_kernel, dims), out_shape=[whole] *...  2.39 us
  transfers between devices with their start and end apart: 21, of which 11 were waited for; matrix products, arithmetic and copies ran while one was open for 0% of the time, Pallas kernels for 10%

profile of v3, /device:TPU:0, one launch (start us, length us, event | category | flops | bytes accessed | tf_op | source)
XLA Modules:
  0.0 115.7 jit_solution(9660719073424102748)
XLA Ops:
  0.6 0.0 copy-start.1
  0.6 2.4 %start.1 = (f32[64,8,128]{2,1,0:T(8,128)S(1)}, f32[64,8,128]{2,1,0:T(8,128)S(1)}, f32[64,8,128]{2,1,0:T(8,128)S(1)}) custom-call(f32[3,4,512]{2,1,0:T(4,128)} %bitcast.16, f32[3,8]{1,0:T(4,128)} %lmn_hbm.1, f32[16,4,2,8,64]{4,3,2,1,0:T(8,128)} %gains_hbm.1), custom_call_target="tpu_custom_call" | custom-call | tf_op jit(solution)/shard_map/start/pallas_call | solution.py:518
  3.0 0.7 collective-permute-start
  3.7 5.7 %collective-permute-start.1 = (f32[64,8,128]{2,1,0:T(8,128)S(1)}, f32[64,8,128]{2,1,0:T(8,128)S(1)}, u32[]{:S(2)}, u32[]{:S(2)}) collective-permute-start(f32[64,8,128]{2,1,0:T(8,128)S(1)} %get-tuple-element.46.mine_ref), channel_id=1, source_target_pairs={{0,16},{1,17},{2,18},{3,19},{4,0},{5,1},{6,2},{7,3},{8,20},{9,21},... | collective-permute-start | bytes 786440 | tf_op jit(solution)/shard_map/ppermute | solution.py:507
  9.4 0.7 copy-done
  10.1 9.1 %setup.1 = (f32[64,128]{1,0:T(8,128)S(1)}, f32[64,128]{1,0:T(8,128)S(1)}, f32[64,128]{1,0:T(8,128)S(1)}, f32[64,8,128]{2,1,0:T(8,128)S(1)}, f32[16,8,128]{2,1,0:...) custom-call(f32[8,16]{1,0:T(8,128)S(1)} %bitcast.10, ...), custom_call_target="tpu_custom_call" | custom-call | tf_op jit(solution)/shard_map/setup/pallas_call | solution.py:537
  19.2 0.5 collective-permute-done.1.b_ref
  19.7 8.0 %sums.2 = (f32[72,16,128]{2,1,0:T(8,128)S(1)}, f32[72,16,128]{2,1,0:T(8,128)S(1)}) custom-call(f32[8,16]{1,0:T(8,128)S(1)} %bitcast.11, bf16[16,4,2,256,128]{4,3,2,1,0:T(8,128)(2,1)} %vis_hbm.5, f32[64,128]{1,0:T(8,128)S(1)} %get-tuple-element.45.live_ref, f32[64,8,128]{2,1,0:T(8,128)S(1)} %collective-permute-done.a_ref, ...), custom_call_target="tpu_custom_call" | custom-call | tf_op jit(solution)/shard_map/sums/pallas_call | solution.py:562
  27.7 0.9 collective-permute-start.2
  28.6 2.2 %collective-permute-start.3 = (f32[64,8,128]{2,1,0:T(8,128)S(1)}, f32[64,8,128]{2,1,0:T(8,128)S(1)}, u32[]{:S(2)}, u32[]{:S(2)}) collective-permute-start(f32[64,8,128]{2,1,0:T(8,128)S(1)} %get-tuple-element.46.mine_ref), channel_id=1, source_target_pairs={{0,8},{1,9},{2,10},{3,11},{4,12},{5,13},{6,14},{7,15},{8,0},{9,1},... | collective-permute-start | bytes 786440 | tf_op jit(solution)/shard_map/ppermute | solution.py:507
  30.7 6.9 %collective-permute-done.3.theirs_ref = f32[64,8,128]{2,1,0:T(8,128)S(1)} collective-permute-done((f32[64,8,128]{2,1,0:T(8,128)S(1)}, f32[64,8,128]{2,1,0:T(8,128)S(1)}, u32[]{:S(2)}, u32[]{:S(2)}) %collective-permute-start.3) | collective-permute-done | bytes 262176 | tf_op jit(solution)/shard_map/ppermute | solution.py:507
  37.6 1.5 %shard_map.86 = (f32[65,8,128]{2,1,0:T(8,128)S(1)}, f32[65,8,128]{2,1,0:T(8,128)S(1)}, f32[32,128]{1,0:T(8,128)}) custom-call(f32[64,128]{1,0:T(8,128)S(1)} %get-tuple-element.40.live_ref, f32[1,128]{1,0:T(1,128)S(1)} %get-tuple-element.44.extra_ref, f32[72,16,128]{2,1,0:T(8,128)S(1)} %get-tuple-element.47.kept_ref, ...), custom_call_target="tpu_custom_call" | custom-call | tf_op jit(solution)/shard_map/pallas_call | solution.py:490
  39.1 1.7 %collective-permute-start.4 = (f32[65,8,128]{2,1,0:T(8,128)S(1)}, f32[65,8,128]{2,1,0:T(8,128)S(1)}, u32[]{:S(2)}, u32[]{:S(2)}) collective-permute-start(f32[65,8,128]{2,1,0:T(8,128)S(1)} %get-tuple-element.51), channel_id=1, source_target_pairs={{0,8},{1,9},{2,10},{3,11},{4,12},{5,13},{6,14},{7,15},{8,0},{9,1},... | collective-permute-start | bytes 798728 | tf_op jit(solution)/shard_map/ppermute | solution.py:507
  40.8 1.6 %collective-permute-start.5 = (f32[16,8,128]{2,1,0:T(8,128)S(1)}, f32[16,8,128]{2,1,0:T(8,128)S(1)}, u32[]{:S(2)}, u32[]{:S(2)}) collective-permute-start(f32[16,8,128]{2,1,0:T(8,128)S(1)} %get-tuple-element.57.refs_0_), channel_id=1, source_target_pairs={{0,1},{1,2},{2,3},{3,0},{4,5},{5,6},{6,7},{7,4},{8,9},{9,10},{10,1... | collective-permute-start | bytes 196616 | tf_op jit(solution)/shard_map/ppermute | solution.py:507
  42.4 2.6 %collective-permute-start.6 = (f32[16,8,128]{2,1,0:T(8,128)S(1)}, f32[16,8,128]{2,1,0:T(8,128)S(1)}, u32[]{:S(2)}, u32[]{:S(2)}) collective-permute-start(f32[16,8,128]{2,1,0:T(8,128)S(1)} %get-tuple-element.57.refs_0_), channel_id=1, source_target_pairs={{0,2},{1,3},{2,0},{3,1},{4,6},{5,7},{6,4},{7,5},{8,10},{9,11},{10,... | collective-permute-start | bytes 196616 | tf_op jit(solution)/shard_map/ppermute | solution.py:507
  45.0 1.3 %collective-permute-start.7 = (f32[16,8,128]{2,1,0:T(8,128)S(1)}, f32[16,8,128]{2,1,0:T(8,128)S(1)}, u32[]{:S(2)}, u32[]{:S(2)}) collective-permute-start(f32[16,8,128]{2,1,0:T(8,128)S(1)} %get-tuple-element.57.refs_0_), channel_id=1, source_target_pairs={{0,3},{1,0},{2,1},{3,2},{4,7},{5,4},{6,5},{7,6},{8,11},{9,8},{10,9... | collective-permute-start | bytes 196616 | tf_op jit(solution)/shard_map/ppermute | solution.py:507
  46.4 2.5 %all-to-all-start = ((f32[32,1,128]{2,1,0:T(1,128)}), f32[32,1,128]{2,1,0:T(1,128)S(1)}, u32[]{:S(2)}, u32[]{:S(2)}) async-start(f32[32,1,128]{2,1,0:T(1,128)} %bitcast.3), calls=%async_computation | async-start | bytes 32768 | tf_op jit(solution)/shard_map/all_to_all | solution.py:581
  48.9 0.7 collective-permute-done.6.refs_2_
  49.6 0.1 collective-permute-done.7.refs_3_
  49.7 0.1 shard_map.88.refs_3_
  49.8 0.5 shard_map.87
  50.3 5.8 %all-to-all-done = f32[32,1,128]{2,1,0:T(1,128)S(1)} async-done(((f32[32,1,128]{2,1,0:T(1,128)}), f32[32,1,128]{2,1,0:T(1,128)S(1)}, u32[]{:S(2)}, u32[]{:S(2)}) %all-to-all-start) | async-done | bytes 16416 | tf_op jit(solution)/shard_map/all_to_all | solution.py:581
  56.0 0.3 shard_map.89
  56.4 0.7 collective-permute-start.8
  57.0 3.3 %collective-permute-start.9 = (f32[64,8,128]{2,1,0:T(8,128)S(1)}, f32[64,8,128]{2,1,0:T(8,128)S(1)}, u32[]{:S(2)}, u32[]{:S(2)}) collective-permute-start(f32[64,8,128]{2,1,0:T(8,128)S(1)} %get-tuple-element.60.mine_ref), channel_id=1, source_target_pairs={{0,16},{1,17},{2,18},{3,19},{4,0},{5,1},{6,2},{7,3},{8,20},{9,21},... | collective-permute-start | bytes 786440 | tf_op jit(solution)/shard_map/ppermute | solution.py:507
  60.4 9.2 %collective-permute-done.9.b_ref = f32[64,8,128]{2,1,0:T(8,128)S(1)} collective-permute-done((f32[64,8,128]{2,1,0:T(8,128)S(1)}, f32[64,8,128]{2,1,0:T(8,128)S(1)}, u32[]{:S(2)}, u32[]{:S(2)}) %collective-permute-start.9) | collective-permute-done | bytes 262176 | tf_op jit(solution)/shard_map/ppermute | solution.py:507
  69.6 8.0 %sums.3 = (f32[72,16,128]{2,1,0:T(8,128)S(1)}, f32[72,16,128]{2,1,0:T(8,128)S(1)}) custom-call(f32[8,16]{1,0:T(8,128)S(1)} %bitcast.12, bf16[16,4,2,256,128]{4,3,2,1,0:T(8,128)(2,1)} %vis_hbm.5, f32[64,128]{1,0:T(8,128)S(1)} %get-tuple-element.45.live_ref, f32[64,8,128]{2,1,0:T(8,128)S(1)} %collective-permute-done.8.a_ref, ...), custom_call_target="tpu_custom_call" | custom-call | tf_op jit(solution)/shard_map/sums/pallas_call | solution.py:562
  77.6 1.6 %collective-permute-start.10 = (f32[72,16,128]{2,1,0:T(8,128)S(1)}, f32[72,16,128]{2,1,0:T(8,128)S(1)}, u32[]{:S(2)}, u32[]{:S(2)}) collective-permute-start(f32[72,16,128]{2,1,0:T(8,128)S(1)} %get-tuple-element.62), channel_id=1, source_target_pairs={{0,4},{1,5},{2,6},{3,7},{4,0},{5,1},{6,2},{7,3},{8,12},{9,13},{10,... | collective-permute-start | bytes 1769480 | tf_op jit(solution)/shard_map/ppermute | solution.py:507
  79.2 1.7 %collective-permute-start.11 = (f32[64,8,128]{2,1,0:T(8,128)S(1)}, f32[64,8,128]{2,1,0:T(8,128)S(1)}, u32[]{:S(2)}, u32[]{:S(2)}) collective-permute-start(f32[64,8,128]{2,1,0:T(8,128)S(1)} %get-tuple-element.60.mine_ref), channel_id=1, source_target_pairs={{0,8},{1,9},{2,10},{3,11},{4,12},{5,13},{6,14},{7,15},{8,0},{9,1},... | collective-permute-start | bytes 786440 | tf_op jit(solution)/shard_map/ppermute | solution.py:507
  80.9 0.9 shard_map.90
  81.8 5.7 %collective-permute-done.11.theirs_ref = f32[64,8,128]{2,1,0:T(8,128)S(1)} collective-permute-done((f32[64,8,128]{2,1,0:T(8,128)S(1)}, f32[64,8,128]{2,1,0:T(8,128)S(1)}, u32[]{:S(2)}, u32[]{:S(2)}) %collective-permute-start.11) | collective-permute-done | bytes 262176 | tf_op jit(solution)/shard_map/ppermute | solution.py:507
  87.5 1.5 %shard_map.91 = (f32[65,8,128]{2,1,0:T(8,128)S(1)}, f32[65,8,128]{2,1,0:T(8,128)S(1)}, f32[32,128]{1,0:T(8,128)}) custom-call(f32[64,128]{1,0:T(8,128)S(1)} %get-tuple-element.40.live_ref, f32[1,128]{1,0:T(1,128)S(1)} %get-tuple-element.59.extra_ref, f32[72,16,128]{2,1,0:T(8,128)S(1)} %get-tuple-element.61.kept_ref, ...), custom_call_target="tpu_custom_call" | custom-call | tf_op jit(solution)/shard_map/pallas_call | solution.py:490
  89.0 1.7 %collective-permute-start.12 = (f32[65,8,128]{2,1,0:T(8,128)S(1)}, f32[65,8,128]{2,1,0:T(8,128)S(1)}, u32[]{:S(2)}, u32[]{:S(2)}) collective-permute-start(f32[65,8,128]{2,1,0:T(8,128)S(1)} %get-tuple-element.65), channel_id=1, source_target_pairs={{0,8},{1,9},{2,10},{3,11},{4,12},{5,13},{6,14},{7,15},{8,0},{9,1},... | collective-permute-start | bytes 798728 | tf_op jit(solution)/shard_map/ppermute | solution.py:507
  90.6 0.6 collective-permute-start.13
  91.3 0.5 collective-permute-start.14
  91.7 2.7 %collective-permute-start.15 = (f32[16,8,128]{2,1,0:T(8,128)S(1)}, f32[16,8,128]{2,1,0:T(8,128)S(1)}, u32[]{:S(2)}, u32[]{:S(2)}) collective-permute-start(f32[16,8,128]{2,1,0:T(8,128)S(1)} %get-tuple-element.70.refs_0_), channel_id=1, source_target_pairs={{0,3},{1,0},{2,1},{3,2},{4,7},{5,4},{6,5},{7,6},{8,11},{9,8},{10,9... | collective-permute-start | bytes 196616 | tf_op jit(solution)/shard_map/ppermute | solution.py:507
  94.5 3.6 %all-to-all-start.1 = ((f32[32,1,128]{2,1,0:T(1,128)}), f32[32,1,128]{2,1,0:T(1,128)S(1)}, u32[]{:S(2)}, u32[]{:S(2)}) async-start(f32[32,1,128]{2,1,0:T(1,128)} %bitcast.6), calls=%async_computation.1 | async-start | bytes 32768 | tf_op jit(solution)/shard_map/all_to_all | solution.py:581
  98.1 0.2 collective-permute-done.14.refs_2_
  98.3 0.1 shard_map.93
  98.5 0.5 shard_map.92
  99.0 6.2 %all-to-all-done.1 = f32[32,1,128]{2,1,0:T(1,128)S(1)} async-done(((f32[32,1,128]{2,1,0:T(1,128)}), f32[32,1,128]{2,1,0:T(1,128)S(1)}, u32[]{:S(2)}, u32[]{:S(2)}) %all-to-all-start.1) | async-done | bytes 16416 | tf_op jit(solution)/shard_map/all_to_all | solution.py:581
  105.2 1.1 shard_map.94
  106.3 0.5 collective-permute-start.16
  106.8 0.6 collective-permute-start.17
  107.4 2.7 %collective-permute-start.18 = (f32[16,8,128]{2,1,0:T(8,128)S(1)}, f32[16,8,128]{2,1,0:T(8,128)S(1)}, u32[]{:S(2)}, u32[]{:S(2)}) collective-permute-start(f32[16,8,128]{2,1,0:T(8,128)S(1)} %get-tuple-element.75.refs_0_), channel_id=1, source_target_pairs={{0,3},{1,0},{2,1},{3,2},{4,7},{5,4},{6,5},{7,6},{8,11},{9,8},{10,9... | collective-permute-start | bytes 196616 | tf_op jit(solution)/shard_map/ppermute | solution.py:507
  110.1 2.9 %collective-permute-done.16.refs_1_ = f32[16,8,128]{2,1,0:T(8,128)S(1)} collective-permute-done((f32[16,8,128]{2,1,0:T(8,128)S(1)}, f32[16,8,128]{2,1,0:T(8,128)S(1)}, u32[]{:S(2)}, u32[]{:S(2)}) %collective-permute-start.16) | collective-permute-done | bytes 65568 | tf_op jit(solution)/shard_map/ppermute | solution.py:507
  113.1 1.7 %collective-permute-done.17.refs_2_ = f32[16,8,128]{2,1,0:T(8,128)S(1)} collective-permute-done((f32[16,8,128]{2,1,0:T(8,128)S(1)}, f32[16,8,128]{2,1,0:T(8,128)S(1)}, u32[]{:S(2)}, u32[]{:S(2)}) %collective-permute-start.17) | collective-permute-done | bytes 65568 | tf_op jit(solution)/shard_map/ppermute | solution.py:507
  114.8 1.0 shard_map.95
  (12 shorter events, 0.0 us)
Async XLA Ops:
  0.6 19.1 %copy-start.1 = (f32[16,8]{0,1:T(8,128)S(1)}, f32[16,8]{0,1:T(8,128)}, u32[]{:S(2)}) copy-start(f32[16,8]{0,1:T(8,128)} %param.11) | copy-start | bytes 1540
  3.0 16.2 %collective-permute-start = (f32[64,8,128]{2,1,0:T(8,128)S(1)}, f32[64,8,128]{2,1,0:T(8,128)S(1)}, u32[]{:S(2)}, u32[]{:S(2)}) collective-permute-start(f32[64,8,128]{2,1,0:T(8,128)S(1)} %get-tuple-element.46.mine_ref), channel_id=1, source_target_pairs={{0,0},{1,1},{2,2},{3,3},{4,16},{5,17},{6,18},{7,19},{8,4},{9,5},{1... | collective-permute-start | bytes 786440 | tf_op jit(solution)/shard_map/ppermute | solution.py:507
  3.7 16.0 %collective-permute-start.1 = (f32[64,8,128]{2,1,0:T(8,128)S(1)}, f32[64,8,128]{2,1,0:T(8,128)S(1)}, u32[]{:S(2)}, u32[]{:S(2)}) collective-permute-start(f32[64,8,128]{2,1,0:T(8,128)S(1)} %get-tuple-element.46.mine_ref), channel_id=1, source_target_pairs={{0,16},{1,17},{2,18},{3,19},{4,0},{5,1},{6,2},{7,3},{8,20},{9,21},... | collective-permute-start | bytes 786440 | tf_op jit(solution)/shard_map/ppermute | solution.py:507
  9.4 0.7 copy-start
  27.7 10.0 %collective-permute-start.2 = (f32[72,16,128]{2,1,0:T(8,128)S(1)}, f32[72,16,128]{2,1,0:T(8,128)S(1)}, u32[]{:S(2)}, u32[]{:S(2)}) collective-permute-start(f32[72,16,128]{2,1,0:T(8,128)S(1)} %get-tuple-element.48), channel_id=1, source_target_pairs={{0,4},{1,5},{2,6},{3,7},{4,0},{5,1},{6,2},{7,3},{8,12},{9,13},{10,... | collective-permute-start | bytes 1769480 | tf_op jit(solution)/shard_map/ppermute | solution.py:507
  28.6 9.1 %collective-permute-start.3 = (f32[64,8,128]{2,1,0:T(8,128)S(1)}, f32[64,8,128]{2,1,0:T(8,128)S(1)}, u32[]{:S(2)}, u32[]{:S(2)}) collective-permute-start(f32[64,8,128]{2,1,0:T(8,128)S(1)} %get-tuple-element.46.mine_ref), channel_id=1, source_target_pairs={{0,8},{1,9},{2,10},{3,11},{4,12},{5,13},{6,14},{7,15},{8,0},{9,1},... | collective-permute-start | bytes 786440 | tf_op jit(solution)/shard_map/ppermute | solution.py:507
  39.1 10.7 %collective-permute-start.4 = (f32[65,8,128]{2,1,0:T(8,128)S(1)}, f32[65,8,128]{2,1,0:T(8,128)S(1)}, u32[]{:S(2)}, u32[]{:S(2)}) collective-permute-start(f32[65,8,128]{2,1,0:T(8,128)S(1)} %get-tuple-element.51), channel_id=1, source_target_pairs={{0,8},{1,9},{2,10},{3,11},{4,12},{5,13},{6,14},{7,15},{8,0},{9,1},... | collective-permute-start | bytes 798728 | tf_op jit(solution)/shard_map/ppermute | solution.py:507
  40.8 8.1 %collective-permute-start.5 = (f32[16,8,128]{2,1,0:T(8,128)S(1)}, f32[16,8,128]{2,1,0:T(8,128)S(1)}, u32[]{:S(2)}, u32[]{:S(2)}) collective-permute-start(f32[16,8,128]{2,1,0:T(8,128)S(1)} %get-tuple-element.57.refs_0_), channel_id=1, source_target_pairs={{0,1},{1,2},{2,3},{3,0},{4,5},{5,6},{6,7},{7,4},{8,9},{9,10},{10,1... | collective-permute-start | bytes 196616 | tf_op jit(solution)/shard_map/ppermute | solution.py:507
  42.4 7.2 %collective-permute-start.6 = (f32[16,8,128]{2,1,0:T(8,128)S(1)}, f32[16,8,128]{2,1,0:T(8,128)S(1)}, u32[]{:S(2)}, u32[]{:S(2)}) collective-permute-start(f32[16,8,128]{2,1,0:T(8,128)S(1)} %get-tuple-element.57.refs_0_), channel_id=1, source_target_pairs={{0,2},{1,3},{2,0},{3,1},{4,6},{5,7},{6,4},{7,5},{8,10},{9,11},{10,... | collective-permute-start | bytes 196616 | tf_op jit(solution)/shard_map/ppermute | solution.py:507
  45.0 4.7 %collective-permute-start.7 = (f32[16,8,128]{2,1,0:T(8,128)S(1)}, f32[16,8,128]{2,1,0:T(8,128)S(1)}, u32[]{:S(2)}, u32[]{:S(2)}) collective-permute-start(f32[16,8,128]{2,1,0:T(8,128)S(1)} %get-tuple-element.57.refs_0_), channel_id=1, source_target_pairs={{0,3},{1,0},{2,1},{3,2},{4,7},{5,4},{6,5},{7,6},{8,11},{9,8},{10,9... | collective-permute-start | bytes 196616 | tf_op jit(solution)/shard_map/ppermute | solution.py:507
  46.4 9.7 %all-to-all-start = ((f32[32,1,128]{2,1,0:T(1,128)}), f32[32,1,128]{2,1,0:T(1,128)S(1)}, u32[]{:S(2)}, u32[]{:S(2)}) async-start(f32[32,1,128]{2,1,0:T(1,128)} %bitcast.3), calls=%async_computation | async-start | bytes 32768 | tf_op jit(solution)/shard_map/all_to_all | solution.py:581
  56.4 4.0 %collective-permute-start.8 = (f32[64,8,128]{2,1,0:T(8,128)S(1)}, f32[64,8,128]{2,1,0:T(8,128)S(1)}, u32[]{:S(2)}, u32[]{:S(2)}) collective-permute-start(f32[64,8,128]{2,1,0:T(8,128)S(1)} %get-tuple-element.60.mine_ref), channel_id=1, source_target_pairs={{0,0},{1,1},{2,2},{3,3},{4,16},{5,17},{6,18},{7,19},{8,4},{9,5},{1... | collective-permute-start | bytes 786440 | tf_op jit(solution)/shard_map/ppermute | solution.py:507
  57.0 12.6 %collective-permute-start.9 = (f32[64,8,128]{2,1,0:T(8,128)S(1)}, f32[64,8,128]{2,1,0:T(8,128)S(1)}, u32[]{:S(2)}, u32[]{:S(2)}) collective-permute-start(f32[64,8,128]{2,1,0:T(8,128)S(1)} %get-tuple-element.60.mine_ref), channel_id=1, source_target_pairs={{0,16},{1,17},{2,18},{3,19},{4,0},{5,1},{6,2},{7,3},{8,20},{9,21},... | collective-permute-start | bytes 786440 | tf_op jit(solution)/shard_map/ppermute | solution.py:507
  77.6 9.9 %collective-permute-start.10 = (f32[72,16,128]{2,1,0:T(8,128)S(1)}, f32[72,16,128]{2,1,0:T(8,128)S(1)}, u32[]{:S(2)}, u32[]{:S(2)}) collective-permute-start(f32[72,16,128]{2,1,0:T(8,128)S(1)} %get-tuple-element.62), channel_id=1, source_target_pairs={{0,4},{1,5},{2,6},{3,7},{4,0},{5,1},{6,2},{7,3},{8,12},{9,13},{10,... | collective-permute-start | bytes 1769480 | tf_op jit(solution)/shard_map/ppermute | solution.py:507
  79.2 8.3 %collective-permute-start.11 = (f32[64,8,128]{2,1,0:T(8,128)S(1)}, f32[64,8,128]{2,1,0:T(8,128)S(1)}, u32[]{:S(2)}, u32[]{:S(2)}) collective-permute-start(f32[64,8,128]{2,1,0:T(8,128)S(1)} %get-tuple-element.60.mine_ref), channel_id=1, source_target_pairs={{0,8},{1,9},{2,10},{3,11},{4,12},{5,13},{6,14},{7,15},{8,0},{9,1},... | collective-permute-start | bytes 786440 | tf_op jit(solution)/shard_map/ppermute | solution.py:507
  89.0 9.5 %collective-permute-start.12 = (f32[65,8,128]{2,1,0:T(8,128)S(1)}, f32[65,8,128]{2,1,0:T(8,128)S(1)}, u32[]{:S(2)}, u32[]{:S(2)}) collective-permute-start(f32[65,8,128]{2,1,0:T(8,128)S(1)} %get-tuple-element.65), channel_id=1, source_target_pairs={{0,8},{1,9},{2,10},{3,11},{4,12},{5,13},{6,14},{7,15},{8,0},{9,1},... | collective-permute-start | bytes 798728 | tf_op jit(solution)/shard_map/ppermute | solution.py:507
  90.6 7.5 %collective-permute-start.13 = (f32[16,8,128]{2,1,0:T(8,128)S(1)}, f32[16,8,128]{2,1,0:T(8,128)S(1)}, u32[]{:S(2)}, u32[]{:S(2)}) collective-permute-start(f32[16,8,128]{2,1,0:T(8,128)S(1)} %get-tuple-element.70.refs_0_), channel_id=1, source_target_pairs={{0,1},{1,2},{2,3},{3,0},{4,5},{5,6},{6,7},{7,4},{8,9},{9,10},{10,1... | collective-permute-start | bytes 196616 | tf_op jit(solution)/shard_map/ppermute | solution.py:507
  91.3 7.1 %collective-permute-start.14 = (f32[16,8,128]{2,1,0:T(8,128)S(1)}, f32[16,8,128]{2,1,0:T(8,128)S(1)}, u32[]{:S(2)}, u32[]{:S(2)}) collective-permute-start(f32[16,8,128]{2,1,0:T(8,128)S(1)} %get-tuple-element.70.refs_0_), channel_id=1, source_target_pairs={{0,2},{1,3},{2,0},{3,1},{4,6},{5,7},{6,4},{7,5},{8,10},{9,11},{10,... | collective-permute-start | bytes 196616 | tf_op jit(solution)/shard_map/ppermute | solution.py:507
  91.7 6.6 %collective-permute-start.15 = (f32[16,8,128]{2,1,0:T(8,128)S(1)}, f32[16,8,128]{2,1,0:T(8,128)S(1)}, u32[]{:S(2)}, u32[]{:S(2)}) collective-permute-start(f32[16,8,128]{2,1,0:T(8,128)S(1)} %get-tuple-element.70.refs_0_), channel_id=1, source_target_pairs={{0,3},{1,0},{2,1},{3,2},{4,7},{5,4},{6,5},{7,6},{8,11},{9,8},{10,9... | collective-permute-start | bytes 196616 | tf_op jit(solution)/shard_map/ppermute | solution.py:507
  94.5 10.8 %all-to-all-start.1 = ((f32[32,1,128]{2,1,0:T(1,128)}), f32[32,1,128]{2,1,0:T(1,128)S(1)}, u32[]{:S(2)}, u32[]{:S(2)}) async-start(f32[32,1,128]{2,1,0:T(1,128)} %bitcast.6), calls=%async_computation.1 | async-start | bytes 32768 | tf_op jit(solution)/shard_map/all_to_all | solution.py:581
  106.3 6.8 %collective-permute-start.16 = (f32[16,8,128]{2,1,0:T(8,128)S(1)}, f32[16,8,128]{2,1,0:T(8,128)S(1)}, u32[]{:S(2)}, u32[]{:S(2)}) collective-permute-start(f32[16,8,128]{2,1,0:T(8,128)S(1)} %get-tuple-element.75.refs_0_), channel_id=1, source_target_pairs={{0,1},{1,2},{2,3},{3,0},{4,5},{5,6},{6,7},{7,4},{8,9},{9,10},{10,1... | collective-permute-start | bytes 196616 | tf_op jit(solution)/shard_map/ppermute | solution.py:507
  106.8 8.0 %collective-permute-start.17 = (f32[16,8,128]{2,1,0:T(8,128)S(1)}, f32[16,8,128]{2,1,0:T(8,128)S(1)}, u32[]{:S(2)}, u32[]{:S(2)}) collective-permute-start(f32[16,8,128]{2,1,0:T(8,128)S(1)} %get-tuple-element.75.refs_0_), channel_id=1, source_target_pairs={{0,2},{1,3},{2,0},{3,1},{4,6},{5,7},{6,4},{7,5},{8,10},{9,11},{10,... | collective-permute-start | bytes 196616 | tf_op jit(solution)/shard_map/ppermute | solution.py:507
  107.4 7.4 %collective-permute-start.18 = (f32[16,8,128]{2,1,0:T(8,128)S(1)}, f32[16,8,128]{2,1,0:T(8,128)S(1)}, u32[]{:S(2)}, u32[]{:S(2)}) collective-permute-start(f32[16,8,128]{2,1,0:T(8,128)S(1)} %get-tuple-element.75.refs_0_), channel_id=1, source_target_pairs={{0,3},{1,0},{2,1},{3,2},{4,7},{5,4},{6,5},{7,6},{8,11},{9,8},{10,9... | collective-permute-start | bytes 196616 | tf_op jit(solution)/shard_map/ppermute | solution.py:507

commit v4 on v3

--- a/solution.py
+++ b/solution.py
@@ -13,6 +13,7 @@
 PENALTY = 0.05
 HIGH = lax.Precision.HIGHEST
 AXES = ("row", "col", "band")
+CHUNK = 4
 LIMIT = pltpu.CompilerParams(vmem_limit_bytes=16 * 2**20)
 
 
@@ -97,7 +98,6 @@
                 lm = jnp.where(rows == d, lmn_ref[k, d], lm)
             total = total + lm * pos[k, t : t + 1, :]
         geometry.append(total)
-    copies[2].wait()
     total_f = F * lax.axis_size("band")
     for f in range(F):
         nu = 1.0 + (first + f).astype(jnp.float32) * (1.0 / total_f)
@@ -105,11 +105,14 @@
             ft = f * T + t
             turns = nu * geometry[t]
             r = turns - jnp.round(turns) + shift
-            e = cos_turns(r - jnp.round(r))
+            e_ref[ft] = cos_turns(r - jnp.round(r))
+    copies[2].wait()
+    for f in range(F):
+        for t in range(T):
+            ft = f * T + t
             g = jnp.concatenate([gains_ref[f, t, 0], gains_ref[f, t, 1]], axis=-1)
-            e_ref[ft] = e
             g_ref[ft] = g
-            p_ref[ft] = rotated(g, e)
+            p_ref[ft] = rotated(g, e_ref[ft])
 
 
 def own_terms(dims, flux_ref, live_ref, g_ref, held_ref, slope_ref):
@@ -179,25 +182,23 @@
     return out
 
 
-def setup_kernel(dims, flux_ref, flags_hbm, vis_hbm, duals_hbm, g_ref,
-                 live_col_ref, live_half_ref, live_own_ref, u_ref, rhs_ref, held_ref,
-                 slope_ref, power_ref, extra_ref, vis_ref, flags_ref, duals_ref, sems):
+def setup_kernel(dims, cols, flux_hbm, flags_hbm, duals_hbm, g_ref, live_col_ref, live_half_ref,
+                 live_own_ref, upright_ref, u_ref, rhs_ref, held_ref, slope_ref, samples_ref,
+                 extra_ref, flux_ref, flags_ref, duals_ref, sems):
     F, T, _, O, R, C = dims
-    rows, cols = vis_ref.shape[3], vis_ref.shape[4]
+    W, rows, full = 2 * O, C * O, flags_ref.shape[2]
     row = lax.axis_index("row")
     col = lax.axis_index("col")
-    flags_copy = pltpu.make_async_copy(flags_hbm, flags_ref, sems.at[F])
-    duals_copy = pltpu.make_async_copy(duals_hbm, duals_ref, sems.at[F + 1])
-    flags_copy.start()
-    duals_copy.start()
-
-    def vis_copy(f):
-        return pltpu.make_async_copy(vis_hbm.at[f], vis_ref.at[f], sems.at[f])
-
-    for f in range(F):
-        vis_copy(f).start()
-    flags_copy.wait()
-    counts = jnp.zeros((T, full_lanes(flags_ref)), jnp.float32)
+    copies = [
+        pltpu.make_async_copy(flags_hbm, flags_ref, sems.at[0]),
+        pltpu.make_async_copy(duals_hbm, duals_ref, sems.at[1]),
+        pltpu.make_async_copy(flux_hbm, flux_ref, sems.at[2]),
+    ]
+    for copy in copies:
+        copy.start()
+    copies[0].wait()
+    counts = jnp.zeros((T, full), jnp.float32)
+    stacked = []
     for f in range(F):
         live = flags_ref[f].astype(jnp.float32)
         at = slice(f * T, (f + 1) * T)
@@ -209,68 +210,41 @@
         live_half_ref[at, :] = pick(col % 2, [even, odd])
         own = pick(col, blocks)
         live_own_ref[at, :] = jnp.concatenate([own, own], axis=1)
+        stacked.append(mine)
         count = jnp.sum(live, axis=1, keepdims=True)
         counts = counts + live * (count - 1.0)
-    samples = jnp.sum(counts) / (R * C)
-    duals_copy.wait()
+    stacked = jnp.concatenate(stacked + [jnp.zeros((W - F * T, rows), jnp.float32)], axis=0)
+    upright_ref[...] = jnp.transpose(stacked)
+    samples = jnp.sum(counts, axis=0, keepdims=True)
+    samples = jnp.sum(samples, axis=1, keepdims=True) / (R * C)
+    copies[1].wait()
+    copies[2].wait()
     for f in range(F):
         for t in range(T):
             u_ref[f * T + t] = jnp.concatenate([duals_ref[f, t, 0], duals_ref[f, t, 1]], axis=-1)
     fit_sums(dims, lambda f, t: u_ref[f * T + t] + g_ref[f * T + t], rhs_ref)
     own = own_terms(dims, flux_ref, live_own_ref, g_ref, held_ref, slope_ref)
-    per = rows // cols
-    p = lax.broadcasted_iota(jnp.int32, (cols, cols), 0)
-    q = lax.broadcasted_iota(jnp.int32, (cols, cols), 1)
-    distinct = jnp.where(p == q, 0.0, 1.0).astype(jnp.bfloat16)
-    corner = pl.multiple_of((col % per) * cols, cols)
-
-    def channel(f, acc):
-        vis_copy(f).wait()
-
-        @pl.when(col // per == row)
-        def _():
-            for t in range(T):
-                for part in range(2):
-                    at = vis_ref.at[f, t, part, pl.ds(corner, cols), :]
-                    at[...] = at[...] * distinct
-
-        live = flags_ref[f].astype(jnp.float32)
-        mine = pick(row, [live[:, r * rows : (r + 1) * rows] for r in range(R)])
-        pair = pick(col, [live[:, c * cols : (c + 1) * cols] for c in range(C)])
-        upright = jnp.transpose(jnp.concatenate([mine] * (8 // T), axis=0))
-        for t in range(T):
-            weight = jnp.broadcast_to(upright[:, t : t + 1], (rows, cols)).astype(jnp.bfloat16)
-            total = jnp.zeros((16, cols), jnp.float32)
-            for part in range(2):
-                seen = (vis_ref[f, t, part] * weight).astype(jnp.float32)
-                total = total + jnp.sum((seen * seen).reshape(rows // 16, 16, cols), axis=0)
-            acc = acc + total * pair[t : t + 1, :]
-        return acc
-
-    power = lax.fori_loop(0, F, channel, jnp.zeros((16, cols), jnp.float32))
-    power = jnp.sum(power, axis=0, keepdims=True)
-    low = low_lanes(power.shape)
-    lanes = lax.broadcasted_iota(jnp.int32, power.shape, 1)
-    row_power = jnp.where(low, power + swap(power), jnp.where(lanes == O, samples, 0.0))
-    power_ref[...] = row_power
-    extra_ref[...] = row_power - jnp.where(low, own, 0.0)
-
-
-def full_lanes(ref):
-    return ref.shape[-1]
-
-
-def again_kernel(dims, flux_ref, power_ref, live_ref, u_ref, g_ref,
+    lanes = lax.broadcasted_iota(jnp.int32, own.shape, 1)
+    samples = jnp.where(lanes == O, samples, 0.0)
+    samples_ref[...] = samples
+    extra_ref[...] = samples - jnp.where(low_lanes(own.shape), own, 0.0)
+
+
+def again_kernel(dims, flux_ref, samples_ref, live_ref, u_ref, g_ref,
                  rhs_ref, held_ref, slope_ref, extra_ref):
     _, T, _, _, _, _ = dims
     fit_sums(dims, lambda f, t: u_ref[f * T + t] + g_ref[f * T + t], rhs_ref)
     own = own_terms(dims, flux_ref, live_ref, g_ref, held_ref, slope_ref)
-    extra_ref[...] = power_ref[...] - jnp.where(low_lanes(own.shape), own, 0.0)
+    extra_ref[...] = samples_ref[...] - jnp.where(low_lanes(own.shape), own, 0.0)
+
+
+def add_kernel(a_ref, b_ref, out_ref):
+    out_ref[...] = a_ref[...] + b_ref[...]
 
 
 def target_kernel(dims, first_pass, u_ref, g_ref, *refs):
     F, T, _, _, _, _ = dims
-    rhs_refs, outs = refs[:4], refs[4:]
+    rhs_refs, outs = refs[:2], refs[2:]
     for t in range(T):
         coeffs = solve(dims, rhs_refs, t)
         for f in range(F):
@@ -290,8 +264,12 @@
     return a == b
 
 
-def sum_kernel(dims, flux_ref, vis_hbm, live_ref, a_ref, b_ref, keep_ref, send_ref, vis_ref, distinct, sems):
+def sum_kernel(dims, flux_hbm, vis_hbm, live_ref, a_ref, b_ref, *refs):
     F, T, D, O, _, _ = dims
+    upright_ref, refs = (refs[0], refs[1:]) if len(refs) == 8 else (None, refs)
+    keep_ref, send_ref, refs = refs[0], refs[1], refs[2:]
+    power_ref, refs = (refs[0], refs[1:]) if upright_ref is not None else (None, refs)
+    vis_ref, distinct, flux_ref, sems = refs
     rows, cols = vis_ref.shape[3], vis_ref.shape[4]
     row = lax.axis_index("row")
     col = lax.axis_index("col")
@@ -300,7 +278,10 @@
     def vis_copy(f):
         return pltpu.make_async_copy(vis_hbm.at[f], vis_ref.at[f], sems.at[f])
 
-    for f in range(F):
+    flux_copy = pltpu.make_async_copy(flux_hbm, flux_ref, sems.at[F])
+    flux_copy.start()
+    ahead = 2 * CHUNK
+    for f in range(ahead):
         vis_copy(f).start()
     p = lax.broadcasted_iota(jnp.int32, (rows, cols), 0) + row * rows
     q = lax.broadcasted_iota(jnp.int32, (rows, cols), 1) + col * cols
@@ -309,12 +290,12 @@
     blocks = block_mask(2 * D)
     nt = (((1,), (1,)), ((), ()))
 
-    def body(step, carry):
+    def body(step, upright, start, power):
         highs, lows = [], []
         lives = live_ref[pl.ds(step * 8, 8), :]
+        mask = distinct[...]
         for i in range(group):
             f = step * group + i
-            vis_copy(f).wait()
             scale = column(flux_ref, f, D, cols)
             for t in range(T):
                 j = i * T + t
@@ -333,14 +314,22 @@
                 highs.append(high)
                 lows.append(low)
                 both = jnp.concatenate([high, low], axis=0)
-                mask = distinct[...]
-                seen = jnp.concatenate([vis_ref[f, t, 0] * mask, vis_ref[f, t, 1] * mask], axis=1)
-                v = lax.dot_general(both, seen, nt, preferred_element_type=jnp.float32)
+                seen = [vis_ref[f, t, part] * mask for part in range(2)]
+                v = lax.dot_general(
+                    both, jnp.concatenate(seen, axis=1), nt, preferred_element_type=jnp.float32
+                )
                 v = v[: 2 * D] + v[2 * D :]
                 v0, v1 = v[:, : 2 * O], v[:, 2 * O :]
                 even, odd = join_low(v0, v1), join_high(v0, v1)
                 keep_ref[step * 9 + j] = jnp.where(parity == 0, even, odd)
                 send_ref[step * 9 + j] = jnp.where(parity == 0, odd, even)
+                if upright is not None:
+                    square = [x.astype(jnp.float32) for x in seen]
+                    square = square[0] * square[0] + square[1] * square[1]
+                    at = start + j
+                    square = square * jnp.broadcast_to(upright[:, at : at + 1], square.shape)
+                    square = jnp.sum(square.reshape(rows // 8, 8, cols), axis=0)
+                    power = power + square * lives[j : j + 1, :]
         high = jnp.concatenate(highs, axis=0)
         low = jnp.concatenate(lows, axis=0)
         gram = lax.dot_general(high, high, nt, preferred_element_type=jnp.float32)
@@ -352,12 +341,32 @@
             folded = folded + gram[i * 2 * D : (i + 1) * 2 * D]
         keep_ref[step * 9 + 8] = folded
         send_ref[step * 9 + 8] = folded
-        return carry
-
-    lax.fori_loop(0, F * T // 8, body, 0, unroll=2)
-
-
-def residual_kernel(dims, live_ref, extra_ref, kept_ref, other_ref, mine_ref, theirs_ref,
+        return power
+
+    def chunk(c, power):
+        for i in range(CHUNK):
+            vis_copy(c * CHUNK + i).wait()
+
+        @pl.when(c * CHUNK + ahead < F)
+        def _():
+            for i in range(CHUNK):
+                vis_copy(c * CHUNK + ahead + i).start()
+
+        upright = None
+        if upright_ref is not None:
+            upright = pltpu.roll(upright_ref[...], (2 * O - c * CHUNK * T) % (2 * O), 1)
+        for j in range(CHUNK // group):
+            power = body(c * (CHUNK // group) + j, upright, j * 8, power)
+        return power
+
+    flux_copy.wait()
+    power = lax.fori_loop(0, F // CHUNK, chunk, jnp.zeros((8, cols), jnp.float32))
+    if power_ref is not None:
+        power = jnp.sum(power, axis=0, keepdims=True)
+        power_ref[...] = jnp.where(low_lanes(power.shape), power + swap(power), 0.0)
+
+
+def residual_kernel(dims, live_ref, extra_ref, power_ref, kept_ref, other_ref, mine_ref, theirs_ref,
                     keep_ref, send_ref, scalar_ref):
     F, T, D, O, _, _ = dims
     W = 2 * O
@@ -395,7 +404,7 @@
             send_ref[ft] = jnp.where(near, high, low)
     squares = -jnp.sum(total, axis=0, keepdims=True)
     squares = squares + swap(squares)
-    scalar = jnp.where(low_lanes(squares.shape), squares, 0.0) + extra_ref[...]
+    scalar = jnp.where(low_lanes(squares.shape), squares, 0.0) + extra_ref[...] + power_ref[...]
     scalar_ref[...] = jnp.broadcast_to(scalar, scalar_ref.shape)
 
 
@@ -533,55 +542,60 @@
         last = step == ITERS - 1
         got = [gather(p, m) for m in range(R)]
         if step == 0:
-            (live_col, live_half, live_own, u, rhs, held, slope, power, extra) = (
+            (live_col, live_half, live_own, upright, u, rhs, held, slope, samples, extra) = (
                 pl.pallas_call(
-                    functools.partial(setup_kernel, dims),
+                    functools.partial(setup_kernel, dims, cols),
                     out_shape=[
-                        array(FT, cols), array(FT, W), array(FT, W), whole, fit, whole, whole,
-                        text, text,
+                        array(FT, cols), array(FT, W), array(FT, W), array(rows, W), whole,
+                        fit, whole, whole, text, text,
                     ],
-                    in_specs=[smem] + [hbm] * 3 + [vmem],
-                    out_specs=[vmem] * 9,
+                    in_specs=[hbm] * 3 + [vmem],
+                    out_specs=[vmem] * 10,
                     scratch_shapes=[
-                        pltpu.VMEM(vis.shape, vis.dtype),
+                        pltpu.SMEM(flux_t.shape, f32),
                         pltpu.VMEM(flags.shape, flags.dtype),
                         pltpu.VMEM(duals.shape, f32),
-                        pltpu.SemaphoreType.DMA((F + 2,)),
+                        pltpu.SemaphoreType.DMA((3,)),
                     ],
                     compiler_params=LIMIT,
                     name="setup",
-                )(flux_t, far(flags), far(vis), far(duals), g)
+                )(far(flux_t), far(flags), far(duals), g)
             )
         else:
             rhs, held, slope, extra = call(
                 functools.partial(again_kernel, dims),
-                [fit, whole, whole, text], [flux_t], [power, live_own, u, g],
+                [fit, whole, whole, text], [flux_t], [samples, live_own, u, g],
             )
-        rhs_all = bands(rhs)
+        rhs_near = permute(rhs, lambda r, c, z: (r, c, z ^ 1))
         theirs = permute(p, lambda r, c, z: (r, c ^ 2, z))
-        keep, send = pl.pallas_call(
+        more = [] if step else [upright]
+        keep, send, *found = pl.pallas_call(
             functools.partial(sum_kernel, dims),
-            out_shape=[pair, pair],
-            in_specs=[smem, hbm] + [vmem] * 3,
-            out_specs=[vmem] * 2,
+            out_shape=[pair, pair] + ([] if step else [array(1, cols)]),
+            in_specs=[hbm] * 2 + [vmem] * (3 + len(more)),
+            out_specs=[vmem] * (2 + len(more)),
             scratch_shapes=[
                 pltpu.VMEM(vis.shape, vis.dtype),
                 pltpu.VMEM((rows, cols), vis.dtype),
-                pltpu.SemaphoreType.DMA((F,)),
+                pltpu.SMEM(flux_t.shape, f32),
+                pltpu.SemaphoreType.DMA((F + 1,)),
             ],
             compiler_params=LIMIT,
             name="sums",
-        )(flux_t, far(vis), live_col, *got)
+        )(far(flux_t), far(vis), live_col, *got, *more)
+        power = power if step else found[0]
         other = permute(send, lambda r, c, z: (r, c ^ 1, z))
+        (rhs,) = call(add_kernel, [fit], [], [rhs, rhs_near])
+        rhs_far = permute(rhs, lambda r, c, z: (r, c, z ^ 2))
         keep, send, scalar = call(
             functools.partial(residual_kernel, dims), [line, line, array(R * C * Z, W)],
-            [], [live_half, extra, keep, other, p, theirs],
+            [], [live_half, extra, power, keep, other, p, theirs],
         )
         come = permute(send, lambda r, c, z: (r, c ^ 2, z))
         scalar = lax.all_to_all(scalar, AXES, 0, 0, tiled=True)
         target = call(
             functools.partial(target_kernel, dims, step == 0),
-            [whole] * (1 if step == 0 else 2), [], [u, g, *rhs_all],
+            [whole] * (1 if step == 0 else 2), [], [u, g, rhs, rhs_far],
         )
         num, den = call(
             functools.partial(merge_kernel, dims), [whole, whole], [],

time: 116 us -> 115 us (level)
  waiting for transfers between devices: 39.9 us -> 53.7 us
  Pallas kernels: 34.8 us -> 24.3 us
  starting transfers between devices: 39.5 us -> 36 us
    ppermute x19 -> x17, waiting for transfers between devices: 27.9 us -> 42 us  [permute(): return lax.ppermute(x, AXES, pairs)]
    pallas_call x1, Pallas kernels: 9.09 us -> 2.33 us  [shards(): pl.pallas_call(functools.partial(setup_kernel, dims, cols), out_shape=[ar...]
    ppermute x19 -> x17, starting transfers between devices: 33.3 us -> 29.4 us  [permute(): return lax.ppermute(x, AXES, pairs)]
    pallas_call x2, Pallas kernels: 16 us -> 12.1 us  [shards(): pl.pallas_call(functools.partial(sum_kernel, dims), out_shape=[pair, pair...]
    pallas_call x10 -> x12, Pallas kernels: 7.4 us -> 7.38 us  [call(): pl.pallas_call(kernel, out_shape=outs, in_specs=[smem] * len(scalars) + [...]
  transfers between devices with their start and end apart: 21 -> 19, of which waited for: 11 -> 11; matrix products, arithmetic and copies ran while one was open for 0% -> 0% of each run, Pallas kernels for 10% -> 4%
where the time goes in v4:
time: 115 us
  waiting for transfers between devices  53.7 us (47%)
  starting transfers between devices  36 us (31%)
  Pallas kernels  24.3 us (21%)
    ppermute x17, waiting for transfers between devices, permute(): return lax.ppermute(x, AXES, pairs)  42 us
    ppermute x17, starting transfers between devices, permute(): return lax.ppermute(x, AXES, pairs)  29.4 us
    pallas_call x2, Pallas kernels, shards(): pl.pallas_call(functools.partial(sum_kernel, dims), out_shape=[pair, pair...  12.1 us
    all_to_all x2, waiting for transfers between devices, shards(): scalar = lax.all_to_all(scalar, AXES, 0, 0, tiled=True)  11.7 us
    pallas_call x12, Pallas kernels, call(): pl.pallas_call(kernel, out_shape=outs, in_specs=[smem] * len(scalars) + [...  7.38 us
    all_to_all x2, starting transfers between devices, shards(): scalar = lax.all_to_all(scalar, AXES, 0, 0, tiled=True)  6.58 us
    pallas_call x1, Pallas kernels, shards(): pl.pallas_call(functools.partial(start_kernel, dims), out_shape=[whole] *...  2.54 us
    pallas_call x1, Pallas kernels, shards(): pl.pallas_call(functools.partial(setup_kernel, dims, cols), out_shape=[ar...  2.33 us
  transfers between devices with their start and end apart: 19, of which 11 were waited for; matrix products, arithmetic and copies ran while one was open for 0% of the time, Pallas kernels for 4%

profile of v4, /device:TPU:0, one launch (start us, length us, event | category | flops | bytes accessed | tf_op | source)
XLA Modules:
  0.0 114.9 jit_solution(10876879205395849325)
XLA Ops:
  0.6 2.5 %start.1 = (f32[64,8,128]{2,1,0:T(8,128)S(1)}, f32[64,8,128]{2,1,0:T(8,128)S(1)}, f32[64,8,128]{2,1,0:T(8,128)S(1)}) custom-call(f32[3,4,512]{2,1,0:T(4,128)} %bitcast.16, f32[3,8]{1,0:T(4,128)} %lmn_hbm.1, f32[16,4,2,8,64]{4,3,2,1,0:T(8,128)} %gains_hbm.1), custom_call_target="tpu_custom_call" | custom-call | tf_op jit(solution)/shard_map/start/pallas_call | solution.py:527
  3.2 0.7 collective-permute-start
  3.9 5.7 %collective-permute-start.1 = (f32[64,8,128]{2,1,0:T(8,128)S(1)}, f32[64,8,128]{2,1,0:T(8,128)S(1)}, u32[]{:S(2)}, u32[]{:S(2)}) collective-permute-start(f32[64,8,128]{2,1,0:T(8,128)S(1)} %get-tuple-element.48.mine_ref), channel_id=1, source_target_pairs={{0,16},{1,17},{2,18},{3,19},{4,0},{5,1},{6,2},{7,3},{8,20},{9,21},... | collective-permute-start | bytes 786440 | tf_op jit(solution)/shard_map/ppermute | solution.py:516
  9.6 2.3 %setup.1 = (f32[64,128]{1,0:T(8,128)S(1)}, f32[64,128]{1,0:T(8,128)S(1)}, f32[64,128]{1,0:T(8,128)S(1)}, f32[256,128]{1,0:T(8,128)S(1)}, f32[64,8,128]{2,1,0:T(8...) custom-call(f32[8,16]{1,0:T(8,128)} %bitcast.10, ...), custom_call_target="tpu_custom_call" | custom-call | tf_op jit(solution)/shard_map/setup/pallas_call | solution.py:546
  11.9 0.0 collective-permute-done.a_ref
  11.9 7.9 %collective-permute-done.1.b_ref = f32[64,8,128]{2,1,0:T(8,128)S(1)} collective-permute-done((f32[64,8,128]{2,1,0:T(8,128)S(1)}, f32[64,8,128]{2,1,0:T(8,128)S(1)}, u32[]{:S(2)}, u32[]{:S(2)}) %collective-permute-start.1) | collective-permute-done | bytes 262176 | tf_op jit(solution)/shard_map/ppermute | solution.py:516
  19.8 6.8 %sums.2 = (f32[72,16,128]{2,1,0:T(8,128)S(1)}, f32[72,16,128]{2,1,0:T(8,128)S(1)}, f32[1,128]{1,0:T(1,128)S(1)}) custom-call(f32[8,16]{1,0:T(8,128)} %bitcast.11, bf16[16,4,2,256,128]{4,3,2,1,0:T(8,128)(2,1)} %vis_hbm.3, f32[64,128]{1,0:T(8,128)S(1)} %get-tuple-element.47.live_ref, f32[64,8,128]{2,1,0:T(8,128)S(1)} %collective-permute-done.a_ref, ...), custom_call_target="tpu_custom_call" | custom-call | tf_op jit(solution)/shard_map/sums/pallas_call | solution.py:572
  26.6 0.0 copy-start
  26.7 0.9 collective-permute-start.2
  27.5 2.2 %collective-permute-start.3 = (f32[64,8,128]{2,1,0:T(8,128)S(1)}, f32[64,8,128]{2,1,0:T(8,128)S(1)}, u32[]{:S(2)}, u32[]{:S(2)}) collective-permute-start(f32[64,8,128]{2,1,0:T(8,128)S(1)} %get-tuple-element.48.mine_ref), channel_id=1, source_target_pairs={{0,8},{1,9},{2,10},{3,11},{4,12},{5,13},{6,14},{7,15},{8,0},{9,1},... | collective-permute-start | bytes 786440 | tf_op jit(solution)/shard_map/ppermute | solution.py:516
  29.7 6.9 %collective-permute-done.3.theirs_ref = f32[64,8,128]{2,1,0:T(8,128)S(1)} collective-permute-done((f32[64,8,128]{2,1,0:T(8,128)S(1)}, f32[64,8,128]{2,1,0:T(8,128)S(1)}, u32[]{:S(2)}, u32[]{:S(2)}) %collective-permute-start.3) | collective-permute-done | bytes 262176 | tf_op jit(solution)/shard_map/ppermute | solution.py:516
  36.6 0.0 collective-permute-done.2.other_ref
  36.6 1.5 %shard_map.86 = (f32[65,8,128]{2,1,0:T(8,128)S(1)}, f32[65,8,128]{2,1,0:T(8,128)S(1)}, f32[32,128]{1,0:T(8,128)}) custom-call(f32[64,128]{1,0:T(8,128)S(1)} %get-tuple-element.42.live_ref, f32[1,128]{1,0:T(1,128)S(1)} %get-tuple-element.46.extra_ref, f32[1,128]{1,0:T(1,128)S(1)} %get-tuple-element.50.power_ref, ...), custom_call_target="tpu_custom_call" | custom-call | tf_op jit(solution)/shard_map/pallas_call | solution.py:499
  38.1 1.7 %collective-permute-start.4 = (f32[65,8,128]{2,1,0:T(8,128)S(1)}, f32[65,8,128]{2,1,0:T(8,128)S(1)}, u32[]{:S(2)}, u32[]{:S(2)}) collective-permute-start(f32[65,8,128]{2,1,0:T(8,128)S(1)} %get-tuple-element.55), channel_id=1, source_target_pairs={{0,8},{1,9},{2,10},{3,11},{4,12},{5,13},{6,14},{7,15},{8,0},{9,1},... | collective-permute-start | bytes 798728 | tf_op jit(solution)/shard_map/ppermute | solution.py:516
  39.8 1.6 %collective-permute-start.5 = (f32[16,8,128]{2,1,0:T(8,128)S(1)}, f32[16,8,128]{2,1,0:T(8,128)S(1)}, u32[]{:S(2)}, u32[]{:S(2)}) collective-permute-start(f32[16,8,128]{2,1,0:T(8,128)S(1)} %get-tuple-element.61.a_ref), channel_id=1, source_target_pairs={{0,1},{1,0},{2,3},{3,2},{4,5},{5,4},{6,7},{7,6},{8,9},{9,8},{10,11... | collective-permute-start | bytes 196616 | tf_op jit(solution)/shard_map/ppermute | solution.py:516
  41.4 2.7 %collective-permute-done.5.b_ref = f32[16,8,128]{2,1,0:T(8,128)S(1)} collective-permute-done((f32[16,8,128]{2,1,0:T(8,128)S(1)}, f32[16,8,128]{2,1,0:T(8,128)S(1)}, u32[]{:S(2)}, u32[]{:S(2)}) %collective-permute-start.5) | collective-permute-done | bytes 65568 | tf_op jit(solution)/shard_map/ppermute | solution.py:516
  44.1 2.7 %collective-permute-start.6 = (f32[16,8,128]{2,1,0:T(8,128)S(1)}, f32[16,8,128]{2,1,0:T(8,128)S(1)}, u32[]{:S(2)}, u32[]{:S(2)}) collective-permute-start(f32[16,8,128]{2,1,0:T(8,128)S(1)} %shard_map.88.refs_0_), channel_id=1, source_target_pairs={{0,2},{1,3},{2,0},{3,1},{4,6},{5,7},{6,4},{7,5},{8,10},{9,11},{10,... | collective-permute-start | bytes 196616 | tf_op jit(solution)/shard_map/ppermute | solution.py:516
  46.7 2.5 %all-to-all-start = ((f32[32,1,128]{2,1,0:T(1,128)}), f32[32,1,128]{2,1,0:T(1,128)S(1)}, u32[]{:S(2)}, u32[]{:S(2)}) async-start(f32[32,1,128]{2,1,0:T(1,128)} %bitcast.3), calls=%async_computation | async-start | bytes 32768 | tf_op jit(solution)/shard_map/all_to_all | solution.py:595
  49.3 0.0 collective-permute-done.6.refs_1_
  49.3 0.1 shard_map.89.refs_3_
  49.4 0.5 shard_map.87
  49.9 6.5 %all-to-all-done = f32[32,1,128]{2,1,0:T(1,128)S(1)} async-done(((f32[32,1,128]{2,1,0:T(1,128)}), f32[32,1,128]{2,1,0:T(1,128)S(1)}, u32[]{:S(2)}, u32[]{:S(2)}) %all-to-all-start) | async-done | bytes 16416 | tf_op jit(solution)/shard_map/all_to_all | solution.py:595
  56.4 0.3 shard_map.90
  56.7 0.7 collective-permute-start.7
  57.4 3.3 %collective-permute-start.8 = (f32[64,8,128]{2,1,0:T(8,128)S(1)}, f32[64,8,128]{2,1,0:T(8,128)S(1)}, u32[]{:S(2)}, u32[]{:S(2)}) collective-permute-start(f32[64,8,128]{2,1,0:T(8,128)S(1)} %get-tuple-element.64.mine_ref), channel_id=1, source_target_pairs={{0,16},{1,17},{2,18},{3,19},{4,0},{5,1},{6,2},{7,3},{8,20},{9,21},... | collective-permute-start | bytes 786440 | tf_op jit(solution)/shard_map/ppermute | solution.py:516
  60.7 9.2 %collective-permute-done.8.b_ref = f32[64,8,128]{2,1,0:T(8,128)S(1)} collective-permute-done((f32[64,8,128]{2,1,0:T(8,128)S(1)}, f32[64,8,128]{2,1,0:T(8,128)S(1)}, u32[]{:S(2)}, u32[]{:S(2)}) %collective-permute-start.8) | collective-permute-done | bytes 262176 | tf_op jit(solution)/shard_map/ppermute | solution.py:516
  70.0 5.3 %sums.3 = (f32[72,16,128]{2,1,0:T(8,128)S(1)}, f32[72,16,128]{2,1,0:T(8,128)S(1)}) custom-call(f32[8,16]{1,0:T(8,128)} %bitcast.12, bf16[16,4,2,256,128]{4,3,2,1,0:T(8,128)(2,1)} %vis_hbm.3, f32[64,128]{1,0:T(8,128)S(1)} %get-tuple-element.47.live_ref, f32[64,8,128]{2,1,0:T(8,128)S(1)} %collective-permute-done.7.a_ref, ...), custom_call_target="tpu_custom_call" | custom-call | tf_op jit(solution)/shard_map/sums/pallas_call | solution.py:572
  75.3 1.6 %collective-permute-start.9 = (f32[72,16,128]{2,1,0:T(8,128)S(1)}, f32[72,16,128]{2,1,0:T(8,128)S(1)}, u32[]{:S(2)}, u32[]{:S(2)}) collective-permute-start(f32[72,16,128]{2,1,0:T(8,128)S(1)} %get-tuple-element.66), channel_id=1, source_target_pairs={{0,4},{1,5},{2,6},{3,7},{4,0},{5,1},{6,2},{7,3},{8,12},{9,13},{10,... | collective-permute-start | bytes 1769480 | tf_op jit(solution)/shard_map/ppermute | solution.py:516
  76.9 1.7 %collective-permute-start.10 = (f32[64,8,128]{2,1,0:T(8,128)S(1)}, f32[64,8,128]{2,1,0:T(8,128)S(1)}, u32[]{:S(2)}, u32[]{:S(2)}) collective-permute-start(f32[64,8,128]{2,1,0:T(8,128)S(1)} %get-tuple-element.64.mine_ref), channel_id=1, source_target_pairs={{0,8},{1,9},{2,10},{3,11},{4,12},{5,13},{6,14},{7,15},{8,0},{9,1},... | collective-permute-start | bytes 786440 | tf_op jit(solution)/shard_map/ppermute | solution.py:516
  78.6 0.9 shard_map.91
  79.5 5.7 %collective-permute-done.10.theirs_ref = f32[64,8,128]{2,1,0:T(8,128)S(1)} collective-permute-done((f32[64,8,128]{2,1,0:T(8,128)S(1)}, f32[64,8,128]{2,1,0:T(8,128)S(1)}, u32[]{:S(2)}, u32[]{:S(2)}) %collective-permute-start.10) | collective-permute-done | bytes 262176 | tf_op jit(solution)/shard_map/ppermute | solution.py:516
  85.2 1.4 %shard_map.92 = (f32[65,8,128]{2,1,0:T(8,128)S(1)}, f32[65,8,128]{2,1,0:T(8,128)S(1)}, f32[32,128]{1,0:T(8,128)}) custom-call(f32[64,128]{1,0:T(8,128)S(1)} %get-tuple-element.42.live_ref, f32[1,128]{1,0:T(1,128)S(1)} %get-tuple-element.63.extra_ref, f32[1,128]{1,0:T(1,128)S(1)} %get-tuple-element.50.power_ref, ...), custom_call_target="tpu_custom_call" | custom-call | tf_op jit(solution)/shard_map/pallas_call | solution.py:499
  86.6 1.7 %collective-permute-start.11 = (f32[65,8,128]{2,1,0:T(8,128)S(1)}, f32[65,8,128]{2,1,0:T(8,128)S(1)}, u32[]{:S(2)}, u32[]{:S(2)}) collective-permute-start(f32[65,8,128]{2,1,0:T(8,128)S(1)} %get-tuple-element.69), channel_id=1, source_target_pairs={{0,8},{1,9},{2,10},{3,11},{4,12},{5,13},{6,14},{7,15},{8,0},{9,1},... | collective-permute-start | bytes 798728 | tf_op jit(solution)/shard_map/ppermute | solution.py:516
  88.3 0.6 collective-permute-start.12
  88.9 3.6 %collective-permute-done.12.b_ref = f32[16,8,128]{2,1,0:T(8,128)S(1)} collective-permute-done((f32[16,8,128]{2,1,0:T(8,128)S(1)}, f32[16,8,128]{2,1,0:T(8,128)S(1)}, u32[]{:S(2)}, u32[]{:S(2)}) %collective-permute-start.12) | collective-permute-done | bytes 65568 | tf_op jit(solution)/shard_map/ppermute | solution.py:516
  92.6 0.6 collective-permute-start.13
  93.2 4.0 %all-to-all-start.1 = ((f32[32,1,128]{2,1,0:T(1,128)}), f32[32,1,128]{2,1,0:T(1,128)S(1)}, u32[]{:S(2)}, u32[]{:S(2)}) async-start(f32[32,1,128]{2,1,0:T(1,128)} %bitcast.6), calls=%async_computation.1 | async-start | bytes 32768 | tf_op jit(solution)/shard_map/all_to_all | solution.py:595
  97.2 1.3 %collective-permute-done.13.refs_1_ = f32[16,8,128]{2,1,0:T(8,128)S(1)} collective-permute-done((f32[16,8,128]{2,1,0:T(8,128)S(1)}, f32[16,8,128]{2,1,0:T(8,128)S(1)}, u32[]{:S(2)}, u32[]{:S(2)}) %collective-permute-start.13) | collective-permute-done | bytes 65568 | tf_op jit(solution)/shard_map/ppermute | solution.py:516
  98.5 0.1 shard_map.95
  98.7 0.5 shard_map.93
  99.2 5.2 %all-to-all-done.1 = f32[32,1,128]{2,1,0:T(1,128)S(1)} async-done(((f32[32,1,128]{2,1,0:T(1,128)}), f32[32,1,128]{2,1,0:T(1,128)S(1)}, u32[]{:S(2)}, u32[]{:S(2)}) %all-to-all-start.1) | async-done | bytes 16416 | tf_op jit(solution)/shard_map/all_to_all | solution.py:595
  104.4 1.1 shard_map.96
  105.4 0.5 collective-permute-start.14
  105.9 0.6 collective-permute-start.15
  106.6 2.7 %collective-permute-start.16 = (f32[16,8,128]{2,1,0:T(8,128)S(1)}, f32[16,8,128]{2,1,0:T(8,128)S(1)}, u32[]{:S(2)}, u32[]{:S(2)}) collective-permute-start(f32[16,8,128]{2,1,0:T(8,128)S(1)} %get-tuple-element.79.refs_0_), channel_id=1, source_target_pairs={{0,3},{1,0},{2,1},{3,2},{4,7},{5,4},{6,5},{7,6},{8,11},{9,8},{10,9... | collective-permute-start | bytes 196616 | tf_op jit(solution)/shard_map/ppermute | solution.py:516
  109.3 2.9 %collective-permute-done.14.refs_1_ = f32[16,8,128]{2,1,0:T(8,128)S(1)} collective-permute-done((f32[16,8,128]{2,1,0:T(8,128)S(1)}, f32[16,8,128]{2,1,0:T(8,128)S(1)}, u32[]{:S(2)}, u32[]{:S(2)}) %collective-permute-start.14) | collective-permute-done | bytes 65568 | tf_op jit(solution)/shard_map/ppermute | solution.py:516
  112.2 1.7 %collective-permute-done.15.refs_2_ = f32[16,8,128]{2,1,0:T(8,128)S(1)} collective-permute-done((f32[16,8,128]{2,1,0:T(8,128)S(1)}, f32[16,8,128]{2,1,0:T(8,128)S(1)}, u32[]{:S(2)}, u32[]{:S(2)}) %collective-permute-start.15) | collective-permute-done | bytes 65568 | tf_op jit(solution)/shard_map/ppermute | solution.py:516
  113.9 1.0 shard_map.97
  (8 shorter events, 0.0 us)
Async XLA Ops:
  3.2 8.7 %collective-permute-start = (f32[64,8,128]{2,1,0:T(8,128)S(1)}, f32[64,8,128]{2,1,0:T(8,128)S(1)}, u32[]{:S(2)}, u32[]{:S(2)}) collective-permute-start(f32[64,8,128]{2,1,0:T(8,128)S(1)} %get-tuple-element.48.mine_ref), channel_id=1, source_target_pairs={{0,0},{1,1},{2,2},{3,3},{4,16},{5,17},{6,18},{7,19},{8,4},{9,5},{1... | collective-permute-start | bytes 786440 | tf_op jit(solution)/shard_map/ppermute | solution.py:516
  3.9 16.0 %collective-permute-start.1 = (f32[64,8,128]{2,1,0:T(8,128)S(1)}, f32[64,8,128]{2,1,0:T(8,128)S(1)}, u32[]{:S(2)}, u32[]{:S(2)}) collective-permute-start(f32[64,8,128]{2,1,0:T(8,128)S(1)} %get-tuple-element.48.mine_ref), channel_id=1, source_target_pairs={{0,16},{1,17},{2,18},{3,19},{4,0},{5,1},{6,2},{7,3},{8,20},{9,21},... | collective-permute-start | bytes 786440 | tf_op jit(solution)/shard_map/ppermute | solution.py:516
  26.6 51.9 %copy-start = (f32[16,8]{0,1:T(8,128)S(1)}, f32[16,8]{0,1:T(8,128)}, u32[]{:S(2)}) copy-start(f32[16,8]{0,1:T(8,128)} %param.11) | copy-start | bytes 1540
  26.7 9.9 %collective-permute-start.2 = (f32[72,16,128]{2,1,0:T(8,128)S(1)}, f32[72,16,128]{2,1,0:T(8,128)S(1)}, u32[]{:S(2)}, u32[]{:S(2)}) collective-permute-start(f32[72,16,128]{2,1,0:T(8,128)S(1)} %get-tuple-element.52), channel_id=1, source_target_pairs={{0,4},{1,5},{2,6},{3,7},{4,0},{5,1},{6,2},{7,3},{8,12},{9,13},{10,... | collective-permute-start | bytes 1769480 | tf_op jit(solution)/shard_map/ppermute | solution.py:516
  27.5 9.1 %collective-permute-start.3 = (f32[64,8,128]{2,1,0:T(8,128)S(1)}, f32[64,8,128]{2,1,0:T(8,128)S(1)}, u32[]{:S(2)}, u32[]{:S(2)}) collective-permute-start(f32[64,8,128]{2,1,0:T(8,128)S(1)} %get-tuple-element.48.mine_ref), channel_id=1, source_target_pairs={{0,8},{1,9},{2,10},{3,11},{4,12},{5,13},{6,14},{7,15},{8,0},{9,1},... | collective-permute-start | bytes 786440 | tf_op jit(solution)/shard_map/ppermute | solution.py:516
  38.1 11.3 %collective-permute-start.4 = (f32[65,8,128]{2,1,0:T(8,128)S(1)}, f32[65,8,128]{2,1,0:T(8,128)S(1)}, u32[]{:S(2)}, u32[]{:S(2)}) collective-permute-start(f32[65,8,128]{2,1,0:T(8,128)S(1)} %get-tuple-element.55), channel_id=1, source_target_pairs={{0,8},{1,9},{2,10},{3,11},{4,12},{5,13},{6,14},{7,15},{8,0},{9,1},... | collective-permute-start | bytes 798728 | tf_op jit(solution)/shard_map/ppermute | solution.py:516
  39.8 4.3 %collective-permute-start.5 = (f32[16,8,128]{2,1,0:T(8,128)S(1)}, f32[16,8,128]{2,1,0:T(8,128)S(1)}, u32[]{:S(2)}, u32[]{:S(2)}) collective-permute-start(f32[16,8,128]{2,1,0:T(8,128)S(1)} %get-tuple-element.61.a_ref), channel_id=1, source_target_pairs={{0,1},{1,0},{2,3},{3,2},{4,5},{5,4},{6,7},{7,6},{8,9},{9,8},{10,11... | collective-permute-start | bytes 196616 | tf_op jit(solution)/shard_map/ppermute | solution.py:516
  44.1 5.2 %collective-permute-start.6 = (f32[16,8,128]{2,1,0:T(8,128)S(1)}, f32[16,8,128]{2,1,0:T(8,128)S(1)}, u32[]{:S(2)}, u32[]{:S(2)}) collective-permute-start(f32[16,8,128]{2,1,0:T(8,128)S(1)} %shard_map.88.refs_0_), channel_id=1, source_target_pairs={{0,2},{1,3},{2,0},{3,1},{4,6},{5,7},{6,4},{7,5},{8,10},{9,11},{10,... | collective-permute-start | bytes 196616 | tf_op jit(solution)/shard_map/ppermute | solution.py:516
  46.7 9.7 %all-to-all-start = ((f32[32,1,128]{2,1,0:T(1,128)}), f32[32,1,128]{2,1,0:T(1,128)S(1)}, u32[]{:S(2)}, u32[]{:S(2)}) async-start(f32[32,1,128]{2,1,0:T(1,128)} %bitcast.3), calls=%async_computation | async-start | bytes 32768 | tf_op jit(solution)/shard_map/all_to_all | solution.py:595
  56.7 4.0 %collective-permute-start.7 = (f32[64,8,128]{2,1,0:T(8,128)S(1)}, f32[64,8,128]{2,1,0:T(8,128)S(1)}, u32[]{:S(2)}, u32[]{:S(2)}) collective-permute-start(f32[64,8,128]{2,1,0:T(8,128)S(1)} %get-tuple-element.64.mine_ref), channel_id=1, source_target_pairs={{0,0},{1,1},{2,2},{3,3},{4,16},{5,17},{6,18},{7,19},{8,4},{9,5},{1... | collective-permute-start | bytes 786440 | tf_op jit(solution)/shard_map/ppermute | solution.py:516
  57.4 12.6 %collective-permute-start.8 = (f32[64,8,128]{2,1,0:T(8,128)S(1)}, f32[64,8,128]{2,1,0:T(8,128)S(1)}, u32[]{:S(2)}, u32[]{:S(2)}) collective-permute-start(f32[64,8,128]{2,1,0:T(8,128)S(1)} %get-tuple-element.64.mine_ref), channel_id=1, source_target_pairs={{0,16},{1,17},{2,18},{3,19},{4,0},{5,1},{6,2},{7,3},{8,20},{9,21},... | collective-permute-start | bytes 786440 | tf_op jit(solution)/shard_map/ppermute | solution.py:516
  75.3 9.9 %collective-permute-start.9 = (f32[72,16,128]{2,1,0:T(8,128)S(1)}, f32[72,16,128]{2,1,0:T(8,128)S(1)}, u32[]{:S(2)}, u32[]{:S(2)}) collective-permute-start(f32[72,16,128]{2,1,0:T(8,128)S(1)} %get-tuple-element.66), channel_id=1, source_target_pairs={{0,4},{1,5},{2,6},{3,7},{4,0},{5,1},{6,2},{7,3},{8,12},{9,13},{10,... | collective-permute-start | bytes 1769480 | tf_op jit(solution)/shard_map/ppermute | solution.py:516
  76.9 8.3 %collective-permute-start.10 = (f32[64,8,128]{2,1,0:T(8,128)S(1)}, f32[64,8,128]{2,1,0:T(8,128)S(1)}, u32[]{:S(2)}, u32[]{:S(2)}) collective-permute-start(f32[64,8,128]{2,1,0:T(8,128)S(1)} %get-tuple-element.64.mine_ref), channel_id=1, source_target_pairs={{0,8},{1,9},{2,10},{3,11},{4,12},{5,13},{6,14},{7,15},{8,0},{9,1},... | collective-permute-start | bytes 786440 | tf_op jit(solution)/shard_map/ppermute | solution.py:516
  86.6 12.0 %collective-permute-start.11 = (f32[65,8,128]{2,1,0:T(8,128)S(1)}, f32[65,8,128]{2,1,0:T(8,128)S(1)}, u32[]{:S(2)}, u32[]{:S(2)}) collective-permute-start(f32[65,8,128]{2,1,0:T(8,128)S(1)} %get-tuple-element.69), channel_id=1, source_target_pairs={{0,8},{1,9},{2,10},{3,11},{4,12},{5,13},{6,14},{7,15},{8,0},{9,1},... | collective-permute-start | bytes 798728 | tf_op jit(solution)/shard_map/ppermute | solution.py:516
  88.3 4.3 %collective-permute-start.12 = (f32[16,8,128]{2,1,0:T(8,128)S(1)}, f32[16,8,128]{2,1,0:T(8,128)S(1)}, u32[]{:S(2)}, u32[]{:S(2)}) collective-permute-start(f32[16,8,128]{2,1,0:T(8,128)S(1)} %get-tuple-element.74.a_ref), channel_id=1, source_target_pairs={{0,1},{1,0},{2,3},{3,2},{4,5},{5,4},{6,7},{7,6},{8,9},{9,8},{10,11... | collective-permute-start | bytes 196616 | tf_op jit(solution)/shard_map/ppermute | solution.py:516
  92.6 5.9 %collective-permute-start.13 = (f32[16,8,128]{2,1,0:T(8,128)S(1)}, f32[16,8,128]{2,1,0:T(8,128)S(1)}, u32[]{:S(2)}, u32[]{:S(2)}) collective-permute-start(f32[16,8,128]{2,1,0:T(8,128)S(1)} %shard_map.94.refs_0_), channel_id=1, source_target_pairs={{0,2},{1,3},{2,0},{3,1},{4,6},{5,7},{6,4},{7,5},{8,10},{9,11},{10,... | collective-permute-start | bytes 196616 | tf_op jit(solution)/shard_map/ppermute | solution.py:516
  93.2 11.2 %all-to-all-start.1 = ((f32[32,1,128]{2,1,0:T(1,128)}), f32[32,1,128]{2,1,0:T(1,128)S(1)}, u32[]{:S(2)}, u32[]{:S(2)}) async-start(f32[32,1,128]{2,1,0:T(1,128)} %bitcast.6), calls=%async_computation.1 | async-start | bytes 32768 | tf_op jit(solution)/shard_map/all_to_all | solution.py:595
  105.4 6.8 %collective-permute-start.14 = (f32[16,8,128]{2,1,0:T(8,128)S(1)}, f32[16,8,128]{2,1,0:T(8,128)S(1)}, u32[]{:S(2)}, u32[]{:S(2)}) collective-permute-start(f32[16,8,128]{2,1,0:T(8,128)S(1)} %get-tuple-element.79.refs_0_), channel_id=1, source_target_pairs={{0,1},{1,2},{2,3},{3,0},{4,5},{5,6},{6,7},{7,4},{8,9},{9,10},{10,1... | collective-permute-start | bytes 196616 | tf_op jit(solution)/shard_map/ppermute | solution.py:516
  105.9 8.0 %collective-permute-start.15 = (f32[16,8,128]{2,1,0:T(8,128)S(1)}, f32[16,8,128]{2,1,0:T(8,128)S(1)}, u32[]{:S(2)}, u32[]{:S(2)}) collective-permute-start(f32[16,8,128]{2,1,0:T(8,128)S(1)} %get-tuple-element.79.refs_0_), channel_id=1, source_target_pairs={{0,2},{1,3},{2,0},{3,1},{4,6},{5,7},{6,4},{7,5},{8,10},{9,11},{10,... | collective-permute-start | bytes 196616 | tf_op jit(solution)/shard_map/ppermute | solution.py:516
  106.6 7.4 %collective-permute-start.16 = (f32[16,8,128]{2,1,0:T(8,128)S(1)}, f32[16,8,128]{2,1,0:T(8,128)S(1)}, u32[]{:S(2)}, u32[]{:S(2)}) collective-permute-start(f32[16,8,128]{2,1,0:T(8,128)S(1)} %get-tuple-element.79.refs_0_), channel_id=1, source_target_pairs={{0,3},{1,0},{2,1},{3,2},{4,7},{5,4},{6,5},{7,6},{8,11},{9,8},{10,9... | collective-permute-start | bytes 196616 | tf_op jit(solution)/shard_map/ppermute | solution.py:516

commit v5 on v4

--- a/solution.py
+++ b/solution.py
@@ -367,10 +367,15 @@
 
 
 def residual_kernel(dims, live_ref, extra_ref, power_ref, kept_ref, other_ref, mine_ref, theirs_ref,
+                    passed_ref, got_ref,
                     keep_ref, send_ref, scalar_ref):
     F, T, D, O, _, _ = dims
     W = 2 * O
-    near = (lax.axis_index("col") // 2) == 0
+    row = lax.axis_index("row")
+    col = lax.axis_index("col")
+    near = col // 2 == 0
+    away = col // 2 != row
+    held = col % 2 != row
     mask = block_mask(2 * D)
     eye = lax.broadcasted_iota(jnp.int32, (2 * D, W), 0) == (
         lax.broadcasted_iota(jnp.int32, (2 * D, W), 1) % (2 * D)
@@ -384,7 +389,9 @@
         spread = jnp.where(mask, jnp.concatenate([gram] * 8, axis=0), 0.0)
         station = []
         for i in range(8):
-            a, b = mine_ref[group * 8 + i], theirs_ref[group * 8 + i]
+            ft = group * 8 + i
+            a = mine_ref[ft]
+            b = jnp.where(away, theirs_ref[ft], jnp.where(held, got_ref[ft], passed_ref[ft]))
             first = jnp.where(near, a, b)
             second = jnp.where(near, b, a)
             station += [join_low(first, second), join_high(first, second)]
@@ -508,10 +515,10 @@
     def where(r, c, z):
         return (r * C + c) * Z + z
 
-    def permute(x, move):
+    def permute(x, move, some=lambda r, c: True):
         pairs = [
             (where(r, c, z), where(*move(r, c, z)))
-            for r in range(R) for c in range(C) for z in range(Z)
+            for r in range(R) for c in range(C) for z in range(Z) if some(r, c)
         ]
         return lax.ppermute(x, AXES, pairs)
 
@@ -567,7 +574,7 @@
                 [fit, whole, whole, text], [flux_t], [samples, live_own, u, g],
             )
         rhs_near = permute(rhs, lambda r, c, z: (r, c, z ^ 1))
-        theirs = permute(p, lambda r, c, z: (r, c ^ 2, z))
+        theirs = permute(p, lambda r, c, z: (r, c ^ 2, z), lambda r, c: r == c // 2)
         more = [] if step else [upright]
         keep, send, *found = pl.pallas_call(
             functools.partial(sum_kernel, dims),
@@ -584,12 +591,15 @@
             name="sums",
         )(far(flux_t), far(vis), live_col, *got, *more)
         power = power if step else found[0]
+        passed = permute(
+            got[0], lambda r, c, z: (r, c ^ 1, z), lambda r, c: c == 3 * r + (1 - 2 * r)
+        )
         other = permute(send, lambda r, c, z: (r, c ^ 1, z))
         (rhs,) = call(add_kernel, [fit], [], [rhs, rhs_near])
         rhs_far = permute(rhs, lambda r, c, z: (r, c, z ^ 2))
         keep, send, scalar = call(
             functools.partial(residual_kernel, dims), [line, line, array(R * C * Z, W)],
-            [], [live_half, extra, power, keep, other, p, theirs],
+            [], [live_half, extra, power, keep, other, p, theirs, passed, got[1]],
         )
         come = permute(send, lambda r, c, z: (r, c ^ 2, z))
         scalar = lax.all_to_all(scalar, AXES, 0, 0, tiled=True)

time: 115 us -> 119 us (1.035)
  starting transfers between devices: 36 us -> 43.9 us
  waiting for transfers between devices: 53.7 us -> 49.5 us
    ppermute x17 -> x19, starting transfers between devices: 29.4 us -> 37.3 us  [permute(): return lax.ppermute(x, AXES, pairs)]
    ppermute x17 -> x19, waiting for transfers between devices: 42 us -> 37.9 us  [permute(): return lax.ppermute(x, AXES, pairs)]
  transfers between devices with their start and end apart: 19 -> 21, of which waited for: 11 -> 11; matrix products, arithmetic and copies ran while one was open for 0% -> 0% of each run, Pallas kernels for 4% -> 4%
where the time goes in v5:
time: 119 us
  waiting for transfers between devices  49.5 us (42%)
  starting transfers between devices  43.9 us (37%)
  Pallas kernels  24.4 us (21%)
    ppermute x19, waiting for transfers between devices, permute(): return lax.ppermute(x, AXES, pairs)  37.9 us
    ppermute x19, starting transfers between devices, permute(): return lax.ppermute(x, AXES, pairs)  37.3 us
    pallas_call x2, Pallas kernels, shards(): pl.pallas_call(functools.partial(sum_kernel, dims), out_shape=[pair, pair...  12.1 us
    all_to_all x2, waiting for transfers between devices, shards(): scalar = lax.all_to_all(scalar, AXES, 0, 0, tiled=True)  11.7 us
    pallas_call x12, Pallas kernels, call(): pl.pallas_call(kernel, out_shape=outs, in_specs=[smem] * len(scalars) + [...  7.41 us
    all_to_all x2, starting transfers between devices, shards(): scalar = lax.all_to_all(scalar, AXES, 0, 0, tiled=True)  6.58 us
    pallas_call x1, Pallas kernels, shards(): pl.pallas_call(functools.partial(start_kernel, dims), out_shape=[whole] *...  2.54 us
  transfers between devices with their start and end apart: 21, of which 11 were waited for; matrix products, arithmetic and copies ran while one was open for 0% of the time, Pallas kernels for 4%

profile of v5, /device:TPU:0, one launch (start us, length us, event | category | flops | bytes accessed | tf_op | source)
XLA Modules:
  0.0 118.6 jit_solution(10698113313536692216)
XLA Ops:
  0.6 2.5 %start.1 = (f32[64,8,128]{2,1,0:T(8,128)S(1)}, f32[64,8,128]{2,1,0:T(8,128)S(1)}, f32[64,8,128]{2,1,0:T(8,128)S(1)}) custom-call(f32[3,4,512]{2,1,0:T(4,128)} %bitcast.16, f32[3,8]{1,0:T(4,128)} %lmn_hbm.1, f32[16,4,2,8,64]{4,3,2,1,0:T(8,128)} %gains_hbm.1), custom_call_target="tpu_custom_call" | custom-call | tf_op jit(solution)/shard_map/start/pallas_call | solution.py:534
  3.2 0.7 collective-permute-start
  3.9 5.7 %collective-permute-start.1 = (f32[64,8,128]{2,1,0:T(8,128)S(1)}, f32[64,8,128]{2,1,0:T(8,128)S(1)}, u32[]{:S(2)}, u32[]{:S(2)}) collective-permute-start(f32[64,8,128]{2,1,0:T(8,128)S(1)} %get-tuple-element.48.mine_ref), channel_id=1, source_target_pairs={{0,16},{1,17},{2,18},{3,19},{4,0},{5,1},{6,2},{7,3},{8,20},{9,21},... | collective-permute-start | bytes 786440 | tf_op jit(solution)/shard_map/ppermute | solution.py:523
  9.6 2.3 %setup.1 = (f32[64,128]{1,0:T(8,128)S(1)}, f32[64,128]{1,0:T(8,128)S(1)}, f32[64,128]{1,0:T(8,128)S(1)}, f32[256,128]{1,0:T(8,128)S(1)}, f32[64,8,128]{2,1,0:T(8...) custom-call(f32[8,16]{1,0:T(8,128)} %bitcast.10, ...), custom_call_target="tpu_custom_call" | custom-call | tf_op jit(solution)/shard_map/setup/pallas_call | solution.py:553
  11.9 7.9 %collective-permute-done.1.b_ref.got_ref = f32[64,8,128]{2,1,0:T(8,128)S(1)} collective-permute-done((f32[64,8,128]{2,1,0:T(8,128)S(1)}, f32[64,8,128]{2,1,0:T(8,128)S(1)}, u32[]{:S(2)}, u32[]{:S(2)}) %collective-permute-start.1) | collective-permute-done | bytes 262176 | tf_op jit(solution)/shard_map/ppermute | solution.py:523
  19.8 6.8 %sums.2 = (f32[72,16,128]{2,1,0:T(8,128)S(1)}, f32[72,16,128]{2,1,0:T(8,128)S(1)}, f32[1,128]{1,0:T(1,128)S(1)}) custom-call(f32[8,16]{1,0:T(8,128)} %bitcast.11, bf16[16,4,2,256,128]{4,3,2,1,0:T(8,128)(2,1)} %vis_hbm.3, f32[64,128]{1,0:T(8,128)S(1)} %get-tuple-element.47.live_ref, f32[64,8,128]{2,1,0:T(8,128)S(1)} %collective-permute-done.a_ref, ...), custom_call_target="tpu_custom_call" | custom-call | tf_op jit(solution)/shard_map/sums/pallas_call | solution.py:579
  26.6 0.0 copy-start
  26.7 0.9 collective-permute-start.2
  27.5 4.0 %collective-permute-start.3 = (f32[64,8,128]{2,1,0:T(8,128)S(1)}, f32[64,8,128]{2,1,0:T(8,128)S(1)}, u32[]{:S(2)}, u32[]{:S(2)}) collective-permute-start(f32[64,8,128]{2,1,0:T(8,128)S(1)} %get-tuple-element.48.mine_ref), channel_id=1, source_target_pairs={{0,8},{1,9},{2,10},{3,11},{4,12},{5,13},{6,14},{7,15},{24,16},{25,... | collective-permute-start | bytes 786440 | tf_op jit(solution)/shard_map/ppermute | solution.py:523
  31.6 1.3 %collective-permute-start.4 = (f32[64,8,128]{2,1,0:T(8,128)S(1)}, f32[64,8,128]{2,1,0:T(8,128)S(1)}, u32[]{:S(2)}, u32[]{:S(2)}) collective-permute-start(f32[64,8,128]{2,1,0:T(8,128)S(1)} %collective-permute-done.a_ref), channel_id=1, source_target_pairs={{4,0},{5,1},{6,2},{7,3},{24,28},{25,29},{26,30},{27,31}} | collective-permute-start | bytes 786440 | tf_op jit(solution)/shard_map/ppermute | solution.py:523
  32.9 4.9 %collective-permute-done.3.theirs_ref = f32[64,8,128]{2,1,0:T(8,128)S(1)} collective-permute-done((f32[64,8,128]{2,1,0:T(8,128)S(1)}, f32[64,8,128]{2,1,0:T(8,128)S(1)}, u32[]{:S(2)}, u32[]{:S(2)}) %collective-permute-start.3) | collective-permute-done | bytes 262176 | tf_op jit(solution)/shard_map/ppermute | solution.py:523
  37.7 1.5 %shard_map.86 = (f32[65,8,128]{2,1,0:T(8,128)S(1)}, f32[65,8,128]{2,1,0:T(8,128)S(1)}, f32[32,128]{1,0:T(8,128)}) custom-call(f32[64,128]{1,0:T(8,128)S(1)} %get-tuple-element.42.live_ref, f32[1,128]{1,0:T(1,128)S(1)} %get-tuple-element.46.extra_ref, f32[1,128]{1,0:T(1,128)S(1)} %get-tuple-element.50.power_ref, ...), custom_call_target="tpu_custom_call" | custom-call | tf_op jit(solution)/shard_map/pallas_call | solution.py:506
  39.2 2.5 %collective-permute-start.5 = (f32[65,8,128]{2,1,0:T(8,128)S(1)}, f32[65,8,128]{2,1,0:T(8,128)S(1)}, u32[]{:S(2)}, u32[]{:S(2)}) collective-permute-start(f32[65,8,128]{2,1,0:T(8,128)S(1)} %get-tuple-element.55), channel_id=1, source_target_pairs={{0,8},{1,9},{2,10},{3,11},{4,12},{5,13},{6,14},{7,15},{8,0},{9,1},... | collective-permute-start | bytes 798728 | tf_op jit(solution)/shard_map/ppermute | solution.py:523
  41.7 1.6 %collective-permute-start.6 = (f32[16,8,128]{2,1,0:T(8,128)S(1)}, f32[16,8,128]{2,1,0:T(8,128)S(1)}, u32[]{:S(2)}, u32[]{:S(2)}) collective-permute-start(f32[16,8,128]{2,1,0:T(8,128)S(1)} %get-tuple-element.61.a_ref), channel_id=1, source_target_pairs={{0,1},{1,0},{2,3},{3,2},{4,5},{5,4},{6,7},{7,6},{8,9},{9,8},{10,11... | collective-permute-start | bytes 196616 | tf_op jit(solution)/shard_map/ppermute | solution.py:523
  43.3 2.7 %collective-permute-done.6.b_ref = f32[16,8,128]{2,1,0:T(8,128)S(1)} collective-permute-done((f32[16,8,128]{2,1,0:T(8,128)S(1)}, f32[16,8,128]{2,1,0:T(8,128)S(1)}, u32[]{:S(2)}, u32[]{:S(2)}) %collective-permute-start.6) | collective-permute-done | bytes 65568 | tf_op jit(solution)/shard_map/ppermute | solution.py:523
  46.0 2.7 %collective-permute-start.7 = (f32[16,8,128]{2,1,0:T(8,128)S(1)}, f32[16,8,128]{2,1,0:T(8,128)S(1)}, u32[]{:S(2)}, u32[]{:S(2)}) collective-permute-start(f32[16,8,128]{2,1,0:T(8,128)S(1)} %shard_map.88.refs_0_), channel_id=1, source_target_pairs={{0,2},{1,3},{2,0},{3,1},{4,6},{5,7},{6,4},{7,5},{8,10},{9,11},{10,... | collective-permute-start | bytes 196616 | tf_op jit(solution)/shard_map/ppermute | solution.py:523
  48.6 2.5 %all-to-all-start = ((f32[32,1,128]{2,1,0:T(1,128)}), f32[32,1,128]{2,1,0:T(1,128)S(1)}, u32[]{:S(2)}, u32[]{:S(2)}) async-start(f32[32,1,128]{2,1,0:T(1,128)} %bitcast.3), calls=%async_computation | async-start | bytes 32768 | tf_op jit(solution)/shard_map/all_to_all | solution.py:605
  51.2 0.0 collective-permute-done.7.refs_1_
  51.2 0.1 shard_map.89.refs_3_
  51.3 0.5 shard_map.87
  51.8 6.5 %all-to-all-done = f32[32,1,128]{2,1,0:T(1,128)S(1)} async-done(((f32[32,1,128]{2,1,0:T(1,128)}), f32[32,1,128]{2,1,0:T(1,128)S(1)}, u32[]{:S(2)}, u32[]{:S(2)}) %all-to-all-start) | async-done | bytes 16416 | tf_op jit(solution)/shard_map/all_to_all | solution.py:605
  58.3 0.3 shard_map.90
  58.6 0.7 collective-permute-start.8
  59.3 3.3 %collective-permute-start.9 = (f32[64,8,128]{2,1,0:T(8,128)S(1)}, f32[64,8,128]{2,1,0:T(8,128)S(1)}, u32[]{:S(2)}, u32[]{:S(2)}) collective-permute-start(f32[64,8,128]{2,1,0:T(8,128)S(1)} %get-tuple-element.64.mine_ref), channel_id=1, source_target_pairs={{0,16},{1,17},{2,18},{3,19},{4,0},{5,1},{6,2},{7,3},{8,20},{9,21},... | collective-permute-start | bytes 786440 | tf_op jit(solution)/shard_map/ppermute | solution.py:523
  62.6 9.2 %collective-permute-done.9.b_ref.got_ref = f32[64,8,128]{2,1,0:T(8,128)S(1)} collective-permute-done((f32[64,8,128]{2,1,0:T(8,128)S(1)}, f32[64,8,128]{2,1,0:T(8,128)S(1)}, u32[]{:S(2)}, u32[]{:S(2)}) %collective-permute-start.9) | collective-permute-done | bytes 262176 | tf_op jit(solution)/shard_map/ppermute | solution.py:523
  71.9 5.3 %sums.3 = (f32[72,16,128]{2,1,0:T(8,128)S(1)}, f32[72,16,128]{2,1,0:T(8,128)S(1)}) custom-call(f32[8,16]{1,0:T(8,128)} %bitcast.12, bf16[16,4,2,256,128]{4,3,2,1,0:T(8,128)(2,1)} %vis_hbm.3, f32[64,128]{1,0:T(8,128)S(1)} %get-tuple-element.47.live_ref, f32[64,8,128]{2,1,0:T(8,128)S(1)} %collective-permute-done.8.a_ref, ...), custom_call_target="tpu_custom_call" | custom-call | tf_op jit(solution)/shard_map/sums/pallas_call | solution.py:579
  77.2 1.6 %collective-permute-start.10 = (f32[72,16,128]{2,1,0:T(8,128)S(1)}, f32[72,16,128]{2,1,0:T(8,128)S(1)}, u32[]{:S(2)}, u32[]{:S(2)}) collective-permute-start(f32[72,16,128]{2,1,0:T(8,128)S(1)} %get-tuple-element.66), channel_id=1, source_target_pairs={{0,4},{1,5},{2,6},{3,7},{4,0},{5,1},{6,2},{7,3},{8,12},{9,13},{10,... | collective-permute-start | bytes 1769480 | tf_op jit(solution)/shard_map/ppermute | solution.py:523
  78.8 3.6 %collective-permute-start.11 = (f32[64,8,128]{2,1,0:T(8,128)S(1)}, f32[64,8,128]{2,1,0:T(8,128)S(1)}, u32[]{:S(2)}, u32[]{:S(2)}) collective-permute-start(f32[64,8,128]{2,1,0:T(8,128)S(1)} %get-tuple-element.64.mine_ref), channel_id=1, source_target_pairs={{0,8},{1,9},{2,10},{3,11},{4,12},{5,13},{6,14},{7,15},{24,16},{25,... | collective-permute-start | bytes 786440 | tf_op jit(solution)/shard_map/ppermute | solution.py:523
  82.4 1.3 %collective-permute-start.12 = (f32[64,8,128]{2,1,0:T(8,128)S(1)}, f32[64,8,128]{2,1,0:T(8,128)S(1)}, u32[]{:S(2)}, u32[]{:S(2)}) collective-permute-start(f32[64,8,128]{2,1,0:T(8,128)S(1)} %collective-permute-done.8.a_ref), channel_id=1, source_target_pairs={{4,0},{5,1},{6,2},{7,3},{24,28},{25,29},{26,30},{27,31}} | collective-permute-start | bytes 786440 | tf_op jit(solution)/shard_map/ppermute | solution.py:523
  83.7 0.9 shard_map.91
  84.6 3.5 %collective-permute-done.11.theirs_ref = f32[64,8,128]{2,1,0:T(8,128)S(1)} collective-permute-done((f32[64,8,128]{2,1,0:T(8,128)S(1)}, f32[64,8,128]{2,1,0:T(8,128)S(1)}, u32[]{:S(2)}, u32[]{:S(2)}) %collective-permute-start.11) | collective-permute-done | bytes 262176 | tf_op jit(solution)/shard_map/ppermute | solution.py:523
  88.1 1.5 %shard_map.92 = (f32[65,8,128]{2,1,0:T(8,128)S(1)}, f32[65,8,128]{2,1,0:T(8,128)S(1)}, f32[32,128]{1,0:T(8,128)}) custom-call(f32[64,128]{1,0:T(8,128)S(1)} %get-tuple-element.42.live_ref, f32[1,128]{1,0:T(1,128)S(1)} %get-tuple-element.63.extra_ref, f32[1,128]{1,0:T(1,128)S(1)} %get-tuple-element.50.power_ref, ...), custom_call_target="tpu_custom_call" | custom-call | tf_op jit(solution)/shard_map/pallas_call | solution.py:506
  89.6 2.5 %collective-permute-start.13 = (f32[65,8,128]{2,1,0:T(8,128)S(1)}, f32[65,8,128]{2,1,0:T(8,128)S(1)}, u32[]{:S(2)}, u32[]{:S(2)}) collective-permute-start(f32[65,8,128]{2,1,0:T(8,128)S(1)} %get-tuple-element.69), channel_id=1, source_target_pairs={{0,8},{1,9},{2,10},{3,11},{4,12},{5,13},{6,14},{7,15},{8,0},{9,1},... | collective-permute-start | bytes 798728 | tf_op jit(solution)/shard_map/ppermute | solution.py:523
  92.1 0.6 collective-permute-start.14
  92.7 3.7 %collective-permute-done.14.b_ref = f32[16,8,128]{2,1,0:T(8,128)S(1)} collective-permute-done((f32[16,8,128]{2,1,0:T(8,128)S(1)}, f32[16,8,128]{2,1,0:T(8,128)S(1)}, u32[]{:S(2)}, u32[]{:S(2)}) %collective-permute-start.14) | collective-permute-done | bytes 65568 | tf_op jit(solution)/shard_map/ppermute | solution.py:523
  96.3 0.6 collective-permute-start.15
  96.9 4.0 %all-to-all-start.1 = ((f32[32,1,128]{2,1,0:T(1,128)}), f32[32,1,128]{2,1,0:T(1,128)S(1)}, u32[]{:S(2)}, u32[]{:S(2)}) async-start(f32[32,1,128]{2,1,0:T(1,128)} %bitcast.6), calls=%async_computation.1 | async-start | bytes 32768 | tf_op jit(solution)/shard_map/all_to_all | solution.py:605
  101.0 1.3 %collective-permute-done.15.refs_1_ = f32[16,8,128]{2,1,0:T(8,128)S(1)} collective-permute-done((f32[16,8,128]{2,1,0:T(8,128)S(1)}, f32[16,8,128]{2,1,0:T(8,128)S(1)}, u32[]{:S(2)}, u32[]{:S(2)}) %collective-permute-start.15) | collective-permute-done | bytes 65568 | tf_op jit(solution)/shard_map/ppermute | solution.py:523
  102.3 0.1 shard_map.95
  102.4 0.5 shard_map.93
  102.9 5.2 %all-to-all-done.1 = f32[32,1,128]{2,1,0:T(1,128)S(1)} async-done(((f32[32,1,128]{2,1,0:T(1,128)}), f32[32,1,128]{2,1,0:T(1,128)S(1)}, u32[]{:S(2)}, u32[]{:S(2)}) %all-to-all-start.1) | async-done | bytes 16416 | tf_op jit(solution)/shard_map/all_to_all | solution.py:605
  108.1 1.1 shard_map.96
  109.2 0.5 collective-permute-start.16
  109.7 0.6 collective-permute-start.17
  110.3 2.7 %collective-permute-start.18 = (f32[16,8,128]{2,1,0:T(8,128)S(1)}, f32[16,8,128]{2,1,0:T(8,128)S(1)}, u32[]{:S(2)}, u32[]{:S(2)}) collective-permute-start(f32[16,8,128]{2,1,0:T(8,128)S(1)} %get-tuple-element.79.refs_0_), channel_id=1, source_target_pairs={{0,3},{1,0},{2,1},{3,2},{4,7},{5,4},{6,5},{7,6},{8,11},{9,8},{10,9... | collective-permute-start | bytes 196616 | tf_op jit(solution)/shard_map/ppermute | solution.py:523
  113.0 2.9 %collective-permute-done.16.refs_1_ = f32[16,8,128]{2,1,0:T(8,128)S(1)} collective-permute-done((f32[16,8,128]{2,1,0:T(8,128)S(1)}, f32[16,8,128]{2,1,0:T(8,128)S(1)}, u32[]{:S(2)}, u32[]{:S(2)}) %collective-permute-start.16) | collective-permute-done | bytes 65568 | tf_op jit(solution)/shard_map/ppermute | solution.py:523
  116.0 1.7 %collective-permute-done.17.refs_2_ = f32[16,8,128]{2,1,0:T(8,128)S(1)} collective-permute-done((f32[16,8,128]{2,1,0:T(8,128)S(1)}, f32[16,8,128]{2,1,0:T(8,128)S(1)}, u32[]{:S(2)}, u32[]{:S(2)}) %collective-permute-start.17) | collective-permute-done | bytes 65568 | tf_op jit(solution)/shard_map/ppermute | solution.py:523
  117.7 1.0 shard_map.97
  (12 shorter events, 0.0 us)
Async XLA Ops:
  3.2 8.7 %collective-permute-start = (f32[64,8,128]{2,1,0:T(8,128)S(1)}, f32[64,8,128]{2,1,0:T(8,128)S(1)}, u32[]{:S(2)}, u32[]{:S(2)}) collective-permute-start(f32[64,8,128]{2,1,0:T(8,128)S(1)} %get-tuple-element.48.mine_ref), channel_id=1, source_target_pairs={{0,0},{1,1},{2,2},{3,3},{4,16},{5,17},{6,18},{7,19},{8,4},{9,5},{1... | collective-permute-start | bytes 786440 | tf_op jit(solution)/shard_map/ppermute | solution.py:523
  3.9 16.0 %collective-permute-start.1 = (f32[64,8,128]{2,1,0:T(8,128)S(1)}, f32[64,8,128]{2,1,0:T(8,128)S(1)}, u32[]{:S(2)}, u32[]{:S(2)}) collective-permute-start(f32[64,8,128]{2,1,0:T(8,128)S(1)} %get-tuple-element.48.mine_ref), channel_id=1, source_target_pairs={{0,16},{1,17},{2,18},{3,19},{4,0},{5,1},{6,2},{7,3},{8,20},{9,21},... | collective-permute-start | bytes 786440 | tf_op jit(solution)/shard_map/ppermute | solution.py:523
  26.6 57.0 %copy-start = (f32[16,8]{0,1:T(8,128)S(1)}, f32[16,8]{0,1:T(8,128)}, u32[]{:S(2)}) copy-start(f32[16,8]{0,1:T(8,128)} %param.11) | copy-start | bytes 1540
  26.7 11.1 %collective-permute-start.2 = (f32[72,16,128]{2,1,0:T(8,128)S(1)}, f32[72,16,128]{2,1,0:T(8,128)S(1)}, u32[]{:S(2)}, u32[]{:S(2)}) collective-permute-start(f32[72,16,128]{2,1,0:T(8,128)S(1)} %get-tuple-element.52), channel_id=1, source_target_pairs={{0,4},{1,5},{2,6},{3,7},{4,0},{5,1},{6,2},{7,3},{8,12},{9,13},{10,... | collective-permute-start | bytes 1769480 | tf_op jit(solution)/shard_map/ppermute | solution.py:523
  27.5 10.2 %collective-permute-start.3 = (f32[64,8,128]{2,1,0:T(8,128)S(1)}, f32[64,8,128]{2,1,0:T(8,128)S(1)}, u32[]{:S(2)}, u32[]{:S(2)}) collective-permute-start(f32[64,8,128]{2,1,0:T(8,128)S(1)} %get-tuple-element.48.mine_ref), channel_id=1, source_target_pairs={{0,8},{1,9},{2,10},{3,11},{4,12},{5,13},{6,14},{7,15},{24,16},{25,... | collective-permute-start | bytes 786440 | tf_op jit(solution)/shard_map/ppermute | solution.py:523
  31.6 6.2 %collective-permute-start.4 = (f32[64,8,128]{2,1,0:T(8,128)S(1)}, f32[64,8,128]{2,1,0:T(8,128)S(1)}, u32[]{:S(2)}, u32[]{:S(2)}) collective-permute-start(f32[64,8,128]{2,1,0:T(8,128)S(1)} %collective-permute-done.a_ref), channel_id=1, source_target_pairs={{4,0},{5,1},{6,2},{7,3},{24,28},{25,29},{26,30},{27,31}} | collective-permute-start | bytes 786440 | tf_op jit(solution)/shard_map/ppermute | solution.py:523
  39.2 12.1 %collective-permute-start.5 = (f32[65,8,128]{2,1,0:T(8,128)S(1)}, f32[65,8,128]{2,1,0:T(8,128)S(1)}, u32[]{:S(2)}, u32[]{:S(2)}) collective-permute-start(f32[65,8,128]{2,1,0:T(8,128)S(1)} %get-tuple-element.55), channel_id=1, source_target_pairs={{0,8},{1,9},{2,10},{3,11},{4,12},{5,13},{6,14},{7,15},{8,0},{9,1},... | collective-permute-start | bytes 798728 | tf_op jit(solution)/shard_map/ppermute | solution.py:523
  41.7 4.3 %collective-permute-start.6 = (f32[16,8,128]{2,1,0:T(8,128)S(1)}, f32[16,8,128]{2,1,0:T(8,128)S(1)}, u32[]{:S(2)}, u32[]{:S(2)}) collective-permute-start(f32[16,8,128]{2,1,0:T(8,128)S(1)} %get-tuple-element.61.a_ref), channel_id=1, source_target_pairs={{0,1},{1,0},{2,3},{3,2},{4,5},{5,4},{6,7},{7,6},{8,9},{9,8},{10,11... | collective-permute-start | bytes 196616 | tf_op jit(solution)/shard_map/ppermute | solution.py:523
  46.0 5.2 %collective-permute-start.7 = (f32[16,8,128]{2,1,0:T(8,128)S(1)}, f32[16,8,128]{2,1,0:T(8,128)S(1)}, u32[]{:S(2)}, u32[]{:S(2)}) collective-permute-start(f32[16,8,128]{2,1,0:T(8,128)S(1)} %shard_map.88.refs_0_), channel_id=1, source_target_pairs={{0,2},{1,3},{2,0},{3,1},{4,6},{5,7},{6,4},{7,5},{8,10},{9,11},{10,... | collective-permute-start | bytes 196616 | tf_op jit(solution)/shard_map/ppermute | solution.py:523
  48.6 9.7 %all-to-all-start = ((f32[32,1,128]{2,1,0:T(1,128)}), f32[32,1,128]{2,1,0:T(1,128)S(1)}, u32[]{:S(2)}, u32[]{:S(2)}) async-start(f32[32,1,128]{2,1,0:T(1,128)} %bitcast.3), calls=%async_computation | async-start | bytes 32768 | tf_op jit(solution)/shard_map/all_to_all | solution.py:605
  58.6 4.0 %collective-permute-start.8 = (f32[64,8,128]{2,1,0:T(8,128)S(1)}, f32[64,8,128]{2,1,0:T(8,128)S(1)}, u32[]{:S(2)}, u32[]{:S(2)}) collective-permute-start(f32[64,8,128]{2,1,0:T(8,128)S(1)} %get-tuple-element.64.mine_ref), channel_id=1, source_target_pairs={{0,0},{1,1},{2,2},{3,3},{4,16},{5,17},{6,18},{7,19},{8,4},{9,5},{1... | collective-permute-start | bytes 786440 | tf_op jit(solution)/shard_map/ppermute | solution.py:523
  59.3 12.6 %collective-permute-start.9 = (f32[64,8,128]{2,1,0:T(8,128)S(1)}, f32[64,8,128]{2,1,0:T(8,128)S(1)}, u32[]{:S(2)}, u32[]{:S(2)}) collective-permute-start(f32[64,8,128]{2,1,0:T(8,128)S(1)} %get-tuple-element.64.mine_ref), channel_id=1, source_target_pairs={{0,16},{1,17},{2,18},{3,19},{4,0},{5,1},{6,2},{7,3},{8,20},{9,21},... | collective-permute-start | bytes 786440 | tf_op jit(solution)/shard_map/ppermute | solution.py:523
  77.2 10.9 %collective-permute-start.10 = (f32[72,16,128]{2,1,0:T(8,128)S(1)}, f32[72,16,128]{2,1,0:T(8,128)S(1)}, u32[]{:S(2)}, u32[]{:S(2)}) collective-permute-start(f32[72,16,128]{2,1,0:T(8,128)S(1)} %get-tuple-element.66), channel_id=1, source_target_pairs={{0,4},{1,5},{2,6},{3,7},{4,0},{5,1},{6,2},{7,3},{8,12},{9,13},{10,... | collective-permute-start | bytes 1769480 | tf_op jit(solution)/shard_map/ppermute | solution.py:523
  78.8 9.3 %collective-permute-start.11 = (f32[64,8,128]{2,1,0:T(8,128)S(1)}, f32[64,8,128]{2,1,0:T(8,128)S(1)}, u32[]{:S(2)}, u32[]{:S(2)}) collective-permute-start(f32[64,8,128]{2,1,0:T(8,128)S(1)} %get-tuple-element.64.mine_ref), channel_id=1, source_target_pairs={{0,8},{1,9},{2,10},{3,11},{4,12},{5,13},{6,14},{7,15},{24,16},{25,... | collective-permute-start | bytes 786440 | tf_op jit(solution)/shard_map/ppermute | solution.py:523
  82.4 5.7 %collective-permute-start.12 = (f32[64,8,128]{2,1,0:T(8,128)S(1)}, f32[64,8,128]{2,1,0:T(8,128)S(1)}, u32[]{:S(2)}, u32[]{:S(2)}) collective-permute-start(f32[64,8,128]{2,1,0:T(8,128)S(1)} %collective-permute-done.8.a_ref), channel_id=1, source_target_pairs={{4,0},{5,1},{6,2},{7,3},{24,28},{25,29},{26,30},{27,31}} | collective-permute-start | bytes 786440 | tf_op jit(solution)/shard_map/ppermute | solution.py:523
  89.6 12.8 %collective-permute-start.13 = (f32[65,8,128]{2,1,0:T(8,128)S(1)}, f32[65,8,128]{2,1,0:T(8,128)S(1)}, u32[]{:S(2)}, u32[]{:S(2)}) collective-permute-start(f32[65,8,128]{2,1,0:T(8,128)S(1)} %get-tuple-element.69), channel_id=1, source_target_pairs={{0,8},{1,9},{2,10},{3,11},{4,12},{5,13},{6,14},{7,15},{8,0},{9,1},... | collective-permute-start | bytes 798728 | tf_op jit(solution)/shard_map/ppermute | solution.py:523
  92.1 4.3 %collective-permute-start.14 = (f32[16,8,128]{2,1,0:T(8,128)S(1)}, f32[16,8,128]{2,1,0:T(8,128)S(1)}, u32[]{:S(2)}, u32[]{:S(2)}) collective-permute-start(f32[16,8,128]{2,1,0:T(8,128)S(1)} %get-tuple-element.74.a_ref), channel_id=1, source_target_pairs={{0,1},{1,0},{2,3},{3,2},{4,5},{5,4},{6,7},{7,6},{8,9},{9,8},{10,11... | collective-permute-start | bytes 196616 | tf_op jit(solution)/shard_map/ppermute | solution.py:523
  96.3 5.9 %collective-permute-start.15 = (f32[16,8,128]{2,1,0:T(8,128)S(1)}, f32[16,8,128]{2,1,0:T(8,128)S(1)}, u32[]{:S(2)}, u32[]{:S(2)}) collective-permute-start(f32[16,8,128]{2,1,0:T(8,128)S(1)} %shard_map.94.refs_0_), channel_id=1, source_target_pairs={{0,2},{1,3},{2,0},{3,1},{4,6},{5,7},{6,4},{7,5},{8,10},{9,11},{10,... | collective-permute-start | bytes 196616 | tf_op jit(solution)/shard_map/ppermute | solution.py:523
  96.9 11.2 %all-to-all-start.1 = ((f32[32,1,128]{2,1,0:T(1,128)}), f32[32,1,128]{2,1,0:T(1,128)S(1)}, u32[]{:S(2)}, u32[]{:S(2)}) async-start(f32[32,1,128]{2,1,0:T(1,128)} %bitcast.6), calls=%async_computation.1 | async-start | bytes 32768 | tf_op jit(solution)/shard_map/all_to_all | solution.py:605
  109.2 6.8 %collective-permute-start.16 = (f32[16,8,128]{2,1,0:T(8,128)S(1)}, f32[16,8,128]{2,1,0:T(8,128)S(1)}, u32[]{:S(2)}, u32[]{:S(2)}) collective-permute-start(f32[16,8,128]{2,1,0:T(8,128)S(1)} %get-tuple-element.79.refs_0_), channel_id=1, source_target_pairs={{0,1},{1,2},{2,3},{3,0},{4,5},{5,6},{6,7},{7,4},{8,9},{9,10},{10,1... | collective-permute-start | bytes 196616 | tf_op jit(solution)/shard_map/ppermute | solution.py:523
  109.7 8.0 %collective-permute-start.17 = (f32[16,8,128]{2,1,0:T(8,128)S(1)}, f32[16,8,128]{2,1,0:T(8,128)S(1)}, u32[]{:S(2)}, u32[]{:S(2)}) collective-permute-start(f32[16,8,128]{2,1,0:T(8,128)S(1)} %get-tuple-element.79.refs_0_), channel_id=1, source_target_pairs={{0,2},{1,3},{2,0},{3,1},{4,6},{5,7},{6,4},{7,5},{8,10},{9,11},{10,... | collective-permute-start | bytes 196616 | tf_op jit(solution)/shard_map/ppermute | solution.py:523
  110.3 7.4 %collective-permute-start.18 = (f32[16,8,128]{2,1,0:T(8,128)S(1)}, f32[16,8,128]{2,1,0:T(8,128)S(1)}, u32[]{:S(2)}, u32[]{:S(2)}) collective-permute-start(f32[16,8,128]{2,1,0:T(8,128)S(1)} %get-tuple-element.79.refs_0_), channel_id=1, source_target_pairs={{0,3},{1,0},{2,1},{3,2},{4,7},{5,4},{6,5},{7,6},{8,11},{9,8},{10,9... | collective-permute-start | bytes 196616 | tf_op jit(solution)/shard_map/ppermute | solution.py:523

commit v6 on v5

--- a/solution.py
+++ b/solution.py
@@ -344,23 +344,33 @@
         return power
 
     def chunk(c, power):
-        for i in range(CHUNK):
-            vis_copy(c * CHUNK + i).wait()
-
-        @pl.when(c * CHUNK + ahead < F)
-        def _():
+        first = isinstance(c, int)
+        if not first:
+            for i in range(CHUNK):
+                vis_copy(c * CHUNK + i).wait()
+
+        def more():
             for i in range(CHUNK):
                 vis_copy(c * CHUNK + ahead + i).start()
+
+        if not first:
+            pl.when(c * CHUNK + ahead < F)(more)
 
         upright = None
         if upright_ref is not None:
             upright = pltpu.roll(upright_ref[...], (2 * O - c * CHUNK * T) % (2 * O), 1)
         for j in range(CHUNK // group):
+            if first:
+                for i in range(group):
+                    vis_copy(j * group + i).wait()
             power = body(c * (CHUNK // group) + j, upright, j * 8, power)
+        if first and ahead < F:
+            more()
         return power
 
     flux_copy.wait()
-    power = lax.fori_loop(0, F // CHUNK, chunk, jnp.zeros((8, cols), jnp.float32))
+    power = chunk(0, jnp.zeros((8, cols), jnp.float32))
+    power = lax.fori_loop(1, F // CHUNK, chunk, power)
     if power_ref is not None:
         power = jnp.sum(power, axis=0, keepdims=True)
         power_ref[...] = jnp.where(low_lanes(power.shape), power + swap(power), 0.0)
@@ -456,8 +466,7 @@
             g = 0.5 * (g_ref[ft] + fresh)
             if last:
                 out_ref, total_ref, rhs_ref = refs[6:]
-                out_ref[f, t, 0] = g[:, :O]
-                out_ref[f, t, 1] = g[:, O:]
+                out_ref[ft] = g
                 total = other_ref[ft] + g
                 total_ref[ft] = total
                 x = place(dims, f)
@@ -473,15 +482,32 @@
                 rhs_ref[k * T + t] = acc[k]
 
 
+def write_out(dims, value, out_hbm, out_ref, sems):
+    F, T, _, O, _, _ = dims
+    copies = []
+    for part in range(F // CHUNK):
+        for f in range(part * CHUNK, (part + 1) * CHUNK):
+            for t in range(T):
+                x = value(f, t)
+                out_ref[f, t, 0] = x[:, :O]
+                out_ref[f, t, 1] = x[:, O:]
+        at = pl.ds(part * CHUNK, CHUNK)
+        copies.append(pltpu.make_async_copy(out_ref.at[at], out_hbm.at[at], sems.at[part]))
+        copies[-1].start()
+    for copy in copies:
+        copy.wait()
+
+
+def emit_kernel(dims, g_ref, out_hbm, out_ref, sems):
+    write_out(dims, lambda f, t: g_ref[f * dims[1] + t], out_hbm, out_ref, sems)
+
+
 def final_kernel(dims, total_ref, *refs):
-    F, T, _, O, _, _ = dims
-    rhs_refs, out_ref = refs[:-1], refs[-1]
-    for t in range(T):
-        coeffs = solve(dims, rhs_refs, t)
-        for f in range(F):
-            dual = total_ref[f * T + t] - curve(coeffs, place(dims, f))
-            out_ref[f, t, 0] = dual[:, :O]
-            out_ref[f, t, 1] = dual[:, O:]
+    T = dims[1]
+    coeffs = [solve(dims, refs[:-3], t) for t in range(T)]
+    write_out(
+        dims, lambda f, t: total_ref[f * T + t] - curve(coeffs[t], place(dims, f)), *refs[-3:]
+    )
 
 
 def shards(sizes, vis, flags, positions, lmn, flux, gains, duals):
@@ -614,16 +640,26 @@
         update = functools.partial(update_kernel, dims, last, float(full))
         arrays = [scalar, num, den, target[0], g]
         if last:
-            gain, total, rhs = call(
-                update, [array(*gains.shape), whole, fit], [],
+            g, total, rhs = call(
+                update, [whole, whole, fit], [],
                 arrays + [target[1]],
             )
         else:
             g, p = call(update, [whole, whole], [], arrays + [rot])
-    (dual,) = call(
-        functools.partial(final_kernel, dims), [array(*gains.shape)], [],
-        [total, *bands(rhs)],
-    )
+
+    def write(kernel, arrays):
+        return pl.pallas_call(
+            functools.partial(kernel, dims),
+            out_shape=array(*gains.shape),
+            in_specs=[vmem] * len(arrays),
+            out_specs=hbm,
+            scratch_shapes=[pltpu.VMEM(gains.shape, f32), pltpu.SemaphoreType.DMA((F // CHUNK,))],
+            compiler_params=LIMIT,
+        )(*arrays)
+
+    rhs_all = bands(rhs)
+    gain = write(emit_kernel, [g])
+    dual = write(final_kernel, [total, *rhs_all])
     return (gain, dual)
 
 

time: 119 us -> 118 us (level)
    pallas_call x0 -> x2, Pallas kernels: none -> 1.84 us  [write(): pl.pallas_call(functools.partial(kernel, dims), out_shape=array(*gains.sh...]
    pallas_call x12 -> x11, Pallas kernels: 7.41 us -> 5.59 us  [call(): pl.pallas_call(kernel, out_shape=outs, in_specs=[smem] * len(scalars) + [...]
  transfers between devices with their start and end apart: 21 -> 21, of which waited for: 11 -> 11; matrix products, arithmetic and copies ran while one was open for 0% -> 0% of each run, Pallas kernels for 4% -> 5%
where the time goes in v6:
time: 118 us
  waiting for transfers between devices  48.6 us (41%)
  starting transfers between devices  43.9 us (37%)
  Pallas kernels  24.3 us (21%)
    ppermute x19, starting transfers between devices, permute(): return lax.ppermute(x, AXES, pairs)  37.3 us
    ppermute x19, waiting for transfers between devices, permute(): return lax.ppermute(x, AXES, pairs)  36.9 us
    pallas_call x2, Pallas kernels, shards(): pl.pallas_call(functools.partial(sum_kernel, dims), out_shape=[pair, pair...  12 us
    all_to_all x2, waiting for transfers between devices, shards(): scalar = lax.all_to_all(scalar, AXES, 0, 0, tiled=True)  11.7 us
    all_to_all x2, starting transfers between devices, shards(): scalar = lax.all_to_all(scalar, AXES, 0, 0, tiled=True)  6.59 us
    pallas_call x11, Pallas kernels, call(): pl.pallas_call(kernel, out_shape=outs, in_specs=[smem] * len(scalars) + [...  5.59 us
    pallas_call x1, Pallas kernels, shards(): pl.pallas_call(functools.partial(start_kernel, dims), out_shape=[whole] *...  2.54 us
  transfers between devices with their start and end apart: 21, of which 11 were waited for; matrix products, arithmetic and copies ran while one was open for 0% of the time, Pallas kernels for 5%

profile of v6, /device:TPU:0, one launch (start us, length us, event | category | flops | bytes accessed | tf_op | source)
XLA Modules:
  0.0 117.8 jit_solution(5400489257575399540)
XLA Ops:
  0.6 2.5 %start.1 = (f32[64,8,128]{2,1,0:T(8,128)S(1)}, f32[64,8,128]{2,1,0:T(8,128)S(1)}, f32[64,8,128]{2,1,0:T(8,128)S(1)}) custom-call(f32[3,4,512]{2,1,0:T(4,128)} %bitcast.16, f32[3,8]{1,0:T(4,128)} %lmn_hbm.1, f32[16,4,2,8,64]{4,3,2,1,0:T(8,128)} %gains_hbm.1), custom_call_target="tpu_custom_call" | custom-call | tf_op jit(solution)/shard_map/start/pallas_call | solution.py:560
  3.2 0.7 collective-permute-start
  3.9 5.7 %collective-permute-start.1 = (f32[64,8,128]{2,1,0:T(8,128)S(1)}, f32[64,8,128]{2,1,0:T(8,128)S(1)}, u32[]{:S(2)}, u32[]{:S(2)}) collective-permute-start(f32[64,8,128]{2,1,0:T(8,128)S(1)} %get-tuple-element.48.mine_ref), channel_id=1, source_target_pairs={{0,16},{1,17},{2,18},{3,19},{4,0},{5,1},{6,2},{7,3},{8,20},{9,21},... | collective-permute-start | bytes 786440 | tf_op jit(solution)/shard_map/ppermute | solution.py:549
  9.6 2.3 %setup.1 = (f32[64,128]{1,0:T(8,128)S(1)}, f32[64,128]{1,0:T(8,128)S(1)}, f32[64,128]{1,0:T(8,128)S(1)}, f32[256,128]{1,0:T(8,128)S(1)}, f32[64,8,128]{2,1,0:T(8...) custom-call(f32[8,16]{1,0:T(8,128)} %bitcast.10, ...), custom_call_target="tpu_custom_call" | custom-call | tf_op jit(solution)/shard_map/setup/pallas_call | solution.py:579
  11.9 7.9 %collective-permute-done.1.b_ref.got_ref = f32[64,8,128]{2,1,0:T(8,128)S(1)} collective-permute-done((f32[64,8,128]{2,1,0:T(8,128)S(1)}, f32[64,8,128]{2,1,0:T(8,128)S(1)}, u32[]{:S(2)}, u32[]{:S(2)}) %collective-permute-start.1) | collective-permute-done | bytes 262176 | tf_op jit(solution)/shard_map/ppermute | solution.py:549
  19.8 6.4 %sums.2 = (f32[72,16,128]{2,1,0:T(8,128)S(1)}, f32[72,16,128]{2,1,0:T(8,128)S(1)}, f32[1,128]{1,0:T(1,128)S(1)}) custom-call(f32[8,16]{1,0:T(8,128)} %bitcast.11, bf16[16,4,2,256,128]{4,3,2,1,0:T(8,128)(2,1)} %vis_hbm.3, f32[64,128]{1,0:T(8,128)S(1)} %get-tuple-element.47.live_ref, f32[64,8,128]{2,1,0:T(8,128)S(1)} %collective-permute-done.a_ref, ...), custom_call_target="tpu_custom_call" | custom-call | tf_op jit(solution)/shard_map/sums/pallas_call | solution.py:605
  26.3 0.9 collective-permute-start.2
  27.2 4.0 %collective-permute-start.3 = (f32[64,8,128]{2,1,0:T(8,128)S(1)}, f32[64,8,128]{2,1,0:T(8,128)S(1)}, u32[]{:S(2)}, u32[]{:S(2)}) collective-permute-start(f32[64,8,128]{2,1,0:T(8,128)S(1)} %get-tuple-element.48.mine_ref), channel_id=1, source_target_pairs={{0,8},{1,9},{2,10},{3,11},{4,12},{5,13},{6,14},{7,15},{24,16},{25,... | collective-permute-start | bytes 786440 | tf_op jit(solution)/shard_map/ppermute | solution.py:549
  31.2 1.3 %collective-permute-start.4 = (f32[64,8,128]{2,1,0:T(8,128)S(1)}, f32[64,8,128]{2,1,0:T(8,128)S(1)}, u32[]{:S(2)}, u32[]{:S(2)}) collective-permute-start(f32[64,8,128]{2,1,0:T(8,128)S(1)} %collective-permute-done.a_ref), channel_id=1, source_target_pairs={{4,0},{5,1},{6,2},{7,3},{24,28},{25,29},{26,30},{27,31}} | collective-permute-start | bytes 786440 | tf_op jit(solution)/shard_map/ppermute | solution.py:549
  32.5 4.9 %collective-permute-done.3.theirs_ref = f32[64,8,128]{2,1,0:T(8,128)S(1)} collective-permute-done((f32[64,8,128]{2,1,0:T(8,128)S(1)}, f32[64,8,128]{2,1,0:T(8,128)S(1)}, u32[]{:S(2)}, u32[]{:S(2)}) %collective-permute-start.3) | collective-permute-done | bytes 262176 | tf_op jit(solution)/shard_map/ppermute | solution.py:549
  37.4 1.5 %shard_map.86 = (f32[65,8,128]{2,1,0:T(8,128)S(1)}, f32[65,8,128]{2,1,0:T(8,128)S(1)}, f32[32,128]{1,0:T(8,128)}) custom-call(f32[64,128]{1,0:T(8,128)S(1)} %get-tuple-element.42.live_ref, f32[1,128]{1,0:T(1,128)S(1)} %get-tuple-element.46.extra_ref, f32[1,128]{1,0:T(1,128)S(1)} %get-tuple-element.50.power_ref, ...), custom_call_target="tpu_custom_call" | custom-call | tf_op jit(solution)/shard_map/pallas_call | solution.py:532
  38.8 2.5 %collective-permute-start.5 = (f32[65,8,128]{2,1,0:T(8,128)S(1)}, f32[65,8,128]{2,1,0:T(8,128)S(1)}, u32[]{:S(2)}, u32[]{:S(2)}) collective-permute-start(f32[65,8,128]{2,1,0:T(8,128)S(1)} %get-tuple-element.55), channel_id=1, source_target_pairs={{0,8},{1,9},{2,10},{3,11},{4,12},{5,13},{6,14},{7,15},{8,0},{9,1},... | collective-permute-start | bytes 798728 | tf_op jit(solution)/shard_map/ppermute | solution.py:549
  41.3 1.6 %collective-permute-start.6 = (f32[16,8,128]{2,1,0:T(8,128)S(1)}, f32[16,8,128]{2,1,0:T(8,128)S(1)}, u32[]{:S(2)}, u32[]{:S(2)}) collective-permute-start(f32[16,8,128]{2,1,0:T(8,128)S(1)} %get-tuple-element.61.a_ref), channel_id=1, source_target_pairs={{0,1},{1,0},{2,3},{3,2},{4,5},{5,4},{6,7},{7,6},{8,9},{9,8},{10,11... | collective-permute-start | bytes 196616 | tf_op jit(solution)/shard_map/ppermute | solution.py:549
  42.9 2.7 %collective-permute-done.6.b_ref = f32[16,8,128]{2,1,0:T(8,128)S(1)} collective-permute-done((f32[16,8,128]{2,1,0:T(8,128)S(1)}, f32[16,8,128]{2,1,0:T(8,128)S(1)}, u32[]{:S(2)}, u32[]{:S(2)}) %collective-permute-start.6) | collective-permute-done | bytes 65568 | tf_op jit(solution)/shard_map/ppermute | solution.py:549
  45.6 2.7 %collective-permute-start.7 = (f32[16,8,128]{2,1,0:T(8,128)S(1)}, f32[16,8,128]{2,1,0:T(8,128)S(1)}, u32[]{:S(2)}, u32[]{:S(2)}) collective-permute-start(f32[16,8,128]{2,1,0:T(8,128)S(1)} %shard_map.88.refs_0_), channel_id=1, source_target_pairs={{0,2},{1,3},{2,0},{3,1},{4,6},{5,7},{6,4},{7,5},{8,10},{9,11},{10,... | collective-permute-start | bytes 196616 | tf_op jit(solution)/shard_map/ppermute | solution.py:549
  48.3 2.5 %all-to-all-start = ((f32[32,1,128]{2,1,0:T(1,128)}), f32[32,1,128]{2,1,0:T(1,128)S(1)}, u32[]{:S(2)}, u32[]{:S(2)}) async-start(f32[32,1,128]{2,1,0:T(1,128)} %bitcast.3), calls=%async_computation | async-start | bytes 32768 | tf_op jit(solution)/shard_map/all_to_all | solution.py:631
  50.8 0.0 collective-permute-done.7.refs_1_
  50.8 0.1 shard_map.89.refs_3_
  50.9 0.5 shard_map.87
  51.4 6.5 %all-to-all-done = f32[32,1,128]{2,1,0:T(1,128)S(1)} async-done(((f32[32,1,128]{2,1,0:T(1,128)}), f32[32,1,128]{2,1,0:T(1,128)S(1)}, u32[]{:S(2)}, u32[]{:S(2)}) %all-to-all-start) | async-done | bytes 16416 | tf_op jit(solution)/shard_map/all_to_all | solution.py:631
  57.9 0.3 shard_map.90
  58.3 0.7 collective-permute-start.8
  58.9 3.3 %collective-permute-start.9 = (f32[64,8,128]{2,1,0:T(8,128)S(1)}, f32[64,8,128]{2,1,0:T(8,128)S(1)}, u32[]{:S(2)}, u32[]{:S(2)}) collective-permute-start(f32[64,8,128]{2,1,0:T(8,128)S(1)} %get-tuple-element.64.mine_ref), channel_id=1, source_target_pairs={{0,16},{1,17},{2,18},{3,19},{4,0},{5,1},{6,2},{7,3},{8,20},{9,21},... | collective-permute-start | bytes 786440 | tf_op jit(solution)/shard_map/ppermute | solution.py:549
  62.3 9.2 %collective-permute-done.9.b_ref.got_ref = f32[64,8,128]{2,1,0:T(8,128)S(1)} collective-permute-done((f32[64,8,128]{2,1,0:T(8,128)S(1)}, f32[64,8,128]{2,1,0:T(8,128)S(1)}, u32[]{:S(2)}, u32[]{:S(2)}) %collective-permute-start.9) | collective-permute-done | bytes 262176 | tf_op jit(solution)/shard_map/ppermute | solution.py:549
  71.5 5.6 %sums.3 = (f32[72,16,128]{2,1,0:T(8,128)S(1)}, f32[72,16,128]{2,1,0:T(8,128)S(1)}) custom-call(f32[8,16]{1,0:T(8,128)} %bitcast.12, bf16[16,4,2,256,128]{4,3,2,1,0:T(8,128)(2,1)} %vis_hbm.3, f32[64,128]{1,0:T(8,128)S(1)} %get-tuple-element.47.live_ref, f32[64,8,128]{2,1,0:T(8,128)S(1)} %collective-permute-done.8.a_ref, ...), custom_call_target="tpu_custom_call" | custom-call | tf_op jit(solution)/shard_map/sums/pallas_call | solution.py:605
  77.1 1.6 %collective-permute-start.10 = (f32[72,16,128]{2,1,0:T(8,128)S(1)}, f32[72,16,128]{2,1,0:T(8,128)S(1)}, u32[]{:S(2)}, u32[]{:S(2)}) collective-permute-start(f32[72,16,128]{2,1,0:T(8,128)S(1)} %get-tuple-element.66), channel_id=1, source_target_pairs={{0,4},{1,5},{2,6},{3,7},{4,0},{5,1},{6,2},{7,3},{8,12},{9,13},{10,... | collective-permute-start | bytes 1769480 | tf_op jit(solution)/shard_map/ppermute | solution.py:549
  78.7 3.6 %collective-permute-start.11 = (f32[64,8,128]{2,1,0:T(8,128)S(1)}, f32[64,8,128]{2,1,0:T(8,128)S(1)}, u32[]{:S(2)}, u32[]{:S(2)}) collective-permute-start(f32[64,8,128]{2,1,0:T(8,128)S(1)} %get-tuple-element.64.mine_ref), channel_id=1, source_target_pairs={{0,8},{1,9},{2,10},{3,11},{4,12},{5,13},{6,14},{7,15},{24,16},{25,... | collective-permute-start | bytes 786440 | tf_op jit(solution)/shard_map/ppermute | solution.py:549
  82.3 1.3 %collective-permute-start.12 = (f32[64,8,128]{2,1,0:T(8,128)S(1)}, f32[64,8,128]{2,1,0:T(8,128)S(1)}, u32[]{:S(2)}, u32[]{:S(2)}) collective-permute-start(f32[64,8,128]{2,1,0:T(8,128)S(1)} %collective-permute-done.8.a_ref), channel_id=1, source_target_pairs={{4,0},{5,1},{6,2},{7,3},{24,28},{25,29},{26,30},{27,31}} | collective-permute-start | bytes 786440 | tf_op jit(solution)/shard_map/ppermute | solution.py:549
  83.6 0.9 shard_map.91
  84.5 3.5 %collective-permute-done.11.theirs_ref = f32[64,8,128]{2,1,0:T(8,128)S(1)} collective-permute-done((f32[64,8,128]{2,1,0:T(8,128)S(1)}, f32[64,8,128]{2,1,0:T(8,128)S(1)}, u32[]{:S(2)}, u32[]{:S(2)}) %collective-permute-start.11) | collective-permute-done | bytes 262176 | tf_op jit(solution)/shard_map/ppermute | solution.py:549
  88.0 1.5 %shard_map.92 = (f32[65,8,128]{2,1,0:T(8,128)S(1)}, f32[65,8,128]{2,1,0:T(8,128)S(1)}, f32[32,128]{1,0:T(8,128)}) custom-call(f32[64,128]{1,0:T(8,128)S(1)} %get-tuple-element.42.live_ref, f32[1,128]{1,0:T(1,128)S(1)} %get-tuple-element.63.extra_ref, f32[1,128]{1,0:T(1,128)S(1)} %get-tuple-element.50.power_ref, ...), custom_call_target="tpu_custom_call" | custom-call | tf_op jit(solution)/shard_map/pallas_call | solution.py:532
  89.5 2.5 %collective-permute-start.13 = (f32[65,8,128]{2,1,0:T(8,128)S(1)}, f32[65,8,128]{2,1,0:T(8,128)S(1)}, u32[]{:S(2)}, u32[]{:S(2)}) collective-permute-start(f32[65,8,128]{2,1,0:T(8,128)S(1)} %get-tuple-element.69), channel_id=1, source_target_pairs={{0,8},{1,9},{2,10},{3,11},{4,12},{5,13},{6,14},{7,15},{8,0},{9,1},... | collective-permute-start | bytes 798728 | tf_op jit(solution)/shard_map/ppermute | solution.py:549
  92.0 0.6 collective-permute-start.14
  92.6 3.6 %collective-permute-done.14.b_ref = f32[16,8,128]{2,1,0:T(8,128)S(1)} collective-permute-done((f32[16,8,128]{2,1,0:T(8,128)S(1)}, f32[16,8,128]{2,1,0:T(8,128)S(1)}, u32[]{:S(2)}, u32[]{:S(2)}) %collective-permute-start.14) | collective-permute-done | bytes 65568 | tf_op jit(solution)/shard_map/ppermute | solution.py:549
  96.3 0.6 collective-permute-start.15
  96.9 4.0 %all-to-all-start.1 = ((f32[32,1,128]{2,1,0:T(1,128)}), f32[32,1,128]{2,1,0:T(1,128)S(1)}, u32[]{:S(2)}, u32[]{:S(2)}) async-start(f32[32,1,128]{2,1,0:T(1,128)} %bitcast.6), calls=%async_computation.1 | async-start | bytes 32768 | tf_op jit(solution)/shard_map/all_to_all | solution.py:631
  100.9 1.3 %collective-permute-done.15.refs_1_ = f32[16,8,128]{2,1,0:T(8,128)S(1)} collective-permute-done((f32[16,8,128]{2,1,0:T(8,128)S(1)}, f32[16,8,128]{2,1,0:T(8,128)S(1)}, u32[]{:S(2)}, u32[]{:S(2)}) %collective-permute-start.15) | collective-permute-done | bytes 65568 | tf_op jit(solution)/shard_map/ppermute | solution.py:549
  102.2 0.1 shard_map.95
  102.3 0.5 shard_map.93
  102.8 5.2 %all-to-all-done.1 = f32[32,1,128]{2,1,0:T(1,128)S(1)} async-done(((f32[32,1,128]{2,1,0:T(1,128)}), f32[32,1,128]{2,1,0:T(1,128)S(1)}, u32[]{:S(2)}, u32[]{:S(2)}) %all-to-all-start.1) | async-done | bytes 16416 | tf_op jit(solution)/shard_map/all_to_all | solution.py:631
  108.0 0.2 shard_map.96
  108.3 0.5 collective-permute-start.16
  108.8 0.6 collective-permute-start.17
  109.5 2.7 %collective-permute-start.18 = (f32[16,8,128]{2,1,0:T(8,128)S(1)}, f32[16,8,128]{2,1,0:T(8,128)S(1)}, u32[]{:S(2)}, u32[]{:S(2)}) collective-permute-start(f32[16,8,128]{2,1,0:T(8,128)S(1)} %get-tuple-element.79.refs_0_), channel_id=1, source_target_pairs={{0,3},{1,0},{2,1},{3,2},{4,7},{5,4},{6,5},{7,6},{8,11},{9,8},{10,9... | collective-permute-start | bytes 196616 | tf_op jit(solution)/shard_map/ppermute | solution.py:549
  112.2 0.9 shard_map.97
  113.1 2.0 %collective-permute-done.16.refs_1_ = f32[16,8,128]{2,1,0:T(8,128)S(1)} collective-permute-done((f32[16,8,128]{2,1,0:T(8,128)S(1)}, f32[16,8,128]{2,1,0:T(8,128)S(1)}, u32[]{:S(2)}, u32[]{:S(2)}) %collective-permute-start.16) | collective-permute-done | bytes 65568 | tf_op jit(solution)/shard_map/ppermute | solution.py:549
  115.1 1.7 %collective-permute-done.17.refs_2_ = f32[16,8,128]{2,1,0:T(8,128)S(1)} collective-permute-done((f32[16,8,128]{2,1,0:T(8,128)S(1)}, f32[16,8,128]{2,1,0:T(8,128)S(1)}, u32[]{:S(2)}, u32[]{:S(2)}) %collective-permute-start.17) | collective-permute-done | bytes 65568 | tf_op jit(solution)/shard_map/ppermute | solution.py:549
  116.8 0.9 shard_map.98
  (13 shorter events, 0.0 us)
Async XLA Ops:
  3.2 8.7 %collective-permute-start = (f32[64,8,128]{2,1,0:T(8,128)S(1)}, f32[64,8,128]{2,1,0:T(8,128)S(1)}, u32[]{:S(2)}, u32[]{:S(2)}) collective-permute-start(f32[64,8,128]{2,1,0:T(8,128)S(1)} %get-tuple-element.48.mine_ref), channel_id=1, source_target_pairs={{0,0},{1,1},{2,2},{3,3},{4,16},{5,17},{6,18},{7,19},{8,4},{9,5},{1... | collective-permute-start | bytes 786440 | tf_op jit(solution)/shard_map/ppermute | solution.py:549
  3.9 16.0 %collective-permute-start.1 = (f32[64,8,128]{2,1,0:T(8,128)S(1)}, f32[64,8,128]{2,1,0:T(8,128)S(1)}, u32[]{:S(2)}, u32[]{:S(2)}) collective-permute-start(f32[64,8,128]{2,1,0:T(8,128)S(1)} %get-tuple-element.48.mine_ref), channel_id=1, source_target_pairs={{0,16},{1,17},{2,18},{3,19},{4,0},{5,1},{6,2},{7,3},{8,20},{9,21},... | collective-permute-start | bytes 786440 | tf_op jit(solution)/shard_map/ppermute | solution.py:549
  26.3 57.3 %copy-start = (f32[16,8]{0,1:T(8,128)S(1)}, f32[16,8]{0,1:T(8,128)}, u32[]{:S(2)}) copy-start(f32[16,8]{0,1:T(8,128)} %param.11) | copy-start | bytes 1540
  26.3 11.1 %collective-permute-start.2 = (f32[72,16,128]{2,1,0:T(8,128)S(1)}, f32[72,16,128]{2,1,0:T(8,128)S(1)}, u32[]{:S(2)}, u32[]{:S(2)}) collective-permute-start(f32[72,16,128]{2,1,0:T(8,128)S(1)} %get-tuple-element.52), channel_id=1, source_target_pairs={{0,4},{1,5},{2,6},{3,7},{4,0},{5,1},{6,2},{7,3},{8,12},{9,13},{10,... | collective-permute-start | bytes 1769480 | tf_op jit(solution)/shard_map/ppermute | solution.py:549
  27.2 10.2 %collective-permute-start.3 = (f32[64,8,128]{2,1,0:T(8,128)S(1)}, f32[64,8,128]{2,1,0:T(8,128)S(1)}, u32[]{:S(2)}, u32[]{:S(2)}) collective-permute-start(f32[64,8,128]{2,1,0:T(8,128)S(1)} %get-tuple-element.48.mine_ref), channel_id=1, source_target_pairs={{0,8},{1,9},{2,10},{3,11},{4,12},{5,13},{6,14},{7,15},{24,16},{25,... | collective-permute-start | bytes 786440 | tf_op jit(solution)/shard_map/ppermute | solution.py:549
  31.2 6.2 %collective-permute-start.4 = (f32[64,8,128]{2,1,0:T(8,128)S(1)}, f32[64,8,128]{2,1,0:T(8,128)S(1)}, u32[]{:S(2)}, u32[]{:S(2)}) collective-permute-start(f32[64,8,128]{2,1,0:T(8,128)S(1)} %collective-permute-done.a_ref), channel_id=1, source_target_pairs={{4,0},{5,1},{6,2},{7,3},{24,28},{25,29},{26,30},{27,31}} | collective-permute-start | bytes 786440 | tf_op jit(solution)/shard_map/ppermute | solution.py:549
  38.8 12.1 %collective-permute-start.5 = (f32[65,8,128]{2,1,0:T(8,128)S(1)}, f32[65,8,128]{2,1,0:T(8,128)S(1)}, u32[]{:S(2)}, u32[]{:S(2)}) collective-permute-start(f32[65,8,128]{2,1,0:T(8,128)S(1)} %get-tuple-element.55), channel_id=1, source_target_pairs={{0,8},{1,9},{2,10},{3,11},{4,12},{5,13},{6,14},{7,15},{8,0},{9,1},... | collective-permute-start | bytes 798728 | tf_op jit(solution)/shard_map/ppermute | solution.py:549
  41.3 4.3 %collective-permute-start.6 = (f32[16,8,128]{2,1,0:T(8,128)S(1)}, f32[16,8,128]{2,1,0:T(8,128)S(1)}, u32[]{:S(2)}, u32[]{:S(2)}) collective-permute-start(f32[16,8,128]{2,1,0:T(8,128)S(1)} %get-tuple-element.61.a_ref), channel_id=1, source_target_pairs={{0,1},{1,0},{2,3},{3,2},{4,5},{5,4},{6,7},{7,6},{8,9},{9,8},{10,11... | collective-permute-start | bytes 196616 | tf_op jit(solution)/shard_map/ppermute | solution.py:549
  45.6 5.2 %collective-permute-start.7 = (f32[16,8,128]{2,1,0:T(8,128)S(1)}, f32[16,8,128]{2,1,0:T(8,128)S(1)}, u32[]{:S(2)}, u32[]{:S(2)}) collective-permute-start(f32[16,8,128]{2,1,0:T(8,128)S(1)} %shard_map.88.refs_0_), channel_id=1, source_target_pairs={{0,2},{1,3},{2,0},{3,1},{4,6},{5,7},{6,4},{7,5},{8,10},{9,11},{10,... | collective-permute-start | bytes 196616 | tf_op jit(solution)/shard_map/ppermute | solution.py:549
  48.3 9.7 %all-to-all-start = ((f32[32,1,128]{2,1,0:T(1,128)}), f32[32,1,128]{2,1,0:T(1,128)S(1)}, u32[]{:S(2)}, u32[]{:S(2)}) async-start(f32[32,1,128]{2,1,0:T(1,128)} %bitcast.3), calls=%async_computation | async-start | bytes 32768 | tf_op jit(solution)/shard_map/all_to_all | solution.py:631
  58.3 4.0 %collective-permute-start.8 = (f32[64,8,128]{2,1,0:T(8,128)S(1)}, f32[64,8,128]{2,1,0:T(8,128)S(1)}, u32[]{:S(2)}, u32[]{:S(2)}) collective-permute-start(f32[64,8,128]{2,1,0:T(8,128)S(1)} %get-tuple-element.64.mine_ref), channel_id=1, source_target_pairs={{0,0},{1,1},{2,2},{3,3},{4,16},{5,17},{6,18},{7,19},{8,4},{9,5},{1... | collective-permute-start | bytes 786440 | tf_op jit(solution)/shard_map/ppermute | solution.py:549
  58.9 12.6 %collective-permute-start.9 = (f32[64,8,128]{2,1,0:T(8,128)S(1)}, f32[64,8,128]{2,1,0:T(8,128)S(1)}, u32[]{:S(2)}, u32[]{:S(2)}) collective-permute-start(f32[64,8,128]{2,1,0:T(8,128)S(1)} %get-tuple-element.64.mine_ref), channel_id=1, source_target_pairs={{0,16},{1,17},{2,18},{3,19},{4,0},{5,1},{6,2},{7,3},{8,20},{9,21},... | collective-permute-start | bytes 786440 | tf_op jit(solution)/shard_map/ppermute | solution.py:549
  77.1 10.9 %collective-permute-start.10 = (f32[72,16,128]{2,1,0:T(8,128)S(1)}, f32[72,16,128]{2,1,0:T(8,128)S(1)}, u32[]{:S(2)}, u32[]{:S(2)}) collective-permute-start(f32[72,16,128]{2,1,0:T(8,128)S(1)} %get-tuple-element.66), channel_id=1, source_target_pairs={{0,4},{1,5},{2,6},{3,7},{4,0},{5,1},{6,2},{7,3},{8,12},{9,13},{10,... | collective-permute-start | bytes 1769480 | tf_op jit(solution)/shard_map/ppermute | solution.py:549
  78.7 9.3 %collective-permute-start.11 = (f32[64,8,128]{2,1,0:T(8,128)S(1)}, f32[64,8,128]{2,1,0:T(8,128)S(1)}, u32[]{:S(2)}, u32[]{:S(2)}) collective-permute-start(f32[64,8,128]{2,1,0:T(8,128)S(1)} %get-tuple-element.64.mine_ref), channel_id=1, source_target_pairs={{0,8},{1,9},{2,10},{3,11},{4,12},{5,13},{6,14},{7,15},{24,16},{25,... | collective-permute-start | bytes 786440 | tf_op jit(solution)/shard_map/ppermute | solution.py:549
  82.3 5.7 %collective-permute-start.12 = (f32[64,8,128]{2,1,0:T(8,128)S(1)}, f32[64,8,128]{2,1,0:T(8,128)S(1)}, u32[]{:S(2)}, u32[]{:S(2)}) collective-permute-start(f32[64,8,128]{2,1,0:T(8,128)S(1)} %collective-permute-done.8.a_ref), channel_id=1, source_target_pairs={{4,0},{5,1},{6,2},{7,3},{24,28},{25,29},{26,30},{27,31}} | collective-permute-start | bytes 786440 | tf_op jit(solution)/shard_map/ppermute | solution.py:549
  89.5 12.8 %collective-permute-start.13 = (f32[65,8,128]{2,1,0:T(8,128)S(1)}, f32[65,8,128]{2,1,0:T(8,128)S(1)}, u32[]{:S(2)}, u32[]{:S(2)}) collective-permute-start(f32[65,8,128]{2,1,0:T(8,128)S(1)} %get-tuple-element.69), channel_id=1, source_target_pairs={{0,8},{1,9},{2,10},{3,11},{4,12},{5,13},{6,14},{7,15},{8,0},{9,1},... | collective-permute-start | bytes 798728 | tf_op jit(solution)/shard_map/ppermute | solution.py:549
  92.0 4.3 %collective-permute-start.14 = (f32[16,8,128]{2,1,0:T(8,128)S(1)}, f32[16,8,128]{2,1,0:T(8,128)S(1)}, u32[]{:S(2)}, u32[]{:S(2)}) collective-permute-start(f32[16,8,128]{2,1,0:T(8,128)S(1)} %get-tuple-element.74.a_ref), channel_id=1, source_target_pairs={{0,1},{1,0},{2,3},{3,2},{4,5},{5,4},{6,7},{7,6},{8,9},{9,8},{10,11... | collective-permute-start | bytes 196616 | tf_op jit(solution)/shard_map/ppermute | solution.py:549
  96.3 5.9 %collective-permute-start.15 = (f32[16,8,128]{2,1,0:T(8,128)S(1)}, f32[16,8,128]{2,1,0:T(8,128)S(1)}, u32[]{:S(2)}, u32[]{:S(2)}) collective-permute-start(f32[16,8,128]{2,1,0:T(8,128)S(1)} %shard_map.94.refs_0_), channel_id=1, source_target_pairs={{0,2},{1,3},{2,0},{3,1},{4,6},{5,7},{6,4},{7,5},{8,10},{9,11},{10,... | collective-permute-start | bytes 196616 | tf_op jit(solution)/shard_map/ppermute | solution.py:549
  96.9 11.2 %all-to-all-start.1 = ((f32[32,1,128]{2,1,0:T(1,128)}), f32[32,1,128]{2,1,0:T(1,128)S(1)}, u32[]{:S(2)}, u32[]{:S(2)}) async-start(f32[32,1,128]{2,1,0:T(1,128)} %bitcast.6), calls=%async_computation.1 | async-start | bytes 32768 | tf_op jit(solution)/shard_map/all_to_all | solution.py:631
  108.3 6.8 %collective-permute-start.16 = (f32[16,8,128]{2,1,0:T(8,128)S(1)}, f32[16,8,128]{2,1,0:T(8,128)S(1)}, u32[]{:S(2)}, u32[]{:S(2)}) collective-permute-start(f32[16,8,128]{2,1,0:T(8,128)S(1)} %get-tuple-element.79.refs_0_), channel_id=1, source_target_pairs={{0,1},{1,2},{2,3},{3,0},{4,5},{5,6},{6,7},{7,4},{8,9},{9,10},{10,1... | collective-permute-start | bytes 196616 | tf_op jit(solution)/shard_map/ppermute | solution.py:549
  108.8 8.0 %collective-permute-start.17 = (f32[16,8,128]{2,1,0:T(8,128)S(1)}, f32[16,8,128]{2,1,0:T(8,128)S(1)}, u32[]{:S(2)}, u32[]{:S(2)}) collective-permute-start(f32[16,8,128]{2,1,0:T(8,128)S(1)} %get-tuple-element.79.refs_0_), channel_id=1, source_target_pairs={{0,2},{1,3},{2,0},{3,1},{4,6},{5,7},{6,4},{7,5},{8,10},{9,11},{10,... | collective-permute-start | bytes 196616 | tf_op jit(solution)/shard_map/ppermute | solution.py:549
  109.5 7.4 %collective-permute-start.18 = (f32[16,8,128]{2,1,0:T(8,128)S(1)}, f32[16,8,128]{2,1,0:T(8,128)S(1)}, u32[]{:S(2)}, u32[]{:S(2)}) collective-permute-start(f32[16,8,128]{2,1,0:T(8,128)S(1)} %get-tuple-element.79.refs_0_), channel_id=1, source_target_pairs={{0,3},{1,0},{2,1},{3,2},{4,7},{5,4},{6,5},{7,6},{8,11},{9,8},{10,9... | collective-permute-start | bytes 196616 | tf_op jit(solution)/shard_map/ppermute | solution.py:549

commit v7 on v6

--- a/solution.py
+++ b/solution.py
@@ -369,8 +369,11 @@
         return power
 
     flux_copy.wait()
-    power = chunk(0, jnp.zeros((8, cols), jnp.float32))
-    power = lax.fori_loop(1, F // CHUNK, chunk, power)
+    power = jnp.zeros((8, cols), jnp.float32)
+    peeled = 1 if power_ref is not None else 0
+    if peeled:
+        power = chunk(0, power)
+    power = lax.fori_loop(peeled, F // CHUNK, chunk, power)
     if power_ref is not None:
         power = jnp.sum(power, axis=0, keepdims=True)
         power_ref[...] = jnp.where(low_lanes(power.shape), power + swap(power), 0.0)
@@ -552,7 +555,7 @@
         return permute(x, lambda r, c, z: (((r * C + c) % R + m) % R, (r * C + c) // R, z))
 
     def bands(x):
-        return [x] + [permute(x, lambda r, c, z, k=k: (r, c, (z + k) % Z)) for k in range(1, Z)]
+        return [x] + [permute(x, lambda r, c, z, k=k: (r, c, z ^ k)) for k in range(1, Z)]
 
     whole, line, fit = array(FT, D, W), array(FT + 1, D, W), array(4 * T, D, W)
     pair, text = array(FT // 8 * 9, 2 * D, W), array(1, W)

time: 118 us -> 118 us (level)
  transfers between devices with their start and end apart: 21 -> 21, of which waited for: 11 -> 10; matrix products, arithmetic and copies ran while one was open for 0% -> 0% of each run, Pallas kernels for 5% -> 5%
where the time goes in v7:
time: 118 us
  waiting for transfers between devices  48.1 us (41%)
  starting transfers between devices  44.5 us (38%)
  Pallas kernels  24 us (20%)
    ppermute x19, starting transfers between devices, permute(): return lax.ppermute(x, AXES, pairs)  37.9 us
    ppermute x19, waiting for transfers between devices, permute(): return lax.ppermute(x, AXES, pairs)  36.4 us
    pallas_call x2, Pallas kernels, shards(): pl.pallas_call(functools.partial(sum_kernel, dims), out_shape=[pair, pair...  11.7 us
    all_to_all x2, waiting for transfers between devices, shards(): scalar = lax.all_to_all(scalar, AXES, 0, 0, tiled=True)  11.7 us
    all_to_all x2, starting transfers between devices, shards(): scalar = lax.all_to_all(scalar, AXES, 0, 0, tiled=True)  6.59 us
    pallas_call x11, Pallas kernels, call(): pl.pallas_call(kernel, out_shape=outs, in_specs=[smem] * len(scalars) + [...  5.59 us
    pallas_call x1, Pallas kernels, shards(): pl.pallas_call(functools.partial(start_kernel, dims), out_shape=[whole] *...  2.54 us
  transfers between devices with their start and end apart: 21, of which 10 were waited for; matrix products, arithmetic and copies ran while one was open for 0% of the time, Pallas kernels for 5%

profile of v7, /device:TPU:0, one launch (start us, length us, event | category | flops | bytes accessed | tf_op | source)
XLA Modules:
  0.0 117.5 jit_solution(18360376490023537031)
XLA Ops:
  0.6 2.5 %start.1 = (f32[64,8,128]{2,1,0:T(8,128)S(1)}, f32[64,8,128]{2,1,0:T(8,128)S(1)}, f32[64,8,128]{2,1,0:T(8,128)S(1)}) custom-call(f32[3,4,512]{2,1,0:T(4,128)} %bitcast.16, f32[3,8]{1,0:T(4,128)} %lmn_hbm.1, f32[16,4,2,8,64]{4,3,2,1,0:T(8,128)} %gains_hbm.1), custom_call_target="tpu_custom_call" | custom-call | tf_op jit(solution)/shard_map/start/pallas_call | solution.py:563
  3.2 0.7 collective-permute-start
  3.9 5.7 %collective-permute-start.1 = (f32[64,8,128]{2,1,0:T(8,128)S(1)}, f32[64,8,128]{2,1,0:T(8,128)S(1)}, u32[]{:S(2)}, u32[]{:S(2)}) collective-permute-start(f32[64,8,128]{2,1,0:T(8,128)S(1)} %get-tuple-element.48.mine_ref), channel_id=1, source_target_pairs={{0,16},{1,17},{2,18},{3,19},{4,0},{5,1},{6,2},{7,3},{8,20},{9,21},... | collective-permute-start | bytes 786440 | tf_op jit(solution)/shard_map/ppermute | solution.py:552
  9.6 2.3 %setup.1 = (f32[64,128]{1,0:T(8,128)S(1)}, f32[64,128]{1,0:T(8,128)S(1)}, f32[64,128]{1,0:T(8,128)S(1)}, f32[256,128]{1,0:T(8,128)S(1)}, f32[64,8,128]{2,1,0:T(8...) custom-call(f32[8,16]{1,0:T(8,128)} %bitcast.10, ...), custom_call_target="tpu_custom_call" | custom-call | tf_op jit(solution)/shard_map/setup/pallas_call | solution.py:582
  11.9 7.9 %collective-permute-done.1.b_ref.got_ref = f32[64,8,128]{2,1,0:T(8,128)S(1)} collective-permute-done((f32[64,8,128]{2,1,0:T(8,128)S(1)}, f32[64,8,128]{2,1,0:T(8,128)S(1)}, u32[]{:S(2)}, u32[]{:S(2)}) %collective-permute-start.1) | collective-permute-done | bytes 262176 | tf_op jit(solution)/shard_map/ppermute | solution.py:552
  19.8 6.4 %sums.2 = (f32[72,16,128]{2,1,0:T(8,128)S(1)}, f32[72,16,128]{2,1,0:T(8,128)S(1)}, f32[1,128]{1,0:T(1,128)S(1)}) custom-call(f32[8,16]{1,0:T(8,128)} %bitcast.11, bf16[16,4,2,256,128]{4,3,2,1,0:T(8,128)(2,1)} %vis_hbm.3, f32[64,128]{1,0:T(8,128)S(1)} %get-tuple-element.47.live_ref, f32[64,8,128]{2,1,0:T(8,128)S(1)} %collective-permute-done.a_ref, ...), custom_call_target="tpu_custom_call" | custom-call | tf_op jit(solution)/shard_map/sums/pallas_call | solution.py:608
  26.3 0.0 copy-start
  26.3 0.9 collective-permute-start.2
  27.2 4.0 %collective-permute-start.3 = (f32[64,8,128]{2,1,0:T(8,128)S(1)}, f32[64,8,128]{2,1,0:T(8,128)S(1)}, u32[]{:S(2)}, u32[]{:S(2)}) collective-permute-start(f32[64,8,128]{2,1,0:T(8,128)S(1)} %get-tuple-element.48.mine_ref), channel_id=1, source_target_pairs={{0,8},{1,9},{2,10},{3,11},{4,12},{5,13},{6,14},{7,15},{24,16},{25,... | collective-permute-start | bytes 786440 | tf_op jit(solution)/shard_map/ppermute | solution.py:552
  31.2 1.3 %collective-permute-start.4 = (f32[64,8,128]{2,1,0:T(8,128)S(1)}, f32[64,8,128]{2,1,0:T(8,128)S(1)}, u32[]{:S(2)}, u32[]{:S(2)}) collective-permute-start(f32[64,8,128]{2,1,0:T(8,128)S(1)} %collective-permute-done.a_ref), channel_id=1, source_target_pairs={{4,0},{5,1},{6,2},{7,3},{24,28},{25,29},{26,30},{27,31}} | collective-permute-start | bytes 786440 | tf_op jit(solution)/shard_map/ppermute | solution.py:552
  32.5 4.9 %collective-permute-done.3.theirs_ref = f32[64,8,128]{2,1,0:T(8,128)S(1)} collective-permute-done((f32[64,8,128]{2,1,0:T(8,128)S(1)}, f32[64,8,128]{2,1,0:T(8,128)S(1)}, u32[]{:S(2)}, u32[]{:S(2)}) %collective-permute-start.3) | collective-permute-done | bytes 262176 | tf_op jit(solution)/shard_map/ppermute | solution.py:552
  37.4 1.5 %shard_map.86 = (f32[65,8,128]{2,1,0:T(8,128)S(1)}, f32[65,8,128]{2,1,0:T(8,128)S(1)}, f32[32,128]{1,0:T(8,128)}) custom-call(f32[64,128]{1,0:T(8,128)S(1)} %get-tuple-element.42.live_ref, f32[1,128]{1,0:T(1,128)S(1)} %get-tuple-element.46.extra_ref, f32[1,128]{1,0:T(1,128)S(1)} %get-tuple-element.50.power_ref, ...), custom_call_target="tpu_custom_call" | custom-call | tf_op jit(solution)/shard_map/pallas_call | solution.py:535
  38.8 2.5 %collective-permute-start.5 = (f32[65,8,128]{2,1,0:T(8,128)S(1)}, f32[65,8,128]{2,1,0:T(8,128)S(1)}, u32[]{:S(2)}, u32[]{:S(2)}) collective-permute-start(f32[65,8,128]{2,1,0:T(8,128)S(1)} %get-tuple-element.55), channel_id=1, source_target_pairs={{0,8},{1,9},{2,10},{3,11},{4,12},{5,13},{6,14},{7,15},{8,0},{9,1},... | collective-permute-start | bytes 798728 | tf_op jit(solution)/shard_map/ppermute | solution.py:552
  41.3 1.6 %collective-permute-start.6 = (f32[16,8,128]{2,1,0:T(8,128)S(1)}, f32[16,8,128]{2,1,0:T(8,128)S(1)}, u32[]{:S(2)}, u32[]{:S(2)}) collective-permute-start(f32[16,8,128]{2,1,0:T(8,128)S(1)} %get-tuple-element.61.a_ref), channel_id=1, source_target_pairs={{0,1},{1,0},{2,3},{3,2},{4,5},{5,4},{6,7},{7,6},{8,9},{9,8},{10,11... | collective-permute-start | bytes 196616 | tf_op jit(solution)/shard_map/ppermute | solution.py:552
  42.9 2.7 %collective-permute-done.6.b_ref = f32[16,8,128]{2,1,0:T(8,128)S(1)} collective-permute-done((f32[16,8,128]{2,1,0:T(8,128)S(1)}, f32[16,8,128]{2,1,0:T(8,128)S(1)}, u32[]{:S(2)}, u32[]{:S(2)}) %collective-permute-start.6) | collective-permute-done | bytes 65568 | tf_op jit(solution)/shard_map/ppermute | solution.py:552
  45.6 2.7 %collective-permute-start.7 = (f32[16,8,128]{2,1,0:T(8,128)S(1)}, f32[16,8,128]{2,1,0:T(8,128)S(1)}, u32[]{:S(2)}, u32[]{:S(2)}) collective-permute-start(f32[16,8,128]{2,1,0:T(8,128)S(1)} %shard_map.88.refs_0_), channel_id=1, source_target_pairs={{0,2},{1,3},{2,0},{3,1},{4,6},{5,7},{6,4},{7,5},{8,10},{9,11},{10,... | collective-permute-start | bytes 196616 | tf_op jit(solution)/shard_map/ppermute | solution.py:552
  48.3 2.5 %all-to-all-start = ((f32[32,1,128]{2,1,0:T(1,128)}), f32[32,1,128]{2,1,0:T(1,128)S(1)}, u32[]{:S(2)}, u32[]{:S(2)}) async-start(f32[32,1,128]{2,1,0:T(1,128)} %bitcast.3), calls=%async_computation | async-start | bytes 32768 | tf_op jit(solution)/shard_map/all_to_all | solution.py:634
  50.8 0.0 collective-permute-done.7.refs_1_
  50.8 0.1 shard_map.89.refs_3_
  50.9 0.5 shard_map.87
  51.4 6.5 %all-to-all-done = f32[32,1,128]{2,1,0:T(1,128)S(1)} async-done(((f32[32,1,128]{2,1,0:T(1,128)}), f32[32,1,128]{2,1,0:T(1,128)S(1)}, u32[]{:S(2)}, u32[]{:S(2)}) %all-to-all-start) | async-done | bytes 16416 | tf_op jit(solution)/shard_map/all_to_all | solution.py:634
  57.9 0.3 shard_map.90
  58.3 0.7 collective-permute-start.8
  58.9 3.3 %collective-permute-start.9 = (f32[64,8,128]{2,1,0:T(8,128)S(1)}, f32[64,8,128]{2,1,0:T(8,128)S(1)}, u32[]{:S(2)}, u32[]{:S(2)}) collective-permute-start(f32[64,8,128]{2,1,0:T(8,128)S(1)} %get-tuple-element.64.mine_ref), channel_id=1, source_target_pairs={{0,16},{1,17},{2,18},{3,19},{4,0},{5,1},{6,2},{7,3},{8,20},{9,21},... | collective-permute-start | bytes 786440 | tf_op jit(solution)/shard_map/ppermute | solution.py:552
  62.3 9.2 %collective-permute-done.9.b_ref.got_ref = f32[64,8,128]{2,1,0:T(8,128)S(1)} collective-permute-done((f32[64,8,128]{2,1,0:T(8,128)S(1)}, f32[64,8,128]{2,1,0:T(8,128)S(1)}, u32[]{:S(2)}, u32[]{:S(2)}) %collective-permute-start.9) | collective-permute-done | bytes 262176 | tf_op jit(solution)/shard_map/ppermute | solution.py:552
  71.5 5.3 %sums.3 = (f32[72,16,128]{2,1,0:T(8,128)S(1)}, f32[72,16,128]{2,1,0:T(8,128)S(1)}) custom-call(f32[8,16]{1,0:T(8,128)} %bitcast.12, bf16[16,4,2,256,128]{4,3,2,1,0:T(8,128)(2,1)} %vis_hbm.3, f32[64,128]{1,0:T(8,128)S(1)} %get-tuple-element.47.live_ref, f32[64,8,128]{2,1,0:T(8,128)S(1)} %collective-permute-done.8.a_ref, ...), custom_call_target="tpu_custom_call" | custom-call | tf_op jit(solution)/shard_map/sums/pallas_call | solution.py:608
  76.8 1.6 %collective-permute-start.10 = (f32[72,16,128]{2,1,0:T(8,128)S(1)}, f32[72,16,128]{2,1,0:T(8,128)S(1)}, u32[]{:S(2)}, u32[]{:S(2)}) collective-permute-start(f32[72,16,128]{2,1,0:T(8,128)S(1)} %get-tuple-element.66), channel_id=1, source_target_pairs={{0,4},{1,5},{2,6},{3,7},{4,0},{5,1},{6,2},{7,3},{8,12},{9,13},{10,... | collective-permute-start | bytes 1769480 | tf_op jit(solution)/shard_map/ppermute | solution.py:552
  78.4 3.6 %collective-permute-start.11 = (f32[64,8,128]{2,1,0:T(8,128)S(1)}, f32[64,8,128]{2,1,0:T(8,128)S(1)}, u32[]{:S(2)}, u32[]{:S(2)}) collective-permute-start(f32[64,8,128]{2,1,0:T(8,128)S(1)} %get-tuple-element.64.mine_ref), channel_id=1, source_target_pairs={{0,8},{1,9},{2,10},{3,11},{4,12},{5,13},{6,14},{7,15},{24,16},{25,... | collective-permute-start | bytes 786440 | tf_op jit(solution)/shard_map/ppermute | solution.py:552
  82.0 1.3 %collective-permute-start.12 = (f32[64,8,128]{2,1,0:T(8,128)S(1)}, f32[64,8,128]{2,1,0:T(8,128)S(1)}, u32[]{:S(2)}, u32[]{:S(2)}) collective-permute-start(f32[64,8,128]{2,1,0:T(8,128)S(1)} %collective-permute-done.8.a_ref), channel_id=1, source_target_pairs={{4,0},{5,1},{6,2},{7,3},{24,28},{25,29},{26,30},{27,31}} | collective-permute-start | bytes 786440 | tf_op jit(solution)/shard_map/ppermute | solution.py:552
  83.3 0.9 shard_map.91
  84.2 3.5 %collective-permute-done.11.theirs_ref = f32[64,8,128]{2,1,0:T(8,128)S(1)} collective-permute-done((f32[64,8,128]{2,1,0:T(8,128)S(1)}, f32[64,8,128]{2,1,0:T(8,128)S(1)}, u32[]{:S(2)}, u32[]{:S(2)}) %collective-permute-start.11) | collective-permute-done | bytes 262176 | tf_op jit(solution)/shard_map/ppermute | solution.py:552
  87.7 1.5 %shard_map.92 = (f32[65,8,128]{2,1,0:T(8,128)S(1)}, f32[65,8,128]{2,1,0:T(8,128)S(1)}, f32[32,128]{1,0:T(8,128)}) custom-call(f32[64,128]{1,0:T(8,128)S(1)} %get-tuple-element.42.live_ref, f32[1,128]{1,0:T(1,128)S(1)} %get-tuple-element.63.extra_ref, f32[1,128]{1,0:T(1,128)S(1)} %get-tuple-element.50.power_ref, ...), custom_call_target="tpu_custom_call" | custom-call | tf_op jit(solution)/shard_map/pallas_call | solution.py:535
  89.2 2.5 %collective-permute-start.13 = (f32[65,8,128]{2,1,0:T(8,128)S(1)}, f32[65,8,128]{2,1,0:T(8,128)S(1)}, u32[]{:S(2)}, u32[]{:S(2)}) collective-permute-start(f32[65,8,128]{2,1,0:T(8,128)S(1)} %get-tuple-element.69), channel_id=1, source_target_pairs={{0,8},{1,9},{2,10},{3,11},{4,12},{5,13},{6,14},{7,15},{8,0},{9,1},... | collective-permute-start | bytes 798728 | tf_op jit(solution)/shard_map/ppermute | solution.py:552
  91.7 0.6 collective-permute-start.14
  92.3 3.6 %collective-permute-done.14.b_ref = f32[16,8,128]{2,1,0:T(8,128)S(1)} collective-permute-done((f32[16,8,128]{2,1,0:T(8,128)S(1)}, f32[16,8,128]{2,1,0:T(8,128)S(1)}, u32[]{:S(2)}, u32[]{:S(2)}) %collective-permute-start.14) | collective-permute-done | bytes 65568 | tf_op jit(solution)/shard_map/ppermute | solution.py:552
  96.0 0.6 collective-permute-start.15
  96.6 4.0 %all-to-all-start.1 = ((f32[32,1,128]{2,1,0:T(1,128)}), f32[32,1,128]{2,1,0:T(1,128)S(1)}, u32[]{:S(2)}, u32[]{:S(2)}) async-start(f32[32,1,128]{2,1,0:T(1,128)} %bitcast.6), calls=%async_computation.1 | async-start | bytes 32768 | tf_op jit(solution)/shard_map/all_to_all | solution.py:634
  100.6 1.3 %collective-permute-done.15.refs_1_ = f32[16,8,128]{2,1,0:T(8,128)S(1)} collective-permute-done((f32[16,8,128]{2,1,0:T(8,128)S(1)}, f32[16,8,128]{2,1,0:T(8,128)S(1)}, u32[]{:S(2)}, u32[]{:S(2)}) %collective-permute-start.15) | collective-permute-done | bytes 65568 | tf_op jit(solution)/shard_map/ppermute | solution.py:552
  101.9 0.1 shard_map.95
  102.1 0.5 shard_map.93
  102.5 5.2 %all-to-all-done.1 = f32[32,1,128]{2,1,0:T(1,128)S(1)} async-done(((f32[32,1,128]{2,1,0:T(1,128)}), f32[32,1,128]{2,1,0:T(1,128)S(1)}, u32[]{:S(2)}, u32[]{:S(2)}) %all-to-all-start.1) | async-done | bytes 16416 | tf_op jit(solution)/shard_map/all_to_all | solution.py:634
  107.7 0.2 shard_map.96
  108.0 0.5 collective-permute-start.16
  108.5 0.6 collective-permute-start.17
  109.2 3.3 %collective-permute-start.18 = (f32[16,8,128]{2,1,0:T(8,128)S(1)}, f32[16,8,128]{2,1,0:T(8,128)S(1)}, u32[]{:S(2)}, u32[]{:S(2)}) collective-permute-start(f32[16,8,128]{2,1,0:T(8,128)S(1)} %get-tuple-element.79.refs_0_), channel_id=1, source_target_pairs={{0,3},{1,2},{2,1},{3,0},{4,7},{5,6},{6,5},{7,4},{8,11},{9,10},{10,... | collective-permute-start | bytes 196616 | tf_op jit(solution)/shard_map/ppermute | solution.py:552
  112.5 0.9 shard_map.97
  113.4 3.2 %collective-permute-done.17.refs_2_ = f32[16,8,128]{2,1,0:T(8,128)S(1)} collective-permute-done((f32[16,8,128]{2,1,0:T(8,128)S(1)}, f32[16,8,128]{2,1,0:T(8,128)S(1)}, u32[]{:S(2)}, u32[]{:S(2)}) %collective-permute-start.17) | collective-permute-done | bytes 65568 | tf_op jit(solution)/shard_map/ppermute | solution.py:552
  116.6 0.9 shard_map.98
  (13 shorter events, 0.0 us)
Async XLA Ops:
  3.2 8.7 %collective-permute-start = (f32[64,8,128]{2,1,0:T(8,128)S(1)}, f32[64,8,128]{2,1,0:T(8,128)S(1)}, u32[]{:S(2)}, u32[]{:S(2)}) collective-permute-start(f32[64,8,128]{2,1,0:T(8,128)S(1)} %get-tuple-element.48.mine_ref), channel_id=1, source_target_pairs={{0,0},{1,1},{2,2},{3,3},{4,16},{5,17},{6,18},{7,19},{8,4},{9,5},{1... | collective-permute-start | bytes 786440 | tf_op jit(solution)/shard_map/ppermute | solution.py:552
  3.9 16.0 %collective-permute-start.1 = (f32[64,8,128]{2,1,0:T(8,128)S(1)}, f32[64,8,128]{2,1,0:T(8,128)S(1)}, u32[]{:S(2)}, u32[]{:S(2)}) collective-permute-start(f32[64,8,128]{2,1,0:T(8,128)S(1)} %get-tuple-element.48.mine_ref), channel_id=1, source_target_pairs={{0,16},{1,17},{2,18},{3,19},{4,0},{5,1},{6,2},{7,3},{8,20},{9,21},... | collective-permute-start | bytes 786440 | tf_op jit(solution)/shard_map/ppermute | solution.py:552
  26.3 57.0 %copy-start = (f32[16,8]{0,1:T(8,128)S(1)}, f32[16,8]{0,1:T(8,128)}, u32[]{:S(2)}) copy-start(f32[16,8]{0,1:T(8,128)} %param.11) | copy-start | bytes 1540
  26.3 11.1 %collective-permute-start.2 = (f32[72,16,128]{2,1,0:T(8,128)S(1)}, f32[72,16,128]{2,1,0:T(8,128)S(1)}, u32[]{:S(2)}, u32[]{:S(2)}) collective-permute-start(f32[72,16,128]{2,1,0:T(8,128)S(1)} %get-tuple-element.52), channel_id=1, source_target_pairs={{0,4},{1,5},{2,6},{3,7},{4,0},{5,1},{6,2},{7,3},{8,12},{9,13},{10,... | collective-permute-start | bytes 1769480 | tf_op jit(solution)/shard_map/ppermute | solution.py:552
  27.2 10.2 %collective-permute-start.3 = (f32[64,8,128]{2,1,0:T(8,128)S(1)}, f32[64,8,128]{2,1,0:T(8,128)S(1)}, u32[]{:S(2)}, u32[]{:S(2)}) collective-permute-start(f32[64,8,128]{2,1,0:T(8,128)S(1)} %get-tuple-element.48.mine_ref), channel_id=1, source_target_pairs={{0,8},{1,9},{2,10},{3,11},{4,12},{5,13},{6,14},{7,15},{24,16},{25,... | collective-permute-start | bytes 786440 | tf_op jit(solution)/shard_map/ppermute | solution.py:552
  31.2 6.2 %collective-permute-start.4 = (f32[64,8,128]{2,1,0:T(8,128)S(1)}, f32[64,8,128]{2,1,0:T(8,128)S(1)}, u32[]{:S(2)}, u32[]{:S(2)}) collective-permute-start(f32[64,8,128]{2,1,0:T(8,128)S(1)} %collective-permute-done.a_ref), channel_id=1, source_target_pairs={{4,0},{5,1},{6,2},{7,3},{24,28},{25,29},{26,30},{27,31}} | collective-permute-start | bytes 786440 | tf_op jit(solution)/shard_map/ppermute | solution.py:552
  38.8 12.1 %collective-permute-start.5 = (f32[65,8,128]{2,1,0:T(8,128)S(1)}, f32[65,8,128]{2,1,0:T(8,128)S(1)}, u32[]{:S(2)}, u32[]{:S(2)}) collective-permute-start(f32[65,8,128]{2,1,0:T(8,128)S(1)} %get-tuple-element.55), channel_id=1, source_target_pairs={{0,8},{1,9},{2,10},{3,11},{4,12},{5,13},{6,14},{7,15},{8,0},{9,1},... | collective-permute-start | bytes 798728 | tf_op jit(solution)/shard_map/ppermute | solution.py:552
  41.3 4.3 %collective-permute-start.6 = (f32[16,8,128]{2,1,0:T(8,128)S(1)}, f32[16,8,128]{2,1,0:T(8,128)S(1)}, u32[]{:S(2)}, u32[]{:S(2)}) collective-permute-start(f32[16,8,128]{2,1,0:T(8,128)S(1)} %get-tuple-element.61.a_ref), channel_id=1, source_target_pairs={{0,1},{1,0},{2,3},{3,2},{4,5},{5,4},{6,7},{7,6},{8,9},{9,8},{10,11... | collective-permute-start | bytes 196616 | tf_op jit(solution)/shard_map/ppermute | solution.py:552
  45.6 5.2 %collective-permute-start.7 = (f32[16,8,128]{2,1,0:T(8,128)S(1)}, f32[16,8,128]{2,1,0:T(8,128)S(1)}, u32[]{:S(2)}, u32[]{:S(2)}) collective-permute-start(f32[16,8,128]{2,1,0:T(8,128)S(1)} %shard_map.88.refs_0_), channel_id=1, source_target_pairs={{0,2},{1,3},{2,0},{3,1},{4,6},{5,7},{6,4},{7,5},{8,10},{9,11},{10,... | collective-permute-start | bytes 196616 | tf_op jit(solution)/shard_map/ppermute | solution.py:552
  48.3 9.7 %all-to-all-start = ((f32[32,1,128]{2,1,0:T(1,128)}), f32[32,1,128]{2,1,0:T(1,128)S(1)}, u32[]{:S(2)}, u32[]{:S(2)}) async-start(f32[32,1,128]{2,1,0:T(1,128)} %bitcast.3), calls=%async_computation | async-start | bytes 32768 | tf_op jit(solution)/shard_map/all_to_all | solution.py:634
  58.3 4.0 %collective-permute-start.8 = (f32[64,8,128]{2,1,0:T(8,128)S(1)}, f32[64,8,128]{2,1,0:T(8,128)S(1)}, u32[]{:S(2)}, u32[]{:S(2)}) collective-permute-start(f32[64,8,128]{2,1,0:T(8,128)S(1)} %get-tuple-element.64.mine_ref), channel_id=1, source_target_pairs={{0,0},{1,1},{2,2},{3,3},{4,16},{5,17},{6,18},{7,19},{8,4},{9,5},{1... | collective-permute-start | bytes 786440 | tf_op jit(solution)/shard_map/ppermute | solution.py:552
  58.9 12.6 %collective-permute-start.9 = (f32[64,8,128]{2,1,0:T(8,128)S(1)}, f32[64,8,128]{2,1,0:T(8,128)S(1)}, u32[]{:S(2)}, u32[]{:S(2)}) collective-permute-start(f32[64,8,128]{2,1,0:T(8,128)S(1)} %get-tuple-element.64.mine_ref), channel_id=1, source_target_pairs={{0,16},{1,17},{2,18},{3,19},{4,0},{5,1},{6,2},{7,3},{8,20},{9,21},... | collective-permute-start | bytes 786440 | tf_op jit(solution)/shard_map/ppermute | solution.py:552
  76.8 10.9 %collective-permute-start.10 = (f32[72,16,128]{2,1,0:T(8,128)S(1)}, f32[72,16,128]{2,1,0:T(8,128)S(1)}, u32[]{:S(2)}, u32[]{:S(2)}) collective-permute-start(f32[72,16,128]{2,1,0:T(8,128)S(1)} %get-tuple-element.66), channel_id=1, source_target_pairs={{0,4},{1,5},{2,6},{3,7},{4,0},{5,1},{6,2},{7,3},{8,12},{9,13},{10,... | collective-permute-start | bytes 1769480 | tf_op jit(solution)/shard_map/ppermute | solution.py:552
  78.4 9.3 %collective-permute-start.11 = (f32[64,8,128]{2,1,0:T(8,128)S(1)}, f32[64,8,128]{2,1,0:T(8,128)S(1)}, u32[]{:S(2)}, u32[]{:S(2)}) collective-permute-start(f32[64,8,128]{2,1,0:T(8,128)S(1)} %get-tuple-element.64.mine_ref), channel_id=1, source_target_pairs={{0,8},{1,9},{2,10},{3,11},{4,12},{5,13},{6,14},{7,15},{24,16},{25,... | collective-permute-start | bytes 786440 | tf_op jit(solution)/shard_map/ppermute | solution.py:552
  82.0 5.7 %collective-permute-start.12 = (f32[64,8,128]{2,1,0:T(8,128)S(1)}, f32[64,8,128]{2,1,0:T(8,128)S(1)}, u32[]{:S(2)}, u32[]{:S(2)}) collective-permute-start(f32[64,8,128]{2,1,0:T(8,128)S(1)} %collective-permute-done.8.a_ref), channel_id=1, source_target_pairs={{4,0},{5,1},{6,2},{7,3},{24,28},{25,29},{26,30},{27,31}} | collective-permute-start | bytes 786440 | tf_op jit(solution)/shard_map/ppermute | solution.py:552
  89.2 12.8 %collective-permute-start.13 = (f32[65,8,128]{2,1,0:T(8,128)S(1)}, f32[65,8,128]{2,1,0:T(8,128)S(1)}, u32[]{:S(2)}, u32[]{:S(2)}) collective-permute-start(f32[65,8,128]{2,1,0:T(8,128)S(1)} %get-tuple-element.69), channel_id=1, source_target_pairs={{0,8},{1,9},{2,10},{3,11},{4,12},{5,13},{6,14},{7,15},{8,0},{9,1},... | collective-permute-start | bytes 798728 | tf_op jit(solution)/shard_map/ppermute | solution.py:552
  91.7 4.3 %collective-permute-start.14 = (f32[16,8,128]{2,1,0:T(8,128)S(1)}, f32[16,8,128]{2,1,0:T(8,128)S(1)}, u32[]{:S(2)}, u32[]{:S(2)}) collective-permute-start(f32[16,8,128]{2,1,0:T(8,128)S(1)} %get-tuple-element.74.a_ref), channel_id=1, source_target_pairs={{0,1},{1,0},{2,3},{3,2},{4,5},{5,4},{6,7},{7,6},{8,9},{9,8},{10,11... | collective-permute-start | bytes 196616 | tf_op jit(solution)/shard_map/ppermute | solution.py:552
  96.0 5.9 %collective-permute-start.15 = (f32[16,8,128]{2,1,0:T(8,128)S(1)}, f32[16,8,128]{2,1,0:T(8,128)S(1)}, u32[]{:S(2)}, u32[]{:S(2)}) collective-permute-start(f32[16,8,128]{2,1,0:T(8,128)S(1)} %shard_map.94.refs_0_), channel_id=1, source_target_pairs={{0,2},{1,3},{2,0},{3,1},{4,6},{5,7},{6,4},{7,5},{8,10},{9,11},{10,... | collective-permute-start | bytes 196616 | tf_op jit(solution)/shard_map/ppermute | solution.py:552
  96.6 11.2 %all-to-all-start.1 = ((f32[32,1,128]{2,1,0:T(1,128)}), f32[32,1,128]{2,1,0:T(1,128)S(1)}, u32[]{:S(2)}, u32[]{:S(2)}) async-start(f32[32,1,128]{2,1,0:T(1,128)} %bitcast.6), calls=%async_computation.1 | async-start | bytes 32768 | tf_op jit(solution)/shard_map/all_to_all | solution.py:634
  108.0 5.4 %collective-permute-start.16 = (f32[16,8,128]{2,1,0:T(8,128)S(1)}, f32[16,8,128]{2,1,0:T(8,128)S(1)}, u32[]{:S(2)}, u32[]{:S(2)}) collective-permute-start(f32[16,8,128]{2,1,0:T(8,128)S(1)} %get-tuple-element.79.refs_0_), channel_id=1, source_target_pairs={{0,1},{1,0},{2,3},{3,2},{4,5},{5,4},{6,7},{7,6},{8,9},{9,8},{10,11... | collective-permute-start | bytes 196616 | tf_op jit(solution)/shard_map/ppermute | solution.py:552
  108.5 8.0 %collective-permute-start.17 = (f32[16,8,128]{2,1,0:T(8,128)S(1)}, f32[16,8,128]{2,1,0:T(8,128)S(1)}, u32[]{:S(2)}, u32[]{:S(2)}) collective-permute-start(f32[16,8,128]{2,1,0:T(8,128)S(1)} %get-tuple-element.79.refs_0_), channel_id=1, source_target_pairs={{0,2},{1,3},{2,0},{3,1},{4,6},{5,7},{6,4},{7,5},{8,10},{9,11},{10,... | collective-permute-start | bytes 196616 | tf_op jit(solution)/shard_map/ppermute | solution.py:552
  109.2 7.4 %collective-permute-start.18 = (f32[16,8,128]{2,1,0:T(8,128)S(1)}, f32[16,8,128]{2,1,0:T(8,128)S(1)}, u32[]{:S(2)}, u32[]{:S(2)}) collective-permute-start(f32[16,8,128]{2,1,0:T(8,128)S(1)} %get-tuple-element.79.refs_0_), channel_id=1, source_target_pairs={{0,3},{1,2},{2,1},{3,0},{4,7},{5,6},{6,5},{7,4},{8,11},{9,10},{10,... | collective-permute-start | bytes 196616 | tf_op jit(solution)/shard_map/ppermute | solution.py:552

commit v8 on v6

--- a/solution.py
+++ b/solution.py
@@ -14,6 +14,7 @@
 HIGH = lax.Precision.HIGHEST
 AXES = ("row", "col", "band")
 CHUNK = 4
+HEAD = 2
 LIMIT = pltpu.CompilerParams(vmem_limit_bytes=16 * 2**20)
 
 
@@ -182,9 +183,9 @@
     return out
 
 
-def setup_kernel(dims, cols, flux_hbm, flags_hbm, duals_hbm, g_ref, live_col_ref, live_half_ref,
+def setup_kernel(dims, cols, flux_hbm, flags_hbm, duals_hbm, vis_hbm, g_ref, live_col_ref, live_half_ref,
                  live_own_ref, upright_ref, u_ref, rhs_ref, held_ref, slope_ref, samples_ref,
-                 extra_ref, flux_ref, flags_ref, duals_ref, sems):
+                 extra_ref, head_ref, flux_ref, flags_ref, duals_ref, sems):
     F, T, _, O, R, C = dims
     W, rows, full = 2 * O, C * O, flags_ref.shape[2]
     row = lax.axis_index("row")
@@ -193,6 +194,7 @@
         pltpu.make_async_copy(flags_hbm, flags_ref, sems.at[0]),
         pltpu.make_async_copy(duals_hbm, duals_ref, sems.at[1]),
         pltpu.make_async_copy(flux_hbm, flux_ref, sems.at[2]),
+        pltpu.make_async_copy(vis_hbm.at[pl.ds(0, HEAD)], head_ref, sems.at[3]),
     ]
     for copy in copies:
         copy.start()
@@ -228,14 +230,18 @@
     samples = jnp.where(lanes == O, samples, 0.0)
     samples_ref[...] = samples
     extra_ref[...] = samples - jnp.where(low_lanes(own.shape), own, 0.0)
-
-
-def again_kernel(dims, flux_ref, samples_ref, live_ref, u_ref, g_ref,
-                 rhs_ref, held_ref, slope_ref, extra_ref):
+    copies[3].wait()
+
+
+def again_kernel(dims, flux_ref, vis_hbm, samples_ref, live_ref, u_ref, g_ref,
+                 rhs_ref, held_ref, slope_ref, extra_ref, head_ref, sem):
     _, T, _, _, _, _ = dims
+    copy = pltpu.make_async_copy(vis_hbm.at[pl.ds(0, HEAD)], head_ref, sem.at[0])
+    copy.start()
     fit_sums(dims, lambda f, t: u_ref[f * T + t] + g_ref[f * T + t], rhs_ref)
     own = own_terms(dims, flux_ref, live_ref, g_ref, held_ref, slope_ref)
     extra_ref[...] = samples_ref[...] - jnp.where(low_lanes(own.shape), own, 0.0)
+    copy.wait()
 
 
 def add_kernel(a_ref, b_ref, out_ref):
@@ -264,12 +270,12 @@
     return a == b
 
 
-def sum_kernel(dims, flux_hbm, vis_hbm, live_ref, a_ref, b_ref, *refs):
+def sum_kernel(dims, flux_hbm, vis_hbm, live_ref, a_ref, b_ref, head_ref, *refs):
     F, T, D, O, _, _ = dims
-    upright_ref, refs = (refs[0], refs[1:]) if len(refs) == 8 else (None, refs)
+    upright_ref, refs = (refs[0], refs[1:]) if len(refs) == 9 else (None, refs)
     keep_ref, send_ref, refs = refs[0], refs[1], refs[2:]
     power_ref, refs = (refs[0], refs[1:]) if upright_ref is not None else (None, refs)
-    vis_ref, distinct, flux_ref, sems = refs
+    vis_ref, distinct, flux_ref, sems = refs[:4]
     rows, cols = vis_ref.shape[3], vis_ref.shape[4]
     row = lax.axis_index("row")
     col = lax.axis_index("col")
@@ -281,7 +287,7 @@
     flux_copy = pltpu.make_async_copy(flux_hbm, flux_ref, sems.at[F])
     flux_copy.start()
     ahead = 2 * CHUNK
-    for f in range(ahead):
+    for f in range(HEAD, ahead):
         vis_copy(f).start()
     p = lax.broadcasted_iota(jnp.int32, (rows, cols), 0) + row * rows
     q = lax.broadcasted_iota(jnp.int32, (rows, cols), 1) + col * cols
@@ -290,7 +296,7 @@
     blocks = block_mask(2 * D)
     nt = (((1,), (1,)), ((), ()))
 
-    def body(step, upright, start, power):
+    def body(step, upright, start, power, source):
         highs, lows = [], []
         lives = live_ref[pl.ds(step * 8, 8), :]
         mask = distinct[...]
@@ -314,7 +320,7 @@
                 highs.append(high)
                 lows.append(low)
                 both = jnp.concatenate([high, low], axis=0)
-                seen = [vis_ref[f, t, part] * mask for part in range(2)]
+                seen = [source[f, t, part] * mask for part in range(2)]
                 v = lax.dot_general(
                     both, jnp.concatenate(seen, axis=1), nt, preferred_element_type=jnp.float32
                 )
@@ -343,33 +349,38 @@
         send_ref[step * 9 + 8] = folded
         return power
 
+    def roll_to(c):
+        if upright_ref is None:
+            return None
+        upright = refs[4]
+        upright[...] = pltpu.roll(upright_ref[...], (2 * O - c * CHUNK * T) % (2 * O), 1)
+        return upright
+
     def chunk(c, power):
-        first = isinstance(c, int)
-        if not first:
-            for i in range(CHUNK):
-                vis_copy(c * CHUNK + i).wait()
-
-        def more():
+        for i in range(CHUNK):
+            vis_copy(c * CHUNK + i).wait()
+
+        @pl.when(c * CHUNK + ahead < F)
+        def _():
             for i in range(CHUNK):
                 vis_copy(c * CHUNK + ahead + i).start()
 
-        if not first:
-            pl.when(c * CHUNK + ahead < F)(more)
-
-        upright = None
-        if upright_ref is not None:
-            upright = pltpu.roll(upright_ref[...], (2 * O - c * CHUNK * T) % (2 * O), 1)
+        upright = roll_to(c)
         for j in range(CHUNK // group):
-            if first:
-                for i in range(group):
-                    vis_copy(j * group + i).wait()
-            power = body(c * (CHUNK // group) + j, upright, j * 8, power)
-        if first and ahead < F:
-            more()
+            power = body(c * (CHUNK // group) + j, upright, j * 8, power, vis_ref)
         return power
 
     flux_copy.wait()
-    power = chunk(0, jnp.zeros((8, cols), jnp.float32))
+    power = jnp.zeros((8, cols), jnp.float32)
+    upright = roll_to(0)
+    for j in range(CHUNK // group):
+        inside = (j + 1) * group <= HEAD
+        if not inside:
+            for i in range(group):
+                vis_copy(j * group + i).wait()
+        power = body(j, upright, j * 8, power, head_ref if inside else vis_ref)
+    for i in range(CHUNK):
+        vis_copy(ahead + i).start()
     power = lax.fori_loop(1, F // CHUNK, chunk, power)
     if power_ref is not None:
         power = jnp.sum(power, axis=0, keepdims=True)
@@ -377,8 +388,7 @@
 
 
 def residual_kernel(dims, live_ref, extra_ref, power_ref, kept_ref, other_ref, mine_ref, theirs_ref,
-                    passed_ref, got_ref,
-                    keep_ref, send_ref, scalar_ref):
+                    passed_ref, got_ref, keep_ref, send_ref, scalar_hbm, num_ref, scalar_ref, sem):
     F, T, D, O, _, _ = dims
     W = 2 * O
     row = lax.axis_index("row")
@@ -390,12 +400,12 @@
     eye = lax.broadcasted_iota(jnp.int32, (2 * D, W), 0) == (
         lax.broadcasted_iota(jnp.int32, (2 * D, W), 1) % (2 * D)
     )
-    total = jnp.zeros((2 * D, W), jnp.float32)
-    for group in range(F * T // 8):
+
+    def body(group, total):
         gram = kept_ref[group * 9 + 8] + other_ref[group * 9 + 8]
         diagonal = jnp.sum(jnp.where(eye, gram, 0.0), axis=0, keepdims=True)
-        keep_ref[F * T, group : group + 1, :] = diagonal
-        send_ref[F * T, group : group + 1, :] = diagonal
+        keep_ref[F * T, pl.ds(group, 1), :] = diagonal
+        send_ref[F * T, pl.ds(group, 1), :] = diagonal
         spread = jnp.where(mask, jnp.concatenate([gram] * 8, axis=0), 0.0)
         station = []
         for i in range(8):
@@ -409,20 +419,32 @@
             spread, jnp.concatenate(station, axis=0), precision=HIGH,
             preferred_element_type=jnp.float32,
         )
+        lives = live_ref[pl.ds(group * 8, 8), :]
         for i in range(8):
             ft = group * 8 + i
-            live = live_ref[ft : ft + 1, :]
+            live = lives[i : i + 1, :]
             v = kept_ref[group * 9 + i] + other_ref[group * 9 + i]
             num = (v - model[i * 2 * D : (i + 1) * 2 * D]) * live
             z = jnp.concatenate(station[2 * i : 2 * i + 2], axis=0)
             total = total + z * (v * live + num)
-            low, high = join_low(num[:D], num[D:]), join_high(num[:D], num[D:])
-            keep_ref[ft] = jnp.where(near, low, high)
-            send_ref[ft] = jnp.where(near, high, low)
+            num_ref[ft] = num
+        return total
+
+    total = jnp.zeros((2 * D, W), jnp.float32)
+    for group in range(F * T // 8):
+        total = body(group, total)
     squares = -jnp.sum(total, axis=0, keepdims=True)
     squares = squares + swap(squares)
     scalar = jnp.where(low_lanes(squares.shape), squares, 0.0) + extra_ref[...] + power_ref[...]
     scalar_ref[...] = jnp.broadcast_to(scalar, scalar_ref.shape)
+    copy = pltpu.make_async_copy(scalar_ref, scalar_hbm, sem.at[0])
+    copy.start()
+    for ft in range(F * T):
+        num = num_ref[ft]
+        low, high = join_low(num[:D], num[D:]), join_high(num[:D], num[D:])
+        keep_ref[ft] = jnp.where(near, low, high)
+        send_ref[ft] = jnp.where(near, high, low)
+    copy.wait()
 
 
 def merge_kernel(dims, keep_ref, come_ref, live_ref, e_ref, g_ref, held_ref, slope_ref,
@@ -552,11 +574,12 @@
         return permute(x, lambda r, c, z: (((r * C + c) % R + m) % R, (r * C + c) // R, z))
 
     def bands(x):
-        return [x] + [permute(x, lambda r, c, z, k=k: (r, c, (z + k) % Z)) for k in range(1, Z)]
+        return [x] + [permute(x, lambda r, c, z, k=k: (r, c, z ^ k)) for k in range(1, Z)]
 
     whole, line, fit = array(FT, D, W), array(FT + 1, D, W), array(4 * T, D, W)
     pair, text = array(FT // 8 * 9, 2 * D, W), array(1, W)
     flux_t = flux.T
+    start = jax.ShapeDtypeStruct((HEAD,) + vis.shape[1:], vis.dtype)
     rot, g, p = pl.pallas_call(
         functools.partial(start_kernel, dims),
         out_shape=[whole] * 3,
@@ -575,47 +598,52 @@
         last = step == ITERS - 1
         got = [gather(p, m) for m in range(R)]
         if step == 0:
-            (live_col, live_half, live_own, upright, u, rhs, held, slope, samples, extra) = (
+            (live_col, live_half, live_own, upright, u, rhs, held, slope, samples, extra, head) = (
                 pl.pallas_call(
                     functools.partial(setup_kernel, dims, cols),
                     out_shape=[
                         array(FT, cols), array(FT, W), array(FT, W), array(rows, W), whole,
-                        fit, whole, whole, text, text,
+                        fit, whole, whole, text, text, start,
                     ],
-                    in_specs=[hbm] * 3 + [vmem],
-                    out_specs=[vmem] * 10,
+                    in_specs=[hbm] * 4 + [vmem],
+                    out_specs=[vmem] * 11,
                     scratch_shapes=[
                         pltpu.SMEM(flux_t.shape, f32),
                         pltpu.VMEM(flags.shape, flags.dtype),
                         pltpu.VMEM(duals.shape, f32),
-                        pltpu.SemaphoreType.DMA((3,)),
+                        pltpu.SemaphoreType.DMA((4,)),
                     ],
                     compiler_params=LIMIT,
                     name="setup",
-                )(far(flux_t), far(flags), far(duals), g)
+                )(far(flux_t), far(flags), far(duals), far(vis), g)
             )
         else:
-            rhs, held, slope, extra = call(
+            rhs, held, slope, extra, head = pl.pallas_call(
                 functools.partial(again_kernel, dims),
-                [fit, whole, whole, text], [flux_t], [samples, live_own, u, g],
-            )
+                out_shape=[fit, whole, whole, text, start],
+                in_specs=[smem, hbm] + [vmem] * 4,
+                out_specs=[vmem] * 5,
+                scratch_shapes=[pltpu.SemaphoreType.DMA((1,))],
+                compiler_params=LIMIT,
+                name="again",
+            )(flux_t, far(vis), samples, live_own, u, g)
         rhs_near = permute(rhs, lambda r, c, z: (r, c, z ^ 1))
         theirs = permute(p, lambda r, c, z: (r, c ^ 2, z), lambda r, c: r == c // 2)
         more = [] if step else [upright]
         keep, send, *found = pl.pallas_call(
             functools.partial(sum_kernel, dims),
             out_shape=[pair, pair] + ([] if step else [array(1, cols)]),
-            in_specs=[hbm] * 2 + [vmem] * (3 + len(more)),
+            in_specs=[hbm] * 2 + [vmem] * (4 + len(more)),
             out_specs=[vmem] * (2 + len(more)),
             scratch_shapes=[
                 pltpu.VMEM(vis.shape, vis.dtype),
                 pltpu.VMEM((rows, cols), vis.dtype),
                 pltpu.SMEM(flux_t.shape, f32),
                 pltpu.SemaphoreType.DMA((F + 1,)),
-            ],
+            ] + [pltpu.VMEM((rows, W), f32)] * len(more),
             compiler_params=LIMIT,
             name="sums",
-        )(far(flux_t), far(vis), live_col, *got, *more)
+        )(far(flux_t), far(vis), live_col, *got, head, *more)
         power = power if step else found[0]
         passed = permute(
             got[0], lambda r, c, z: (r, c ^ 1, z), lambda r, c: c == 3 * r + (1 - 2 * r)
@@ -623,10 +651,19 @@
         other = permute(send, lambda r, c, z: (r, c ^ 1, z))
         (rhs,) = call(add_kernel, [fit], [], [rhs, rhs_near])
         rhs_far = permute(rhs, lambda r, c, z: (r, c, z ^ 2))
-        keep, send, scalar = call(
-            functools.partial(residual_kernel, dims), [line, line, array(R * C * Z, W)],
-            [], [live_half, extra, power, keep, other, p, theirs, passed, got[1]],
-        )
+        everyone = array(R * C * Z, W)
+        keep, send, scalar = pl.pallas_call(
+            functools.partial(residual_kernel, dims),
+            out_shape=[line, line, everyone],
+            in_specs=[vmem] * 9,
+            out_specs=[vmem, vmem, hbm],
+            scratch_shapes=[
+                pltpu.VMEM((FT, 2 * D, W), f32), pltpu.VMEM(everyone.shape, f32),
+                pltpu.SemaphoreType.DMA((1,)),
+            ],
+            compiler_params=LIMIT,
+            name="residual",
+        )(live_half, extra, power, keep, other, p, theirs, passed, got[1])
         come = permute(send, lambda r, c, z: (r, c ^ 2, z))
         scalar = lax.all_to_all(scalar, AXES, 0, 0, tiled=True)
         target = call(

time: 118 us -> 117 us (level)
  waiting for transfers between devices: 48.6 us -> 47 us
    pallas_call x0 -> x3, Pallas kernels: none -> 4.96 us  [the longest x2 2.97 us: shards(): pl.pallas_call(functools.partial(residual_kernel, dims), out_shape=[line,...]
    pallas_call x11 -> x8, Pallas kernels: 5.59 us -> 1.76 us  [call(): pl.pallas_call(kernel, out_shape=outs, in_specs=[smem] * len(scalars) + [...]
    ppermute x19, waiting for transfers between devices: 36.9 us -> 35.3 us  [permute(): return lax.ppermute(x, AXES, pairs)]
  transfers between devices with their start and end apart: 21 -> 21, of which waited for: 11 -> 10; matrix products, arithmetic and copies ran while one was open for 0% -> 0% of each run, Pallas kernels for 5% -> 6%
where the time goes in v8:
time: 117 us
  waiting for transfers between devices  47 us (40%)
  starting transfers between devices  44.6 us (38%)
  Pallas kernels  24.6 us (21%)
    ppermute x19, starting transfers between devices, permute(): return lax.ppermute(x, AXES, pairs)  38.1 us
    ppermute x19, waiting for transfers between devices, permute(): return lax.ppermute(x, AXES, pairs)  35.3 us
    all_to_all x2, waiting for transfers between devices, shards(): scalar = lax.all_to_all(scalar, AXES, 0, 0, tiled=True)  11.7 us
    pallas_call x2, Pallas kernels, shards(): pl.pallas_call(functools.partial(sum_kernel, dims), out_shape=[pair, pair...  11.1 us
    all_to_all x2, starting transfers between devices, shards(): scalar = lax.all_to_all(scalar, AXES, 0, 0, tiled=True)  6.59 us
    pallas_call x2, Pallas kernels, shards(): pl.pallas_call(functools.partial(residual_kernel, dims), out_shape=[line,...  2.97 us
    pallas_call x1, Pallas kernels, shards(): pl.pallas_call(functools.partial(start_kernel, dims), out_shape=[whole] *...  2.54 us
  transfers between devices with their start and end apart: 21, of which 10 were waited for; matrix products, arithmetic and copies ran while one was open for 0% of the time, Pallas kernels for 6%

profile of v8, /device:TPU:0, one launch (start us, length us, event | category | flops | bytes accessed | tf_op | source)
XLA Modules:
  0.0 117.1 jit_solution(10778192131097428967)
XLA Ops:
  0.6 2.5 %start.1 = (f32[64,8,128]{2,1,0:T(8,128)S(1)}, f32[64,8,128]{2,1,0:T(8,128)S(1)}, f32[64,8,128]{2,1,0:T(8,128)S(1)}) custom-call(f32[3,4,512]{2,1,0:T(4,128)} %bitcast.16, f32[3,8]{1,0:T(4,128)} %lmn_hbm.1, f32[16,4,2,8,64]{4,3,2,1,0:T(8,128)} %gains_hbm.1), custom_call_target="tpu_custom_call" | custom-call | tf_op jit(solution)/shard_map/start/pallas_call | solution.py:583
  3.2 0.7 collective-permute-start
  3.9 5.7 %collective-permute-start.1 = (f32[64,8,128]{2,1,0:T(8,128)S(1)}, f32[64,8,128]{2,1,0:T(8,128)S(1)}, u32[]{:S(2)}, u32[]{:S(2)}) collective-permute-start(f32[64,8,128]{2,1,0:T(8,128)S(1)} %get-tuple-element.50.mine_ref), channel_id=1, source_target_pairs={{0,16},{1,17},{2,18},{3,19},{4,0},{5,1},{6,2},{7,3},{8,20},{9,21},... | collective-permute-start | bytes 786440 | tf_op jit(solution)/shard_map/ppermute | solution.py:571
  9.6 2.3 %setup.1 = (f32[64,128]{1,0:T(8,128)S(1)}, f32[64,128]{1,0:T(8,128)S(1)}, f32[64,128]{1,0:T(8,128)S(1)}, f32[256,128]{1,0:T(8,128)S(1)}, f32[64,8,128]{2,1,0:T(8...) custom-call(f32[8,16]{1,0:T(8,128)} %bitcast.10, ...), custom_call_target="tpu_custom_call" | custom-call | tf_op jit(solution)/shard_map/setup/pallas_call | solution.py:602
  11.9 0.0 copy-start
  12.0 7.9 %collective-permute-done.1.b_ref.got_ref = f32[64,8,128]{2,1,0:T(8,128)S(1)} collective-permute-done((f32[64,8,128]{2,1,0:T(8,128)S(1)}, f32[64,8,128]{2,1,0:T(8,128)S(1)}, u32[]{:S(2)}, u32[]{:S(2)}) %collective-permute-start.1) | collective-permute-done | bytes 262176 | tf_op jit(solution)/shard_map/ppermute | solution.py:571
  19.8 6.0 %sums.2 = (f32[72,16,128]{2,1,0:T(8,128)S(1)}, f32[72,16,128]{2,1,0:T(8,128)S(1)}, f32[1,128]{1,0:T(1,128)S(1)}) custom-call(f32[8,16]{1,0:T(8,128)} %bitcast.11, bf16[16,4,2,256,128]{4,3,2,1,0:T(8,128)(2,1)} %vis_hbm.7, f32[64,128]{1,0:T(8,128)S(1)} %get-tuple-element.49.live_ref, f32[64,8,128]{2,1,0:T(8,128)S(1)} %collective-permute-done.a_ref, ...), custom_call_target="tpu_custom_call" | custom-call | tf_op jit(solution)/shard_map/sums/pallas_call | solution.py:633
  25.9 0.9 collective-permute-start.2
  26.7 4.0 %collective-permute-start.3 = (f32[64,8,128]{2,1,0:T(8,128)S(1)}, f32[64,8,128]{2,1,0:T(8,128)S(1)}, u32[]{:S(2)}, u32[]{:S(2)}) collective-permute-start(f32[64,8,128]{2,1,0:T(8,128)S(1)} %get-tuple-element.50.mine_ref), channel_id=1, source_target_pairs={{0,8},{1,9},{2,10},{3,11},{4,12},{5,13},{6,14},{7,15},{24,16},{25,... | collective-permute-start | bytes 786440 | tf_op jit(solution)/shard_map/ppermute | solution.py:571
  30.8 1.3 %collective-permute-start.4 = (f32[64,8,128]{2,1,0:T(8,128)S(1)}, f32[64,8,128]{2,1,0:T(8,128)S(1)}, u32[]{:S(2)}, u32[]{:S(2)}) collective-permute-start(f32[64,8,128]{2,1,0:T(8,128)S(1)} %collective-permute-done.a_ref), channel_id=1, source_target_pairs={{4,0},{5,1},{6,2},{7,3},{24,28},{25,29},{26,30},{27,31}} | collective-permute-start | bytes 786440 | tf_op jit(solution)/shard_map/ppermute | solution.py:571
  32.1 4.9 %collective-permute-done.3.theirs_ref = f32[64,8,128]{2,1,0:T(8,128)S(1)} collective-permute-done((f32[64,8,128]{2,1,0:T(8,128)S(1)}, f32[64,8,128]{2,1,0:T(8,128)S(1)}, u32[]{:S(2)}, u32[]{:S(2)}) %collective-permute-start.3) | collective-permute-done | bytes 262176 | tf_op jit(solution)/shard_map/ppermute | solution.py:571
  37.0 1.5 %residual.2 = (f32[65,8,128]{2,1,0:T(8,128)S(1)}, f32[65,8,128]{2,1,0:T(8,128)S(1)}, f32[32,128]{1,0:T(8,128)}) custom-call(f32[64,128]{1,0:T(8,128)S(1)} %get-tuple-element.44.live_ref, f32[1,128]{1,0:T(1,128)S(1)} %get-tuple-element.48.extra_ref, f32[1,128]{1,0:T(1,128)S(1)} %get-tuple-element.53.power_ref, f32[72,16,128]{2,1,0:T(8,128)S(1)} %get-tuple-element.54.kept_ref, ...), custom_call_target="tpu_custom_call" | custom-call | tf_op jit(solution)/shard_map/residual/pallas_call | solution.py:655
  38.5 2.5 %collective-permute-start.5 = (f32[65,8,128]{2,1,0:T(8,128)S(1)}, f32[65,8,128]{2,1,0:T(8,128)S(1)}, u32[]{:S(2)}, u32[]{:S(2)}) collective-permute-start(f32[65,8,128]{2,1,0:T(8,128)S(1)} %get-tuple-element.58), channel_id=1, source_target_pairs={{0,8},{1,9},{2,10},{3,11},{4,12},{5,13},{6,14},{7,15},{8,0},{9,1},... | collective-permute-start | bytes 798728 | tf_op jit(solution)/shard_map/ppermute | solution.py:571
  41.0 1.6 %collective-permute-start.6 = (f32[16,8,128]{2,1,0:T(8,128)S(1)}, f32[16,8,128]{2,1,0:T(8,128)S(1)}, u32[]{:S(2)}, u32[]{:S(2)}) collective-permute-start(f32[16,8,128]{2,1,0:T(8,128)S(1)} %get-tuple-element.64.a_ref), channel_id=1, source_target_pairs={{0,1},{1,0},{2,3},{3,2},{4,5},{5,4},{6,7},{7,6},{8,9},{9,8},{10,11... | collective-permute-start | bytes 196616 | tf_op jit(solution)/shard_map/ppermute | solution.py:571
  42.6 2.7 %collective-permute-done.6.b_ref = f32[16,8,128]{2,1,0:T(8,128)S(1)} collective-permute-done((f32[16,8,128]{2,1,0:T(8,128)S(1)}, f32[16,8,128]{2,1,0:T(8,128)S(1)}, u32[]{:S(2)}, u32[]{:S(2)}) %collective-permute-start.6) | collective-permute-done | bytes 65568 | tf_op jit(solution)/shard_map/ppermute | solution.py:571
  45.3 2.7 %collective-permute-start.7 = (f32[16,8,128]{2,1,0:T(8,128)S(1)}, f32[16,8,128]{2,1,0:T(8,128)S(1)}, u32[]{:S(2)}, u32[]{:S(2)}) collective-permute-start(f32[16,8,128]{2,1,0:T(8,128)S(1)} %shard_map.87.refs_0_), channel_id=1, source_target_pairs={{0,2},{1,3},{2,0},{3,1},{4,6},{5,7},{6,4},{7,5},{8,10},{9,11},{10,... | collective-permute-start | bytes 196616 | tf_op jit(solution)/shard_map/ppermute | solution.py:571
  47.9 2.5 %all-to-all-start = ((f32[32,1,128]{2,1,0:T(1,128)}), f32[32,1,128]{2,1,0:T(1,128)S(1)}, u32[]{:S(2)}, u32[]{:S(2)}) async-start(f32[32,1,128]{2,1,0:T(1,128)} %bitcast.3), calls=%async_computation | async-start | bytes 32768 | tf_op jit(solution)/shard_map/all_to_all | solution.py:668
  50.5 0.0 collective-permute-done.7.refs_1_
  50.5 0.1 shard_map.88.refs_3_
  50.6 0.5 shard_map.86
  51.1 6.5 %all-to-all-done = f32[32,1,128]{2,1,0:T(1,128)S(1)} async-done(((f32[32,1,128]{2,1,0:T(1,128)}), f32[32,1,128]{2,1,0:T(1,128)S(1)}, u32[]{:S(2)}, u32[]{:S(2)}) %all-to-all-start) | async-done | bytes 16416 | tf_op jit(solution)/shard_map/all_to_all | solution.py:668
  57.6 0.3 shard_map.89
  57.9 0.7 collective-permute-start.8
  58.6 3.3 %collective-permute-start.9 = (f32[64,8,128]{2,1,0:T(8,128)S(1)}, f32[64,8,128]{2,1,0:T(8,128)S(1)}, u32[]{:S(2)}, u32[]{:S(2)}) collective-permute-start(f32[64,8,128]{2,1,0:T(8,128)S(1)} %get-tuple-element.67.mine_ref), channel_id=1, source_target_pairs={{0,16},{1,17},{2,18},{3,19},{4,0},{5,1},{6,2},{7,3},{8,20},{9,21},... | collective-permute-start | bytes 786440 | tf_op jit(solution)/shard_map/ppermute | solution.py:571
  62.0 2.0 %again.1 = (f32[16,8,128]{2,1,0:T(8,128)S(1)}, f32[64,8,128]{2,1,0:T(8,128)S(1)}, f32[64,8,128]{2,1,0:T(8,128)S(1)}, f32[1,128]{1,0:T(1,128)S(1)}, bf16[2,4,2,256,128]{4,3,2,1,0:T(8,128)(2,1)S(1)}) custom-call(f32[8,16]{1,0:T(8,128)S(1)} %bitcast.13, bf16[16,4,2,256,128]{4,3,2,1,0:T(8,128)(2,1)} %vis_hbm.7, f32[1,128]{1,0:T(1,128)S(1)} %get-tuple-element.45.samples_ref, ...), custom_call_target="tpu_custom_call" | custom-call | tf_op jit(solution)/shard_map/again/pallas_call | solution.py:621
  64.0 7.2 %collective-permute-done.9.b_ref.got_ref = f32[64,8,128]{2,1,0:T(8,128)S(1)} collective-permute-done((f32[64,8,128]{2,1,0:T(8,128)S(1)}, f32[64,8,128]{2,1,0:T(8,128)S(1)}, u32[]{:S(2)}, u32[]{:S(2)}) %collective-permute-start.9) | collective-permute-done | bytes 262176 | tf_op jit(solution)/shard_map/ppermute | solution.py:571
  71.2 5.1 %sums.3 = (f32[72,16,128]{2,1,0:T(8,128)S(1)}, f32[72,16,128]{2,1,0:T(8,128)S(1)}) custom-call(f32[8,16]{1,0:T(8,128)} %bitcast.12, bf16[16,4,2,256,128]{4,3,2,1,0:T(8,128)(2,1)} %vis_hbm.7, f32[64,128]{1,0:T(8,128)S(1)} %get-tuple-element.49.live_ref, f32[64,8,128]{2,1,0:T(8,128)S(1)} %collective-permute-done.8.a_ref, ...), custom_call_target="tpu_custom_call" | custom-call | tf_op jit(solution)/shard_map/sums/pallas_call | solution.py:633
  76.3 1.6 %collective-permute-start.10 = (f32[72,16,128]{2,1,0:T(8,128)S(1)}, f32[72,16,128]{2,1,0:T(8,128)S(1)}, u32[]{:S(2)}, u32[]{:S(2)}) collective-permute-start(f32[72,16,128]{2,1,0:T(8,128)S(1)} %get-tuple-element.70), channel_id=1, source_target_pairs={{0,4},{1,5},{2,6},{3,7},{4,0},{5,1},{6,2},{7,3},{8,12},{9,13},{10,... | collective-permute-start | bytes 1769480 | tf_op jit(solution)/shard_map/ppermute | solution.py:571
  77.9 3.6 %collective-permute-start.11 = (f32[64,8,128]{2,1,0:T(8,128)S(1)}, f32[64,8,128]{2,1,0:T(8,128)S(1)}, u32[]{:S(2)}, u32[]{:S(2)}) collective-permute-start(f32[64,8,128]{2,1,0:T(8,128)S(1)} %get-tuple-element.67.mine_ref), channel_id=1, source_target_pairs={{0,8},{1,9},{2,10},{3,11},{4,12},{5,13},{6,14},{7,15},{24,16},{25,... | collective-permute-start | bytes 786440 | tf_op jit(solution)/shard_map/ppermute | solution.py:571
  81.5 1.3 %collective-permute-start.12 = (f32[64,8,128]{2,1,0:T(8,128)S(1)}, f32[64,8,128]{2,1,0:T(8,128)S(1)}, u32[]{:S(2)}, u32[]{:S(2)}) collective-permute-start(f32[64,8,128]{2,1,0:T(8,128)S(1)} %collective-permute-done.8.a_ref), channel_id=1, source_target_pairs={{4,0},{5,1},{6,2},{7,3},{24,28},{25,29},{26,30},{27,31}} | collective-permute-start | bytes 786440 | tf_op jit(solution)/shard_map/ppermute | solution.py:571
  82.8 4.4 %collective-permute-done.11.theirs_ref = f32[64,8,128]{2,1,0:T(8,128)S(1)} collective-permute-done((f32[64,8,128]{2,1,0:T(8,128)S(1)}, f32[64,8,128]{2,1,0:T(8,128)S(1)}, u32[]{:S(2)}, u32[]{:S(2)}) %collective-permute-start.11) | collective-permute-done | bytes 262176 | tf_op jit(solution)/shard_map/ppermute | solution.py:571
  87.2 1.5 %residual.3 = (f32[65,8,128]{2,1,0:T(8,128)S(1)}, f32[65,8,128]{2,1,0:T(8,128)S(1)}, f32[32,128]{1,0:T(8,128)}) custom-call(f32[64,128]{1,0:T(8,128)S(1)} %get-tuple-element.44.live_ref, f32[1,128]{1,0:T(1,128)S(1)} %get-tuple-element.66.extra_ref, f32[1,128]{1,0:T(1,128)S(1)} %get-tuple-element.53.power_ref, f32[72,16,128]{2,1,0:T(8,128)S(1)} %get-tuple-element.69.kept_ref, ...), custom_call_target="tpu_custom_call" | custom-call | tf_op jit(solution)/shard_map/residual/pallas_call | solution.py:655
  88.7 2.5 %collective-permute-start.13 = (f32[65,8,128]{2,1,0:T(8,128)S(1)}, f32[65,8,128]{2,1,0:T(8,128)S(1)}, u32[]{:S(2)}, u32[]{:S(2)}) collective-permute-start(f32[65,8,128]{2,1,0:T(8,128)S(1)} %get-tuple-element.73), channel_id=1, source_target_pairs={{0,8},{1,9},{2,10},{3,11},{4,12},{5,13},{6,14},{7,15},{8,0},{9,1},... | collective-permute-start | bytes 798728 | tf_op jit(solution)/shard_map/ppermute | solution.py:571
  91.3 0.6 collective-permute-start.14
  91.9 3.6 %collective-permute-done.14.b_ref = f32[16,8,128]{2,1,0:T(8,128)S(1)} collective-permute-done((f32[16,8,128]{2,1,0:T(8,128)S(1)}, f32[16,8,128]{2,1,0:T(8,128)S(1)}, u32[]{:S(2)}, u32[]{:S(2)}) %collective-permute-start.14) | collective-permute-done | bytes 65568 | tf_op jit(solution)/shard_map/ppermute | solution.py:571
  95.5 0.6 collective-permute-start.15
  96.1 4.0 %all-to-all-start.1 = ((f32[32,1,128]{2,1,0:T(1,128)}), f32[32,1,128]{2,1,0:T(1,128)S(1)}, u32[]{:S(2)}, u32[]{:S(2)}) async-start(f32[32,1,128]{2,1,0:T(1,128)} %bitcast.6), calls=%async_computation.1 | async-start | bytes 32768 | tf_op jit(solution)/shard_map/all_to_all | solution.py:668
  100.2 1.3 %collective-permute-done.15.refs_1_ = f32[16,8,128]{2,1,0:T(8,128)S(1)} collective-permute-done((f32[16,8,128]{2,1,0:T(8,128)S(1)}, f32[16,8,128]{2,1,0:T(8,128)S(1)}, u32[]{:S(2)}, u32[]{:S(2)}) %collective-permute-start.15) | collective-permute-done | bytes 65568 | tf_op jit(solution)/shard_map/ppermute | solution.py:571
  101.5 0.1 shard_map.92
  101.6 0.5 shard_map.90
  102.1 5.2 %all-to-all-done.1 = f32[32,1,128]{2,1,0:T(1,128)S(1)} async-done(((f32[32,1,128]{2,1,0:T(1,128)}), f32[32,1,128]{2,1,0:T(1,128)S(1)}, u32[]{:S(2)}, u32[]{:S(2)}) %all-to-all-start.1) | async-done | bytes 16416 | tf_op jit(solution)/shard_map/all_to_all | solution.py:668
  107.3 0.2 shard_map.93
  107.6 0.5 collective-permute-start.16
  108.1 0.6 collective-permute-start.17
  108.8 3.3 %collective-permute-start.18 = (f32[16,8,128]{2,1,0:T(8,128)S(1)}, f32[16,8,128]{2,1,0:T(8,128)S(1)}, u32[]{:S(2)}, u32[]{:S(2)}) collective-permute-start(f32[16,8,128]{2,1,0:T(8,128)S(1)} %get-tuple-element.83.refs_0_), channel_id=1, source_target_pairs={{0,3},{1,2},{2,1},{3,0},{4,7},{5,6},{6,5},{7,4},{8,11},{9,10},{10,... | collective-permute-start | bytes 196616 | tf_op jit(solution)/shard_map/ppermute | solution.py:571
  112.0 0.9 shard_map.94
  112.9 3.2 %collective-permute-done.17.refs_2_ = f32[16,8,128]{2,1,0:T(8,128)S(1)} collective-permute-done((f32[16,8,128]{2,1,0:T(8,128)S(1)}, f32[16,8,128]{2,1,0:T(8,128)S(1)}, u32[]{:S(2)}, u32[]{:S(2)}) %collective-permute-start.17) | collective-permute-done | bytes 65568 | tf_op jit(solution)/shard_map/ppermute | solution.py:571
  116.1 0.9 shard_map.95
  (13 shorter events, 0.0 us)
Async XLA Ops:
  3.2 8.8 %collective-permute-start = (f32[64,8,128]{2,1,0:T(8,128)S(1)}, f32[64,8,128]{2,1,0:T(8,128)S(1)}, u32[]{:S(2)}, u32[]{:S(2)}) collective-permute-start(f32[64,8,128]{2,1,0:T(8,128)S(1)} %get-tuple-element.50.mine_ref), channel_id=1, source_target_pairs={{0,0},{1,1},{2,2},{3,3},{4,16},{5,17},{6,18},{7,19},{8,4},{9,5},{1... | collective-permute-start | bytes 786440 | tf_op jit(solution)/shard_map/ppermute | solution.py:571
  3.9 16.0 %collective-permute-start.1 = (f32[64,8,128]{2,1,0:T(8,128)S(1)}, f32[64,8,128]{2,1,0:T(8,128)S(1)}, u32[]{:S(2)}, u32[]{:S(2)}) collective-permute-start(f32[64,8,128]{2,1,0:T(8,128)S(1)} %get-tuple-element.50.mine_ref), channel_id=1, source_target_pairs={{0,16},{1,17},{2,18},{3,19},{4,0},{5,1},{6,2},{7,3},{8,20},{9,21},... | collective-permute-start | bytes 786440 | tf_op jit(solution)/shard_map/ppermute | solution.py:571
  11.9 50.0 %copy-start = (f32[16,8]{0,1:T(8,128)S(1)}, f32[16,8]{0,1:T(8,128)}, u32[]{:S(2)}) copy-start(f32[16,8]{0,1:T(8,128)} %param.11) | copy-start | bytes 1540
  25.9 11.1 %collective-permute-start.2 = (f32[72,16,128]{2,1,0:T(8,128)S(1)}, f32[72,16,128]{2,1,0:T(8,128)S(1)}, u32[]{:S(2)}, u32[]{:S(2)}) collective-permute-start(f32[72,16,128]{2,1,0:T(8,128)S(1)} %get-tuple-element.55), channel_id=1, source_target_pairs={{0,4},{1,5},{2,6},{3,7},{4,0},{5,1},{6,2},{7,3},{8,12},{9,13},{10,... | collective-permute-start | bytes 1769480 | tf_op jit(solution)/shard_map/ppermute | solution.py:571
  26.7 10.2 %collective-permute-start.3 = (f32[64,8,128]{2,1,0:T(8,128)S(1)}, f32[64,8,128]{2,1,0:T(8,128)S(1)}, u32[]{:S(2)}, u32[]{:S(2)}) collective-permute-start(f32[64,8,128]{2,1,0:T(8,128)S(1)} %get-tuple-element.50.mine_ref), channel_id=1, source_target_pairs={{0,8},{1,9},{2,10},{3,11},{4,12},{5,13},{6,14},{7,15},{24,16},{25,... | collective-permute-start | bytes 786440 | tf_op jit(solution)/shard_map/ppermute | solution.py:571
  30.8 6.2 %collective-permute-start.4 = (f32[64,8,128]{2,1,0:T(8,128)S(1)}, f32[64,8,128]{2,1,0:T(8,128)S(1)}, u32[]{:S(2)}, u32[]{:S(2)}) collective-permute-start(f32[64,8,128]{2,1,0:T(8,128)S(1)} %collective-permute-done.a_ref), channel_id=1, source_target_pairs={{4,0},{5,1},{6,2},{7,3},{24,28},{25,29},{26,30},{27,31}} | collective-permute-start | bytes 786440 | tf_op jit(solution)/shard_map/ppermute | solution.py:571
  38.5 12.2 %collective-permute-start.5 = (f32[65,8,128]{2,1,0:T(8,128)S(1)}, f32[65,8,128]{2,1,0:T(8,128)S(1)}, u32[]{:S(2)}, u32[]{:S(2)}) collective-permute-start(f32[65,8,128]{2,1,0:T(8,128)S(1)} %get-tuple-element.58), channel_id=1, source_target_pairs={{0,8},{1,9},{2,10},{3,11},{4,12},{5,13},{6,14},{7,15},{8,0},{9,1},... | collective-permute-start | bytes 798728 | tf_op jit(solution)/shard_map/ppermute | solution.py:571
  41.0 4.3 %collective-permute-start.6 = (f32[16,8,128]{2,1,0:T(8,128)S(1)}, f32[16,8,128]{2,1,0:T(8,128)S(1)}, u32[]{:S(2)}, u32[]{:S(2)}) collective-permute-start(f32[16,8,128]{2,1,0:T(8,128)S(1)} %get-tuple-element.64.a_ref), channel_id=1, source_target_pairs={{0,1},{1,0},{2,3},{3,2},{4,5},{5,4},{6,7},{7,6},{8,9},{9,8},{10,11... | collective-permute-start | bytes 196616 | tf_op jit(solution)/shard_map/ppermute | solution.py:571
  45.3 5.2 %collective-permute-start.7 = (f32[16,8,128]{2,1,0:T(8,128)S(1)}, f32[16,8,128]{2,1,0:T(8,128)S(1)}, u32[]{:S(2)}, u32[]{:S(2)}) collective-permute-start(f32[16,8,128]{2,1,0:T(8,128)S(1)} %shard_map.87.refs_0_), channel_id=1, source_target_pairs={{0,2},{1,3},{2,0},{3,1},{4,6},{5,7},{6,4},{7,5},{8,10},{9,11},{10,... | collective-permute-start | bytes 196616 | tf_op jit(solution)/shard_map/ppermute | solution.py:571
  47.9 9.7 %all-to-all-start = ((f32[32,1,128]{2,1,0:T(1,128)}), f32[32,1,128]{2,1,0:T(1,128)S(1)}, u32[]{:S(2)}, u32[]{:S(2)}) async-start(f32[32,1,128]{2,1,0:T(1,128)} %bitcast.3), calls=%async_computation | async-start | bytes 32768 | tf_op jit(solution)/shard_map/all_to_all | solution.py:668
  57.9 6.0 %collective-permute-start.8 = (f32[64,8,128]{2,1,0:T(8,128)S(1)}, f32[64,8,128]{2,1,0:T(8,128)S(1)}, u32[]{:S(2)}, u32[]{:S(2)}) collective-permute-start(f32[64,8,128]{2,1,0:T(8,128)S(1)} %get-tuple-element.67.mine_ref), channel_id=1, source_target_pairs={{0,0},{1,1},{2,2},{3,3},{4,16},{5,17},{6,18},{7,19},{8,4},{9,5},{1... | collective-permute-start | bytes 786440 | tf_op jit(solution)/shard_map/ppermute | solution.py:571
  58.6 12.6 %collective-permute-start.9 = (f32[64,8,128]{2,1,0:T(8,128)S(1)}, f32[64,8,128]{2,1,0:T(8,128)S(1)}, u32[]{:S(2)}, u32[]{:S(2)}) collective-permute-start(f32[64,8,128]{2,1,0:T(8,128)S(1)} %get-tuple-element.67.mine_ref), channel_id=1, source_target_pairs={{0,16},{1,17},{2,18},{3,19},{4,0},{5,1},{6,2},{7,3},{8,20},{9,21},... | collective-permute-start | bytes 786440 | tf_op jit(solution)/shard_map/ppermute | solution.py:571
  76.3 10.9 %collective-permute-start.10 = (f32[72,16,128]{2,1,0:T(8,128)S(1)}, f32[72,16,128]{2,1,0:T(8,128)S(1)}, u32[]{:S(2)}, u32[]{:S(2)}) collective-permute-start(f32[72,16,128]{2,1,0:T(8,128)S(1)} %get-tuple-element.70), channel_id=1, source_target_pairs={{0,4},{1,5},{2,6},{3,7},{4,0},{5,1},{6,2},{7,3},{8,12},{9,13},{10,... | collective-permute-start | bytes 1769480 | tf_op jit(solution)/shard_map/ppermute | solution.py:571
  77.9 9.3 %collective-permute-start.11 = (f32[64,8,128]{2,1,0:T(8,128)S(1)}, f32[64,8,128]{2,1,0:T(8,128)S(1)}, u32[]{:S(2)}, u32[]{:S(2)}) collective-permute-start(f32[64,8,128]{2,1,0:T(8,128)S(1)} %get-tuple-element.67.mine_ref), channel_id=1, source_target_pairs={{0,8},{1,9},{2,10},{3,11},{4,12},{5,13},{6,14},{7,15},{24,16},{25,... | collective-permute-start | bytes 786440 | tf_op jit(solution)/shard_map/ppermute | solution.py:571
  81.5 5.7 %collective-permute-start.12 = (f32[64,8,128]{2,1,0:T(8,128)S(1)}, f32[64,8,128]{2,1,0:T(8,128)S(1)}, u32[]{:S(2)}, u32[]{:S(2)}) collective-permute-start(f32[64,8,128]{2,1,0:T(8,128)S(1)} %collective-permute-done.8.a_ref), channel_id=1, source_target_pairs={{4,0},{5,1},{6,2},{7,3},{24,28},{25,29},{26,30},{27,31}} | collective-permute-start | bytes 786440 | tf_op jit(solution)/shard_map/ppermute | solution.py:571
  88.7 12.9 %collective-permute-start.13 = (f32[65,8,128]{2,1,0:T(8,128)S(1)}, f32[65,8,128]{2,1,0:T(8,128)S(1)}, u32[]{:S(2)}, u32[]{:S(2)}) collective-permute-start(f32[65,8,128]{2,1,0:T(8,128)S(1)} %get-tuple-element.73), channel_id=1, source_target_pairs={{0,8},{1,9},{2,10},{3,11},{4,12},{5,13},{6,14},{7,15},{8,0},{9,1},... | collective-permute-start | bytes 798728 | tf_op jit(solution)/shard_map/ppermute | solution.py:571
  91.3 4.3 %collective-permute-start.14 = (f32[16,8,128]{2,1,0:T(8,128)S(1)}, f32[16,8,128]{2,1,0:T(8,128)S(1)}, u32[]{:S(2)}, u32[]{:S(2)}) collective-permute-start(f32[16,8,128]{2,1,0:T(8,128)S(1)} %get-tuple-element.78.a_ref), channel_id=1, source_target_pairs={{0,1},{1,0},{2,3},{3,2},{4,5},{5,4},{6,7},{7,6},{8,9},{9,8},{10,11... | collective-permute-start | bytes 196616 | tf_op jit(solution)/shard_map/ppermute | solution.py:571
  95.5 5.9 %collective-permute-start.15 = (f32[16,8,128]{2,1,0:T(8,128)S(1)}, f32[16,8,128]{2,1,0:T(8,128)S(1)}, u32[]{:S(2)}, u32[]{:S(2)}) collective-permute-start(f32[16,8,128]{2,1,0:T(8,128)S(1)} %shard_map.91.refs_0_), channel_id=1, source_target_pairs={{0,2},{1,3},{2,0},{3,1},{4,6},{5,7},{6,4},{7,5},{8,10},{9,11},{10,... | collective-permute-start | bytes 196616 | tf_op jit(solution)/shard_map/ppermute | solution.py:571
  96.1 11.2 %all-to-all-start.1 = ((f32[32,1,128]{2,1,0:T(1,128)}), f32[32,1,128]{2,1,0:T(1,128)S(1)}, u32[]{:S(2)}, u32[]{:S(2)}) async-start(f32[32,1,128]{2,1,0:T(1,128)} %bitcast.6), calls=%async_computation.1 | async-start | bytes 32768 | tf_op jit(solution)/shard_map/all_to_all | solution.py:668
  107.6 5.4 %collective-permute-start.16 = (f32[16,8,128]{2,1,0:T(8,128)S(1)}, f32[16,8,128]{2,1,0:T(8,128)S(1)}, u32[]{:S(2)}, u32[]{:S(2)}) collective-permute-start(f32[16,8,128]{2,1,0:T(8,128)S(1)} %get-tuple-element.83.refs_0_), channel_id=1, source_target_pairs={{0,1},{1,0},{2,3},{3,2},{4,5},{5,4},{6,7},{7,6},{8,9},{9,8},{10,11... | collective-permute-start | bytes 196616 | tf_op jit(solution)/shard_map/ppermute | solution.py:571
  108.1 8.0 %collective-permute-start.17 = (f32[16,8,128]{2,1,0:T(8,128)S(1)}, f32[16,8,128]{2,1,0:T(8,128)S(1)}, u32[]{:S(2)}, u32[]{:S(2)}) collective-permute-start(f32[16,8,128]{2,1,0:T(8,128)S(1)} %get-tuple-element.83.refs_0_), channel_id=1, source_target_pairs={{0,2},{1,3},{2,0},{3,1},{4,6},{5,7},{6,4},{7,5},{8,10},{9,11},{10,... | collective-permute-start | bytes 196616 | tf_op jit(solution)/shard_map/ppermute | solution.py:571
  108.8 7.4 %collective-permute-start.18 = (f32[16,8,128]{2,1,0:T(8,128)S(1)}, f32[16,8,128]{2,1,0:T(8,128)S(1)}, u32[]{:S(2)}, u32[]{:S(2)}) collective-permute-start(f32[16,8,128]{2,1,0:T(8,128)S(1)} %get-tuple-element.83.refs_0_), channel_id=1, source_target_pairs={{0,3},{1,2},{2,1},{3,0},{4,7},{5,6},{6,5},{7,4},{8,11},{9,10},{10,... | collective-permute-start | bytes 196616 | tf_op jit(solution)/shard_map/ppermute | solution.py:571

commit v9 on v8

--- a/solution.py
+++ b/solution.py
@@ -14,6 +14,7 @@
 HIGH = lax.Precision.HIGHEST
 AXES = ("row", "col", "band")
 CHUNK = 4
+PARTS = 4
 HEAD = 2
 LIMIT = pltpu.CompilerParams(vmem_limit_bytes=16 * 2**20)
 
@@ -75,8 +76,11 @@
     copies = [
         pltpu.make_async_copy(pos_hbm, pos_ref, sems.at[0]),
         pltpu.make_async_copy(lmn_hbm, lmn_ref, sems.at[1]),
-        pltpu.make_async_copy(gains_hbm, gains_ref, sems.at[2]),
     ]
+    part = F // PARTS
+    for i in range(PARTS):
+        at = pl.ds(i * part, part)
+        copies.append(pltpu.make_async_copy(gains_hbm.at[at], gains_ref.at[at], sems.at[2 + i]))
     for copy in copies:
         copy.start()
     own = lax.axis_index("row") * C + lax.axis_index("col")
@@ -107,8 +111,9 @@
             turns = nu * geometry[t]
             r = turns - jnp.round(turns) + shift
             e_ref[ft] = cos_turns(r - jnp.round(r))
-    copies[2].wait()
     for f in range(F):
+        if f % part == 0:
+            copies[2 + f // part].wait()
         for t in range(T):
             ft = f * T + t
             g = jnp.concatenate([gains_ref[f, t, 0], gains_ref[f, t, 1]], axis=-1)
@@ -263,6 +268,18 @@
             outs[0][ft] = smooth - u
 
 
+def halves(x):
+    high = x.astype(jnp.bfloat16)
+    return high, (x - high.astype(jnp.float32)).astype(jnp.bfloat16)
+
+
+def product(a, b):
+    (a0, a1), (b0, b1) = halves(a), halves(b)
+    out = jnp.dot(a0, b1, preferred_element_type=jnp.float32)
+    out = out + jnp.dot(a1, b0, preferred_element_type=jnp.float32)
+    return out + jnp.dot(a0, b0, preferred_element_type=jnp.float32)
+
+
 def block_mask(size):
     shape = (8 * size, 8 * size)
     a = lax.broadcasted_iota(jnp.int32, shape, 0) // size
@@ -286,8 +303,7 @@
 
     flux_copy = pltpu.make_async_copy(flux_hbm, flux_ref, sems.at[F])
     flux_copy.start()
-    ahead = 2 * CHUNK
-    for f in range(HEAD, ahead):
+    for f in range(HEAD, F):
         vis_copy(f).start()
     p = lax.broadcasted_iota(jnp.int32, (rows, cols), 0) + row * rows
     q = lax.broadcasted_iota(jnp.int32, (rows, cols), 1) + col * cols
@@ -360,11 +376,6 @@
         for i in range(CHUNK):
             vis_copy(c * CHUNK + i).wait()
 
-        @pl.when(c * CHUNK + ahead < F)
-        def _():
-            for i in range(CHUNK):
-                vis_copy(c * CHUNK + ahead + i).start()
-
         upright = roll_to(c)
         for j in range(CHUNK // group):
             power = body(c * (CHUNK // group) + j, upright, j * 8, power, vis_ref)
@@ -379,8 +390,6 @@
             for i in range(group):
                 vis_copy(j * group + i).wait()
         power = body(j, upright, j * 8, power, head_ref if inside else vis_ref)
-    for i in range(CHUNK):
-        vis_copy(ahead + i).start()
     power = lax.fori_loop(1, F // CHUNK, chunk, power)
     if power_ref is not None:
         power = jnp.sum(power, axis=0, keepdims=True)
@@ -415,10 +424,7 @@
             first = jnp.where(near, a, b)
             second = jnp.where(near, b, a)
             station += [join_low(first, second), join_high(first, second)]
-        model = jnp.dot(
-            spread, jnp.concatenate(station, axis=0), precision=HIGH,
-            preferred_element_type=jnp.float32,
-        )
+        model = product(spread, jnp.concatenate(station, axis=0))
         lives = live_ref[pl.ds(group * 8, 8), :]
         for i in range(8):
             ft = group * 8 + i
@@ -455,12 +461,14 @@
     a = lax.broadcasted_iota(jnp.int32, shape, 0)
     b = lax.broadcasted_iota(jnp.int32, shape, 1)
     eye = a // D * (2 * D) + a % D == b
-    ones = jnp.ones((W, W), jnp.float32)
+    ones = jnp.ones((W, W), jnp.bfloat16)
     for group in range(F * T // 8):
         diagonal = keep_ref[F * T, group : group + 1, :] + come_ref[F * T, group : group + 1, :]
-        spread = jnp.dot(
-            jnp.where(eye, diagonal, 0.0), ones, precision=HIGH, preferred_element_type=jnp.float32
-        )
+        rest, spread = jnp.where(eye, diagonal, 0.0), 0.0
+        for _ in range(3):
+            high = rest.astype(jnp.bfloat16)
+            rest = rest - high.astype(jnp.float32)
+            spread = spread + jnp.dot(high, ones, preferred_element_type=jnp.float32)
         for i in range(8):
             ft = group * 8 + i
             around = live_ref[ft : ft + 1, :] * spread[i * D : (i + 1) * D]
@@ -589,7 +597,7 @@
             pltpu.VMEM((3, T, full), f32),
             pltpu.SMEM(lmn.shape, f32),
             pltpu.VMEM(gains.shape, f32),
-            pltpu.SemaphoreType.DMA((3,)),
+            pltpu.SemaphoreType.DMA((2 + PARTS,)),
         ],
         compiler_params=LIMIT,
         name="start",

time: 117 us -> 116 us (level)
  Pallas kernels: 24.6 us -> 23.1 us
  transfers between devices with their start and end apart: 21 -> 21, of which waited for: 10 -> 10; matrix products, arithmetic and copies ran while one was open for 0% -> 0% of each run, Pallas kernels for 6% -> 5%
where the time goes in v9:
time: 116 us
  waiting for transfers between devices  47.2 us (41%)
  starting transfers between devices  44.7 us (39%)
  Pallas kernels  23.1 us (20%)
    ppermute x19, starting transfers between devices, permute(): return lax.ppermute(x, AXES, pairs)  38.1 us
    ppermute x19, waiting for transfers between devices, permute(): return lax.ppermute(x, AXES, pairs)  35.3 us
    all_to_all x2, waiting for transfers between devices, shards(): scalar = lax.all_to_all(scalar, AXES, 0, 0, tiled=True)  12 us
    pallas_call x2, Pallas kernels, shards(): pl.pallas_call(functools.partial(sum_kernel, dims), out_shape=[pair, pair...  10.7 us
    all_to_all x2, starting transfers between devices, shards(): scalar = lax.all_to_all(scalar, AXES, 0, 0, tiled=True)  6.59 us
    pallas_call x2, Pallas kernels, shards(): pl.pallas_call(functools.partial(residual_kernel, dims), out_shape=[line,...  2.43 us
    pallas_call x1, Pallas kernels, shards(): pl.pallas_call(functools.partial(setup_kernel, dims, cols), out_shape=[ar...  2.34 us
  transfers between devices with their start and end apart: 21, of which 10 were waited for; matrix products, arithmetic and copies ran while one was open for 0% of the time, Pallas kernels for 5%

profile of v9, /device:TPU:0, one launch (start us, length us, event | category | flops | bytes accessed | tf_op | source)
XLA Modules:
  0.0 115.8 jit_solution(1976201608380885123)
XLA Ops:
  0.6 2.2 %start.1 = (f32[64,8,128]{2,1,0:T(8,128)S(1)}, f32[64,8,128]{2,1,0:T(8,128)S(1)}, f32[64,8,128]{2,1,0:T(8,128)S(1)}) custom-call(f32[3,4,512]{2,1,0:T(4,128)} %bitcast.16, f32[3,8]{1,0:T(4,128)} %lmn_hbm.1, f32[16,4,2,8,64]{4,3,2,1,0:T(8,128)} %gains_hbm.1), custom_call_target="tpu_custom_call" | custom-call | tf_op jit(solution)/shard_map/start/pallas_call | solution.py:591
  2.9 0.7 collective-permute-start
  3.6 5.7 %collective-permute-start.1 = (f32[64,8,128]{2,1,0:T(8,128)S(1)}, f32[64,8,128]{2,1,0:T(8,128)S(1)}, u32[]{:S(2)}, u32[]{:S(2)}) collective-permute-start(f32[64,8,128]{2,1,0:T(8,128)S(1)} %get-tuple-element.50.mine_ref), channel_id=1, source_target_pairs={{0,16},{1,17},{2,18},{3,19},{4,0},{5,1},{6,2},{7,3},{8,20},{9,21},... | collective-permute-start | bytes 786440 | tf_op jit(solution)/shard_map/ppermute | solution.py:579
  9.3 2.3 %setup.1 = (f32[64,128]{1,0:T(8,128)S(1)}, f32[64,128]{1,0:T(8,128)S(1)}, f32[64,128]{1,0:T(8,128)S(1)}, f32[256,128]{1,0:T(8,128)S(1)}, f32[64,8,128]{2,1,0:T(8...) custom-call(f32[8,16]{1,0:T(8,128)} %bitcast.10, ...), custom_call_target="tpu_custom_call" | custom-call | tf_op jit(solution)/shard_map/setup/pallas_call | solution.py:610
  11.6 0.0 copy-start
  11.7 7.9 %collective-permute-done.1.b_ref.got_ref = f32[64,8,128]{2,1,0:T(8,128)S(1)} collective-permute-done((f32[64,8,128]{2,1,0:T(8,128)S(1)}, f32[64,8,128]{2,1,0:T(8,128)S(1)}, u32[]{:S(2)}, u32[]{:S(2)}) %collective-permute-start.1) | collective-permute-done | bytes 262176 | tf_op jit(solution)/shard_map/ppermute | solution.py:579
  19.6 6.0 %sums.2 = (f32[72,16,128]{2,1,0:T(8,128)S(1)}, f32[72,16,128]{2,1,0:T(8,128)S(1)}, f32[1,128]{1,0:T(1,128)S(1)}) custom-call(f32[8,16]{1,0:T(8,128)} %bitcast.11, bf16[16,4,2,256,128]{4,3,2,1,0:T(8,128)(2,1)} %vis_hbm.7, f32[64,128]{1,0:T(8,128)S(1)} %get-tuple-element.49.live_ref, f32[64,8,128]{2,1,0:T(8,128)S(1)} %collective-permute-done.a_ref, ...), custom_call_target="tpu_custom_call" | custom-call | tf_op jit(solution)/shard_map/sums/pallas_call | solution.py:641
  25.5 0.9 collective-permute-start.2
  26.4 4.0 %collective-permute-start.3 = (f32[64,8,128]{2,1,0:T(8,128)S(1)}, f32[64,8,128]{2,1,0:T(8,128)S(1)}, u32[]{:S(2)}, u32[]{:S(2)}) collective-permute-start(f32[64,8,128]{2,1,0:T(8,128)S(1)} %get-tuple-element.50.mine_ref), channel_id=1, source_target_pairs={{0,8},{1,9},{2,10},{3,11},{4,12},{5,13},{6,14},{7,15},{24,16},{25,... | collective-permute-start | bytes 786440 | tf_op jit(solution)/shard_map/ppermute | solution.py:579
  30.4 1.3 %collective-permute-start.4 = (f32[64,8,128]{2,1,0:T(8,128)S(1)}, f32[64,8,128]{2,1,0:T(8,128)S(1)}, u32[]{:S(2)}, u32[]{:S(2)}) collective-permute-start(f32[64,8,128]{2,1,0:T(8,128)S(1)} %collective-permute-done.a_ref), channel_id=1, source_target_pairs={{4,0},{5,1},{6,2},{7,3},{24,28},{25,29},{26,30},{27,31}} | collective-permute-start | bytes 786440 | tf_op jit(solution)/shard_map/ppermute | solution.py:579
  31.7 4.9 %collective-permute-done.3.theirs_ref = f32[64,8,128]{2,1,0:T(8,128)S(1)} collective-permute-done((f32[64,8,128]{2,1,0:T(8,128)S(1)}, f32[64,8,128]{2,1,0:T(8,128)S(1)}, u32[]{:S(2)}, u32[]{:S(2)}) %collective-permute-start.3) | collective-permute-done | bytes 262176 | tf_op jit(solution)/shard_map/ppermute | solution.py:579
  36.6 1.2 %residual.2 = (f32[65,8,128]{2,1,0:T(8,128)S(1)}, f32[65,8,128]{2,1,0:T(8,128)S(1)}, f32[32,128]{1,0:T(8,128)}) custom-call(f32[64,128]{1,0:T(8,128)S(1)} %get-tuple-element.44.live_ref, f32[1,128]{1,0:T(1,128)S(1)} %get-tuple-element.48.extra_ref, f32[1,128]{1,0:T(1,128)S(1)} %get-tuple-element.53.power_ref, f32[72,16,128]{2,1,0:T(8,128)S(1)} %get-tuple-element.54.kept_ref, ...), custom_call_target="tpu_custom_call" | custom-call | tf_op jit(solution)/shard_map/residual/pallas_call | solution.py:663
  37.9 2.5 %collective-permute-start.5 = (f32[65,8,128]{2,1,0:T(8,128)S(1)}, f32[65,8,128]{2,1,0:T(8,128)S(1)}, u32[]{:S(2)}, u32[]{:S(2)}) collective-permute-start(f32[65,8,128]{2,1,0:T(8,128)S(1)} %get-tuple-element.58), channel_id=1, source_target_pairs={{0,8},{1,9},{2,10},{3,11},{4,12},{5,13},{6,14},{7,15},{8,0},{9,1},... | collective-permute-start | bytes 798728 | tf_op jit(solution)/shard_map/ppermute | solution.py:579
  40.4 1.6 %collective-permute-start.6 = (f32[16,8,128]{2,1,0:T(8,128)S(1)}, f32[16,8,128]{2,1,0:T(8,128)S(1)}, u32[]{:S(2)}, u32[]{:S(2)}) collective-permute-start(f32[16,8,128]{2,1,0:T(8,128)S(1)} %get-tuple-element.64.a_ref), channel_id=1, source_target_pairs={{0,1},{1,0},{2,3},{3,2},{4,5},{5,4},{6,7},{7,6},{8,9},{9,8},{10,11... | collective-permute-start | bytes 196616 | tf_op jit(solution)/shard_map/ppermute | solution.py:579
  42.0 2.7 %collective-permute-done.6.b_ref = f32[16,8,128]{2,1,0:T(8,128)S(1)} collective-permute-done((f32[16,8,128]{2,1,0:T(8,128)S(1)}, f32[16,8,128]{2,1,0:T(8,128)S(1)}, u32[]{:S(2)}, u32[]{:S(2)}) %collective-permute-start.6) | collective-permute-done | bytes 65568 | tf_op jit(solution)/shard_map/ppermute | solution.py:579
  44.7 2.7 %collective-permute-start.7 = (f32[16,8,128]{2,1,0:T(8,128)S(1)}, f32[16,8,128]{2,1,0:T(8,128)S(1)}, u32[]{:S(2)}, u32[]{:S(2)}) collective-permute-start(f32[16,8,128]{2,1,0:T(8,128)S(1)} %shard_map.87.refs_0_), channel_id=1, source_target_pairs={{0,2},{1,3},{2,0},{3,1},{4,6},{5,7},{6,4},{7,5},{8,10},{9,11},{10,... | collective-permute-start | bytes 196616 | tf_op jit(solution)/shard_map/ppermute | solution.py:579
  47.3 2.5 %all-to-all-start = ((f32[32,1,128]{2,1,0:T(1,128)}), f32[32,1,128]{2,1,0:T(1,128)S(1)}, u32[]{:S(2)}, u32[]{:S(2)}) async-start(f32[32,1,128]{2,1,0:T(1,128)} %bitcast.3), calls=%async_computation | async-start | bytes 32768 | tf_op jit(solution)/shard_map/all_to_all | solution.py:676
  49.9 0.0 collective-permute-done.7.refs_1_
  49.9 0.1 shard_map.88.refs_3_
  50.0 0.4 shard_map.86
  50.4 6.6 %all-to-all-done = f32[32,1,128]{2,1,0:T(1,128)S(1)} async-done(((f32[32,1,128]{2,1,0:T(1,128)}), f32[32,1,128]{2,1,0:T(1,128)S(1)}, u32[]{:S(2)}, u32[]{:S(2)}) %all-to-all-start) | async-done | bytes 16416 | tf_op jit(solution)/shard_map/all_to_all | solution.py:676
  57.0 0.3 shard_map.89
  57.3 0.7 collective-permute-start.8
  58.0 3.3 %collective-permute-start.9 = (f32[64,8,128]{2,1,0:T(8,128)S(1)}, f32[64,8,128]{2,1,0:T(8,128)S(1)}, u32[]{:S(2)}, u32[]{:S(2)}) collective-permute-start(f32[64,8,128]{2,1,0:T(8,128)S(1)} %get-tuple-element.67.mine_ref), channel_id=1, source_target_pairs={{0,16},{1,17},{2,18},{3,19},{4,0},{5,1},{6,2},{7,3},{8,20},{9,21},... | collective-permute-start | bytes 786440 | tf_op jit(solution)/shard_map/ppermute | solution.py:579
  61.3 2.0 %again.1 = (f32[16,8,128]{2,1,0:T(8,128)S(1)}, f32[64,8,128]{2,1,0:T(8,128)S(1)}, f32[64,8,128]{2,1,0:T(8,128)S(1)}, f32[1,128]{1,0:T(1,128)S(1)}, bf16[2,4,2,256,128]{4,3,2,1,0:T(8,128)(2,1)S(1)}) custom-call(f32[8,16]{1,0:T(8,128)S(1)} %bitcast.13, bf16[16,4,2,256,128]{4,3,2,1,0:T(8,128)(2,1)} %vis_hbm.7, f32[1,128]{1,0:T(1,128)S(1)} %get-tuple-element.45.samples_ref, ...), custom_call_target="tpu_custom_call" | custom-call | tf_op jit(solution)/shard_map/again/pallas_call | solution.py:629
  63.4 7.2 %collective-permute-done.9.b_ref.got_ref = f32[64,8,128]{2,1,0:T(8,128)S(1)} collective-permute-done((f32[64,8,128]{2,1,0:T(8,128)S(1)}, f32[64,8,128]{2,1,0:T(8,128)S(1)}, u32[]{:S(2)}, u32[]{:S(2)}) %collective-permute-start.9) | collective-permute-done | bytes 262176 | tf_op jit(solution)/shard_map/ppermute | solution.py:579
  70.6 4.7 %sums.3 = (f32[72,16,128]{2,1,0:T(8,128)S(1)}, f32[72,16,128]{2,1,0:T(8,128)S(1)}) custom-call(f32[8,16]{1,0:T(8,128)} %bitcast.12, bf16[16,4,2,256,128]{4,3,2,1,0:T(8,128)(2,1)} %vis_hbm.7, f32[64,128]{1,0:T(8,128)S(1)} %get-tuple-element.49.live_ref, f32[64,8,128]{2,1,0:T(8,128)S(1)} %collective-permute-done.8.a_ref, ...), custom_call_target="tpu_custom_call" | custom-call | tf_op jit(solution)/shard_map/sums/pallas_call | solution.py:641
  75.3 1.6 %collective-permute-start.10 = (f32[72,16,128]{2,1,0:T(8,128)S(1)}, f32[72,16,128]{2,1,0:T(8,128)S(1)}, u32[]{:S(2)}, u32[]{:S(2)}) collective-permute-start(f32[72,16,128]{2,1,0:T(8,128)S(1)} %get-tuple-element.70), channel_id=1, source_target_pairs={{0,4},{1,5},{2,6},{3,7},{4,0},{5,1},{6,2},{7,3},{8,12},{9,13},{10,... | collective-permute-start | bytes 1769480 | tf_op jit(solution)/shard_map/ppermute | solution.py:579
  76.9 3.6 %collective-permute-start.11 = (f32[64,8,128]{2,1,0:T(8,128)S(1)}, f32[64,8,128]{2,1,0:T(8,128)S(1)}, u32[]{:S(2)}, u32[]{:S(2)}) collective-permute-start(f32[64,8,128]{2,1,0:T(8,128)S(1)} %get-tuple-element.67.mine_ref), channel_id=1, source_target_pairs={{0,8},{1,9},{2,10},{3,11},{4,12},{5,13},{6,14},{7,15},{24,16},{25,... | collective-permute-start | bytes 786440 | tf_op jit(solution)/shard_map/ppermute | solution.py:579
  80.5 1.3 %collective-permute-start.12 = (f32[64,8,128]{2,1,0:T(8,128)S(1)}, f32[64,8,128]{2,1,0:T(8,128)S(1)}, u32[]{:S(2)}, u32[]{:S(2)}) collective-permute-start(f32[64,8,128]{2,1,0:T(8,128)S(1)} %collective-permute-done.8.a_ref), channel_id=1, source_target_pairs={{4,0},{5,1},{6,2},{7,3},{24,28},{25,29},{26,30},{27,31}} | collective-permute-start | bytes 786440 | tf_op jit(solution)/shard_map/ppermute | solution.py:579
  81.8 4.4 %collective-permute-done.11.theirs_ref = f32[64,8,128]{2,1,0:T(8,128)S(1)} collective-permute-done((f32[64,8,128]{2,1,0:T(8,128)S(1)}, f32[64,8,128]{2,1,0:T(8,128)S(1)}, u32[]{:S(2)}, u32[]{:S(2)}) %collective-permute-start.11) | collective-permute-done | bytes 262176 | tf_op jit(solution)/shard_map/ppermute | solution.py:579
  86.2 1.2 %residual.3 = (f32[65,8,128]{2,1,0:T(8,128)S(1)}, f32[65,8,128]{2,1,0:T(8,128)S(1)}, f32[32,128]{1,0:T(8,128)}) custom-call(f32[64,128]{1,0:T(8,128)S(1)} %get-tuple-element.44.live_ref, f32[1,128]{1,0:T(1,128)S(1)} %get-tuple-element.66.extra_ref, f32[1,128]{1,0:T(1,128)S(1)} %get-tuple-element.53.power_ref, f32[72,16,128]{2,1,0:T(8,128)S(1)} %get-tuple-element.69.kept_ref, ...), custom_call_target="tpu_custom_call" | custom-call | tf_op jit(solution)/shard_map/residual/pallas_call | solution.py:663
  87.4 2.5 %collective-permute-start.13 = (f32[65,8,128]{2,1,0:T(8,128)S(1)}, f32[65,8,128]{2,1,0:T(8,128)S(1)}, u32[]{:S(2)}, u32[]{:S(2)}) collective-permute-start(f32[65,8,128]{2,1,0:T(8,128)S(1)} %get-tuple-element.73), channel_id=1, source_target_pairs={{0,8},{1,9},{2,10},{3,11},{4,12},{5,13},{6,14},{7,15},{8,0},{9,1},... | collective-permute-start | bytes 798728 | tf_op jit(solution)/shard_map/ppermute | solution.py:579
  90.0 0.6 collective-permute-start.14
  90.6 3.6 %collective-permute-done.14.b_ref = f32[16,8,128]{2,1,0:T(8,128)S(1)} collective-permute-done((f32[16,8,128]{2,1,0:T(8,128)S(1)}, f32[16,8,128]{2,1,0:T(8,128)S(1)}, u32[]{:S(2)}, u32[]{:S(2)}) %collective-permute-start.14) | collective-permute-done | bytes 65568 | tf_op jit(solution)/shard_map/ppermute | solution.py:579
  94.3 0.6 collective-permute-start.15
  94.9 4.0 %all-to-all-start.1 = ((f32[32,1,128]{2,1,0:T(1,128)}), f32[32,1,128]{2,1,0:T(1,128)S(1)}, u32[]{:S(2)}, u32[]{:S(2)}) async-start(f32[32,1,128]{2,1,0:T(1,128)} %bitcast.6), calls=%async_computation.1 | async-start | bytes 32768 | tf_op jit(solution)/shard_map/all_to_all | solution.py:676
  98.9 1.3 %collective-permute-done.15.refs_1_ = f32[16,8,128]{2,1,0:T(8,128)S(1)} collective-permute-done((f32[16,8,128]{2,1,0:T(8,128)S(1)}, f32[16,8,128]{2,1,0:T(8,128)S(1)}, u32[]{:S(2)}, u32[]{:S(2)}) %collective-permute-start.15) | collective-permute-done | bytes 65568 | tf_op jit(solution)/shard_map/ppermute | solution.py:579
  100.2 0.1 shard_map.92
  100.3 0.4 shard_map.90
  100.7 5.3 %all-to-all-done.1 = f32[32,1,128]{2,1,0:T(1,128)S(1)} async-done(((f32[32,1,128]{2,1,0:T(1,128)}), f32[32,1,128]{2,1,0:T(1,128)S(1)}, u32[]{:S(2)}, u32[]{:S(2)}) %all-to-all-start.1) | async-done | bytes 16416 | tf_op jit(solution)/shard_map/all_to_all | solution.py:676
  106.0 0.2 shard_map.93
  106.3 0.5 collective-permute-start.16
  106.8 0.6 collective-permute-start.17
  107.5 3.3 %collective-permute-start.18 = (f32[16,8,128]{2,1,0:T(8,128)S(1)}, f32[16,8,128]{2,1,0:T(8,128)S(1)}, u32[]{:S(2)}, u32[]{:S(2)}) collective-permute-start(f32[16,8,128]{2,1,0:T(8,128)S(1)} %get-tuple-element.83.refs_0_), channel_id=1, source_target_pairs={{0,3},{1,2},{2,1},{3,0},{4,7},{5,6},{6,5},{7,4},{8,11},{9,10},{10,... | collective-permute-start | bytes 196616 | tf_op jit(solution)/shard_map/ppermute | solution.py:579
  110.7 0.9 shard_map.94
  111.7 3.2 %collective-permute-done.17.refs_2_ = f32[16,8,128]{2,1,0:T(8,128)S(1)} collective-permute-done((f32[16,8,128]{2,1,0:T(8,128)S(1)}, f32[16,8,128]{2,1,0:T(8,128)S(1)}, u32[]{:S(2)}, u32[]{:S(2)}) %collective-permute-start.17) | collective-permute-done | bytes 65568 | tf_op jit(solution)/shard_map/ppermute | solution.py:579
  114.9 0.9 shard_map.95
  (13 shorter events, 0.0 us)
Async XLA Ops:
  2.9 8.8 %collective-permute-start = (f32[64,8,128]{2,1,0:T(8,128)S(1)}, f32[64,8,128]{2,1,0:T(8,128)S(1)}, u32[]{:S(2)}, u32[]{:S(2)}) collective-permute-start(f32[64,8,128]{2,1,0:T(8,128)S(1)} %get-tuple-element.50.mine_ref), channel_id=1, source_target_pairs={{0,0},{1,1},{2,2},{3,3},{4,16},{5,17},{6,18},{7,19},{8,4},{9,5},{1... | collective-permute-start | bytes 786440 | tf_op jit(solution)/shard_map/ppermute | solution.py:579
  3.6 16.0 %collective-permute-start.1 = (f32[64,8,128]{2,1,0:T(8,128)S(1)}, f32[64,8,128]{2,1,0:T(8,128)S(1)}, u32[]{:S(2)}, u32[]{:S(2)}) collective-permute-start(f32[64,8,128]{2,1,0:T(8,128)S(1)} %get-tuple-element.50.mine_ref), channel_id=1, source_target_pairs={{0,16},{1,17},{2,18},{3,19},{4,0},{5,1},{6,2},{7,3},{8,20},{9,21},... | collective-permute-start | bytes 786440 | tf_op jit(solution)/shard_map/ppermute | solution.py:579
  11.6 49.7 %copy-start = (f32[16,8]{0,1:T(8,128)S(1)}, f32[16,8]{0,1:T(8,128)}, u32[]{:S(2)}) copy-start(f32[16,8]{0,1:T(8,128)} %param.11) | copy-start | bytes 1540
  25.5 11.1 %collective-permute-start.2 = (f32[72,16,128]{2,1,0:T(8,128)S(1)}, f32[72,16,128]{2,1,0:T(8,128)S(1)}, u32[]{:S(2)}, u32[]{:S(2)}) collective-permute-start(f32[72,16,128]{2,1,0:T(8,128)S(1)} %get-tuple-element.55), channel_id=1, source_target_pairs={{0,4},{1,5},{2,6},{3,7},{4,0},{5,1},{6,2},{7,3},{8,12},{9,13},{10,... | collective-permute-start | bytes 1769480 | tf_op jit(solution)/shard_map/ppermute | solution.py:579
  26.4 10.2 %collective-permute-start.3 = (f32[64,8,128]{2,1,0:T(8,128)S(1)}, f32[64,8,128]{2,1,0:T(8,128)S(1)}, u32[]{:S(2)}, u32[]{:S(2)}) collective-permute-start(f32[64,8,128]{2,1,0:T(8,128)S(1)} %get-tuple-element.50.mine_ref), channel_id=1, source_target_pairs={{0,8},{1,9},{2,10},{3,11},{4,12},{5,13},{6,14},{7,15},{24,16},{25,... | collective-permute-start | bytes 786440 | tf_op jit(solution)/shard_map/ppermute | solution.py:579
  30.4 6.2 %collective-permute-start.4 = (f32[64,8,128]{2,1,0:T(8,128)S(1)}, f32[64,8,128]{2,1,0:T(8,128)S(1)}, u32[]{:S(2)}, u32[]{:S(2)}) collective-permute-start(f32[64,8,128]{2,1,0:T(8,128)S(1)} %collective-permute-done.a_ref), channel_id=1, source_target_pairs={{4,0},{5,1},{6,2},{7,3},{24,28},{25,29},{26,30},{27,31}} | collective-permute-start | bytes 786440 | tf_op jit(solution)/shard_map/ppermute | solution.py:579
  37.9 12.2 %collective-permute-start.5 = (f32[65,8,128]{2,1,0:T(8,128)S(1)}, f32[65,8,128]{2,1,0:T(8,128)S(1)}, u32[]{:S(2)}, u32[]{:S(2)}) collective-permute-start(f32[65,8,128]{2,1,0:T(8,128)S(1)} %get-tuple-element.58), channel_id=1, source_target_pairs={{0,8},{1,9},{2,10},{3,11},{4,12},{5,13},{6,14},{7,15},{8,0},{9,1},... | collective-permute-start | bytes 798728 | tf_op jit(solution)/shard_map/ppermute | solution.py:579
  40.4 4.3 %collective-permute-start.6 = (f32[16,8,128]{2,1,0:T(8,128)S(1)}, f32[16,8,128]{2,1,0:T(8,128)S(1)}, u32[]{:S(2)}, u32[]{:S(2)}) collective-permute-start(f32[16,8,128]{2,1,0:T(8,128)S(1)} %get-tuple-element.64.a_ref), channel_id=1, source_target_pairs={{0,1},{1,0},{2,3},{3,2},{4,5},{5,4},{6,7},{7,6},{8,9},{9,8},{10,11... | collective-permute-start | bytes 196616 | tf_op jit(solution)/shard_map/ppermute | solution.py:579
  44.7 5.2 %collective-permute-start.7 = (f32[16,8,128]{2,1,0:T(8,128)S(1)}, f32[16,8,128]{2,1,0:T(8,128)S(1)}, u32[]{:S(2)}, u32[]{:S(2)}) collective-permute-start(f32[16,8,128]{2,1,0:T(8,128)S(1)} %shard_map.87.refs_0_), channel_id=1, source_target_pairs={{0,2},{1,3},{2,0},{3,1},{4,6},{5,7},{6,4},{7,5},{8,10},{9,11},{10,... | collective-permute-start | bytes 196616 | tf_op jit(solution)/shard_map/ppermute | solution.py:579
  47.3 9.7 %all-to-all-start = ((f32[32,1,128]{2,1,0:T(1,128)}), f32[32,1,128]{2,1,0:T(1,128)S(1)}, u32[]{:S(2)}, u32[]{:S(2)}) async-start(f32[32,1,128]{2,1,0:T(1,128)} %bitcast.3), calls=%async_computation | async-start | bytes 32768 | tf_op jit(solution)/shard_map/all_to_all | solution.py:676
  57.3 6.0 %collective-permute-start.8 = (f32[64,8,128]{2,1,0:T(8,128)S(1)}, f32[64,8,128]{2,1,0:T(8,128)S(1)}, u32[]{:S(2)}, u32[]{:S(2)}) collective-permute-start(f32[64,8,128]{2,1,0:T(8,128)S(1)} %get-tuple-element.67.mine_ref), channel_id=1, source_target_pairs={{0,0},{1,1},{2,2},{3,3},{4,16},{5,17},{6,18},{7,19},{8,4},{9,5},{1... | collective-permute-start | bytes 786440 | tf_op jit(solution)/shard_map/ppermute | solution.py:579
  58.0 12.6 %collective-permute-start.9 = (f32[64,8,128]{2,1,0:T(8,128)S(1)}, f32[64,8,128]{2,1,0:T(8,128)S(1)}, u32[]{:S(2)}, u32[]{:S(2)}) collective-permute-start(f32[64,8,128]{2,1,0:T(8,128)S(1)} %get-tuple-element.67.mine_ref), channel_id=1, source_target_pairs={{0,16},{1,17},{2,18},{3,19},{4,0},{5,1},{6,2},{7,3},{8,20},{9,21},... | collective-permute-start | bytes 786440 | tf_op jit(solution)/shard_map/ppermute | solution.py:579
  75.3 10.9 %collective-permute-start.10 = (f32[72,16,128]{2,1,0:T(8,128)S(1)}, f32[72,16,128]{2,1,0:T(8,128)S(1)}, u32[]{:S(2)}, u32[]{:S(2)}) collective-permute-start(f32[72,16,128]{2,1,0:T(8,128)S(1)} %get-tuple-element.70), channel_id=1, source_target_pairs={{0,4},{1,5},{2,6},{3,7},{4,0},{5,1},{6,2},{7,3},{8,12},{9,13},{10,... | collective-permute-start | bytes 1769480 | tf_op jit(solution)/shard_map/ppermute | solution.py:579
  76.9 9.3 %collective-permute-start.11 = (f32[64,8,128]{2,1,0:T(8,128)S(1)}, f32[64,8,128]{2,1,0:T(8,128)S(1)}, u32[]{:S(2)}, u32[]{:S(2)}) collective-permute-start(f32[64,8,128]{2,1,0:T(8,128)S(1)} %get-tuple-element.67.mine_ref), channel_id=1, source_target_pairs={{0,8},{1,9},{2,10},{3,11},{4,12},{5,13},{6,14},{7,15},{24,16},{25,... | collective-permute-start | bytes 786440 | tf_op jit(solution)/shard_map/ppermute | solution.py:579
  80.5 5.7 %collective-permute-start.12 = (f32[64,8,128]{2,1,0:T(8,128)S(1)}, f32[64,8,128]{2,1,0:T(8,128)S(1)}, u32[]{:S(2)}, u32[]{:S(2)}) collective-permute-start(f32[64,8,128]{2,1,0:T(8,128)S(1)} %collective-permute-done.8.a_ref), channel_id=1, source_target_pairs={{4,0},{5,1},{6,2},{7,3},{24,28},{25,29},{26,30},{27,31}} | collective-permute-start | bytes 786440 | tf_op jit(solution)/shard_map/ppermute | solution.py:579
  87.4 12.9 %collective-permute-start.13 = (f32[65,8,128]{2,1,0:T(8,128)S(1)}, f32[65,8,128]{2,1,0:T(8,128)S(1)}, u32[]{:S(2)}, u32[]{:S(2)}) collective-permute-start(f32[65,8,128]{2,1,0:T(8,128)S(1)} %get-tuple-element.73), channel_id=1, source_target_pairs={{0,8},{1,9},{2,10},{3,11},{4,12},{5,13},{6,14},{7,15},{8,0},{9,1},... | collective-permute-start | bytes 798728 | tf_op jit(solution)/shard_map/ppermute | solution.py:579
  90.0 4.3 %collective-permute-start.14 = (f32[16,8,128]{2,1,0:T(8,128)S(1)}, f32[16,8,128]{2,1,0:T(8,128)S(1)}, u32[]{:S(2)}, u32[]{:S(2)}) collective-permute-start(f32[16,8,128]{2,1,0:T(8,128)S(1)} %get-tuple-element.78.a_ref), channel_id=1, source_target_pairs={{0,1},{1,0},{2,3},{3,2},{4,5},{5,4},{6,7},{7,6},{8,9},{9,8},{10,11... | collective-permute-start | bytes 196616 | tf_op jit(solution)/shard_map/ppermute | solution.py:579
  94.3 5.9 %collective-permute-start.15 = (f32[16,8,128]{2,1,0:T(8,128)S(1)}, f32[16,8,128]{2,1,0:T(8,128)S(1)}, u32[]{:S(2)}, u32[]{:S(2)}) collective-permute-start(f32[16,8,128]{2,1,0:T(8,128)S(1)} %shard_map.91.refs_0_), channel_id=1, source_target_pairs={{0,2},{1,3},{2,0},{3,1},{4,6},{5,7},{6,4},{7,5},{8,10},{9,11},{10,... | collective-permute-start | bytes 196616 | tf_op jit(solution)/shard_map/ppermute | solution.py:579
  94.9 11.2 %all-to-all-start.1 = ((f32[32,1,128]{2,1,0:T(1,128)}), f32[32,1,128]{2,1,0:T(1,128)S(1)}, u32[]{:S(2)}, u32[]{:S(2)}) async-start(f32[32,1,128]{2,1,0:T(1,128)} %bitcast.6), calls=%async_computation.1 | async-start | bytes 32768 | tf_op jit(solution)/shard_map/all_to_all | solution.py:676
  106.3 5.4 %collective-permute-start.16 = (f32[16,8,128]{2,1,0:T(8,128)S(1)}, f32[16,8,128]{2,1,0:T(8,128)S(1)}, u32[]{:S(2)}, u32[]{:S(2)}) collective-permute-start(f32[16,8,128]{2,1,0:T(8,128)S(1)} %get-tuple-element.83.refs_0_), channel_id=1, source_target_pairs={{0,1},{1,0},{2,3},{3,2},{4,5},{5,4},{6,7},{7,6},{8,9},{9,8},{10,11... | collective-permute-start | bytes 196616 | tf_op jit(solution)/shard_map/ppermute | solution.py:579
  106.8 8.0 %collective-permute-start.17 = (f32[16,8,128]{2,1,0:T(8,128)S(1)}, f32[16,8,128]{2,1,0:T(8,128)S(1)}, u32[]{:S(2)}, u32[]{:S(2)}) collective-permute-start(f32[16,8,128]{2,1,0:T(8,128)S(1)} %get-tuple-element.83.refs_0_), channel_id=1, source_target_pairs={{0,2},{1,3},{2,0},{3,1},{4,6},{5,7},{6,4},{7,5},{8,10},{9,11},{10,... | collective-permute-start | bytes 196616 | tf_op jit(solution)/shard_map/ppermute | solution.py:579
  107.5 7.4 %collective-permute-start.18 = (f32[16,8,128]{2,1,0:T(8,128)S(1)}, f32[16,8,128]{2,1,0:T(8,128)S(1)}, u32[]{:S(2)}, u32[]{:S(2)}) collective-permute-start(f32[16,8,128]{2,1,0:T(8,128)S(1)} %get-tuple-element.83.refs_0_), channel_id=1, source_target_pairs={{0,3},{1,2},{2,1},{3,0},{4,7},{5,6},{6,5},{7,4},{8,11},{9,10},{10,... | collective-permute-start | bytes 196616 | tf_op jit(solution)/shard_map/ppermute | solution.py:579

commit v10 on v9

--- a/solution.py
+++ b/solution.py
@@ -70,7 +70,13 @@
     return g * cos2 - swap(g) * sin2
 
 
-def start_kernel(dims, pos_hbm, lmn_hbm, gains_hbm, e_ref, g_ref, p_ref, pos_ref, lmn_ref, gains_ref, sems):
+def store_parts(ft, value, whole, part0, part1):
+    half = part0.shape[0]
+    whole[ft] = value
+    (part0 if ft < half else part1)[ft % half] = value
+
+
+def start_kernel(dims, pos_hbm, lmn_hbm, gains_hbm, e_ref, g_ref, p_ref, p0_ref, p1_ref, pos_ref, lmn_ref, gains_ref, sems):
     F, T, D, O, R, C = dims
     W = 2 * O
     copies = [
@@ -118,7 +124,7 @@
             ft = f * T + t
             g = jnp.concatenate([gains_ref[f, t, 0], gains_ref[f, t, 1]], axis=-1)
             g_ref[ft] = g
-            p_ref[ft] = rotated(g, e_ref[ft])
+            store_parts(ft, rotated(g, e_ref[ft]), p_ref, p0_ref, p1_ref)
 
 
 def own_terms(dims, flux_ref, live_ref, g_ref, held_ref, slope_ref):
@@ -287,19 +293,22 @@
     return a == b
 
 
-def sum_kernel(dims, flux_hbm, vis_hbm, live_ref, a_ref, b_ref, head_ref, *refs):
+def sum_kernel(dims, skip, flux_hbm, vis_hbm, live_ref, a_ref, b_ref, *refs):
     F, T, D, O, _, _ = dims
-    upright_ref, refs = (refs[0], refs[1:]) if len(refs) == 9 else (None, refs)
+    F = F // 2
+    head_ref, refs = (None, refs) if skip else (refs[0], refs[1:])
+    HEAD = 0 if skip else head_ref.shape[0]
+    upright_ref, refs = (refs[0], refs[1:]) if len(refs) == 8 else (None, refs)
     keep_ref, send_ref, refs = refs[0], refs[1], refs[2:]
     power_ref, refs = (refs[0], refs[1:]) if upright_ref is not None else (None, refs)
-    vis_ref, distinct, flux_ref, sems = refs[:4]
+    vis_ref, distinct, flux_ref, sems = refs
     rows, cols = vis_ref.shape[3], vis_ref.shape[4]
     row = lax.axis_index("row")
     col = lax.axis_index("col")
     parity = col % 2
 
     def vis_copy(f):
-        return pltpu.make_async_copy(vis_hbm.at[f], vis_ref.at[f], sems.at[f])
+        return pltpu.make_async_copy(vis_hbm.at[skip + f], vis_ref.at[f], sems.at[f])
 
     flux_copy = pltpu.make_async_copy(flux_hbm, flux_ref, sems.at[F])
     flux_copy.start()
@@ -312,13 +321,13 @@
     blocks = block_mask(2 * D)
     nt = (((1,), (1,)), ((), ()))
 
-    def body(step, upright, start, power, source):
+    def body(step, power, source):
         highs, lows = [], []
-        lives = live_ref[pl.ds(step * 8, 8), :]
+        lives = live_ref[pl.ds(skip * T + step * 8, 8), :]
         mask = distinct[...]
         for i in range(group):
             f = step * group + i
-            scale = column(flux_ref, f, D, cols)
+            scale = column(flux_ref, skip + f, D, cols)
             for t in range(T):
                 j = i * T + t
                 ft = step * 8 + j
@@ -345,11 +354,13 @@
                 even, odd = join_low(v0, v1), join_high(v0, v1)
                 keep_ref[step * 9 + j] = jnp.where(parity == 0, even, odd)
                 send_ref[step * 9 + j] = jnp.where(parity == 0, odd, even)
-                if upright is not None:
+                if upright_ref is not None:
                     square = [x.astype(jnp.float32) for x in seen]
                     square = square[0] * square[0] + square[1] * square[1]
-                    at = start + j
-                    square = square * jnp.broadcast_to(upright[:, at : at + 1], square.shape)
+                    at = jnp.full(square.shape, skip * T + ft, jnp.int32)
+                    square = square * jnp.take_along_axis(
+                        upright_ref[...], at, axis=1, mode="promise_in_bounds"
+                    )
                     square = jnp.sum(square.reshape(rows // 8, 8, cols), axis=0)
                     power = power + square * lives[j : j + 1, :]
         high = jnp.concatenate(highs, axis=0)
@@ -365,39 +376,31 @@
         send_ref[step * 9 + 8] = folded
         return power
 
-    def roll_to(c):
-        if upright_ref is None:
-            return None
-        upright = refs[4]
-        upright[...] = pltpu.roll(upright_ref[...], (2 * O - c * CHUNK * T) % (2 * O), 1)
-        return upright
-
     def chunk(c, power):
         for i in range(CHUNK):
             vis_copy(c * CHUNK + i).wait()
 
-        upright = roll_to(c)
         for j in range(CHUNK // group):
-            power = body(c * (CHUNK // group) + j, upright, j * 8, power, vis_ref)
+            power = body(c * (CHUNK // group) + j, power, vis_ref)
         return power
 
     flux_copy.wait()
     power = jnp.zeros((8, cols), jnp.float32)
-    upright = roll_to(0)
     for j in range(CHUNK // group):
         inside = (j + 1) * group <= HEAD
         if not inside:
             for i in range(group):
                 vis_copy(j * group + i).wait()
-        power = body(j, upright, j * 8, power, head_ref if inside else vis_ref)
+        power = body(j, power, head_ref if inside else vis_ref)
     power = lax.fori_loop(1, F // CHUNK, chunk, power)
     if power_ref is not None:
         power = jnp.sum(power, axis=0, keepdims=True)
         power_ref[...] = jnp.where(low_lanes(power.shape), power + swap(power), 0.0)
 
 
-def residual_kernel(dims, live_ref, extra_ref, power_ref, kept_ref, other_ref, mine_ref, theirs_ref,
-                    passed_ref, got_ref, keep_ref, send_ref, scalar_hbm, num_ref, scalar_ref, sem):
+def residual_kernel(dims, live_ref, extra_ref, power0_ref, power1_ref, kept0_ref, kept1_ref,
+                    other0_ref, other1_ref, mine_ref, theirs_ref, passed0_ref, passed1_ref,
+                    got0_ref, got1_ref, keep_ref, send_ref, scalar_hbm, num_ref, scalar_ref, sem):
     F, T, D, O, _, _ = dims
     W = 2 * O
     row = lax.axis_index("row")
@@ -410,24 +413,30 @@
         lax.broadcasted_iota(jnp.int32, (2 * D, W), 1) % (2 * D)
     )
 
-    def body(group, total):
+    def body(whole_group, total):
+        late = whole_group >= F * T // 16
+        kept_ref, other_ref, passed_ref, got_ref = (
+            (kept1_ref, other1_ref, passed1_ref, got1_ref) if late
+            else (kept0_ref, other0_ref, passed0_ref, got0_ref)
+        )
+        group = whole_group % (F * T // 16)
         gram = kept_ref[group * 9 + 8] + other_ref[group * 9 + 8]
         diagonal = jnp.sum(jnp.where(eye, gram, 0.0), axis=0, keepdims=True)
-        keep_ref[F * T, pl.ds(group, 1), :] = diagonal
-        send_ref[F * T, pl.ds(group, 1), :] = diagonal
+        keep_ref[F * T, pl.ds(whole_group, 1), :] = diagonal
+        send_ref[F * T, pl.ds(whole_group, 1), :] = diagonal
         spread = jnp.where(mask, jnp.concatenate([gram] * 8, axis=0), 0.0)
         station = []
         for i in range(8):
-            ft = group * 8 + i
+            ft, at = whole_group * 8 + i, group * 8 + i
             a = mine_ref[ft]
-            b = jnp.where(away, theirs_ref[ft], jnp.where(held, got_ref[ft], passed_ref[ft]))
+            b = jnp.where(away, theirs_ref[ft], jnp.where(held, got_ref[at], passed_ref[at]))
             first = jnp.where(near, a, b)
             second = jnp.where(near, b, a)
             station += [join_low(first, second), join_high(first, second)]
         model = product(spread, jnp.concatenate(station, axis=0))
-        lives = live_ref[pl.ds(group * 8, 8), :]
+        lives = live_ref[pl.ds(whole_group * 8, 8), :]
         for i in range(8):
-            ft = group * 8 + i
+            ft = whole_group * 8 + i
             live = lives[i : i + 1, :]
             v = kept_ref[group * 9 + i] + other_ref[group * 9 + i]
             num = (v - model[i * 2 * D : (i + 1) * 2 * D]) * live
@@ -441,7 +450,7 @@
         total = body(group, total)
     squares = -jnp.sum(total, axis=0, keepdims=True)
     squares = squares + swap(squares)
-    scalar = jnp.where(low_lanes(squares.shape), squares, 0.0) + extra_ref[...] + power_ref[...]
+    scalar = jnp.where(low_lanes(squares.shape), squares, 0.0) + extra_ref[...] + power0_ref[...] + power1_ref[...]
     scalar_ref[...] = jnp.broadcast_to(scalar, scalar_ref.shape)
     copy = pltpu.make_async_copy(scalar_ref, scalar_hbm, sem.at[0])
     copy.start()
@@ -504,9 +513,8 @@
                     acc[k] = acc[k] + total
                     total = total * x if k < 3 else total
             else:
-                g_out, p_out = refs[6:]
-                g_out[ft] = g
-                p_out[ft] = rotated(g, other_ref[ft])
+                refs[6][ft] = g
+                store_parts(ft, rotated(g, other_ref[ft]), *refs[7:])
         if last:
             for k in range(4):
                 rhs_ref[k * T + t] = acc[k]
@@ -584,15 +592,16 @@
     def bands(x):
         return [x] + [permute(x, lambda r, c, z, k=k: (r, c, z ^ k)) for k in range(1, Z)]
 
+    part = array(FT // 2, D, W)
     whole, line, fit = array(FT, D, W), array(FT + 1, D, W), array(4 * T, D, W)
     pair, text = array(FT // 8 * 9, 2 * D, W), array(1, W)
     flux_t = flux.T
     start = jax.ShapeDtypeStruct((HEAD,) + vis.shape[1:], vis.dtype)
-    rot, g, p = pl.pallas_call(
+    rot, g, p, *parts = pl.pallas_call(
         functools.partial(start_kernel, dims),
-        out_shape=[whole] * 3,
+        out_shape=[whole] * 3 + [part] * 2,
         in_specs=[hbm] * 3,
-        out_specs=[vmem] * 3,
+        out_specs=[vmem] * 5,
         scratch_shapes=[
             pltpu.VMEM((3, T, full), f32),
             pltpu.SMEM(lmn.shape, f32),
@@ -604,7 +613,7 @@
     )(far(positions.transpose(1, 0, 2)), far(lmn), far(gains))
     for step in range(ITERS):
         last = step == ITERS - 1
-        got = [gather(p, m) for m in range(R)]
+        got = [[gather(x, m) for m in range(R)] for x in parts]
         if step == 0:
             (live_col, live_half, live_own, upright, u, rhs, held, slope, samples, extra, head) = (
                 pl.pallas_call(
@@ -637,33 +646,38 @@
             )(flux_t, far(vis), samples, live_own, u, g)
         rhs_near = permute(rhs, lambda r, c, z: (r, c, z ^ 1))
         theirs = permute(p, lambda r, c, z: (r, c ^ 2, z), lambda r, c: r == c // 2)
-        more = [] if step else [upright]
-        keep, send, *found = pl.pallas_call(
-            functools.partial(sum_kernel, dims),
-            out_shape=[pair, pair] + ([] if step else [array(1, cols)]),
-            in_specs=[hbm] * 2 + [vmem] * (4 + len(more)),
-            out_specs=[vmem] * (2 + len(more)),
-            scratch_shapes=[
-                pltpu.VMEM(vis.shape, vis.dtype),
-                pltpu.VMEM((rows, cols), vis.dtype),
-                pltpu.SMEM(flux_t.shape, f32),
-                pltpu.SemaphoreType.DMA((F + 1,)),
-            ] + [pltpu.VMEM((rows, W), f32)] * len(more),
-            compiler_params=LIMIT,
-            name="sums",
-        )(far(flux_t), far(vis), live_col, *got, head, *more)
-        power = power if step else found[0]
-        passed = permute(
-            got[0], lambda r, c, z: (r, c ^ 1, z), lambda r, c: c == 3 * r + (1 - 2 * r)
-        )
-        other = permute(send, lambda r, c, z: (r, c ^ 1, z))
         (rhs,) = call(add_kernel, [fit], [], [rhs, rhs_near])
         rhs_far = permute(rhs, lambda r, c, z: (r, c, z ^ 2))
+        pair = array(FT // 16 * 9, 2 * D, W)
+        keeps, others, passed = [], [], []
+        for i in range(2):
+            more = ([] if i else [head]) + ([] if step else [upright])
+            keep, send, *found = pl.pallas_call(
+                functools.partial(sum_kernel, dims, i * (F // 2)),
+                out_shape=[pair, pair] + ([] if step else [array(1, cols)]),
+                in_specs=[hbm] * 2 + [vmem] * (3 + len(more)),
+                out_specs=[vmem] * (2 + len([] if step else [upright])),
+                scratch_shapes=[
+                    pltpu.VMEM((F // 2,) + vis.shape[1:], vis.dtype),
+                    pltpu.VMEM((rows, cols), vis.dtype),
+                    pltpu.SMEM(flux_t.shape, f32),
+                    pltpu.SemaphoreType.DMA((F // 2 + 1,)),
+                ],
+                compiler_params=LIMIT,
+            )(far(flux_t), far(vis), live_col, *got[i], *more)
+            if not step:
+                powers = [*found] if i == 0 else powers + [*found]
+            keeps.append(keep)
+            others.append(permute(send, lambda r, c, z: (r, c ^ 1, z)))
+            passed.append(permute(
+                got[i][0], lambda r, c, z: (r, c ^ 1, z),
+                lambda r, c: c == 3 * r + (1 - 2 * r),
+            ))
         everyone = array(R * C * Z, W)
         keep, send, scalar = pl.pallas_call(
             functools.partial(residual_kernel, dims),
             out_shape=[line, line, everyone],
-            in_specs=[vmem] * 9,
+            in_specs=[vmem] * 14,
             out_specs=[vmem, vmem, hbm],
             scratch_shapes=[
                 pltpu.VMEM((FT, 2 * D, W), f32), pltpu.VMEM(everyone.shape, f32),
@@ -671,7 +685,7 @@
             ],
             compiler_params=LIMIT,
             name="residual",
-        )(live_half, extra, power, keep, other, p, theirs, passed, got[1])
+        )(live_half, extra, *powers, *keeps, *others, p, theirs, *passed, got[0][1], got[1][1])
         come = permute(send, lambda r, c, z: (r, c ^ 2, z))
         scalar = lax.all_to_all(scalar, AXES, 0, 0, tiled=True)
         target = call(
@@ -690,7 +704,7 @@
                 arrays + [target[1]],
             )
         else:
-            g, p = call(update, [whole, whole], [], arrays + [rot])
+            g, p, *parts = call(update, [whole, whole, part, part], [], arrays + [rot])
 
     def write(kernel, arrays):
         return pl.pallas_call(

time: 116 us -> 112 us (0.966)
  waiting for transfers between devices: 47.2 us -> 30.1 us
  starting transfers between devices: 44.7 us -> 55.9 us
  Pallas kernels: 23.1 us -> 25.1 us
    ppermute x19 -> x27, waiting for transfers between devices: 35.3 us -> 18.1 us  [permute(): return lax.ppermute(x, AXES, pairs)]
    ppermute x19 -> x27, starting transfers between devices: 38.1 us -> 49.2 us  [permute(): return lax.ppermute(x, AXES, pairs)]
    pallas_call x2 -> x4, Pallas kernels: 10.7 us -> 12.7 us  [shards(): pl.pallas_call(functools.partial(sum_kernel, dims, i * (F // 2)), out_sha...]
  transfers between devices with their start and end apart: 21 -> 29, of which waited for: 10 -> 12; matrix products, arithmetic and copies ran while one was open for 0% -> 0% of each run, Pallas kernels for 5% -> 17%
where the time goes in v10:
time: 112 us
  starting transfers between devices  55.9 us (50%)
  waiting for transfers between devices  30.1 us (27%)
  Pallas kernels  25.1 us (22%)
    ppermute x27, starting transfers between devices, permute(): return lax.ppermute(x, AXES, pairs)  49.2 us
    ppermute x27, waiting for transfers between devices, permute(): return lax.ppermute(x, AXES, pairs)  18.1 us
    pallas_call x4, Pallas kernels, shards(): pl.pallas_call(functools.partial(sum_kernel, dims, i * (F // 2)), out_sha...  12.7 us
    all_to_all x2, waiting for transfers between devices, shards(): scalar = lax.all_to_all(scalar, AXES, 0, 0, tiled=True)  12 us
    all_to_all x2, starting transfers between devices, shards(): scalar = lax.all_to_all(scalar, AXES, 0, 0, tiled=True)  6.64 us
    pallas_call x2, Pallas kernels, shards(): pl.pallas_call(functools.partial(residual_kernel, dims), out_shape=[line,...  2.43 us
    pallas_call x1, Pallas kernels, shards(): pl.pallas_call(functools.partial(setup_kernel, dims, cols), out_shape=[ar...  2.34 us
    pallas_call x1, Pallas kernels, shards(): pl.pallas_call(functools.partial(start_kernel, dims), out_shape=[whole] *...  2.25 us
  transfers between devices with their start and end apart: 29, of which 12 were waited for; matrix products, arithmetic and copies ran while one was open for 0% of the time, Pallas kernels for 17%

profile of v10, /device:TPU:0, one launch (start us, length us, event | category | flops | bytes accessed | tf_op | source)
XLA Modules:
  0.0 112.0 jit_solution(4378817691100300386)
XLA Ops:
  0.6 2.2 %start.1 = (f32[64,8,128]{2,1,0:T(8,128)S(1)}, f32[64,8,128]{2,1,0:T(8,128)S(1)}, f32[64,8,128]{2,1,0:T(8,128)S(1)}, f32[32,8,128]{2,1,0:T(8,128)S(1)}, f32[32,8,128]{2,1,0:T(8,128)S(1)}) custom-call(f32[3,4,512]{2,1,0:T(4,128)} %bitcast.18, f32[3,8]{1,0:T(4,128)} %lmn_hbm.1, f32[16,4,2,8,64]{4,3,2,1,0:T(8,128)} %gains_hbm.1), custom_call_target="tpu_custom_call" | custom-call | tf_op jit(solution)/shard_map/start/pallas_call | solution.py:600
  2.9 0.7 collective-permute-start
  3.6 5.7 %collective-permute-start.1 = (f32[32,8,128]{2,1,0:T(8,128)S(1)}, f32[32,8,128]{2,1,0:T(8,128)S(1)}, u32[]{:S(2)}, u32[]{:S(2)}) collective-permute-start(f32[32,8,128]{2,1,0:T(8,128)S(1)} %get-tuple-element.59), channel_id=1, source_target_pairs={{0,16},{1,17},{2,18},{3,19},{4,0},{5,1},{6,2},{7,3},{8,20},{9,21},... | collective-permute-start | bytes 393224 | tf_op jit(solution)/shard_map/ppermute | solution.py:587
  9.3 0.7 collective-permute-start.2
  10.0 4.0 %collective-permute-start.3 = (f32[32,8,128]{2,1,0:T(8,128)S(1)}, f32[32,8,128]{2,1,0:T(8,128)S(1)}, u32[]{:S(2)}, u32[]{:S(2)}) collective-permute-start(f32[32,8,128]{2,1,0:T(8,128)S(1)} %get-tuple-element.63), channel_id=1, source_target_pairs={{0,16},{1,17},{2,18},{3,19},{4,0},{5,1},{6,2},{7,3},{8,20},{9,21},... | collective-permute-start | bytes 393224 | tf_op jit(solution)/shard_map/ppermute | solution.py:587
  14.0 2.3 %setup.1 = (f32[64,128]{1,0:T(8,128)S(1)}, f32[64,128]{1,0:T(8,128)S(1)}, f32[64,128]{1,0:T(8,128)S(1)}, f32[256,128]{1,0:T(8,128)S(1)}, f32[64,8,128]{2,1,0:T(8...) custom-call(f32[8,16]{1,0:T(8,128)} %bitcast.10, ...), custom_call_target="tpu_custom_call" | custom-call | tf_op jit(solution)/shard_map/setup/pallas_call | solution.py:619
  16.3 3.1 %shard_map.86 = (f32[36,16,128]{2,1,0:T(8,128)S(1)}, f32[36,16,128]{2,1,0:T(8,128)S(1)}, f32[1,128]{1,0:T(1,128)S(1)}) custom-call(f32[8,16]{1,0:T(8,128)} %bitcast.11, bf16[16,4,2,256,128]{4,3,2,1,0:T(8,128)(2,1)} %vis_hbm.11, f32[64,128]{1,0:T(8,128)S(1)} %get-tuple-element.58.live_ref, f32[32,8,128]{2,1,0:T(8,128)S(1)} %collective-permute-done.a_ref, ...), custom_call_target="tpu_custom_call" | custom-call | tf_op jit(solution)/shard_map/pallas_call | solution.py:655
  19.5 3.5 %shard_map.87 = (f32[36,16,128]{2,1,0:T(8,128)S(1)}, f32[36,16,128]{2,1,0:T(8,128)S(1)}, f32[1,128]{1,0:T(1,128)S(1)}) custom-call(f32[8,16]{1,0:T(8,128)} %bitcast.12, bf16[16,4,2,256,128]{4,3,2,1,0:T(8,128)(2,1)} %vis_hbm.11, f32[64,128]{1,0:T(8,128)S(1)} %get-tuple-element.58.live_ref, f32[32,8,128]{2,1,0:T(8,128)S(1)} %collective-permute-done.2.a_ref, ...), custom_call_target="tpu_custom_call" | custom-call | tf_op jit(solution)/shard_map/pallas_call | solution.py:655
  23.1 0.9 collective-permute-start.5
  24.0 4.1 %collective-permute-start.6 = (f32[64,8,128]{2,1,0:T(8,128)S(1)}, f32[64,8,128]{2,1,0:T(8,128)S(1)}, u32[]{:S(2)}, u32[]{:S(2)}) collective-permute-start(f32[64,8,128]{2,1,0:T(8,128)S(1)} %get-tuple-element.69.mine_ref), channel_id=1, source_target_pairs={{0,8},{1,9},{2,10},{3,11},{4,12},{5,13},{6,14},{7,15},{24,16},{25,... | collective-permute-start | bytes 786440 | tf_op jit(solution)/shard_map/ppermute | solution.py:587
  28.0 1.3 %collective-permute-start.7 = (f32[32,8,128]{2,1,0:T(8,128)S(1)}, f32[32,8,128]{2,1,0:T(8,128)S(1)}, u32[]{:S(2)}, u32[]{:S(2)}) collective-permute-start(f32[32,8,128]{2,1,0:T(8,128)S(1)} %collective-permute-done.a_ref), channel_id=1, source_target_pairs={{4,0},{5,1},{6,2},{7,3},{24,28},{25,29},{26,30},{27,31}} | collective-permute-start | bytes 393224 | tf_op jit(solution)/shard_map/ppermute | solution.py:587
  29.3 1.3 %collective-permute-start.8 = (f32[32,8,128]{2,1,0:T(8,128)S(1)}, f32[32,8,128]{2,1,0:T(8,128)S(1)}, u32[]{:S(2)}, u32[]{:S(2)}) collective-permute-start(f32[32,8,128]{2,1,0:T(8,128)S(1)} %collective-permute-done.2.a_ref), channel_id=1, source_target_pairs={{4,0},{5,1},{6,2},{7,3},{24,28},{25,29},{26,30},{27,31}} | collective-permute-start | bytes 393224 | tf_op jit(solution)/shard_map/ppermute | solution.py:587
  30.6 3.6 %collective-permute-done.6.theirs_ref = f32[64,8,128]{2,1,0:T(8,128)S(1)} collective-permute-done((f32[64,8,128]{2,1,0:T(8,128)S(1)}, f32[64,8,128]{2,1,0:T(8,128)S(1)}, u32[]{:S(2)}, u32[]{:S(2)}) %collective-permute-start.6) | collective-permute-done | bytes 262176 | tf_op jit(solution)/shard_map/ppermute | solution.py:587
  34.2 1.2 %residual.2 = (f32[65,8,128]{2,1,0:T(8,128)S(1)}, f32[65,8,128]{2,1,0:T(8,128)S(1)}, f32[32,128]{1,0:T(8,128)}) custom-call(f32[64,128]{1,0:T(8,128)S(1)} %get-tuple-element.53.live_ref, f32[1,128]{1,0:T(1,128)S(1)} %get-tuple-element.57.extra_ref, f32[1,128]{1,0:T(1,128)S(1)} %get-tuple-element.62.power0_ref, f32[1,128]{1,0:T(1,128)S(1)} %get-tuple-element.64.power1_ref, ...), custom_call_target="tpu_custom_call" | custom-call | tf_op jit(solution)/shard_map/residual/pallas_call | solution.py:677
  35.5 2.5 %collective-permute-start.9 = (f32[65,8,128]{2,1,0:T(8,128)S(1)}, f32[65,8,128]{2,1,0:T(8,128)S(1)}, u32[]{:S(2)}, u32[]{:S(2)}) collective-permute-start(f32[65,8,128]{2,1,0:T(8,128)S(1)} %get-tuple-element.72), channel_id=1, source_target_pairs={{0,8},{1,9},{2,10},{3,11},{4,12},{5,13},{6,14},{7,15},{8,0},{9,1},... | collective-permute-start | bytes 798728 | tf_op jit(solution)/shard_map/ppermute | solution.py:587
  38.0 1.6 %collective-permute-start.10 = (f32[16,8,128]{2,1,0:T(8,128)S(1)}, f32[16,8,128]{2,1,0:T(8,128)S(1)}, u32[]{:S(2)}, u32[]{:S(2)}) collective-permute-start(f32[16,8,128]{2,1,0:T(8,128)S(1)} %get-tuple-element.78.a_ref), channel_id=1, source_target_pairs={{0,1},{1,0},{2,3},{3,2},{4,5},{5,4},{6,7},{7,6},{8,9},{9,8},{10,11... | collective-permute-start | bytes 196616 | tf_op jit(solution)/shard_map/ppermute | solution.py:587
  39.6 2.7 %collective-permute-done.10.b_ref = f32[16,8,128]{2,1,0:T(8,128)S(1)} collective-permute-done((f32[16,8,128]{2,1,0:T(8,128)S(1)}, f32[16,8,128]{2,1,0:T(8,128)S(1)}, u32[]{:S(2)}, u32[]{:S(2)}) %collective-permute-start.10) | collective-permute-done | bytes 65568 | tf_op jit(solution)/shard_map/ppermute | solution.py:587
  42.3 2.7 %collective-permute-start.11 = (f32[16,8,128]{2,1,0:T(8,128)S(1)}, f32[16,8,128]{2,1,0:T(8,128)S(1)}, u32[]{:S(2)}, u32[]{:S(2)}) collective-permute-start(f32[16,8,128]{2,1,0:T(8,128)S(1)} %shard_map.89.refs_0_), channel_id=1, source_target_pairs={{0,2},{1,3},{2,0},{3,1},{4,6},{5,7},{6,4},{7,5},{8,10},{9,11},{10,... | collective-permute-start | bytes 196616 | tf_op jit(solution)/shard_map/ppermute | solution.py:587
  45.0 2.5 %all-to-all-start = ((f32[32,1,128]{2,1,0:T(1,128)}), f32[32,1,128]{2,1,0:T(1,128)S(1)}, u32[]{:S(2)}, u32[]{:S(2)}) async-start(f32[32,1,128]{2,1,0:T(1,128)} %bitcast.3), calls=%async_computation | async-start | bytes 32768 | tf_op jit(solution)/shard_map/all_to_all | solution.py:690
  48.0 6.6 %all-to-all-done = f32[32,1,128]{2,1,0:T(1,128)S(1)} async-done(((f32[32,1,128]{2,1,0:T(1,128)}), f32[32,1,128]{2,1,0:T(1,128)S(1)}, u32[]{:S(2)}, u32[]{:S(2)}) %all-to-all-start) | async-done | bytes 16416 | tf_op jit(solution)/shard_map/all_to_all | solution.py:690
  54.9 0.7 collective-permute-start.12
  55.6 3.3 %collective-permute-start.13 = (f32[32,8,128]{2,1,0:T(8,128)S(1)}, f32[32,8,128]{2,1,0:T(8,128)S(1)}, u32[]{:S(2)}, u32[]{:S(2)}) collective-permute-start(f32[32,8,128]{2,1,0:T(8,128)S(1)} %get-tuple-element.81), channel_id=1, source_target_pairs={{0,16},{1,17},{2,18},{3,19},{4,0},{5,1},{6,2},{7,3},{8,20},{9,21},... | collective-permute-start | bytes 393224 | tf_op jit(solution)/shard_map/ppermute | solution.py:587
  59.0 0.7 collective-permute-start.14
  59.6 3.0 %collective-permute-start.15 = (f32[32,8,128]{2,1,0:T(8,128)S(1)}, f32[32,8,128]{2,1,0:T(8,128)S(1)}, u32[]{:S(2)}, u32[]{:S(2)}) collective-permute-start(f32[32,8,128]{2,1,0:T(8,128)S(1)} %get-tuple-element.84), channel_id=1, source_target_pairs={{0,16},{1,17},{2,18},{3,19},{4,0},{5,1},{6,2},{7,3},{8,20},{9,21},... | collective-permute-start | bytes 393224 | tf_op jit(solution)/shard_map/ppermute | solution.py:587
  62.6 2.0 %again.1 = (f32[16,8,128]{2,1,0:T(8,128)S(1)}, f32[64,8,128]{2,1,0:T(8,128)S(1)}, f32[64,8,128]{2,1,0:T(8,128)S(1)}, f32[1,128]{1,0:T(1,128)S(1)}, bf16[2,4,2,256,128]{4,3,2,1,0:T(8,128)(2,1)S(1)}) custom-call(f32[8,16]{1,0:T(8,128)S(1)} %bitcast.15, bf16[16,4,2,256,128]{4,3,2,1,0:T(8,128)(2,1)} %vis_hbm.11, f32[1,128]{1,0:T(1,128)S(1)} %get-tuple-element.54.samples_ref, ...), custom_call_target="tpu_custom_call" | custom-call | tf_op jit(solution)/shard_map/again/pallas_call | solution.py:638
  64.8 2.8 %shard_map.92 = (f32[36,16,128]{2,1,0:T(8,128)S(1)}, f32[36,16,128]{2,1,0:T(8,128)S(1)}) custom-call(f32[8,16]{1,0:T(8,128)} %bitcast.13, bf16[16,4,2,256,128]{4,3,2,1,0:T(8,128)(2,1)} %vis_hbm.11, f32[64,128]{1,0:T(8,128)S(1)} %get-tuple-element.58.live_ref, f32[32,8,128]{2,1,0:T(8,128)S(1)} %collective-permute-done.12.a_ref, ...), custom_call_target="tpu_custom_call" | custom-call | tf_op jit(solution)/shard_map/pallas_call | solution.py:655
  68.2 3.3 %shard_map.93 = (f32[36,16,128]{2,1,0:T(8,128)S(1)}, f32[36,16,128]{2,1,0:T(8,128)S(1)}) custom-call(f32[8,16]{1,0:T(8,128)} %bitcast.14, bf16[16,4,2,256,128]{4,3,2,1,0:T(8,128)(2,1)} %vis_hbm.11, f32[64,128]{1,0:T(8,128)S(1)} %get-tuple-element.58.live_ref, f32[32,8,128]{2,1,0:T(8,128)S(1)} %collective-permute-done.14.a_ref, ...), custom_call_target="tpu_custom_call" | custom-call | tf_op jit(solution)/shard_map/pallas_call | solution.py:655
  71.5 1.7 %collective-permute-start.17 = (f32[36,16,128]{2,1,0:T(8,128)S(1)}, f32[36,16,128]{2,1,0:T(8,128)S(1)}, u32[]{:S(2)}, u32[]{:S(2)}) collective-permute-start(f32[36,16,128]{2,1,0:T(8,128)S(1)} %get-tuple-element.87), channel_id=1, source_target_pairs={{0,4},{1,5},{2,6},{3,7},{4,0},{5,1},{6,2},{7,3},{8,12},{9,13},{10,... | collective-permute-start | bytes 884744 | tf_op jit(solution)/shard_map/ppermute | solution.py:587
  73.1 3.5 %collective-permute-start.18 = (f32[64,8,128]{2,1,0:T(8,128)S(1)}, f32[64,8,128]{2,1,0:T(8,128)S(1)}, u32[]{:S(2)}, u32[]{:S(2)}) collective-permute-start(f32[64,8,128]{2,1,0:T(8,128)S(1)} %get-tuple-element.88.mine_ref), channel_id=1, source_target_pairs={{0,8},{1,9},{2,10},{3,11},{4,12},{5,13},{6,14},{7,15},{24,16},{25,... | collective-permute-start | bytes 786440 | tf_op jit(solution)/shard_map/ppermute | solution.py:587
  76.7 1.3 %collective-permute-start.19 = (f32[32,8,128]{2,1,0:T(8,128)S(1)}, f32[32,8,128]{2,1,0:T(8,128)S(1)}, u32[]{:S(2)}, u32[]{:S(2)}) collective-permute-start(f32[32,8,128]{2,1,0:T(8,128)S(1)} %collective-permute-done.12.a_ref), channel_id=1, source_target_pairs={{4,0},{5,1},{6,2},{7,3},{24,28},{25,29},{26,30},{27,31}} | collective-permute-start | bytes 393224 | tf_op jit(solution)/shard_map/ppermute | solution.py:587
  78.0 1.3 %collective-permute-start.20 = (f32[32,8,128]{2,1,0:T(8,128)S(1)}, f32[32,8,128]{2,1,0:T(8,128)S(1)}, u32[]{:S(2)}, u32[]{:S(2)}) collective-permute-start(f32[32,8,128]{2,1,0:T(8,128)S(1)} %collective-permute-done.14.a_ref), channel_id=1, source_target_pairs={{4,0},{5,1},{6,2},{7,3},{24,28},{25,29},{26,30},{27,31}} | collective-permute-start | bytes 393224 | tf_op jit(solution)/shard_map/ppermute | solution.py:587
  79.3 0.6 collective-permute-done.19.passed0_ref
  79.9 1.3 %collective-permute-done.20.passed1_ref = f32[32,8,128]{2,1,0:T(8,128)S(1)} collective-permute-done((f32[32,8,128]{2,1,0:T(8,128)S(1)}, f32[32,8,128]{2,1,0:T(8,128)S(1)}, u32[]{:S(2)}, u32[]{:S(2)}) %collective-permute-start.20) | collective-permute-done | bytes 131104 | tf_op jit(solution)/shard_map/ppermute | solution.py:587
  81.2 1.2 %collective-permute-done.18.theirs_ref = f32[64,8,128]{2,1,0:T(8,128)S(1)} collective-permute-done((f32[64,8,128]{2,1,0:T(8,128)S(1)}, f32[64,8,128]{2,1,0:T(8,128)S(1)}, u32[]{:S(2)}, u32[]{:S(2)}) %collective-permute-start.18) | collective-permute-done | bytes 262176 | tf_op jit(solution)/shard_map/ppermute | solution.py:587
  82.4 1.2 %residual.3 = (f32[65,8,128]{2,1,0:T(8,128)S(1)}, f32[65,8,128]{2,1,0:T(8,128)S(1)}, f32[32,128]{1,0:T(8,128)}) custom-call(f32[64,128]{1,0:T(8,128)S(1)} %get-tuple-element.53.live_ref, f32[1,128]{1,0:T(1,128)S(1)} %get-tuple-element.80.extra_ref, f32[1,128]{1,0:T(1,128)S(1)} %get-tuple-element.62.power0_ref, f32[1,128]{1,0:T(1,128)S(1)} %get-tuple-element.64.power1_ref, ...), custom_call_target="tpu_custom_call" | custom-call | tf_op jit(solution)/shard_map/residual/pallas_call | solution.py:677
  83.6 2.5 %collective-permute-start.21 = (f32[65,8,128]{2,1,0:T(8,128)S(1)}, f32[65,8,128]{2,1,0:T(8,128)S(1)}, u32[]{:S(2)}, u32[]{:S(2)}) collective-permute-start(f32[65,8,128]{2,1,0:T(8,128)S(1)} %get-tuple-element.91), channel_id=1, source_target_pairs={{0,8},{1,9},{2,10},{3,11},{4,12},{5,13},{6,14},{7,15},{8,0},{9,1},... | collective-permute-start | bytes 798728 | tf_op jit(solution)/shard_map/ppermute | solution.py:587
  86.2 0.6 collective-permute-start.22
  86.8 3.6 %collective-permute-done.22.b_ref = f32[16,8,128]{2,1,0:T(8,128)S(1)} collective-permute-done((f32[16,8,128]{2,1,0:T(8,128)S(1)}, f32[16,8,128]{2,1,0:T(8,128)S(1)}, u32[]{:S(2)}, u32[]{:S(2)}) %collective-permute-start.22) | collective-permute-done | bytes 65568 | tf_op jit(solution)/shard_map/ppermute | solution.py:587
  90.5 0.6 collective-permute-start.23
  91.1 4.1 %all-to-all-start.1 = ((f32[32,1,128]{2,1,0:T(1,128)}), f32[32,1,128]{2,1,0:T(1,128)S(1)}, u32[]{:S(2)}, u32[]{:S(2)}) async-start(f32[32,1,128]{2,1,0:T(1,128)} %bitcast.6), calls=%async_computation.1 | async-start | bytes 32768 | tf_op jit(solution)/shard_map/all_to_all | solution.py:690
  95.2 1.2 %collective-permute-done.23.refs_1_ = f32[16,8,128]{2,1,0:T(8,128)S(1)} collective-permute-done((f32[16,8,128]{2,1,0:T(8,128)S(1)}, f32[16,8,128]{2,1,0:T(8,128)S(1)}, u32[]{:S(2)}, u32[]{:S(2)}) %collective-permute-start.23) | collective-permute-done | bytes 65568 | tf_op jit(solution)/shard_map/ppermute | solution.py:587
  96.9 5.4 %all-to-all-done.1 = f32[32,1,128]{2,1,0:T(1,128)S(1)} async-done(((f32[32,1,128]{2,1,0:T(1,128)}), f32[32,1,128]{2,1,0:T(1,128)S(1)}, u32[]{:S(2)}, u32[]{:S(2)}) %all-to-all-start.1) | async-done | bytes 16416 | tf_op jit(solution)/shard_map/all_to_all | solution.py:690
  102.5 0.5 collective-permute-start.24
  103.1 0.6 collective-permute-start.25
  103.7 3.3 %collective-permute-start.26 = (f32[16,8,128]{2,1,0:T(8,128)S(1)}, f32[16,8,128]{2,1,0:T(8,128)S(1)}, u32[]{:S(2)}, u32[]{:S(2)}) collective-permute-start(f32[16,8,128]{2,1,0:T(8,128)S(1)} %get-tuple-element.101.refs_0_), channel_id=1, source_target_pairs={{0,3},{1,2},{2,1},{3,0},{4,7},{5,6},{6,5},{7,4},{8,11},{9,10},{10,... | collective-permute-start | bytes 196616 | tf_op jit(solution)/shard_map/ppermute | solution.py:587
  107.0 0.9 shard_map.98
  107.9 3.2 %collective-permute-done.25.refs_2_ = f32[16,8,128]{2,1,0:T(8,128)S(1)} collective-permute-done((f32[16,8,128]{2,1,0:T(8,128)S(1)}, f32[16,8,128]{2,1,0:T(8,128)S(1)}, u32[]{:S(2)}, u32[]{:S(2)}) %collective-permute-start.25) | collective-permute-done | bytes 65568 | tf_op jit(solution)/shard_map/ppermute | solution.py:587
  111.1 0.9 shard_map.99
  (31 shorter events, 2.3 us)
Async XLA Ops:
  2.9 13.4 %collective-permute-start = (f32[32,8,128]{2,1,0:T(8,128)S(1)}, f32[32,8,128]{2,1,0:T(8,128)S(1)}, u32[]{:S(2)}, u32[]{:S(2)}) collective-permute-start(f32[32,8,128]{2,1,0:T(8,128)S(1)} %get-tuple-element.59), channel_id=1, source_target_pairs={{0,0},{1,1},{2,2},{3,3},{4,16},{5,17},{6,18},{7,19},{8,4},{9,5},{1... | collective-permute-start | bytes 393224 | tf_op jit(solution)/shard_map/ppermute | solution.py:587
  3.6 12.8 %collective-permute-start.1 = (f32[32,8,128]{2,1,0:T(8,128)S(1)}, f32[32,8,128]{2,1,0:T(8,128)S(1)}, u32[]{:S(2)}, u32[]{:S(2)}) collective-permute-start(f32[32,8,128]{2,1,0:T(8,128)S(1)} %get-tuple-element.59), channel_id=1, source_target_pairs={{0,16},{1,17},{2,18},{3,19},{4,0},{5,1},{6,2},{7,3},{8,20},{9,21},... | collective-permute-start | bytes 393224 | tf_op jit(solution)/shard_map/ppermute | solution.py:587
  9.3 10.2 %collective-permute-start.2 = (f32[32,8,128]{2,1,0:T(8,128)S(1)}, f32[32,8,128]{2,1,0:T(8,128)S(1)}, u32[]{:S(2)}, u32[]{:S(2)}) collective-permute-start(f32[32,8,128]{2,1,0:T(8,128)S(1)} %get-tuple-element.63), channel_id=1, source_target_pairs={{0,0},{1,1},{2,2},{3,3},{4,16},{5,17},{6,18},{7,19},{8,4},{9,5},{1... | collective-permute-start | bytes 393224 | tf_op jit(solution)/shard_map/ppermute | solution.py:587
  10.0 9.6 %collective-permute-start.3 = (f32[32,8,128]{2,1,0:T(8,128)S(1)}, f32[32,8,128]{2,1,0:T(8,128)S(1)}, u32[]{:S(2)}, u32[]{:S(2)}) collective-permute-start(f32[32,8,128]{2,1,0:T(8,128)S(1)} %get-tuple-element.63), channel_id=1, source_target_pairs={{0,16},{1,17},{2,18},{3,19},{4,0},{5,1},{6,2},{7,3},{8,20},{9,21},... | collective-permute-start | bytes 393224 | tf_op jit(solution)/shard_map/ppermute | solution.py:587
  19.4 43.2 %copy-start = (f32[16,8]{0,1:T(8,128)S(1)}, f32[16,8]{0,1:T(8,128)}, u32[]{:S(2)}) copy-start(f32[16,8]{0,1:T(8,128)} %param.11) | copy-start | bytes 1540
  19.4 14.8 %collective-permute-start.4 = (f32[36,16,128]{2,1,0:T(8,128)S(1)}, f32[36,16,128]{2,1,0:T(8,128)S(1)}, u32[]{:S(2)}, u32[]{:S(2)}) collective-permute-start(f32[36,16,128]{2,1,0:T(8,128)S(1)} %get-tuple-element.67), channel_id=1, source_target_pairs={{0,4},{1,5},{2,6},{3,7},{4,0},{5,1},{6,2},{7,3},{8,12},{9,13},{10,... | collective-permute-start | bytes 884744 | tf_op jit(solution)/shard_map/ppermute | solution.py:587
  23.1 11.2 %collective-permute-start.5 = (f32[36,16,128]{2,1,0:T(8,128)S(1)}, f32[36,16,128]{2,1,0:T(8,128)S(1)}, u32[]{:S(2)}, u32[]{:S(2)}) collective-permute-start(f32[36,16,128]{2,1,0:T(8,128)S(1)} %get-tuple-element.68), channel_id=1, source_target_pairs={{0,4},{1,5},{2,6},{3,7},{4,0},{5,1},{6,2},{7,3},{8,12},{9,13},{10,... | collective-permute-start | bytes 884744 | tf_op jit(solution)/shard_map/ppermute | solution.py:587
  24.0 10.3 %collective-permute-start.6 = (f32[64,8,128]{2,1,0:T(8,128)S(1)}, f32[64,8,128]{2,1,0:T(8,128)S(1)}, u32[]{:S(2)}, u32[]{:S(2)}) collective-permute-start(f32[64,8,128]{2,1,0:T(8,128)S(1)} %get-tuple-element.69.mine_ref), channel_id=1, source_target_pairs={{0,8},{1,9},{2,10},{3,11},{4,12},{5,13},{6,14},{7,15},{24,16},{25,... | collective-permute-start | bytes 786440 | tf_op jit(solution)/shard_map/ppermute | solution.py:587
  28.0 6.2 %collective-permute-start.7 = (f32[32,8,128]{2,1,0:T(8,128)S(1)}, f32[32,8,128]{2,1,0:T(8,128)S(1)}, u32[]{:S(2)}, u32[]{:S(2)}) collective-permute-start(f32[32,8,128]{2,1,0:T(8,128)S(1)} %collective-permute-done.a_ref), channel_id=1, source_target_pairs={{4,0},{5,1},{6,2},{7,3},{24,28},{25,29},{26,30},{27,31}} | collective-permute-start | bytes 393224 | tf_op jit(solution)/shard_map/ppermute | solution.py:587
  29.3 4.9 %collective-permute-start.8 = (f32[32,8,128]{2,1,0:T(8,128)S(1)}, f32[32,8,128]{2,1,0:T(8,128)S(1)}, u32[]{:S(2)}, u32[]{:S(2)}) collective-permute-start(f32[32,8,128]{2,1,0:T(8,128)S(1)} %collective-permute-done.2.a_ref), channel_id=1, source_target_pairs={{4,0},{5,1},{6,2},{7,3},{24,28},{25,29},{26,30},{27,31}} | collective-permute-start | bytes 393224 | tf_op jit(solution)/shard_map/ppermute | solution.py:587
  35.5 12.2 %collective-permute-start.9 = (f32[65,8,128]{2,1,0:T(8,128)S(1)}, f32[65,8,128]{2,1,0:T(8,128)S(1)}, u32[]{:S(2)}, u32[]{:S(2)}) collective-permute-start(f32[65,8,128]{2,1,0:T(8,128)S(1)} %get-tuple-element.72), channel_id=1, source_target_pairs={{0,8},{1,9},{2,10},{3,11},{4,12},{5,13},{6,14},{7,15},{8,0},{9,1},... | collective-permute-start | bytes 798728 | tf_op jit(solution)/shard_map/ppermute | solution.py:587
  38.0 4.3 %collective-permute-start.10 = (f32[16,8,128]{2,1,0:T(8,128)S(1)}, f32[16,8,128]{2,1,0:T(8,128)S(1)}, u32[]{:S(2)}, u32[]{:S(2)}) collective-permute-start(f32[16,8,128]{2,1,0:T(8,128)S(1)} %get-tuple-element.78.a_ref), channel_id=1, source_target_pairs={{0,1},{1,0},{2,3},{3,2},{4,5},{5,4},{6,7},{7,6},{8,9},{9,8},{10,11... | collective-permute-start | bytes 196616 | tf_op jit(solution)/shard_map/ppermute | solution.py:587
  42.3 5.2 %collective-permute-start.11 = (f32[16,8,128]{2,1,0:T(8,128)S(1)}, f32[16,8,128]{2,1,0:T(8,128)S(1)}, u32[]{:S(2)}, u32[]{:S(2)}) collective-permute-start(f32[16,8,128]{2,1,0:T(8,128)S(1)} %shard_map.89.refs_0_), channel_id=1, source_target_pairs={{0,2},{1,3},{2,0},{3,1},{4,6},{5,7},{6,4},{7,5},{8,10},{9,11},{10,... | collective-permute-start | bytes 196616 | tf_op jit(solution)/shard_map/ppermute | solution.py:587
  45.0 9.7 %all-to-all-start = ((f32[32,1,128]{2,1,0:T(1,128)}), f32[32,1,128]{2,1,0:T(1,128)S(1)}, u32[]{:S(2)}, u32[]{:S(2)}) async-start(f32[32,1,128]{2,1,0:T(1,128)} %bitcast.3), calls=%async_computation | async-start | bytes 32768 | tf_op jit(solution)/shard_map/all_to_all | solution.py:690
  54.9 9.7 %collective-permute-start.12 = (f32[32,8,128]{2,1,0:T(8,128)S(1)}, f32[32,8,128]{2,1,0:T(8,128)S(1)}, u32[]{:S(2)}, u32[]{:S(2)}) collective-permute-start(f32[32,8,128]{2,1,0:T(8,128)S(1)} %get-tuple-element.81), channel_id=1, source_target_pairs={{0,0},{1,1},{2,2},{3,3},{4,16},{5,17},{6,18},{7,19},{8,4},{9,5},{1... | collective-permute-start | bytes 393224 | tf_op jit(solution)/shard_map/ppermute | solution.py:587
  55.6 9.2 %collective-permute-start.13 = (f32[32,8,128]{2,1,0:T(8,128)S(1)}, f32[32,8,128]{2,1,0:T(8,128)S(1)}, u32[]{:S(2)}, u32[]{:S(2)}) collective-permute-start(f32[32,8,128]{2,1,0:T(8,128)S(1)} %get-tuple-element.81), channel_id=1, source_target_pairs={{0,16},{1,17},{2,18},{3,19},{4,0},{5,1},{6,2},{7,3},{8,20},{9,21},... | collective-permute-start | bytes 393224 | tf_op jit(solution)/shard_map/ppermute | solution.py:587
  59.0 8.8 %collective-permute-start.14 = (f32[32,8,128]{2,1,0:T(8,128)S(1)}, f32[32,8,128]{2,1,0:T(8,128)S(1)}, u32[]{:S(2)}, u32[]{:S(2)}) collective-permute-start(f32[32,8,128]{2,1,0:T(8,128)S(1)} %get-tuple-element.84), channel_id=1, source_target_pairs={{0,0},{1,1},{2,2},{3,3},{4,16},{5,17},{6,18},{7,19},{8,4},{9,5},{1... | collective-permute-start | bytes 393224 | tf_op jit(solution)/shard_map/ppermute | solution.py:587
  59.6 8.5 %collective-permute-start.15 = (f32[32,8,128]{2,1,0:T(8,128)S(1)}, f32[32,8,128]{2,1,0:T(8,128)S(1)}, u32[]{:S(2)}, u32[]{:S(2)}) collective-permute-start(f32[32,8,128]{2,1,0:T(8,128)S(1)} %get-tuple-element.84), channel_id=1, source_target_pairs={{0,16},{1,17},{2,18},{3,19},{4,0},{5,1},{6,2},{7,3},{8,20},{9,21},... | collective-permute-start | bytes 393224 | tf_op jit(solution)/shard_map/ppermute | solution.py:587
  67.7 14.7 %collective-permute-start.16 = (f32[36,16,128]{2,1,0:T(8,128)S(1)}, f32[36,16,128]{2,1,0:T(8,128)S(1)}, u32[]{:S(2)}, u32[]{:S(2)}) collective-permute-start(f32[36,16,128]{2,1,0:T(8,128)S(1)} %get-tuple-element.86), channel_id=1, source_target_pairs={{0,4},{1,5},{2,6},{3,7},{4,0},{5,1},{6,2},{7,3},{8,12},{9,13},{10,... | collective-permute-start | bytes 884744 | tf_op jit(solution)/shard_map/ppermute | solution.py:587
  71.5 11.0 %collective-permute-start.17 = (f32[36,16,128]{2,1,0:T(8,128)S(1)}, f32[36,16,128]{2,1,0:T(8,128)S(1)}, u32[]{:S(2)}, u32[]{:S(2)}) collective-permute-start(f32[36,16,128]{2,1,0:T(8,128)S(1)} %get-tuple-element.87), channel_id=1, source_target_pairs={{0,4},{1,5},{2,6},{3,7},{4,0},{5,1},{6,2},{7,3},{8,12},{9,13},{10,... | collective-permute-start | bytes 884744 | tf_op jit(solution)/shard_map/ppermute | solution.py:587
  73.1 9.3 %collective-permute-start.18 = (f32[64,8,128]{2,1,0:T(8,128)S(1)}, f32[64,8,128]{2,1,0:T(8,128)S(1)}, u32[]{:S(2)}, u32[]{:S(2)}) collective-permute-start(f32[64,8,128]{2,1,0:T(8,128)S(1)} %get-tuple-element.88.mine_ref), channel_id=1, source_target_pairs={{0,8},{1,9},{2,10},{3,11},{4,12},{5,13},{6,14},{7,15},{24,16},{25,... | collective-permute-start | bytes 786440 | tf_op jit(solution)/shard_map/ppermute | solution.py:587
  76.7 3.2 %collective-permute-start.19 = (f32[32,8,128]{2,1,0:T(8,128)S(1)}, f32[32,8,128]{2,1,0:T(8,128)S(1)}, u32[]{:S(2)}, u32[]{:S(2)}) collective-permute-start(f32[32,8,128]{2,1,0:T(8,128)S(1)} %collective-permute-done.12.a_ref), channel_id=1, source_target_pairs={{4,0},{5,1},{6,2},{7,3},{24,28},{25,29},{26,30},{27,31}} | collective-permute-start | bytes 393224 | tf_op jit(solution)/shard_map/ppermute | solution.py:587
  78.0 3.2 %collective-permute-start.20 = (f32[32,8,128]{2,1,0:T(8,128)S(1)}, f32[32,8,128]{2,1,0:T(8,128)S(1)}, u32[]{:S(2)}, u32[]{:S(2)}) collective-permute-start(f32[32,8,128]{2,1,0:T(8,128)S(1)} %collective-permute-done.14.a_ref), channel_id=1, source_target_pairs={{4,0},{5,1},{6,2},{7,3},{24,28},{25,29},{26,30},{27,31}} | collective-permute-start | bytes 393224 | tf_op jit(solution)/shard_map/ppermute | solution.py:587
  83.6 12.9 %collective-permute-start.21 = (f32[65,8,128]{2,1,0:T(8,128)S(1)}, f32[65,8,128]{2,1,0:T(8,128)S(1)}, u32[]{:S(2)}, u32[]{:S(2)}) collective-permute-start(f32[65,8,128]{2,1,0:T(8,128)S(1)} %get-tuple-element.91), channel_id=1, source_target_pairs={{0,8},{1,9},{2,10},{3,11},{4,12},{5,13},{6,14},{7,15},{8,0},{9,1},... | collective-permute-start | bytes 798728 | tf_op jit(solution)/shard_map/ppermute | solution.py:587
  86.2 4.3 %collective-permute-start.22 = (f32[16,8,128]{2,1,0:T(8,128)S(1)}, f32[16,8,128]{2,1,0:T(8,128)S(1)}, u32[]{:S(2)}, u32[]{:S(2)}) collective-permute-start(f32[16,8,128]{2,1,0:T(8,128)S(1)} %get-tuple-element.96.a_ref), channel_id=1, source_target_pairs={{0,1},{1,0},{2,3},{3,2},{4,5},{5,4},{6,7},{7,6},{8,9},{9,8},{10,11... | collective-permute-start | bytes 196616 | tf_op jit(solution)/shard_map/ppermute | solution.py:587
  90.5 5.9 %collective-permute-start.23 = (f32[16,8,128]{2,1,0:T(8,128)S(1)}, f32[16,8,128]{2,1,0:T(8,128)S(1)}, u32[]{:S(2)}, u32[]{:S(2)}) collective-permute-start(f32[16,8,128]{2,1,0:T(8,128)S(1)} %shard_map.95.refs_0_), channel_id=1, source_target_pairs={{0,2},{1,3},{2,0},{3,1},{4,6},{5,7},{6,4},{7,5},{8,10},{9,11},{10,... | collective-permute-start | bytes 196616 | tf_op jit(solution)/shard_map/ppermute | solution.py:587
  91.1 11.2 %all-to-all-start.1 = ((f32[32,1,128]{2,1,0:T(1,128)}), f32[32,1,128]{2,1,0:T(1,128)S(1)}, u32[]{:S(2)}, u32[]{:S(2)}) async-start(f32[32,1,128]{2,1,0:T(1,128)} %bitcast.6), calls=%async_computation.1 | async-start | bytes 32768 | tf_op jit(solution)/shard_map/all_to_all | solution.py:690
  102.5 5.4 %collective-permute-start.24 = (f32[16,8,128]{2,1,0:T(8,128)S(1)}, f32[16,8,128]{2,1,0:T(8,128)S(1)}, u32[]{:S(2)}, u32[]{:S(2)}) collective-permute-start(f32[16,8,128]{2,1,0:T(8,128)S(1)} %get-tuple-element.101.refs_0_), channel_id=1, source_target_pairs={{0,1},{1,0},{2,3},{3,2},{4,5},{5,4},{6,7},{7,6},{8,9},{9,8},{10,11... | collective-permute-start | bytes 196616 | tf_op jit(solution)/shard_map/ppermute | solution.py:587
  103.1 8.0 %collective-permute-start.25 = (f32[16,8,128]{2,1,0:T(8,128)S(1)}, f32[16,8,128]{2,1,0:T(8,128)S(1)}, u32[]{:S(2)}, u32[]{:S(2)}) collective-permute-start(f32[16,8,128]{2,1,0:T(8,128)S(1)} %get-tuple-element.101.refs_0_), channel_id=1, source_target_pairs={{0,2},{1,3},{2,0},{3,1},{4,6},{5,7},{6,4},{7,5},{8,10},{9,11},{10,... | collective-permute-start | bytes 196616 | tf_op jit(solution)/shard_map/ppermute | solution.py:587
  103.7 7.4 %collective-permute-start.26 = (f32[16,8,128]{2,1,0:T(8,128)S(1)}, f32[16,8,128]{2,1,0:T(8,128)S(1)}, u32[]{:S(2)}, u32[]{:S(2)}) collective-permute-start(f32[16,8,128]{2,1,0:T(8,128)S(1)} %get-tuple-element.101.refs_0_), channel_id=1, source_target_pairs={{0,3},{1,2},{2,1},{3,0},{4,7},{5,6},{6,5},{7,4},{8,11},{9,10},{10,... | collective-permute-start | bytes 196616 | tf_op jit(solution)/shard_map/ppermute | solution.py:587

commit v11 on v9

--- a/solution.py
+++ b/solution.py
@@ -15,7 +15,7 @@
 AXES = ("row", "col", "band")
 CHUNK = 4
 PARTS = 4
-HEAD = 2
+HEAD = 4
 LIMIT = pltpu.CompilerParams(vmem_limit_bytes=16 * 2**20)
 
 
@@ -289,10 +289,10 @@
 
 def sum_kernel(dims, flux_hbm, vis_hbm, live_ref, a_ref, b_ref, head_ref, *refs):
     F, T, D, O, _, _ = dims
-    upright_ref, refs = (refs[0], refs[1:]) if len(refs) == 9 else (None, refs)
+    upright_ref, refs = (refs[0], refs[1:]) if len(refs) == 8 else (None, refs)
     keep_ref, send_ref, refs = refs[0], refs[1], refs[2:]
     power_ref, refs = (refs[0], refs[1:]) if upright_ref is not None else (None, refs)
-    vis_ref, distinct, flux_ref, sems = refs[:4]
+    vis_ref, distinct, flux_ref, sems = refs
     rows, cols = vis_ref.shape[3], vis_ref.shape[4]
     row = lax.axis_index("row")
     col = lax.axis_index("col")
@@ -312,7 +312,7 @@
     blocks = block_mask(2 * D)
     nt = (((1,), (1,)), ((), ()))
 
-    def body(step, upright, start, power, source):
+    def body(step, power, source):
         highs, lows = [], []
         lives = live_ref[pl.ds(step * 8, 8), :]
         mask = distinct[...]
@@ -345,11 +345,13 @@
                 even, odd = join_low(v0, v1), join_high(v0, v1)
                 keep_ref[step * 9 + j] = jnp.where(parity == 0, even, odd)
                 send_ref[step * 9 + j] = jnp.where(parity == 0, odd, even)
-                if upright is not None:
+                if upright_ref is not None:
                     square = [x.astype(jnp.float32) for x in seen]
                     square = square[0] * square[0] + square[1] * square[1]
-                    at = start + j
-                    square = square * jnp.broadcast_to(upright[:, at : at + 1], square.shape)
+                    at = jnp.full(square.shape, ft, jnp.int32)
+                    square = square * jnp.take_along_axis(
+                        upright_ref[...], at, axis=1, mode="promise_in_bounds"
+                    )
                     square = jnp.sum(square.reshape(rows // 8, 8, cols), axis=0)
                     power = power + square * lives[j : j + 1, :]
         high = jnp.concatenate(highs, axis=0)
@@ -365,31 +367,22 @@
         send_ref[step * 9 + 8] = folded
         return power
 
-    def roll_to(c):
-        if upright_ref is None:
-            return None
-        upright = refs[4]
-        upright[...] = pltpu.roll(upright_ref[...], (2 * O - c * CHUNK * T) % (2 * O), 1)
-        return upright
-
     def chunk(c, power):
         for i in range(CHUNK):
             vis_copy(c * CHUNK + i).wait()
 
-        upright = roll_to(c)
         for j in range(CHUNK // group):
-            power = body(c * (CHUNK // group) + j, upright, j * 8, power, vis_ref)
+            power = body(c * (CHUNK // group) + j, power, vis_ref)
         return power
 
     flux_copy.wait()
     power = jnp.zeros((8, cols), jnp.float32)
-    upright = roll_to(0)
     for j in range(CHUNK // group):
         inside = (j + 1) * group <= HEAD
         if not inside:
             for i in range(group):
                 vis_copy(j * group + i).wait()
-        power = body(j, upright, j * 8, power, head_ref if inside else vis_ref)
+        power = body(j, power, head_ref if inside else vis_ref)
     power = lax.fori_loop(1, F // CHUNK, chunk, power)
     if power_ref is not None:
         power = jnp.sum(power, axis=0, keepdims=True)
@@ -648,7 +641,7 @@
                 pltpu.VMEM((rows, cols), vis.dtype),
                 pltpu.SMEM(flux_t.shape, f32),
                 pltpu.SemaphoreType.DMA((F + 1,)),
-            ] + [pltpu.VMEM((rows, W), f32)] * len(more),
+            ],
             compiler_params=LIMIT,
             name="sums",
         )(far(flux_t), far(vis), live_col, *got, head, *more)

time: 116 us -> 116 us (level)
  transfers between devices with their start and end apart: 21 -> 21, of which waited for: 10 -> 10; matrix products, arithmetic and copies ran while one was open for 0% -> 0% of each run, Pallas kernels for 5% -> 6%
where the time goes in v11:
time: 116 us; the launch traced here: 115 us
  waiting for transfers between devices  46.9 us (40%)
  starting transfers between devices  44.6 us (38%)
  Pallas kernels  22.8 us (20%)
    ppermute x19, starting transfers between devices, permute(): return lax.ppermute(x, AXES, pairs)  38.1 us
    ppermute x19, waiting for transfers between devices, permute(): return lax.ppermute(x, AXES, pairs)  34.9 us
    all_to_all x2, waiting for transfers between devices, shards(): scalar = lax.all_to_all(scalar, AXES, 0, 0, tiled=True)  12 us
    pallas_call x2, Pallas kernels, shards(): pl.pallas_call(functools.partial(sum_kernel, dims), out_shape=[pair, pair...  10.1 us
    all_to_all x2, starting transfers between devices, shards(): scalar = lax.all_to_all(scalar, AXES, 0, 0, tiled=True)  6.59 us
    pallas_call x2, Pallas kernels, shards(): pl.pallas_call(functools.partial(residual_kernel, dims), out_shape=[line,...  2.43 us
    pallas_call x1, Pallas kernels, shards(): pl.pallas_call(functools.partial(again_kernel, dims), out_shape=[fit, who...  2.36 us
    pallas_call x1, Pallas kernels, shards(): pl.pallas_call(functools.partial(setup_kernel, dims, cols), out_shape=[ar...  2.34 us
  transfers between devices with their start and end apart: 21, of which 10 were waited for; matrix products, arithmetic and copies ran while one was open for 0% of the time, Pallas kernels for 6%

profile of v11, /device:TPU:0, one launch (start us, length us, event | category | flops | bytes accessed | tf_op | source)
XLA Modules:
  0.0 115.2 jit_solution(3468814840981473084)
XLA Ops:
  0.6 2.2 %start.1 = (f32[64,8,128]{2,1,0:T(8,128)S(1)}, f32[64,8,128]{2,1,0:T(8,128)S(1)}, f32[64,8,128]{2,1,0:T(8,128)S(1)}) custom-call(f32[3,4,512]{2,1,0:T(4,128)} %bitcast.16, f32[3,8]{1,0:T(4,128)} %lmn_hbm.1, f32[16,4,2,8,64]{4,3,2,1,0:T(8,128)} %gains_hbm.1), custom_call_target="tpu_custom_call" | custom-call | tf_op jit(solution)/shard_map/start/pallas_call | solution.py:584
  2.9 0.7 collective-permute-start
  3.6 5.7 %collective-permute-start.1 = (f32[64,8,128]{2,1,0:T(8,128)S(1)}, f32[64,8,128]{2,1,0:T(8,128)S(1)}, u32[]{:S(2)}, u32[]{:S(2)}) collective-permute-start(f32[64,8,128]{2,1,0:T(8,128)S(1)} %get-tuple-element.50.mine_ref), channel_id=1, source_target_pairs={{0,16},{1,17},{2,18},{3,19},{4,0},{5,1},{6,2},{7,3},{8,20},{9,21},... | collective-permute-start | bytes 786440 | tf_op jit(solution)/shard_map/ppermute | solution.py:572
  9.3 2.3 %setup.1 = (f32[64,128]{1,0:T(8,128)S(1)}, f32[64,128]{1,0:T(8,128)S(1)}, f32[64,128]{1,0:T(8,128)S(1)}, f32[256,128]{1,0:T(8,128)S(1)}, f32[64,8,128]{2,1,0:T(8...) custom-call(f32[8,16]{1,0:T(8,128)} %bitcast.10, ...), custom_call_target="tpu_custom_call" | custom-call | tf_op jit(solution)/shard_map/setup/pallas_call | solution.py:603
  11.6 7.9 %collective-permute-done.1.b_ref.got_ref = f32[64,8,128]{2,1,0:T(8,128)S(1)} collective-permute-done((f32[64,8,128]{2,1,0:T(8,128)S(1)}, f32[64,8,128]{2,1,0:T(8,128)S(1)}, u32[]{:S(2)}, u32[]{:S(2)}) %collective-permute-start.1) | collective-permute-done | bytes 262176 | tf_op jit(solution)/shard_map/ppermute | solution.py:572
  19.6 5.6 %sums.2 = (f32[72,16,128]{2,1,0:T(8,128)S(1)}, f32[72,16,128]{2,1,0:T(8,128)S(1)}, f32[1,128]{1,0:T(1,128)S(1)}) custom-call(f32[8,16]{1,0:T(8,128)} %bitcast.11, bf16[16,4,2,256,128]{4,3,2,1,0:T(8,128)(2,1)} %vis_hbm.7, f32[64,128]{1,0:T(8,128)S(1)} %get-tuple-element.49.live_ref, f32[64,8,128]{2,1,0:T(8,128)S(1)} %collective-permute-done.a_ref, ...), custom_call_target="tpu_custom_call" | custom-call | tf_op jit(solution)/shard_map/sums/pallas_call | solution.py:634
  25.1 0.9 collective-permute-start.2
  26.0 4.0 %collective-permute-start.3 = (f32[64,8,128]{2,1,0:T(8,128)S(1)}, f32[64,8,128]{2,1,0:T(8,128)S(1)}, u32[]{:S(2)}, u32[]{:S(2)}) collective-permute-start(f32[64,8,128]{2,1,0:T(8,128)S(1)} %get-tuple-element.50.mine_ref), channel_id=1, source_target_pairs={{0,8},{1,9},{2,10},{3,11},{4,12},{5,13},{6,14},{7,15},{24,16},{25,... | collective-permute-start | bytes 786440 | tf_op jit(solution)/shard_map/ppermute | solution.py:572
  30.1 1.3 %collective-permute-start.4 = (f32[64,8,128]{2,1,0:T(8,128)S(1)}, f32[64,8,128]{2,1,0:T(8,128)S(1)}, u32[]{:S(2)}, u32[]{:S(2)}) collective-permute-start(f32[64,8,128]{2,1,0:T(8,128)S(1)} %collective-permute-done.a_ref), channel_id=1, source_target_pairs={{4,0},{5,1},{6,2},{7,3},{24,28},{25,29},{26,30},{27,31}} | collective-permute-start | bytes 786440 | tf_op jit(solution)/shard_map/ppermute | solution.py:572
  31.4 4.9 %collective-permute-done.3.theirs_ref = f32[64,8,128]{2,1,0:T(8,128)S(1)} collective-permute-done((f32[64,8,128]{2,1,0:T(8,128)S(1)}, f32[64,8,128]{2,1,0:T(8,128)S(1)}, u32[]{:S(2)}, u32[]{:S(2)}) %collective-permute-start.3) | collective-permute-done | bytes 262176 | tf_op jit(solution)/shard_map/ppermute | solution.py:572
  36.2 1.2 %residual.2 = (f32[65,8,128]{2,1,0:T(8,128)S(1)}, f32[65,8,128]{2,1,0:T(8,128)S(1)}, f32[32,128]{1,0:T(8,128)}) custom-call(f32[64,128]{1,0:T(8,128)S(1)} %get-tuple-element.44.live_ref, f32[1,128]{1,0:T(1,128)S(1)} %get-tuple-element.48.extra_ref, f32[1,128]{1,0:T(1,128)S(1)} %get-tuple-element.53.power_ref, f32[72,16,128]{2,1,0:T(8,128)S(1)} %get-tuple-element.54.kept_ref, ...), custom_call_target="tpu_custom_call" | custom-call | tf_op jit(solution)/shard_map/residual/pallas_call | solution.py:656
  37.5 0.0 copy-start
  37.5 2.5 %collective-permute-start.5 = (f32[65,8,128]{2,1,0:T(8,128)S(1)}, f32[65,8,128]{2,1,0:T(8,128)S(1)}, u32[]{:S(2)}, u32[]{:S(2)}) collective-permute-start(f32[65,8,128]{2,1,0:T(8,128)S(1)} %get-tuple-element.58), channel_id=1, source_target_pairs={{0,8},{1,9},{2,10},{3,11},{4,12},{5,13},{6,14},{7,15},{8,0},{9,1},... | collective-permute-start | bytes 798728 | tf_op jit(solution)/shard_map/ppermute | solution.py:572
  40.0 1.6 %collective-permute-start.6 = (f32[16,8,128]{2,1,0:T(8,128)S(1)}, f32[16,8,128]{2,1,0:T(8,128)S(1)}, u32[]{:S(2)}, u32[]{:S(2)}) collective-permute-start(f32[16,8,128]{2,1,0:T(8,128)S(1)} %get-tuple-element.64.a_ref), channel_id=1, source_target_pairs={{0,1},{1,0},{2,3},{3,2},{4,5},{5,4},{6,7},{7,6},{8,9},{9,8},{10,11... | collective-permute-start | bytes 196616 | tf_op jit(solution)/shard_map/ppermute | solution.py:572
  41.6 2.7 %collective-permute-done.6.b_ref = f32[16,8,128]{2,1,0:T(8,128)S(1)} collective-permute-done((f32[16,8,128]{2,1,0:T(8,128)S(1)}, f32[16,8,128]{2,1,0:T(8,128)S(1)}, u32[]{:S(2)}, u32[]{:S(2)}) %collective-permute-start.6) | collective-permute-done | bytes 65568 | tf_op jit(solution)/shard_map/ppermute | solution.py:572
  44.3 2.7 %collective-permute-start.7 = (f32[16,8,128]{2,1,0:T(8,128)S(1)}, f32[16,8,128]{2,1,0:T(8,128)S(1)}, u32[]{:S(2)}, u32[]{:S(2)}) collective-permute-start(f32[16,8,128]{2,1,0:T(8,128)S(1)} %shard_map.87.refs_0_), channel_id=1, source_target_pairs={{0,2},{1,3},{2,0},{3,1},{4,6},{5,7},{6,4},{7,5},{8,10},{9,11},{10,... | collective-permute-start | bytes 196616 | tf_op jit(solution)/shard_map/ppermute | solution.py:572
  47.0 2.5 %all-to-all-start = ((f32[32,1,128]{2,1,0:T(1,128)}), f32[32,1,128]{2,1,0:T(1,128)S(1)}, u32[]{:S(2)}, u32[]{:S(2)}) async-start(f32[32,1,128]{2,1,0:T(1,128)} %bitcast.3), calls=%async_computation | async-start | bytes 32768 | tf_op jit(solution)/shard_map/all_to_all | solution.py:669
  49.5 0.0 collective-permute-done.7.refs_1_
  49.5 0.1 shard_map.88.refs_3_
  49.6 0.4 shard_map.86
  50.0 6.6 %all-to-all-done = f32[32,1,128]{2,1,0:T(1,128)S(1)} async-done(((f32[32,1,128]{2,1,0:T(1,128)}), f32[32,1,128]{2,1,0:T(1,128)S(1)}, u32[]{:S(2)}, u32[]{:S(2)}) %all-to-all-start) | async-done | bytes 16416 | tf_op jit(solution)/shard_map/all_to_all | solution.py:669
  56.6 0.3 shard_map.89
  57.0 0.7 collective-permute-start.8
  57.6 3.3 %collective-permute-start.9 = (f32[64,8,128]{2,1,0:T(8,128)S(1)}, f32[64,8,128]{2,1,0:T(8,128)S(1)}, u32[]{:S(2)}, u32[]{:S(2)}) collective-permute-start(f32[64,8,128]{2,1,0:T(8,128)S(1)} %get-tuple-element.67.mine_ref), channel_id=1, source_target_pairs={{0,16},{1,17},{2,18},{3,19},{4,0},{5,1},{6,2},{7,3},{8,20},{9,21},... | collective-permute-start | bytes 786440 | tf_op jit(solution)/shard_map/ppermute | solution.py:572
  61.0 2.4 %again.1 = (f32[16,8,128]{2,1,0:T(8,128)S(1)}, f32[64,8,128]{2,1,0:T(8,128)S(1)}, f32[64,8,128]{2,1,0:T(8,128)S(1)}, f32[1,128]{1,0:T(1,128)S(1)}, bf16[4,4,2,256,128]{4,3,2,1,0:T(8,128)(2,1)S(1)}) custom-call(f32[8,16]{1,0:T(8,128)S(1)} %bitcast.13, bf16[16,4,2,256,128]{4,3,2,1,0:T(8,128)(2,1)} %vis_hbm.7, f32[1,128]{1,0:T(1,128)S(1)} %get-tuple-element.45.samples_ref, ...), custom_call_target="tpu_custom_call" | custom-call | tf_op jit(solution)/shard_map/again/pallas_call | solution.py:622
  63.4 6.9 %collective-permute-done.9.b_ref.got_ref = f32[64,8,128]{2,1,0:T(8,128)S(1)} collective-permute-done((f32[64,8,128]{2,1,0:T(8,128)S(1)}, f32[64,8,128]{2,1,0:T(8,128)S(1)}, u32[]{:S(2)}, u32[]{:S(2)}) %collective-permute-start.9) | collective-permute-done | bytes 262176 | tf_op jit(solution)/shard_map/ppermute | solution.py:572
  70.2 4.5 %sums.3 = (f32[72,16,128]{2,1,0:T(8,128)S(1)}, f32[72,16,128]{2,1,0:T(8,128)S(1)}) custom-call(f32[8,16]{1,0:T(8,128)} %bitcast.12, bf16[16,4,2,256,128]{4,3,2,1,0:T(8,128)(2,1)} %vis_hbm.7, f32[64,128]{1,0:T(8,128)S(1)} %get-tuple-element.49.live_ref, f32[64,8,128]{2,1,0:T(8,128)S(1)} %collective-permute-done.8.a_ref, ...), custom_call_target="tpu_custom_call" | custom-call | tf_op jit(solution)/shard_map/sums/pallas_call | solution.py:634
  74.7 1.6 %collective-permute-start.10 = (f32[72,16,128]{2,1,0:T(8,128)S(1)}, f32[72,16,128]{2,1,0:T(8,128)S(1)}, u32[]{:S(2)}, u32[]{:S(2)}) collective-permute-start(f32[72,16,128]{2,1,0:T(8,128)S(1)} %get-tuple-element.70), channel_id=1, source_target_pairs={{0,4},{1,5},{2,6},{3,7},{4,0},{5,1},{6,2},{7,3},{8,12},{9,13},{10,... | collective-permute-start | bytes 1769480 | tf_op jit(solution)/shard_map/ppermute | solution.py:572
  76.3 3.6 %collective-permute-start.11 = (f32[64,8,128]{2,1,0:T(8,128)S(1)}, f32[64,8,128]{2,1,0:T(8,128)S(1)}, u32[]{:S(2)}, u32[]{:S(2)}) collective-permute-start(f32[64,8,128]{2,1,0:T(8,128)S(1)} %get-tuple-element.67.mine_ref), channel_id=1, source_target_pairs={{0,8},{1,9},{2,10},{3,11},{4,12},{5,13},{6,14},{7,15},{24,16},{25,... | collective-permute-start | bytes 786440 | tf_op jit(solution)/shard_map/ppermute | solution.py:572
  79.9 1.3 %collective-permute-start.12 = (f32[64,8,128]{2,1,0:T(8,128)S(1)}, f32[64,8,128]{2,1,0:T(8,128)S(1)}, u32[]{:S(2)}, u32[]{:S(2)}) collective-permute-start(f32[64,8,128]{2,1,0:T(8,128)S(1)} %collective-permute-done.8.a_ref), channel_id=1, source_target_pairs={{4,0},{5,1},{6,2},{7,3},{24,28},{25,29},{26,30},{27,31}} | collective-permute-start | bytes 786440 | tf_op jit(solution)/shard_map/ppermute | solution.py:572
  81.2 4.4 %collective-permute-done.11.theirs_ref = f32[64,8,128]{2,1,0:T(8,128)S(1)} collective-permute-done((f32[64,8,128]{2,1,0:T(8,128)S(1)}, f32[64,8,128]{2,1,0:T(8,128)S(1)}, u32[]{:S(2)}, u32[]{:S(2)}) %collective-permute-start.11) | collective-permute-done | bytes 262176 | tf_op jit(solution)/shard_map/ppermute | solution.py:572
  85.6 1.2 %residual.3 = (f32[65,8,128]{2,1,0:T(8,128)S(1)}, f32[65,8,128]{2,1,0:T(8,128)S(1)}, f32[32,128]{1,0:T(8,128)}) custom-call(f32[64,128]{1,0:T(8,128)S(1)} %get-tuple-element.44.live_ref, f32[1,128]{1,0:T(1,128)S(1)} %get-tuple-element.66.extra_ref, f32[1,128]{1,0:T(1,128)S(1)} %get-tuple-element.53.power_ref, f32[72,16,128]{2,1,0:T(8,128)S(1)} %get-tuple-element.69.kept_ref, ...), custom_call_target="tpu_custom_call" | custom-call | tf_op jit(solution)/shard_map/residual/pallas_call | solution.py:656
  86.9 2.5 %collective-permute-start.13 = (f32[65,8,128]{2,1,0:T(8,128)S(1)}, f32[65,8,128]{2,1,0:T(8,128)S(1)}, u32[]{:S(2)}, u32[]{:S(2)}) collective-permute-start(f32[65,8,128]{2,1,0:T(8,128)S(1)} %get-tuple-element.73), channel_id=1, source_target_pairs={{0,8},{1,9},{2,10},{3,11},{4,12},{5,13},{6,14},{7,15},{8,0},{9,1},... | collective-permute-start | bytes 798728 | tf_op jit(solution)/shard_map/ppermute | solution.py:572
  89.4 0.6 collective-permute-start.14
  90.0 3.6 %collective-permute-done.14.b_ref = f32[16,8,128]{2,1,0:T(8,128)S(1)} collective-permute-done((f32[16,8,128]{2,1,0:T(8,128)S(1)}, f32[16,8,128]{2,1,0:T(8,128)S(1)}, u32[]{:S(2)}, u32[]{:S(2)}) %collective-permute-start.14) | collective-permute-done | bytes 65568 | tf_op jit(solution)/shard_map/ppermute | solution.py:572
  93.7 0.6 collective-permute-start.15
  94.3 4.0 %all-to-all-start.1 = ((f32[32,1,128]{2,1,0:T(1,128)}), f32[32,1,128]{2,1,0:T(1,128)S(1)}, u32[]{:S(2)}, u32[]{:S(2)}) async-start(f32[32,1,128]{2,1,0:T(1,128)} %bitcast.6), calls=%async_computation.1 | async-start | bytes 32768 | tf_op jit(solution)/shard_map/all_to_all | solution.py:669
  98.3 1.3 %collective-permute-done.15.refs_1_ = f32[16,8,128]{2,1,0:T(8,128)S(1)} collective-permute-done((f32[16,8,128]{2,1,0:T(8,128)S(1)}, f32[16,8,128]{2,1,0:T(8,128)S(1)}, u32[]{:S(2)}, u32[]{:S(2)}) %collective-permute-start.15) | collective-permute-done | bytes 65568 | tf_op jit(solution)/shard_map/ppermute | solution.py:572
  99.6 0.1 shard_map.92
  99.8 0.4 shard_map.90
  100.1 5.3 %all-to-all-done.1 = f32[32,1,128]{2,1,0:T(1,128)S(1)} async-done(((f32[32,1,128]{2,1,0:T(1,128)}), f32[32,1,128]{2,1,0:T(1,128)S(1)}, u32[]{:S(2)}, u32[]{:S(2)}) %all-to-all-start.1) | async-done | bytes 16416 | tf_op jit(solution)/shard_map/all_to_all | solution.py:669
  105.5 0.2 shard_map.93
  105.7 0.5 collective-permute-start.16
  106.3 0.6 collective-permute-start.17
  106.9 3.3 %collective-permute-start.18 = (f32[16,8,128]{2,1,0:T(8,128)S(1)}, f32[16,8,128]{2,1,0:T(8,128)S(1)}, u32[]{:S(2)}, u32[]{:S(2)}) collective-permute-start(f32[16,8,128]{2,1,0:T(8,128)S(1)} %get-tuple-element.83.refs_0_), channel_id=1, source_target_pairs={{0,3},{1,2},{2,1},{3,0},{4,7},{5,6},{6,5},{7,4},{8,11},{9,10},{10,... | collective-permute-start | bytes 196616 | tf_op jit(solution)/shard_map/ppermute | solution.py:572
  110.2 0.9 shard_map.94
  111.1 3.2 %collective-permute-done.17.refs_2_ = f32[16,8,128]{2,1,0:T(8,128)S(1)} collective-permute-done((f32[16,8,128]{2,1,0:T(8,128)S(1)}, f32[16,8,128]{2,1,0:T(8,128)S(1)}, u32[]{:S(2)}, u32[]{:S(2)}) %collective-permute-start.17) | collective-permute-done | bytes 65568 | tf_op jit(solution)/shard_map/ppermute | solution.py:572
  114.3 0.9 shard_map.95
  (13 shorter events, 0.0 us)
Async XLA Ops:
  2.9 8.8 %collective-permute-start = (f32[64,8,128]{2,1,0:T(8,128)S(1)}, f32[64,8,128]{2,1,0:T(8,128)S(1)}, u32[]{:S(2)}, u32[]{:S(2)}) collective-permute-start(f32[64,8,128]{2,1,0:T(8,128)S(1)} %get-tuple-element.50.mine_ref), channel_id=1, source_target_pairs={{0,0},{1,1},{2,2},{3,3},{4,16},{5,17},{6,18},{7,19},{8,4},{9,5},{1... | collective-permute-start | bytes 786440 | tf_op jit(solution)/shard_map/ppermute | solution.py:572
  3.6 16.0 %collective-permute-start.1 = (f32[64,8,128]{2,1,0:T(8,128)S(1)}, f32[64,8,128]{2,1,0:T(8,128)S(1)}, u32[]{:S(2)}, u32[]{:S(2)}) collective-permute-start(f32[64,8,128]{2,1,0:T(8,128)S(1)} %get-tuple-element.50.mine_ref), channel_id=1, source_target_pairs={{0,16},{1,17},{2,18},{3,19},{4,0},{5,1},{6,2},{7,3},{8,20},{9,21},... | collective-permute-start | bytes 786440 | tf_op jit(solution)/shard_map/ppermute | solution.py:572
  25.1 11.1 %collective-permute-start.2 = (f32[72,16,128]{2,1,0:T(8,128)S(1)}, f32[72,16,128]{2,1,0:T(8,128)S(1)}, u32[]{:S(2)}, u32[]{:S(2)}) collective-permute-start(f32[72,16,128]{2,1,0:T(8,128)S(1)} %get-tuple-element.55), channel_id=1, source_target_pairs={{0,4},{1,5},{2,6},{3,7},{4,0},{5,1},{6,2},{7,3},{8,12},{9,13},{10,... | collective-permute-start | bytes 1769480 | tf_op jit(solution)/shard_map/ppermute | solution.py:572
  26.0 10.2 %collective-permute-start.3 = (f32[64,8,128]{2,1,0:T(8,128)S(1)}, f32[64,8,128]{2,1,0:T(8,128)S(1)}, u32[]{:S(2)}, u32[]{:S(2)}) collective-permute-start(f32[64,8,128]{2,1,0:T(8,128)S(1)} %get-tuple-element.50.mine_ref), channel_id=1, source_target_pairs={{0,8},{1,9},{2,10},{3,11},{4,12},{5,13},{6,14},{7,15},{24,16},{25,... | collective-permute-start | bytes 786440 | tf_op jit(solution)/shard_map/ppermute | solution.py:572
  30.1 6.2 %collective-permute-start.4 = (f32[64,8,128]{2,1,0:T(8,128)S(1)}, f32[64,8,128]{2,1,0:T(8,128)S(1)}, u32[]{:S(2)}, u32[]{:S(2)}) collective-permute-start(f32[64,8,128]{2,1,0:T(8,128)S(1)} %collective-permute-done.a_ref), channel_id=1, source_target_pairs={{4,0},{5,1},{6,2},{7,3},{24,28},{25,29},{26,30},{27,31}} | collective-permute-start | bytes 786440 | tf_op jit(solution)/shard_map/ppermute | solution.py:572
  37.5 23.5 %copy-start = (f32[16,8]{0,1:T(8,128)S(1)}, f32[16,8]{0,1:T(8,128)}, u32[]{:S(2)}) copy-start(f32[16,8]{0,1:T(8,128)} %param.11) | copy-start | bytes 1540
  37.5 12.2 %collective-permute-start.5 = (f32[65,8,128]{2,1,0:T(8,128)S(1)}, f32[65,8,128]{2,1,0:T(8,128)S(1)}, u32[]{:S(2)}, u32[]{:S(2)}) collective-permute-start(f32[65,8,128]{2,1,0:T(8,128)S(1)} %get-tuple-element.58), channel_id=1, source_target_pairs={{0,8},{1,9},{2,10},{3,11},{4,12},{5,13},{6,14},{7,15},{8,0},{9,1},... | collective-permute-start | bytes 798728 | tf_op jit(solution)/shard_map/ppermute | solution.py:572
  40.0 4.3 %collective-permute-start.6 = (f32[16,8,128]{2,1,0:T(8,128)S(1)}, f32[16,8,128]{2,1,0:T(8,128)S(1)}, u32[]{:S(2)}, u32[]{:S(2)}) collective-permute-start(f32[16,8,128]{2,1,0:T(8,128)S(1)} %get-tuple-element.64.a_ref), channel_id=1, source_target_pairs={{0,1},{1,0},{2,3},{3,2},{4,5},{5,4},{6,7},{7,6},{8,9},{9,8},{10,11... | collective-permute-start | bytes 196616 | tf_op jit(solution)/shard_map/ppermute | solution.py:572
  44.3 5.2 %collective-permute-start.7 = (f32[16,8,128]{2,1,0:T(8,128)S(1)}, f32[16,8,128]{2,1,0:T(8,128)S(1)}, u32[]{:S(2)}, u32[]{:S(2)}) collective-permute-start(f32[16,8,128]{2,1,0:T(8,128)S(1)} %shard_map.87.refs_0_), channel_id=1, source_target_pairs={{0,2},{1,3},{2,0},{3,1},{4,6},{5,7},{6,4},{7,5},{8,10},{9,11},{10,... | collective-permute-start | bytes 196616 | tf_op jit(solution)/shard_map/ppermute | solution.py:572
  47.0 9.7 %all-to-all-start = ((f32[32,1,128]{2,1,0:T(1,128)}), f32[32,1,128]{2,1,0:T(1,128)S(1)}, u32[]{:S(2)}, u32[]{:S(2)}) async-start(f32[32,1,128]{2,1,0:T(1,128)} %bitcast.3), calls=%async_computation | async-start | bytes 32768 | tf_op jit(solution)/shard_map/all_to_all | solution.py:669
  57.0 6.4 %collective-permute-start.8 = (f32[64,8,128]{2,1,0:T(8,128)S(1)}, f32[64,8,128]{2,1,0:T(8,128)S(1)}, u32[]{:S(2)}, u32[]{:S(2)}) collective-permute-start(f32[64,8,128]{2,1,0:T(8,128)S(1)} %get-tuple-element.67.mine_ref), channel_id=1, source_target_pairs={{0,0},{1,1},{2,2},{3,3},{4,16},{5,17},{6,18},{7,19},{8,4},{9,5},{1... | collective-permute-start | bytes 786440 | tf_op jit(solution)/shard_map/ppermute | solution.py:572
  57.6 12.6 %collective-permute-start.9 = (f32[64,8,128]{2,1,0:T(8,128)S(1)}, f32[64,8,128]{2,1,0:T(8,128)S(1)}, u32[]{:S(2)}, u32[]{:S(2)}) collective-permute-start(f32[64,8,128]{2,1,0:T(8,128)S(1)} %get-tuple-element.67.mine_ref), channel_id=1, source_target_pairs={{0,16},{1,17},{2,18},{3,19},{4,0},{5,1},{6,2},{7,3},{8,20},{9,21},... | collective-permute-start | bytes 786440 | tf_op jit(solution)/shard_map/ppermute | solution.py:572
  74.7 10.9 %collective-permute-start.10 = (f32[72,16,128]{2,1,0:T(8,128)S(1)}, f32[72,16,128]{2,1,0:T(8,128)S(1)}, u32[]{:S(2)}, u32[]{:S(2)}) collective-permute-start(f32[72,16,128]{2,1,0:T(8,128)S(1)} %get-tuple-element.70), channel_id=1, source_target_pairs={{0,4},{1,5},{2,6},{3,7},{4,0},{5,1},{6,2},{7,3},{8,12},{9,13},{10,... | collective-permute-start | bytes 1769480 | tf_op jit(solution)/shard_map/ppermute | solution.py:572
  76.3 9.3 %collective-permute-start.11 = (f32[64,8,128]{2,1,0:T(8,128)S(1)}, f32[64,8,128]{2,1,0:T(8,128)S(1)}, u32[]{:S(2)}, u32[]{:S(2)}) collective-permute-start(f32[64,8,128]{2,1,0:T(8,128)S(1)} %get-tuple-element.67.mine_ref), channel_id=1, source_target_pairs={{0,8},{1,9},{2,10},{3,11},{4,12},{5,13},{6,14},{7,15},{24,16},{25,... | collective-permute-start | bytes 786440 | tf_op jit(solution)/shard_map/ppermute | solution.py:572
  79.9 5.7 %collective-permute-start.12 = (f32[64,8,128]{2,1,0:T(8,128)S(1)}, f32[64,8,128]{2,1,0:T(8,128)S(1)}, u32[]{:S(2)}, u32[]{:S(2)}) collective-permute-start(f32[64,8,128]{2,1,0:T(8,128)S(1)} %collective-permute-done.8.a_ref), channel_id=1, source_target_pairs={{4,0},{5,1},{6,2},{7,3},{24,28},{25,29},{26,30},{27,31}} | collective-permute-start | bytes 786440 | tf_op jit(solution)/shard_map/ppermute | solution.py:572
  86.9 12.9 %collective-permute-start.13 = (f32[65,8,128]{2,1,0:T(8,128)S(1)}, f32[65,8,128]{2,1,0:T(8,128)S(1)}, u32[]{:S(2)}, u32[]{:S(2)}) collective-permute-start(f32[65,8,128]{2,1,0:T(8,128)S(1)} %get-tuple-element.73), channel_id=1, source_target_pairs={{0,8},{1,9},{2,10},{3,11},{4,12},{5,13},{6,14},{7,15},{8,0},{9,1},... | collective-permute-start | bytes 798728 | tf_op jit(solution)/shard_map/ppermute | solution.py:572
  89.4 4.3 %collective-permute-start.14 = (f32[16,8,128]{2,1,0:T(8,128)S(1)}, f32[16,8,128]{2,1,0:T(8,128)S(1)}, u32[]{:S(2)}, u32[]{:S(2)}) collective-permute-start(f32[16,8,128]{2,1,0:T(8,128)S(1)} %get-tuple-element.78.a_ref), channel_id=1, source_target_pairs={{0,1},{1,0},{2,3},{3,2},{4,5},{5,4},{6,7},{7,6},{8,9},{9,8},{10,11... | collective-permute-start | bytes 196616 | tf_op jit(solution)/shard_map/ppermute | solution.py:572
  93.7 5.9 %collective-permute-start.15 = (f32[16,8,128]{2,1,0:T(8,128)S(1)}, f32[16,8,128]{2,1,0:T(8,128)S(1)}, u32[]{:S(2)}, u32[]{:S(2)}) collective-permute-start(f32[16,8,128]{2,1,0:T(8,128)S(1)} %shard_map.91.refs_0_), channel_id=1, source_target_pairs={{0,2},{1,3},{2,0},{3,1},{4,6},{5,7},{6,4},{7,5},{8,10},{9,11},{10,... | collective-permute-start | bytes 196616 | tf_op jit(solution)/shard_map/ppermute | solution.py:572
  94.3 11.2 %all-to-all-start.1 = ((f32[32,1,128]{2,1,0:T(1,128)}), f32[32,1,128]{2,1,0:T(1,128)S(1)}, u32[]{:S(2)}, u32[]{:S(2)}) async-start(f32[32,1,128]{2,1,0:T(1,128)} %bitcast.6), calls=%async_computation.1 | async-start | bytes 32768 | tf_op jit(solution)/shard_map/all_to_all | solution.py:669
  105.7 5.4 %collective-permute-start.16 = (f32[16,8,128]{2,1,0:T(8,128)S(1)}, f32[16,8,128]{2,1,0:T(8,128)S(1)}, u32[]{:S(2)}, u32[]{:S(2)}) collective-permute-start(f32[16,8,128]{2,1,0:T(8,128)S(1)} %get-tuple-element.83.refs_0_), channel_id=1, source_target_pairs={{0,1},{1,0},{2,3},{3,2},{4,5},{5,4},{6,7},{7,6},{8,9},{9,8},{10,11... | collective-permute-start | bytes 196616 | tf_op jit(solution)/shard_map/ppermute | solution.py:572
  106.3 8.0 %collective-permute-start.17 = (f32[16,8,128]{2,1,0:T(8,128)S(1)}, f32[16,8,128]{2,1,0:T(8,128)S(1)}, u32[]{:S(2)}, u32[]{:S(2)}) collective-permute-start(f32[16,8,128]{2,1,0:T(8,128)S(1)} %get-tuple-element.83.refs_0_), channel_id=1, source_target_pairs={{0,2},{1,3},{2,0},{3,1},{4,6},{5,7},{6,4},{7,5},{8,10},{9,11},{10,... | collective-permute-start | bytes 196616 | tf_op jit(solution)/shard_map/ppermute | solution.py:572
  106.9 7.4 %collective-permute-start.18 = (f32[16,8,128]{2,1,0:T(8,128)S(1)}, f32[16,8,128]{2,1,0:T(8,128)S(1)}, u32[]{:S(2)}, u32[]{:S(2)}) collective-permute-start(f32[16,8,128]{2,1,0:T(8,128)S(1)} %get-tuple-element.83.refs_0_), channel_id=1, source_target_pairs={{0,3},{1,2},{2,1},{3,0},{4,7},{5,6},{6,5},{7,4},{8,11},{9,10},{10,... | collective-permute-start | bytes 196616 | tf_op jit(solution)/shard_map/ppermute | solution.py:572
